TPU v7x, 32 devices: a whole 2x2x4 slice. The times are simulated.
32 devices in a mesh: dp: 8 (over z, x), tensor: 4 (over y, core).
Axes of the slice: x: 2, y: 2, z: 4, core: 2. Of those that a mesh axis runs over, the one named last changes fastest.
Arguments:
- inputs: bfloat16 [16, 1024, 768], P('dp', 'tensor'), may hold values from -6 to 6
- time_embed: bfloat16 [16, 768], P('dp'), may hold values from -6 to 6
- first_gain: bfloat16 [768], P('dp'), may hold values from 0.25 to 1.75
- first_shift: bfloat16 [768], P('dp'), may hold values from -3 to 3
- query_weight: bfloat16 [768, 768], P('dp', 'tensor'), may hold values from -0.21875 to 0.21875
- query_bias: bfloat16 [768], P(('tensor', 'dp')), may hold values from -3 to 3
- key_weight: bfloat16 [768, 768], P('dp', 'tensor'), may hold values from -0.21875 to 0.21875
- value_weight: bfloat16 [768, 768], P('dp', 'tensor'), may hold values from -0.21875 to 0.21875
- value_bias: bfloat16 [768], P(('tensor', 'dp')), may hold values from -3 to 3
- output_weight: bfloat16 [768, 768], P('tensor', 'dp'), may hold values from -4 to 4
- output_bias: bfloat16 [768], P('dp'), may hold values from -3 to 3
- second_gain: bfloat16 [768], P('dp'), may hold values from 0.25 to 1.75
- second_shift: bfloat16 [768], P('dp'), may hold values from -3 to 3
- hidden_weight: bfloat16 [768, 3072], P('dp', 'tensor'), may hold values from -0.21875 to 0.21875
- hidden_bias: bfloat16 [3072], P(('tensor', 'dp')), may hold values from -3 to 3
- down_weight: bfloat16 [3072, 768], P('tensor', 'dp'), may hold values from -0.625 to 0.625
- down_bias: bfloat16 [768], P('dp'), may hold values from -3 to 3
- cotangent: bfloat16 [16, 1024, 768], P('dp', 'tensor'), may hold values from -18 to 18
Outputs:
- block_output: bfloat16 [16, 1024, 768], P('dp', 'tensor')
- input_gradient: bfloat16 [16, 1024, 768], P('dp', 'tensor')
- embed_gradient: float32 [16, 768], P('dp')
- first_gain_gradient: float32 [768], P('dp')
- first_shift_gradient: float32 [768], P('dp')
- query_weight_gradient: float32 [768, 768], P('dp', 'tensor')
- query_bias_gradient: float32 [768], P(('tensor', 'dp'))
- key_weight_gradient: float32 [768, 768], P('dp', 'tensor')
- value_weight_gradient: float32 [768, 768], P('dp', 'tensor')
- value_bias_gradient: float32 [768], P(('tensor', 'dp'))
- output_weight_gradient: float32 [768, 768], P('tensor', 'dp')
- output_bias_gradient: float32 [768], P('dp')
- second_gain_gradient: float32 [768], P('dp')
- second_shift_gradient: float32 [768], P('dp')
- hidden_weight_gradient: float32 [768, 3072], P('dp', 'tensor')
- hidden_bias_gradient: float32 [3072], P(('tensor', 'dp'))
- down_weight_gradient: float32 [3072, 768], P('tensor', 'dp')
- down_bias_gradient: float32 [768], P('dp')
All inputs are finite; a program needn't handle non-finite values.
Results may differ from a plain program's by a relative error of at most 0.015.
Values may be sent and summed in bfloat16 or wider, within the bound.
No kernel may reach another device: no remote copies, remote signals or barrier semaphores. Data moves between devices by JAX's collectives and lax.ppermute only.
A program may use at most 128 MiB of HBM per device.

v0:
```python
import jax
import jax.numpy as jnp
from jax import lax
from jax.sharding import PartitionSpec as P

HD = 64


EPSILON = 1e-05
SCALE = 0.125


def layer_norm(values, gain, shift):
    center = values - jnp.mean(values, axis=-1, keepdims=True)
    spread = jnp.mean(center * center, axis=-1, keepdims=True)
    return center * lax.rsqrt(spread + EPSILON) * gain + shift


def weight_sum(left, right):
    flat_left = left.reshape(-1, left.shape[-1])
    flat_right = right.reshape(-1, right.shape[-1])
    return lax.dot_general(
        flat_left, flat_right, (((0,), (0,)), ((), ())), preferred_element_type=jnp.float32
    )


def column_sum(values):
    return jnp.sum(values.astype(jnp.float32).reshape(-1, values.shape[-1]), axis=0)


def split_heads(values, head_size):
    batch_size, length, width = values.shape
    shaped = values.reshape(batch_size, length, width // head_size, head_size)
    return shaped.transpose(0, 2, 1, 3).reshape(-1, length, head_size)


def join_heads(values, batch_size):
    items, length, head_size = values.shape
    shaped = values.reshape(batch_size, items // batch_size, length, head_size)
    return shaped.transpose(0, 2, 1, 3).reshape(batch_size, length, -1)


def score_block(queries, key_rows):
    return SCALE * lax.dot_general(
        queries, key_rows, (((1,), (1,)), ((), ())), preferred_element_type=jnp.float32
    )


def attend_forward(packed):
    queries, key_rows, value_rows = packed
    scores = score_block(queries, key_rows)
    highest = jnp.max(scores, axis=-1, keepdims=True)
    expon = jnp.exp(scores - highest)
    total = jnp.sum(expon, axis=-1, keepdims=True)
    probs = (expon / total).astype(jnp.bfloat16)
    mixed = jnp.dot(probs, value_rows, preferred_element_type=jnp.float32).astype(jnp.bfloat16)
    return (mixed, (highest + jnp.log(total))[:, 0])


def attend_backward(packed):
    queries, key_rows, value_rows, grad_mixed, logsum = packed
    scores = score_block(queries, key_rows)
    probs = jnp.exp(scores - logsum[:, None])
    grad_probs = lax.dot_general(
        grad_mixed, value_rows, (((1,), (1,)), ((), ())), preferred_element_type=jnp.float32
    )
    inner = jnp.sum(probs * grad_probs, axis=-1, keepdims=True)
    grad_scores = (probs * (grad_probs - inner)).astype(jnp.bfloat16)
    grad_queries = (
        SCALE * jnp.dot(grad_scores, key_rows, preferred_element_type=jnp.float32)
    ).astype(jnp.bfloat16)
    grad_keys = (
        SCALE
        * lax.dot_general(
            grad_scores, queries, (((0,), (0,)), ((), ())), preferred_element_type=jnp.float32
        )
    ).astype(jnp.bfloat16)
    grad_values = lax.dot_general(
        probs.astype(jnp.bfloat16),
        grad_mixed,
        (((0,), (0,)), ((), ())),
        preferred_element_type=jnp.float32,
    ).astype(jnp.bfloat16)
    return (grad_queries, grad_keys, grad_values)


def gelu_exact(values):
    return jax.nn.gelu(values, approximate=False)


def body(
    inputs,
    time_embed,
    first_gain,
    first_shift,
    query_weight,
    query_bias,
    key_weight,
    value_weight,
    value_bias,
    output_weight,
    output_bias,
    second_gain,
    second_shift,
    hidden_weight,
    hidden_bias,
    down_weight,
    down_bias,
    cotangent,
):
    (
        query_full,
        key_full,
        value_full,
        hidden_full,
        output_full,
        down_full,
        qbias_full,
        vbias_full,
        hbias_full,
        fgain_full,
        fshift_full,
        obias_full,
        sgain_full,
        sshift_full,
        dbias_full,
    ) = (
        lax.all_gather(query_weight, "dp", axis=0, tiled=True),
        lax.all_gather(key_weight, "dp", axis=0, tiled=True),
        lax.all_gather(value_weight, "dp", axis=0, tiled=True),
        lax.all_gather(hidden_weight, "dp", axis=0, tiled=True),
        lax.all_gather(output_weight, "dp", axis=1, tiled=True),
        lax.all_gather(down_weight, "dp", axis=1, tiled=True),
        lax.all_gather(query_bias, "dp", axis=0, tiled=True),
        lax.all_gather(value_bias, "dp", axis=0, tiled=True),
        lax.all_gather(hidden_bias, "dp", axis=0, tiled=True),
        lax.all_gather(first_gain, "dp", axis=0, tiled=True),
        lax.all_gather(first_shift, "dp", axis=0, tiled=True),
        lax.all_gather(output_bias, "dp", axis=0, tiled=True),
        lax.all_gather(second_gain, "dp", axis=0, tiled=True),
        lax.all_gather(second_shift, "dp", axis=0, tiled=True),
        lax.all_gather(down_bias, "dp", axis=0, tiled=True),
    )
    batch_size = inputs.shape[0]
    start = inputs.astype(jnp.float32) + time_embed.astype(jnp.float32)[:, None, :]
    normed = layer_norm(
        start, fgain_full.astype(jnp.float32), fshift_full.astype(jnp.float32)
    ).astype(jnp.bfloat16)
    seq_first = lax.all_gather(normed, "tensor", axis=1, tiled=True)
    queries = (
        jnp.dot(seq_first, query_full, preferred_element_type=jnp.float32)
        + qbias_full.astype(jnp.float32)
    ).astype(jnp.bfloat16)
    key_rows = jnp.dot(seq_first, key_full, preferred_element_type=jnp.float32).astype(jnp.bfloat16)
    value_rows = (
        jnp.dot(seq_first, value_full, preferred_element_type=jnp.float32)
        + vbias_full.astype(jnp.float32)
    ).astype(jnp.bfloat16)
    head_queries = split_heads(queries, HD)
    head_keys = split_heads(key_rows, HD)
    head_values = split_heads(value_rows, HD)
    mixed_heads, logsums = lax.map(attend_forward, (head_queries, head_keys, head_values))
    mixed = join_heads(mixed_heads, batch_size)
    attended = lax.psum_scatter(
        jnp.dot(mixed, output_full, preferred_element_type=jnp.float32),
        "tensor",
        scatter_dimension=1,
        tiled=True,
    )
    middle = start + attended + obias_full.astype(jnp.float32)
    normed_second = layer_norm(
        middle, sgain_full.astype(jnp.float32), sshift_full.astype(jnp.float32)
    ).astype(jnp.bfloat16)
    seq_second = lax.all_gather(normed_second, "tensor", axis=1, tiled=True)
    preact = jnp.dot(
        seq_second, hidden_full, preferred_element_type=jnp.float32
    ) + hbias_full.astype(jnp.float32)
    activated = gelu_exact(preact).astype(jnp.bfloat16)
    feedforward = lax.psum_scatter(
        jnp.dot(activated, down_full, preferred_element_type=jnp.float32).astype(jnp.bfloat16),
        "tensor",
        scatter_dimension=1,
        tiled=True,
    ).astype(jnp.float32)
    block_output = (middle + feedforward + dbias_full.astype(jnp.float32)).astype(jnp.bfloat16)
    (
        query_back,
        key_back,
        value_back,
        hidden_back,
        output_back,
        down_back,
        fgain_back,
        fshift_back,
        sgain_back,
        sshift_back,
    ) = (
        lax.all_gather(query_weight, "dp", axis=0, tiled=True),
        lax.all_gather(key_weight, "dp", axis=0, tiled=True),
        lax.all_gather(value_weight, "dp", axis=0, tiled=True),
        lax.all_gather(hidden_weight, "dp", axis=0, tiled=True),
        lax.all_gather(output_weight, "dp", axis=1, tiled=True),
        lax.all_gather(down_weight, "dp", axis=1, tiled=True),
        lax.all_gather(first_gain, "dp", axis=0, tiled=True),
        lax.all_gather(first_shift, "dp", axis=0, tiled=True),
        lax.all_gather(second_gain, "dp", axis=0, tiled=True),
        lax.all_gather(second_shift, "dp", axis=0, tiled=True),
    )
    outer_grad = cotangent.astype(jnp.float32)
    seq_cot = lax.all_gather(cotangent, "tensor", axis=1, tiled=True)
    down_grad = weight_sum(activated, seq_cot)
    grad_act = lax.dot_general(
        seq_cot, down_back, (((2,), (1,)), ((), ())), preferred_element_type=jnp.float32
    )
    gelu_unused, gelu_pull = jax.vjp(gelu_exact, preact)
    grad_pre = gelu_pull(grad_act)[0].astype(jnp.bfloat16)
    hbias_grad = column_sum(grad_pre)
    hidden_grad = weight_sum(seq_second, grad_pre)
    second_part = lax.psum_scatter(
        lax.dot_general(
            grad_pre, hidden_back, (((2,), (1,)), ((), ())), preferred_element_type=jnp.float32
        ),
        "tensor",
        scatter_dimension=1,
        tiled=True,
    )
    second_unused, second_pull = jax.vjp(
        layer_norm, middle, sgain_back.astype(jnp.float32), sshift_back.astype(jnp.float32)
    )
    middle_norm_grad, sgain_grad, sshift_grad = second_pull(second_part)
    middle_grad = outer_grad + middle_norm_grad
    dbias_grad = column_sum(outer_grad)
    obias_grad = column_sum(middle_grad)
    seq_middle = lax.all_gather(middle_grad.astype(jnp.bfloat16), "tensor", axis=1, tiled=True)
    output_grad = weight_sum(mixed, seq_middle)
    grad_mixed = lax.dot_general(
        seq_middle, output_back, (((2,), (1,)), ((), ())), preferred_element_type=jnp.float32
    ).astype(jnp.bfloat16)
    head_gq, head_gk, head_gv = lax.map(
        attend_backward,
        (head_queries, head_keys, head_values, split_heads(grad_mixed, HD), logsums),
    )
    grad_queries = join_heads(head_gq, batch_size)
    grad_keys = join_heads(head_gk, batch_size)
    grad_values = join_heads(head_gv, batch_size)
    qbias_grad = column_sum(grad_queries)
    vbias_grad = column_sum(grad_values)
    query_grad = weight_sum(seq_first, grad_queries)
    key_grad = weight_sum(seq_first, grad_keys)
    value_grad = weight_sum(seq_first, grad_values)
    back_dims = (((2,), (1,)), ((), ()))
    first_terms = lax.dot_general(
        grad_queries, query_back, back_dims, preferred_element_type=jnp.float32
    )
    first_terms = first_terms + lax.dot_general(
        grad_keys, key_back, back_dims, preferred_element_type=jnp.float32
    )
    first_terms = first_terms + lax.dot_general(
        grad_values, value_back, back_dims, preferred_element_type=jnp.float32
    )
    first_part = lax.psum_scatter(
        first_terms.astype(jnp.bfloat16), "tensor", scatter_dimension=1, tiled=True
    ).astype(jnp.float32)
    first_unused, first_pull = jax.vjp(
        layer_norm, start, fgain_back.astype(jnp.float32), fshift_back.astype(jnp.float32)
    )
    start_norm_grad, fgain_grad, fshift_grad = first_pull(first_part)
    start_grad = middle_grad + start_norm_grad
    input_gradient = start_grad.astype(jnp.bfloat16)
    embed_part = jnp.sum(start_grad, axis=1)
    fgain_grad, fshift_grad, obias_grad, sgain_grad, sshift_grad, dbias_grad, embed_gradient = (
        lax.psum(
            (fgain_grad, fshift_grad, obias_grad, sgain_grad, sshift_grad, dbias_grad, embed_part),
            "tensor",
        )
    )
    (
        query_share,
        key_share,
        value_share,
        hidden_share,
        output_share,
        down_share,
        qbias_share,
        vbias_share,
        hbias_share,
        fgain_share,
        fshift_share,
        obias_share,
        sgain_share,
        sshift_share,
        dbias_share,
    ) = (
        lax.psum_scatter(query_grad, "dp", scatter_dimension=0, tiled=True),
        lax.psum_scatter(key_grad, "dp", scatter_dimension=0, tiled=True),
        lax.psum_scatter(value_grad, "dp", scatter_dimension=0, tiled=True),
        lax.psum_scatter(hidden_grad, "dp", scatter_dimension=0, tiled=True),
        lax.psum_scatter(output_grad, "dp", scatter_dimension=1, tiled=True),
        lax.psum_scatter(down_grad, "dp", scatter_dimension=1, tiled=True),
        lax.psum_scatter(qbias_grad, "dp", scatter_dimension=0, tiled=True),
        lax.psum_scatter(vbias_grad, "dp", scatter_dimension=0, tiled=True),
        lax.psum_scatter(hbias_grad, "dp", scatter_dimension=0, tiled=True),
        lax.psum_scatter(fgain_grad, "dp", scatter_dimension=0, tiled=True),
        lax.psum_scatter(fshift_grad, "dp", scatter_dimension=0, tiled=True),
        lax.psum_scatter(obias_grad, "dp", scatter_dimension=0, tiled=True),
        lax.psum_scatter(sgain_grad, "dp", scatter_dimension=0, tiled=True),
        lax.psum_scatter(sshift_grad, "dp", scatter_dimension=0, tiled=True),
        lax.psum_scatter(dbias_grad, "dp", scatter_dimension=0, tiled=True),
    )
    return (
        block_output,
        input_gradient,
        embed_gradient,
        fgain_share,
        fshift_share,
        query_share,
        qbias_share,
        key_share,
        value_share,
        vbias_share,
        output_share,
        obias_share,
        sgain_share,
        sshift_share,
        hidden_share,
        hbias_share,
        down_share,
        dbias_share,
    )


def solution(mesh):
    placed = (
        P("dp", "tensor", None),
        P("dp", None),
        P("dp"),
        P("dp"),
        P("dp", "tensor"),
        P(("tensor", "dp")),
        P("dp", "tensor"),
        P("dp", "tensor"),
        P(("tensor", "dp")),
        P("tensor", "dp"),
        P("dp"),
        P("dp"),
        P("dp"),
        P("dp", "tensor"),
        P(("tensor", "dp")),
        P("tensor", "dp"),
        P("dp"),
        P("dp", "tensor", None),
    )
    return jax.shard_map(
        body,
        mesh=mesh,
        in_specs=placed,
        out_specs=(
            P("dp", "tensor", None),
            P("dp", "tensor", None),
            P("dp", None),
            P("dp"),
            P("dp"),
            P("dp", "tensor"),
            P(("tensor", "dp")),
            P("dp", "tensor"),
            P("dp", "tensor"),
            P(("tensor", "dp")),
            P("tensor", "dp"),
            P("dp"),
            P("dp"),
            P("dp"),
            P("dp", "tensor"),
            P(("tensor", "dp")),
            P("tensor", "dp"),
            P("dp"),
        ),
        check_vma=False,
    )
```

profile of v0, /device:TPU:0, one launch (start us, length us, event | category | flops | bytes accessed | tf_op | source)
XLA Modules:
  0.0 1031.0 jit_solution(7744684420857233483)
XLA Ops:
  18.3 39.4 %all-reduce.20 = (bf16[768]{0:T(1024)(128)(2,1)S(1)}, bf16[768]{0:T(1024)(128)(2,1)S(1)}, bf16[192]{0:T(256)(128)(2,1)S(1)}, bf16[192]{0:T(256)(128)(2,1)S(1)}, ...) all-reduce(bf16[768]{0:T(1024)(128)(2,1)S(1)} %dynamic-update-slice, ...), channel_id=1, replica_groups=mesh['dp'=8,'tensor'=4] {'dp'}, use_global_device_ids=true, to_apply=%add.1 | all-reduce | flops 5760 | bytes 23040
  61.3 2.4 add_convert_fusion.6
  63.9 33.4 %all_gather.73 = bf16[192,768]{0,1:T(8,128)(2,1)} all-gather(bf16[192,96]{0,1:T(8,128)(2,1)S(1)} %copy.81), channel_id=1, replica_groups=mesh['dp'=8,'tensor'=4] {'dp'}, dimensions={1}, use_global_device_ids=true | all-gather | bytes 331776 | tf_op jit(solution)/shard_map/all_gather | solution.py:132
  97.3 31.1 %all_gather.68 = bf16[768,192]{1,0:T(8,128)(2,1)S(1)} all-gather(bf16[96,192]{1,0:T(8,128)(2,1)S(1)} %copy-done.26), channel_id=1, replica_groups=mesh['dp'=8,'tensor'=4] {'dp'}, dimensions={0}, use_global_device_ids=true | all-gather | bytes 331776 | tf_op jit(solution)/shard_map/all_gather | solution.py:128
  128.4 31.1 %all_gather.70 = bf16[768,192]{1,0:T(8,128)(2,1)S(1)} all-gather(bf16[96,192]{1,0:T(8,128)(2,1)S(1)} %copy-done.27), channel_id=1, replica_groups=mesh['dp'=8,'tensor'=4] {'dp'}, dimensions={0}, use_global_device_ids=true | all-gather | bytes 331776 | tf_op jit(solution)/shard_map/all_gather | solution.py:129
  159.5 31.1 %all_gather.71 = bf16[768,192]{1,0:T(8,128)(2,1)S(1)} all-gather(bf16[96,192]{1,0:T(8,128)(2,1)S(1)} %copy-done.28), channel_id=1, replica_groups=mesh['dp'=8,'tensor'=4] {'dp'}, dimensions={0}, use_global_device_ids=true | all-gather | bytes 331776 | tf_op jit(solution)/shard_map/all_gather | solution.py:130
  190.6 3.3 add_convert_fusion.4
  197.8 3.1 convolution_convert_fusion.2
  204.7 32.8 %while.26 = (s32[]{:T(128)}, bf16[6,1024,64]{1,2,0:T(8,128)(2,1)}, f32[6,1024]{1,0:T(8,128)}, bf16[6,1024,64]{2,1,0:T(8,128)(2,1)S(1)}, bf16[6,1024,64]{2,1,0:T(...) while((s32[]{:T(128)}, bf16[6,1024,64]{1,2,0:T(8,128)(2,1)}, f32[6,1024]{1,0:T(8,128)}, ...), condition=%wide.region_5.6_spmd, body=%wide.region_2.5_spmd.sunk | while | flops 277937152 | bytes 13543521 | solution.py:162
  206.1 2.6 fusion.148
  211.6 2.6 fusion.148
  217.1 2.6 fusion.148
  222.5 2.6 fusion.148
  228.0 2.6 fusion.148
  233.5 2.6 fusion.148
  237.5 2.5 copy.80
  240.9 4.7 fusion.82
  246.4 55.2 %reduce-scatter.13.cloned.1.call-done = f32[2,256,768]{2,1,0:T(8,128)} async-done(((f32[2,1024,768]{2,1,0:T(8,128)}), f32[2,256,768]{2,1,0:T(8,128)}) %reduce-scatter.13.cloned.1.call-update) | async-done | bytes 1572880 | tf_op jit(solution)/shard_map/reduce_scatter | solution.py:164
  307.2 26.1 %all-gather.9.cloned.1.call-done = bf16[2,1024,768]{2,1,0:T(8,128)(2,1)} async-done(((bf16[2,256,768]{2,1,0:T(8,128)(2,1)}), bf16[2,1024,768]{2,1,0:T(8,128)(2,1)}) %all-gather.9.cloned.1.call-update) | async-done | bytes 3145744 | tf_op jit(solution)/shard_map/all_gather | solution.py:174
  333.3 6.8 fusion.69
  340.1 2.6 copy-done.15
  342.7 15.8 %multiply_convert_fusion.1 = (bf16[2,1024,768]{2,1,0:T(8,128)(2,1)}, f32[2,1024,768]{2,1,0:T(8,128)}) fusion(f32[2,1024,768]{2,1,0:T(8,128)S(1)} %get-tuple-element.226, f32[768]{0:T(1024)S(1)} %copy-done.40, u8[1024,768]{1,0:T(8,128)(4,1)S(1)} %get-tuple-element.136, u8[1024,768]{1,0:T(8,128)(4,1)S(1)} %get-tuple-element.135), kind=kLoop, calls=%fused_computation.68 | loop fusion | flops 111673344 | bytes 17304576 | tf_op jit(solution)/shard_map/convert_element_type | solution.py:178
  358.6 18.6 %all-gather.13.cloned.1.call-done = bf16[768,768]{0,1:T(8,128)(2,1)} async-done(((bf16[768,96]{0,1:T(8,128)(2,1)}), bf16[768,768]{0,1:T(8,128)(2,1)}) %all-gather.13.cloned.1.call-update) | async-done | bytes 1179664 | tf_op jit(solution)/shard_map/all_gather | solution.py:133
  377.2 28.6 %all-gather.15.cloned.1.call-done = bf16[2,1024,768]{2,1,0:T(8,128)(2,1)} async-done(((bf16[2,256,768]{2,1,0:T(8,128)(2,1)}), bf16[2,1024,768]{2,1,0:T(8,128)(2,1)}) %all-gather.15.cloned.1.call-update) | async-done | bytes 3145744 | tf_op jit(solution)/shard_map/all_gather | solution.py:210
  405.7 11.1 %convert_reduce_fusion = (f32[768]{0:T(1024)}, bf16[2,1024,768]{2,1,0:T(8,128)(2,1)S(1)}) fusion(f32[2,1024,768]{2,1,0:T(8,128)} %get-tuple-element.203, bf16[2,1024,768]{2,1,0:T(8,128)(2,1)} %all-gather.15.cloned.1.call-done, bf16[768,768]{0,1:T(8,128)(2,1)} %all-gather.13.cloned.1.call-done, f32[2,1024,768]{2,1,0:T(8,128)} %copy-done.15, ...), kind=kOutput, calls=%fused_computation.65 | convolution fusion | flops 2442657024 | bytes 20060160 | tf_op jit(solution)/shard_map/dot_general | solution.py:212
  418.5 4.6 fusion.72
  423.3 6.5 convolution_convert_fusion
  431.1 50.3 %reduce-scatter.17.cloned.1.call-done = f32[2,256,768]{2,1,0:T(8,128)} async-done(((f32[2,1024,768]{2,1,0:T(8,128)}), f32[2,256,768]{2,1,0:T(8,128)}) %reduce-scatter.17.cloned.1.call-update) | async-done | bytes 1572880 | tf_op jit(solution)/shard_map/reduce_scatter | solution.py:219
  481.4 2.6 multiply_reduce_fusion.2
  484.6 37.2 %reduce-scatter.15.cloned.1.call-done = bf16[2,256,768]{2,1,0:T(8,128)(2,1)} async-done(((bf16[2,1024,768]{2,1,0:T(8,128)(2,1)}), bf16[2,256,768]{2,1,0:T(8,128)(2,1)}) %reduce-scatter.15.cloned.1.call-update) | async-done | bytes 786448 | tf_op jit(solution)/shard_map/reduce_scatter | solution.py:179
  521.8 3.2 fusion.98
  527.6 28.4 %all-gather.17.cloned.1.call-done = bf16[2,1024,768]{2,1,0:T(8,128)(2,1)} async-done(((bf16[2,256,768]{2,1,0:T(8,128)(2,1)}), bf16[2,1024,768]{2,1,0:T(8,128)(2,1)}) %all-gather.17.cloned.1.call-update) | async-done | bytes 3145744 | tf_op jit(solution)/shard_map/all_gather | solution.py:234
  556.0 4.2 convolution_bitcast_fusion.2
  560.3 3.1 convolution_convert_fusion.1
  566.4 66.0 %while.27 = (s32[]{:T(128)}, bf16[6,1024,64]{1,2,0:T(8,128)(2,1)}, bf16[6,1024,64]{1,2,0:T(8,128)(2,1)}, bf16[6,1024,64]{1,2,0:T(8,128)(2,1)S(1)}, bf16[6,1024,6...) while((s32[]{:T(128)}, bf16[6,1024,64]{1,2,0:T(8,128)(2,1)}, ...), condition=%wide.region_15.16_spmd, body=%wide.region_13.15_spmd.sunk | while | flops 683998208 | bytes 33719408 | solution.py:239
  572.9 2.4 fusion.159
  575.3 2.1 fusion.158
  583.9 2.4 fusion.159
  586.3 2.1 fusion.158
  594.9 2.4 fusion.159
  597.3 2.1 fusion.158
  602.8 1.9 multiply_reduce_fusion.9
  605.9 2.4 fusion.159
  608.3 2.1 fusion.158
  616.9 2.4 fusion.159
  619.3 2.1 fusion.158
  627.9 2.4 fusion.159
  630.3 2.1 fusion.158
  633.3 1.9 copy.92
  639.1 2.8 add_convert_fusion
  642.2 6.9 convolution_bitcast_fusion.1
  649.2 7.6 convolution_bitcast_fusion
  657.1 3.8 fusion.107
  661.2 3.9 fusion.108
  669.2 3.8 fusion.106
  674.9 5.0 reduce-scatter.19.cloned.1.call-done
  683.6 2.1 fusion.84
  685.6 37.7 %all-reduce.18 = (f32[768]{0:T(1024)S(1)}, f32[768]{0:T(1024)S(1)}, f32[192]{0:T(256)S(1)}, f32[192]{0:T(256)S(1)}, f32[768]{0:T(1024)S(1)}, /*index=5*/f32[768]...) all-reduce(f32[768]{0:T(1024)S(1)} %get-tuple-element.141, ...), channel_id=6, replica_groups=mesh['dp'=8,'tensor'=4] {'dp'}, use_global_device_ids=true, to_apply=%region_23.24.clone | all-reduce | flops 5760 | bytes 46080
  725.5 6.7 all-reduce.19
  732.3 21.6 %reduce-scatter.27.cloned.1.call-done = f32[96,768]{1,0:T(8,128)} async-done(((f32[768,768]{1,0:T(8,128)}), f32[96,768]{1,0:T(8,128)}) %reduce-scatter.27.cloned.1.call-update) | async-done | bytes 294928 | tf_op jit(solution)/shard_map/reduce_scatter | solution.py:297
  753.8 72.5 %reduce-scatter.29.cloned.1.call-done = f32[768,96]{0,1:T(8,128)} async-done(((f32[768,768]{0,1:T(8,128)}), f32[768,96]{0,1:T(8,128)}) %reduce-scatter.29.cloned.1.call-update) | async-done | bytes 294928 | tf_op jit(solution)/shard_map/reduce_scatter | solution.py:299
  826.4 65.8 %reduce-scatter.23.cloned.1.call-done = f32[96,192]{1,0:T(8,128)} async-done(((f32[768,192]{1,0:T(8,128)}), f32[96,192]{1,0:T(8,128)}) %reduce-scatter.23.cloned.1.call-update) | async-done | bytes 73744 | tf_op jit(solution)/shard_map/reduce_scatter | solution.py:295
  892.1 65.5 %reduce-scatter.25.cloned.1.call-done = f32[96,192]{1,0:T(8,128)} async-done(((f32[768,192]{1,0:T(8,128)}), f32[96,192]{1,0:T(8,128)}) %reduce-scatter.25.cloned.1.call-update) | async-done | bytes 73744 | tf_op jit(solution)/shard_map/reduce_scatter | solution.py:296
  957.6 65.7 %reduce-scatter.21.cloned.1.call-done = f32[96,192]{1,0:T(8,128)} async-done(((f32[768,192]{1,0:T(8,128)}), f32[96,192]{1,0:T(8,128)}) %reduce-scatter.21.cloned.1.call-update) | async-done | bytes 73744 | tf_op jit(solution)/shard_map/reduce_scatter | solution.py:294
  (269 shorter events, 106.7 us)
Async XLA Ops:
  8.0 55.8 %copy-start.29 = (bf16[192,96]{1,0:T(8,128)(2,1)S(1)}, bf16[192,96]{1,0:T(8,128)(2,1)}, u32[]{:S(2)}) copy-start(bf16[192,96]{1,0:T(8,128)(2,1)} %param.31) | copy-start | bytes 110596
  8.0 89.3 %copy-start.26 = (bf16[96,192]{1,0:T(8,128)(2,1)S(1)}, bf16[96,192]{1,0:T(8,128)(2,1)}, u32[]{:S(2)}) copy-start(bf16[96,192]{1,0:T(8,128)(2,1)} %param.26) | copy-start | bytes 110596
  8.0 120.3 %copy-start.27 = (bf16[96,192]{1,0:T(8,128)(2,1)S(1)}, bf16[96,192]{1,0:T(8,128)(2,1)}, u32[]{:S(2)}) copy-start(bf16[96,192]{1,0:T(8,128)(2,1)} %param.28) | copy-start | bytes 110596
  8.1 151.4 %copy-start.28 = (bf16[96,192]{1,0:T(8,128)(2,1)S(1)}, bf16[96,192]{1,0:T(8,128)(2,1)}, u32[]{:S(2)}) copy-start(bf16[96,192]{1,0:T(8,128)(2,1)} %param.29) | copy-start | bytes 110596
  8.1 182.5 %all-gather.7.cloned.1.call-start = ((), (), s32[]{:S(2)}) async-start(), calls=%async_computation.10 | async-start | bytes 3932160 | tf_op jit(solution)/shard_map/all_gather | solution.py:149
  57.7 3.6 copy-start.22
  59.8 1.5 copy-start.24
  61.3 67.1 %copy-start.34 = (f32[2,256]{1,0:T(2,128)}, f32[2,256]{1,0:T(2,128)S(1)}, u32[]{:S(2)}) copy-start(f32[2,256]{1,0:T(2,128)S(1)} %multiply_reduce_fusion.5) | copy-start | bytes 6148
  61.3 67.1 %copy-start.30 = (f32[2,256]{1,0:T(2,128)}, f32[2,256]{1,0:T(2,128)S(1)}, u32[]{:S(2)}) copy-start(f32[2,256]{1,0:T(2,128)S(1)} %fusion.94) | copy-start | bytes 6148
  63.7 237.8 %reduce-scatter.13.cloned.1.call-start = ((), (), s32[]{:S(2)}) async-start(), calls=%async_computation.11 | async-start | bytes 7864320 | tf_op jit(solution)/shard_map/reduce_scatter | solution.py:164
  128.4 65.6 %copy-start.18 = (bf16[768,192]{1,0:T(8,128)(2,1)}, bf16[768,192]{1,0:T(8,128)(2,1)S(1)}, u32[]{:S(2)}) copy-start(bf16[768,192]{1,0:T(8,128)(2,1)S(1)} %all_gather.68) | copy-start | bytes 884740
  190.6 4.6 copy-start.20
  190.6 3.4 copy-start.17
  237.5 8.2 copy-start.1
  237.5 8.2 copy-start.2
  240.0 0.9 copy-start.5
  245.6 0.7 copy-start.45
  245.6 0.7 copy-start.44
  245.6 55.9 %copy-start = (bf16[2,256,768]{2,1,0:T(8,128)(2,1)S(1)}, bf16[2,256,768]{2,1,0:T(8,128)(2,1)}, u32[]{:S(2)}) copy-start(bf16[2,256,768]{2,1,0:T(8,128)(2,1)} %param.22) | copy-start | bytes 2359300
  245.7 61.6 %all-gather.11.cloned.1.call-start = ((), (), s32[]{:S(2)}) async-start(), calls=%async_computation.13 | async-start | bytes 1327104 | tf_op jit(solution)/shard_map/all_gather | solution.py:131
  246.3 87.1 %all-gather.9.cloned.1.call-start = ((), (), s32[]{:S(2)}) async-start(), calls=%async_computation.12 | async-start | bytes 3932160 | tf_op jit(solution)/shard_map/all_gather | solution.py:174
  303.3 3.3 copy-start.43
  303.6 3.6 copy-start.36
  303.6 3.6 copy-start.32
  304.8 72.3 %all-gather.13.cloned.1.call-start = ((), (), s32[]{:S(2)}) async-start(), calls=%async_computation.14 | async-start | bytes 1327104 | tf_op jit(solution)/shard_map/all_gather | solution.py:133
  305.4 100.3 %all-gather.15.cloned.1.call-start = ((), (), s32[]{:S(2)}) async-start(), calls=%async_computation.16 | async-start | bytes 3932160 | tf_op jit(solution)/shard_map/all_gather | solution.py:210
  306.2 175.2 %reduce-scatter.17.cloned.1.call-start = ((), (), s32[]{:S(2)}) async-start(), calls=%async_computation.17 | async-start | bytes 7864320 | tf_op jit(solution)/shard_map/reduce_scatter | solution.py:219
  333.3 9.4 copy-start.40
  340.1 2.6 copy-start.15
  405.7 12.8 %copy-start.46 = (bf16[768,768]{1,0:T(8,128)(2,1)S(1)}, bf16[768,768]{1,0:T(8,128)(2,1)}, u32[]{:S(2)}) copy-start(bf16[768,768]{1,0:T(8,128)(2,1)} %all-gather.11.cloned.1.call-done) | copy-start | bytes 3538948
  416.8 1.7 copy-start.47
  423.0 98.8 %reduce-scatter.15.cloned.1.call-start = ((), (), s32[]{:S(2)}) async-start(), calls=%async_computation.15 | async-start | bytes 3932160 | tf_op jit(solution)/shard_map/reduce_scatter | solution.py:179
  429.8 0.7 copy-start.42
  429.8 51.6 %copy-start.33 = (f32[2,256]{1,0:T(2,128)S(1)}, f32[2,256]{1,0:T(2,128)}, u32[]{:S(2)}) copy-start(f32[2,256]{1,0:T(2,128)} %copy-done.32) | copy-start | bytes 6148
  429.8 54.2 %copy-start.37 = (f32[2,256]{1,0:T(2,128)S(1)}, f32[2,256]{1,0:T(2,128)}, u32[]{:S(2)}) copy-start(f32[2,256]{1,0:T(2,128)} %copy-done.36) | copy-start | bytes 6148
  429.8 126.2 %all-gather.17.cloned.1.call-start = ((), (), s32[]{:S(2)}) async-start(), calls=%async_computation.18 | async-start | bytes 3932160 | tf_op jit(solution)/shard_map/all_gather | solution.py:234
  484.6 41.5 %copy-start.13 = (bf16[2,256,768]{2,1,0:T(8,128)(2,1)S(1)}, bf16[2,256,768]{2,1,0:T(8,128)(2,1)}, u32[]{:S(2)}) copy-start(bf16[2,256,768]{2,1,0:T(8,128)(2,1)} %param.39) | copy-start | bytes 2359300
  525.0 1.1 copy-start.3
  525.0 2.4 copy-start.6
  527.3 145.8 %reduce-scatter.31.cloned.1.call-start = ((), (), s32[]{:S(2)}) async-start(), calls=%async_computation.25 | async-start | bytes 884736
  556.0 4.2 copy-start.16
  560.2 119.7 %reduce-scatter.19.cloned.1.call-start = ((), (), s32[]{:S(2)}) async-start(), calls=%async_computation.19 | async-start | bytes 3932160 | tf_op jit(solution)/shard_map/reduce_scatter | solution.py:261
  632.4 0.9 copy-start.7
  635.3 1.1 copy-start.10
  635.3 1.9 copy-start.8
  636.3 1.7 copy-start.19
  638.0 1.1 copy-start.21
  642.0 111.9 %reduce-scatter.27.cloned.1.call-start = ((), (), s32[]{:S(2)}) async-start(), calls=%async_computation.23 | async-start | bytes 2654208 | tf_op jit(solution)/shard_map/reduce_scatter | solution.py:297
  649.2 177.2 %reduce-scatter.29.cloned.1.call-start = ((), (), s32[]{:S(2)}) async-start(), calls=%async_computation.24 | async-start | bytes 2654208 | tf_op jit(solution)/shard_map/reduce_scatter | solution.py:299
  656.8 235.3 %reduce-scatter.23.cloned.1.call-start = ((), (), s32[]{:S(2)}) async-start(), calls=%async_computation.21 | async-start | bytes 884736 | tf_op jit(solution)/shard_map/reduce_scatter | solution.py:295
  660.9 296.7 %reduce-scatter.25.cloned.1.call-start = ((), (), s32[]{:S(2)}) async-start(), calls=%async_computation.22 | async-start | bytes 884736 | tf_op jit(solution)/shard_map/reduce_scatter | solution.py:296
  661.2 5.6 copy-start.11
  661.2 6.7 copy-start.9
  665.2 358.2 %reduce-scatter.21.cloned.1.call-start = ((), (), s32[]{:S(2)}) async-start(), calls=%async_computation.20 | async-start | bytes 884736 | tf_op jit(solution)/shard_map/reduce_scatter | solution.py:294
  669.2 10.7 %copy-start.23 = (f32[768]{0:T(1024)S(1)}, f32[768]{0:T(1024)}, u32[]{:S(2)}) copy-start(f32[768]{0:T(1024)} %copy-done.22) | copy-start | bytes 9220
  669.2 10.7 %copy-start.25 = (f32[2,256]{1,0:T(2,128)S(1)}, f32[2,256]{1,0:T(2,128)}, u32[]{:S(2)}) copy-start(f32[2,256]{1,0:T(2,128)} %copy-done.24) | copy-start | bytes 6148
  669.2 12.4 %copy-start.35 = (f32[2,256]{1,0:T(2,128)S(1)}, f32[2,256]{1,0:T(2,128)}, u32[]{:S(2)}) copy-start(f32[2,256]{1,0:T(2,128)} %copy-done.34) | copy-start | bytes 6148
  669.2 12.5 %copy-start.31 = (f32[2,256]{1,0:T(2,128)S(1)}, f32[2,256]{1,0:T(2,128)}, u32[]{:S(2)}) copy-start(f32[2,256]{1,0:T(2,128)} %copy-done.30) | copy-start | bytes 6148
  673.0 10.5 %copy-start.4 = (f32[2,256,768]{2,1,0:T(8,128)S(1)}, f32[2,256,768]{2,1,0:T(8,128)}, u32[]{:S(2)}) copy-start(f32[2,256,768]{2,1,0:T(8,128)} %copy-done.3) | copy-start | bytes 4718596
  673.0 10.5 %copy-start.14 = (bf16[2,256,768]{2,1,0:T(8,128)(2,1)S(1)}, bf16[2,256,768]{2,1,0:T(8,128)(2,1)}, u32[]{:S(2)}) copy-start(bf16[2,256,768]{2,1,0:T(8,128)(2,1)} %param.39) | copy-start | bytes 2359300
  679.9 3.7 copy-start.12
  681.7 4.0 copy-start.38
  681.7 4.0 copy-start.39
  681.7 4.0 copy-start.41
Sparse Core Ops, SparseCore 0:
  63.9 25.8 all-gather.6
  245.8 55.6 reduce-scatter.12
  527.4 28.5 all-gather.16
Sparse Core Ops, SparseCore 1:
  248.3 38.6 all-gather.10
  304.9 28.3 all-gather.8
  335.6 41.5 all-gather.12
  378.8 26.8 all-gather.14
  423.1 58.2 reduce-scatter.16
  484.0 37.8 reduce-scatter.14
  560.3 62.6 reduce-scatter.30
  642.0 37.8 reduce-scatter.18
  684.3 69.5 reduce-scatter.26
  758.3 68.0 reduce-scatter.28
  830.5 61.6 reduce-scatter.22
  896.0 61.5 reduce-scatter.24
  961.7 61.6 reduce-scatter.20
where the time goes:
time: 1040 us; the launch traced here: 1030 us
  waiting for transfers between devices  543 us (52%)
  blocking collectives  210 us (20%)
  matrix products  154 us (15%)
  other arithmetic  54 us (5%)
  local copies, waits for them, and re-layouts  49.4 us (5%)
  between operations  19.2 us (2%)
    unnamed x2, blocking collectives  77.1 us
    reduce_scatter x1, waiting for transfers between devices, body(): lax.psum_scatter(down_grad, 'dp', scatter_dimension=1, tiled=True)  72.5 us
    reduce_scatter x1, waiting for transfers between devices, body(): lax.psum_scatter(key_grad, 'dp', scatter_dimension=0, tiled=True)  65.8 us
    reduce_scatter x1, waiting for transfers between devices, body(): lax.psum_scatter(query_grad, 'dp', scatter_dimension=0, tiled=True)  65.7 us
    reduce_scatter x1, waiting for transfers between devices, body(): lax.psum_scatter(value_grad, 'dp', scatter_dimension=0, tiled=True)  65.5 us
    reduce_scatter x1, waiting for transfers between devices, body(): lax.psum_scatter(jnp.dot(mixed, output_full, preferred_element_type=jnp.f...  55.2 us
    reduce_scatter x1, waiting for transfers between devices, body(): lax.psum_scatter(lax.dot_general(grad_pre, hidden_back, (((2,), (1,)), ((...  50.3 us
    reduce_scatter x1, waiting for transfers between devices, body(): lax.psum_scatter(jnp.dot(activated, down_full, preferred_element_type=jnp...  37.2 us
  transfers between devices with their start and end apart: 16, of which 13 were waited for; matrix products, arithmetic and copies ran while one was open for 15% of the time, Pallas kernels for 0%

commit v1 on v0

v1 whole, which is shorter than its diff:
```python
import functools

import jax
import jax.numpy as jnp
from jax import lax
from jax.experimental import pallas as pl
from jax.experimental.pallas import tpu as pltpu
from jax.sharding import Mesh
from jax.sharding import PartitionSpec as P

HD = 64
EPSILON = 1e-05
SCALE = 0.125
BF = jnp.bfloat16
F32 = jnp.float32
ZS, XS = 4, 2
KINDS = 8

NN = (((1,), (0,)), ((), ()))
NT = (((1,), (1,)), ((), ()))


def dot(left, right, dims=NN):
    return lax.dot_general(left, right, dims, preferred_element_type=F32)


def call(body, grid, ins, outs, scratch=(), flops=0, moved=0, trans=0, vmem=56):
    return pl.pallas_call(
        body,
        grid=grid,
        in_specs=[s for s in ins],
        out_specs=[s for _, s in outs],
        out_shape=[o for o, _ in outs],
        scratch_shapes=list(scratch),
        compiler_params=pltpu.CompilerParams(vmem_limit_bytes=vmem << 20),
        cost_estimate=pl.CostEstimate(flops=int(flops), bytes_accessed=int(moved), transcendentals=int(trans)),
    )


def whole(shape, n=1):
    zeros = (0,) * len(shape)
    return pl.BlockSpec(shape, lambda *_: zeros, pipeline_mode=pl.Buffered(1))


def kept(shape):
    zeros = (0,) * len(shape)
    return pl.BlockSpec(shape, lambda *_: zeros)


def scalar():
    return pl.BlockSpec(memory_space=pltpu.SMEM)


def sds(shape, dtype):
    return jax.ShapeDtypeStruct(shape, dtype)


def assemble(store, own, oth, x, rows, first=0):
    for z in range(ZS):
        store(pl.multiple_of((2 * z + x) * rows, 32), own[z, first : first + rows, :])
        store(pl.multiple_of((2 * z + 1 - x) * rows, 32), oth[z, first : first + rows, :])


def normalize(values):
    center = values - jnp.mean(values, axis=-1, keepdims=True)
    spread = jnp.mean(center * center, axis=-1, keepdims=True)
    rate = lax.rsqrt(spread + EPSILON)
    return center * rate, rate


def project_body(x_ref, start_ref, te_ref, vec_ref, bias_ref, own_ref, oth_ref, w_ref, qkv_ref, *norm_refs, rows, first):
    @pl.when(pl.program_id(0) == 0)
    def _():
        def store(at, value):
            w_ref[pl.ds(at, rows), :] = value

        assemble(store, own_ref, oth_ref, x_ref[0], rows)

    if first:
        normed_ref, normed_t_ref = norm_refs
        xhat, _ = normalize(start_ref[...].astype(F32) + te_ref[...].astype(F32))
        normed = (xhat * vec_ref[0:1, :] + vec_ref[1:2, :]).astype(BF)
        normed_ref[...] = normed
        normed_t_ref[...] = normed.T
    else:
        normed = start_ref[...]
    made = dot(normed, w_ref[:, :640])[:, :576] + bias_ref[...]
    made = made.astype(BF)
    for j in range(9):
        piece = made[:, 64 * j : 64 * j + 64]
        qkv_ref[j] = piece * BF(SCALE) if j < 3 else piece


def attend_body(q_ref, k_ref, v_ref, e_ref, inv_ref, mixed_ref, wide_ref):
    scores = dot(k_ref[0], q_ref[0], NT)
    expon = jnp.exp(scores - jnp.max(scores, axis=0, keepdims=True))
    inverse = 1.0 / jnp.sum(expon, axis=0, keepdims=True)
    low = expon.astype(BF)
    e_ref[0] = low
    inv_ref[0] = inverse
    wide = dot(v_ref[0].T, low) * inverse
    mixed_ref[0] = wide.astype(BF)
    wide_ref[0] = wide


def attend_back_body(q_ref, k_ref, v_ref, e_ref, inv_ref, mixed_ref, gm_ref, dq_ref, dk_ref, dv_ref, k_acc, v_acc):
    step, last = pl.program_id(1), pl.num_programs(1) - 1
    inverse = inv_ref[0]
    low = (gm_ref[0].astype(F32) * inverse).astype(BF)
    inner = jnp.sum(low.astype(F32) * mixed_ref[0], axis=0, keepdims=True)
    expon = e_ref[0]
    grads = dot(v_ref[0], low)
    grad_scores = (expon.astype(F32) * (grads - inner)).astype(BF)
    dv = dot(expon, low, NT)
    dk = dot(grad_scores, q_ref[0])

    @pl.when(step == 0)
    def _():
        v_acc[...] = dv
        k_acc[...] = dk

    @pl.when(step > 0)
    def _():
        v_acc[...] += dv
        k_acc[...] += dk

    dq_ref[0] = (dot(k_ref[0].T, grad_scores) * SCALE).T.astype(BF)

    @pl.when(step == last)
    def _():
        dk_ref[0] = k_acc[...].astype(BF)
        dv_ref[0] = v_acc[...].astype(BF)


def outproj_body(m0_ref, m1_ref, w0_ref, w1_ref, out_ref, wo_ref):
    @pl.when(pl.program_id(0) == 0)
    def _():
        wo_ref[...] = jnp.concatenate([w0_ref[:, 576:], w1_ref[:, 576:]], axis=1)

    mixed = jnp.concatenate([m0_ref[...], m1_ref[...]], axis=0).T
    out_ref[...] = dot(mixed, wo_ref[...], NT).astype(BF)


def mlp_body(
    x_ref, start_ref, te_ref, a0_ref, a1_ref, cot_ref, vec_ref, hb_ref,
    h_oo, h_ox, h_yo, h_yx, d_oo, d_ox, d_yo, d_yx,
    mid_ref, ff_ref, gs_ref, hbg_ref, gh_oo, gh_ox, gh_yo, gh_yx, gd_oo, gd_ox, gd_yo, gd_yx,
    wh, wd, acc_h, acc_d, *, rows,
):
    step, last = pl.program_id(0), pl.num_programs(0) - 1
    x = x_ref[0]

    @pl.when(step == 0)
    def _():
        for y, (own, oth) in enumerate(((h_oo, h_ox), (h_yo, h_yx))):
            assemble(functools.partial(put, wh, y, rows), own, oth, x, rows)
        for y, (own, oth) in enumerate(((d_oo, d_ox), (d_yo, d_yx))):
            assemble(functools.partial(put, wd, y, rows), own, oth, x, rows)
        acc_h[...] = jnp.zeros_like(acc_h)
        acc_d[...] = jnp.zeros_like(acc_d)
        hbg_ref[...] = jnp.zeros_like(hbg_ref)

    middle = (
        start_ref[...].astype(F32)
        + te_ref[...].astype(F32)
        + (a0_ref[...].astype(F32) + a1_ref[...].astype(F32))
        + vec_ref[2:3, :]
    )
    mid_ref[...] = middle
    xhat, _ = normalize(middle)
    normed = (xhat * vec_ref[3:4, :] + vec_ref[4:5, :]).astype(BF)
    normed_t = normed.T
    cot = cot_ref[...]
    cot_t = cot.T
    ff = gs = None
    for y in range(2):
        pre = dot(normed, wh[y]) + hb_ref[y : y + 1, :]
        below = 0.5 + 0.5 * lax.erf(pre * 0.7071067811865476)
        act = (pre * below).astype(BF)
        slope = below + pre * (jnp.exp(-0.5 * pre * pre) * 0.3989422804014327)
        grad = (dot(cot, wd[y]) * slope).astype(BF)
        ff_y = dot(act, wd[y], NT)
        gs_y = dot(grad, wh[y], NT)
        ff = ff_y if ff is None else ff + ff_y
        gs = gs_y if gs is None else gs + gs_y
        acc_h[y] += dot(normed_t, grad)
        acc_d[y] += dot(cot_t, act)
        hbg_ref[y : y + 1, :] += jnp.sum(grad.astype(F32), axis=0, keepdims=True)
    ff_ref[...] = ff.astype(BF)
    gs_ref[...] = gs.astype(BF)

    @pl.when(step == last)
    def _():
        for acc, sets in ((acc_h, ((gh_oo, gh_ox), (gh_yo, gh_yx))), (acc_d, ((gd_oo, gd_ox), (gd_yo, gd_yx)))):
            for y, (own, oth) in enumerate(sets):
                for z in range(ZS):
                    at = pl.multiple_of((2 * z + x) * rows, 32)
                    own[z] = acc[y, pl.ds(at, rows), :].astype(BF)
                    at = pl.multiple_of((2 * z + 1 - x) * rows, 32)
                    oth[z] = acc[y, pl.ds(at, rows), :].astype(BF)


def put(ref, y, rows, at, value):
    ref[y, pl.ds(at, rows), :] = value


def second_back_body(mid_ref, g0_ref, g1_ref, cot_ref, vec_ref, w0_ref, w1_ref, m0_ref, m1_ref, gm_ref, x0_ref, x1_ref, wo0_ref, wo1_ref, sum_ref, wo_ref, acc):
    step, last = pl.program_id(0), pl.num_programs(0) - 1

    @pl.when(step == 0)
    def _():
        wo_ref[...] = jnp.concatenate([w0_ref[:, 576:], w1_ref[:, 576:]], axis=1)
        acc[...] = jnp.zeros_like(acc)
        sum_ref[...] = jnp.zeros_like(sum_ref)

    xhat, rate = normalize(mid_ref[...])
    second = g0_ref[...].astype(F32) + g1_ref[...].astype(F32)
    cot = cot_ref[...].astype(F32)
    scaled = second * vec_ref[3:4, :]
    inner = jnp.mean(scaled * xhat, axis=-1, keepdims=True)
    grad = cot + rate * (scaled - jnp.mean(scaled, axis=-1, keepdims=True) - xhat * inner)
    gm_ref[...] = grad
    sum_ref[0:1, :] += jnp.sum(second * xhat, axis=0, keepdims=True)
    sum_ref[1:2, :] += jnp.sum(second, axis=0, keepdims=True)
    sum_ref[2:3, :] += jnp.sum(grad, axis=0, keepdims=True)
    sum_ref[3:4, :] += jnp.sum(cot, axis=0, keepdims=True)
    low = grad.astype(BF)
    back = dot(low, wo_ref[...]).astype(BF).T
    x0_ref[...] = back[:192]
    x1_ref[...] = back[192:]
    mixed = jnp.concatenate([m0_ref[...], m1_ref[...]], axis=0)
    acc[...] += dot(low.T, mixed, NT)

    @pl.when(step == last)
    def _():
        wo0_ref[...] = acc[:, :192].astype(BF)
        wo1_ref[...] = acc[:, 192:].astype(BF)


def project_back_body(x_ref, q_ref, k_ref, v_ref, nt_ref, w_ref, wo_ref, *refs, rows, more):
    refs = list(refs)
    prev_ref = refs.pop(0) if more else None
    own_ref, oth_ref, first_ref, sum_ref, acc = refs
    step, last = pl.program_id(0), pl.num_programs(0) - 1
    x = x_ref[0]
    grads = jnp.concatenate([r[h] for r in (q_ref, k_ref, v_ref) for h in range(3)], axis=1)
    made = dot(nt_ref[...], grads)
    total = jnp.sum(grads.astype(F32), axis=0, keepdims=True)

    @pl.when(step == 0)
    def _():
        acc[...] = made
        sum_ref[...] = total

    @pl.when(step > 0)
    def _():
        acc[...] += made
        sum_ref[...] += total

    back = dot(grads, w_ref[:, :576], NT)
    if more:
        back = back + prev_ref[...]
    first_ref[...] = back.astype(first_ref.dtype)

    @pl.when(step == last)
    def _():
        for z in range(ZS):
            for ref, side in ((own_ref, x), (oth_ref, 1 - x)):
                at = pl.multiple_of((2 * z + side) * rows, 32)
                ref[z] = jnp.concatenate(
                    [acc[pl.ds(at, rows), :].astype(BF), wo_ref[pl.ds(at, rows), :]], axis=1
                )


def first_back_body(start_ref, te_ref, vec_ref, g0_ref, g1_ref, gm_ref, out_ref, sum_ref):
    @pl.when(pl.program_id(0) == 0)
    def _():
        sum_ref[...] = jnp.zeros_like(sum_ref)

    xhat, rate = normalize(start_ref[...].astype(F32) + te_ref[...].astype(F32))
    first = g0_ref[...].astype(F32) + g1_ref[...].astype(F32)
    scaled = first * vec_ref[0:1, :]
    inner = jnp.mean(scaled * xhat, axis=-1, keepdims=True)
    grad = gm_ref[...] + rate * (scaled - jnp.mean(scaled, axis=-1, keepdims=True) - xhat * inner)
    out_ref[...] = grad.astype(BF)
    sum_ref[0:1, :] += jnp.sum(first * xhat, axis=0, keepdims=True)
    sum_ref[1:2, :] += jnp.sum(first, axis=0, keepdims=True)
    sum_ref[2:3, :] += jnp.sum(grad, axis=0, keepdims=True)


def output_body(mid_ref, f0_ref, f1_ref, vec_ref, out_ref):
    out_ref[...] = (
        mid_ref[...] + (f0_ref[...].astype(F32) + f1_ref[...].astype(F32)) + vec_ref[5:6, :]
    ).astype(BF)


def swap(size):
    return [(i, size - 1 - i) for i in range(size)]


def to_y(values):
    return lax.ppermute(values, "y", swap(2))


def to_x(values):
    return lax.ppermute(values, "b", swap(2))


def to_core(values):
    return lax.ppermute(values, "c", swap(2))


def spread_z(values):
    return lax.all_to_all(values, "a", 0, 0, tiled=True)


def after(value, *others):
    return lax.optimization_barrier((value, *others))[0]


def body(
    fast,
    inputs,
    time_embed,
    first_gain,
    first_shift,
    query_weight,
    query_bias,
    key_weight,
    value_weight,
    value_bias,
    output_weight,
    output_bias,
    second_gain,
    second_shift,
    hidden_weight,
    hidden_bias,
    down_weight,
    down_bias,
    cotangent,
):
    _, block, width = inputs.shape
    shard = query_weight.shape[0]
    rows = width // (ZS * XS)
    seq = 4 * block
    tile = block
    tiles = seq // tile
    hidden = hidden_weight.shape[1]
    yi = lax.axis_index("y")
    xi = lax.axis_index("b") if fast else jnp.int32(0)
    x_arr = xi.astype(jnp.int32)[None]

    def tokens(values):
        mine = lax.dynamic_index_in_dim(values, yi, 0, keepdims=False)
        sent = lax.dynamic_index_in_dim(values, 1 - yi, 0, keepdims=False)
        pair = jnp.concatenate([mine, to_y(sent)], axis=0)
        return jnp.concatenate([pair, to_core(pair)], axis=0)

    start = tokens(inputs)
    te = lax.dynamic_index_in_dim(time_embed, yi, 0, keepdims=True)

    small = jnp.stack(
        [first_gain, first_shift, output_bias, second_gain, second_shift, down_bias, hidden_bias,
         jnp.pad(jnp.concatenate([query_bias, value_bias]), (0, shard - 2 * query_bias.shape[0]))]
    )
    small = jnp.pad(small, ((0, 0), (0, width - shard)))
    attn_pack = jnp.concatenate(
        [jnp.concatenate([query_weight, key_weight, value_weight, output_weight.T], axis=1), small], axis=0
    )
    h_pack, d_pack = hidden_weight, down_weight.T

    def vectors(own, oth):
        both = jnp.stack([own, oth], axis=1)
        both = jnp.where(xi == 0, both, both[:, ::-1])
        return both.reshape(ZS * XS, KINDS, -1)

    if fast:
        def copies(values):
            return jnp.broadcast_to(values[None], (ZS, *values.shape))

        attn_oo = spread_z(copies(attn_pack))
        h_pack, d_pack = lax.optimization_barrier((h_pack, d_pack, attn_oo))[:2]
        attn_ox = to_x(attn_oo)
        attn_yo = to_y(attn_oo)
        attn_yx = to_y(attn_ox)
        mlp_z = spread_z(copies(jnp.concatenate([h_pack, d_pack], axis=0)))
        h_oo, d_oo = mlp_z[:, :rows], mlp_z[:, rows:]
        h_ox = to_x(h_oo)
        h_yo = to_y(h_oo)
        h_yx = to_y(h_ox)
        d_yo = to_y(d_oo)
        d_ox = to_x(d_oo)
        d_yx = to_x(d_yo)
        vec_o = vectors(attn_oo[:, rows:, :rows], attn_ox[:, rows:, :rows])
        vec_y = vectors(attn_yo[:, rows:, :rows], attn_yx[:, rows:, :rows])
        bias_of = vec_o.shape[-1] // 4
    else:
        def natural(values):
            full = lax.all_gather(values, ("a", "b"), axis=0, tiled=True)
            full = full.reshape(ZS, XS, rows, width)
            return full[:, 0], full[:, 1]

        gathered = lax.all_gather(attn_pack, ("a", "b"), axis=0, tiled=False)
        matrix = gathered[:, :shard].reshape(ZS, XS, rows, width)
        attn_oo, attn_ox = matrix[:, 0], matrix[:, 1]
        attn_yo, attn_yx = to_y(attn_oo), to_y(attn_ox)
        h_oo, h_ox = natural(h_pack)
        d_oo, d_ox = natural(d_pack)
        h_yo, h_yx, d_yo, d_yx = to_y(h_oo), to_y(h_ox), to_y(d_oo), to_y(d_ox)
        vec_o = gathered[:, shard:, :shard]
        vec_y = to_y(vec_o)
        bias_of = shard // 4

    def flat(values):
        return values.astype(F32).transpose(1, 0, 2).reshape(KINDS, -1)

    def qkv_bias(values):
        part = values[:, 7, : 2 * bias_of].astype(F32)
        q_part, v_part = part[:, :bias_of].reshape(1, -1), part[:, bias_of:].reshape(1, -1)
        return jnp.concatenate([q_part, jnp.zeros_like(q_part), v_part], axis=1)

    vec = flat(vec_o)
    bias_o, bias_y = qkv_bias(vec_o), qkv_bias(vec_y)
    hb = jnp.concatenate([vec[6:7], flat(vec_y)[6:7]], axis=0)

    cot = tokens(cotangent)

    by_tile = pl.BlockSpec((tile, width), lambda i: (i, 0))
    by_mate = pl.BlockSpec((tile, width), lambda i: ((i + tiles // 2) % tiles, 0))
    row = kept((1, width))
    vecs = kept((KINDS, width))
    square = whole((width, width))
    part_rows = attn_oo.shape[1]
    heads9 = pl.BlockSpec((9, tile, HD), lambda i: (0, i, 0))

    def project(first, source, bias, own, oth):
        outs = [
            (sds((width, width), BF), kept((width, width))),
            (sds((9, seq, HD), BF), heads9),
        ]
        if first:
            outs += [
                (sds((seq, width), BF), by_tile),
                (sds((width, seq), BF), pl.BlockSpec((width, tile), lambda i: (0, i))),
            ]
        return call(
            functools.partial(project_body, rows=rows, first=first),
            (tiles,),
            [scalar(), by_tile, row, vecs, kept((1, 576)), whole((ZS, part_rows, width)), whole((ZS, part_rows, width))],
            outs,
            flops=2 * seq * width * 576,
            moved=8e6,
        )(x_arr, source, te, vec, bias, own, oth)

    chunks = tiles
    q_spec = pl.BlockSpec((1, tile, HD), lambda h, i: (h, i, 0))
    k_spec = pl.BlockSpec((1, seq, HD), lambda h, i: (3 + h, 0, 0))
    v_spec = pl.BlockSpec((1, seq, HD), lambda h, i: (6 + h, 0, 0))
    e_spec = pl.BlockSpec((1, seq, tile), lambda h, i: (h, 0, i))
    inv_spec = pl.BlockSpec((1, 1, tile), lambda h, i: (h, 0, i))
    t_spec = pl.BlockSpec((1, HD, tile), lambda h, i: (h, 0, i))

    def attend(qkv):
        return call(
            attend_body,
            (3, chunks),
            [q_spec, k_spec, v_spec],
            [
                (sds((3, seq, seq), BF), e_spec),
                (sds((3, 1, seq), F32), inv_spec),
                (sds((3, HD, seq), BF), t_spec),
                (sds((3, HD, seq), F32), t_spec),
            ],
            flops=3 * 16 * seq * seq * HD,
            moved=8e6,
            trans=3 * seq * seq,
        )(qkv, qkv, qkv)

    def attend_back(qkv, expon, inverse, mixed, grad_mixed):
        full = pl.BlockSpec((1, seq, HD), lambda h, i: (h, 0, 0))
        return call(
            attend_back_body,
            (3, chunks),
            [q_spec, k_spec, v_spec, e_spec, inv_spec, t_spec, t_spec],
            [(sds((3, seq, HD), BF), q_spec), (sds((3, seq, HD), BF), full), (sds((3, seq, HD), BF), full)],
            scratch=[pltpu.VMEM((seq, HD), F32), pltpu.VMEM((seq, HD), F32)],
            flops=3 * 40 * seq * seq * HD,
            moved=9e6,
        )(qkv, qkv, qkv, expon, inverse, mixed, grad_mixed)

    w_o, qkv_o, normed, normed_t = project(True, start, bias_o, attn_oo, attn_ox)
    exp_o, inv_o, mixed_o, wide_o = attend(qkv_o)
    w_y, qkv_y = project(False, normed, bias_y, attn_yo, attn_yx)
    exp_y, inv_y, mixed_y, wide_y = attend(qkv_y)

    half_t = pl.BlockSpec((3 * HD, tile), lambda i: (0, i))
    flat_o, flat_y = mixed_o.reshape(3 * HD, seq), mixed_y.reshape(3 * HD, seq)
    (attended,) = call(
        outproj_body,
        (tiles,),
        [half_t, half_t, square, square],
        [(sds((seq, width), BF), by_tile)],
        scratch=[pltpu.VMEM((width, 6 * HD), BF)],
        flops=2 * seq * width * 384,
        moved=6e6,
    )(flat_o, flat_y, w_o, w_y)
    attended_mate = to_core(attended)

    part = (ZS, rows, hidden)
    middle, ff, gs, hb_sum, gh_oo, gh_ox, gh_yo, gh_yx, gd_oo, gd_ox, gd_yo, gd_yx = call(
        functools.partial(mlp_body, rows=rows),
        (tiles,),
        [scalar(), by_tile, row, by_tile, by_mate, by_tile, vecs, kept((2, hidden))] + [whole(part)] * 8,
        [
            (sds((seq, width), F32), by_tile),
            (sds((seq, width), BF), by_tile),
            (sds((seq, width), BF), by_tile),
            (sds((2, hidden), F32), kept((2, hidden))),
        ]
        + [(sds(part, BF), kept(part))] * 8,
        scratch=[
            pltpu.VMEM((2, width, hidden), BF),
            pltpu.VMEM((2, width, hidden), BF),
            pltpu.VMEM((2, width, hidden), F32),
            pltpu.VMEM((2, width, hidden), F32),
        ],
        flops=12 * seq * width * hidden * 2,
        moved=24e6,
        trans=seq * hidden * 4,
    )(x_arr, start, te, attended, attended_mate, cot, vec, hb, h_oo, h_ox, h_yo, h_yx, d_oo, d_ox, d_yo, d_yx)
    gs_mate = to_core(gs)

    grad_middle, gx_o, gx_y, wo_o, wo_y, second_sums = call(
        second_back_body,
        (tiles,),
        [by_tile, by_tile, by_mate, by_tile, vecs, square, square, half_t, half_t],
        [
            (sds((seq, width), F32), by_tile),
            (sds((3 * HD, seq), BF), half_t),
            (sds((3 * HD, seq), BF), half_t),
            (sds((width, 3 * HD), BF), kept((width, 3 * HD))),
            (sds((width, 3 * HD), BF), kept((width, 3 * HD))),
            (sds((KINDS, width), F32), kept((KINDS, width))),
        ],
        scratch=[pltpu.VMEM((width, 6 * HD), BF), pltpu.VMEM((width, 6 * HD), F32)],
        flops=4 * seq * width * 384,
        moved=16e6,
    )(middle, gs, gs_mate, cot, vec, w_o, w_y, flat_o, flat_y)

    heads = pl.BlockSpec((3, tile, HD), lambda i: (0, i, 0))
    attn_part = (ZS, rows, width)

    def project_back(grads, weights, wo, prev):
        more = prev is not None
        return call(
            functools.partial(project_back_body, rows=rows, more=more),
            (tiles,),
            [scalar(), heads, heads, heads, pl.BlockSpec((width, tile), lambda i: (0, i)), square, whole((width, 3 * HD))]
            + ([by_tile] if more else []),
            [
                (sds(attn_part, BF), kept(attn_part)),
                (sds(attn_part, BF), kept(attn_part)),
                (sds((seq, width), BF if more else F32), by_tile),
                (sds((1, 576), F32), kept((1, 576))),
            ],
            scratch=[pltpu.VMEM((width, 576), F32)],
            flops=4 * seq * width * 576,
            moved=10e6,
        )(x_arr, *grads, normed_t, weights, wo, *((prev,) if more else ()))

    grads_y = attend_back(qkv_y, exp_y, inv_y, wide_y, gx_y.reshape(3, HD, seq))
    ga_yo, ga_yx, first_part, qkv_sum_y = project_back(grads_y, w_y, wo_y, None)
    grads_o = attend_back(qkv_o, exp_o, inv_o, wide_o, gx_o.reshape(3, HD, seq))
    ga_oo, ga_ox, first, qkv_sum_o = project_back(grads_o, w_o, wo_o, first_part)
    first_mate = to_core(first)

    input_grad, first_sums = call(
        first_back_body,
        (tiles,),
        [by_tile, row, vecs, by_tile, by_mate, by_tile],
        [(sds((seq, width), BF), by_tile), (sds((KINDS, width), F32), kept((KINDS, width)))],
        flops=1e6,
        moved=12e6,
    )(start, te, vec, first, first_mate, grad_middle)

    half = tiles // 2
    ff_mate = to_core(ff[seq // 2 :])
    (out_tokens,) = call(
        output_body,
        (half,),
        [by_tile, by_tile, by_tile, vecs],
        [(sds((seq // 2, width), BF), by_tile)],
        flops=1e6,
        moved=5e6,
    )(middle, ff, ff_mate, vec)

    def placed(values):
        mine, sent = values[:block], values[block : 2 * block]
        got = to_y(sent)
        return jnp.where(yi == 0, jnp.stack([mine, got]), jnp.stack([got, mine]))

    block_output = placed(out_tokens)
    input_gradient = placed(input_grad)

    def total(values):
        return jnp.sum(values.astype(F32), axis=0)

    def scatter_xy(oo, ox, yo, yx):
        got_o, got_y = to_x(ox), to_x(yx)
        own, oth = oo + got_o, yo + got_y
        return own + to_y(oth)

    def scatter_yx(oo, ox, yo, yx):
        got_y, got_x = to_y(yo), to_y(yx)
        own, oth = oo + got_y, ox + got_x
        return own + to_x(oth)

    def scatter_slow(oo, ox, yo, yx):
        own, oth = oo + to_y(yo), ox + to_y(yx)
        full = jnp.stack([own, oth], axis=1).reshape(width, -1).astype(F32)
        return lax.psum_scatter(full, ("a", "b"), scatter_dimension=0, tiled=True)

    if fast:
        gh = total(spread_z(scatter_xy(gh_oo, gh_ox, gh_yo, gh_yx)))
        gd = total(spread_z(scatter_yx(gd_oo, gd_ox, gd_yo, gd_yx)))
        ga = total(spread_z(scatter_yx(ga_oo, ga_ox, ga_yo, ga_yx)))
    else:
        gh = scatter_slow(gh_oo, gh_ox, gh_yo, gh_yx)
        gd = scatter_slow(gd_oo, gd_ox, gd_yo, gd_yx)
        ga = scatter_slow(ga_oo, ga_ox, ga_yo, ga_yx)

    owners = width // shard

    def pieces(hb_row, qkv_row, shared):
        kinds = [v.reshape(owners, 1, shard) for v in shared + [hb_row]]
        q_part, v_part = qkv_row[:192].reshape(owners, -1), qkv_row[384:].reshape(owners, -1)
        bias = jnp.concatenate([q_part, v_part], axis=1)
        bias = jnp.pad(bias, ((0, 0), (0, shard - bias.shape[1])))
        return jnp.concatenate(kinds + [bias[:, None]], axis=1)

    shared = [first_sums[0], first_sums[1], second_sums[2], second_sums[0], second_sums[1], second_sums[3]]
    small_o = pieces(hb_sum[0], qkv_sum_o[0], shared)
    small_y = pieces(hb_sum[1], qkv_sum_y[0], shared)
    embed = first_sums[2]
    sent = jnp.concatenate([small_y, embed.reshape(owners, 1, shard)], axis=1)
    got = to_y(sent)
    embed_got = got[:, KINDS].reshape(width)
    embed_gradient = jnp.where(yi == 0, jnp.stack([embed, embed_got]), jnp.stack([embed_got, embed]))
    small_sum = small_o + got[:, :KINDS]
    if fast:
        by_x = small_sum.reshape(ZS, XS, KINDS, shard)
        mine = lax.dynamic_index_in_dim(by_x, xi, 1, keepdims=False)
        other = lax.dynamic_index_in_dim(by_x, 1 - xi, 1, keepdims=False)
        sums = total(spread_z(mine + to_x(other)))
    else:
        sums = lax.psum_scatter(small_sum, ("a", "b"), scatter_dimension=0, tiled=True)[0]
    n_bias = query_bias.shape[0]
    n_head = query_weight.shape[1]
    return (
        block_output,
        input_gradient,
        embed_gradient,
        sums[0],
        sums[1],
        ga[:, :n_head],
        sums[7, :n_bias],
        ga[:, n_head : 2 * n_head],
        ga[:, 2 * n_head : 3 * n_head],
        sums[7, n_bias : 2 * n_bias],
        ga[:, 3 * n_head :].T,
        sums[2],
        sums[3],
        sums[4],
        gh,
        sums[6],
        gd.T,
        sums[5],
    )


def solution(mesh):
    dp, tensor = mesh.shape["dp"], mesh.shape["tensor"]
    fine = Mesh(mesh.devices.reshape(dp // 2, 2, tensor // 2, 2), ("a", "b", "y", "c"))
    by_dp, by_tensor = ("a", "b"), ("y", "c")
    both = by_tensor + by_dp
    column, matrix, turned = P(by_dp), P(by_dp, by_tensor), P(by_tensor, by_dp)
    seqs = P(by_dp, by_tensor, None)
    return jax.shard_map(
        functools.partial(body, dp == ZS * XS),
        mesh=fine,
        in_specs=(
            seqs, P(by_dp, None), column, column, matrix, P(both), matrix, matrix, P(both), turned,
            column, column, column, matrix, P(both), turned, column, seqs,
        ),
        out_specs=(
            seqs, seqs, P(by_dp, None), column, column, matrix, P(both), matrix, matrix, P(both), turned,
            column, column, column, matrix, P(both), turned, column,
        ),
        check_vma=False,
    )
```

time: 1040 us -> 352 us (0.34)
  waiting for transfers between devices: 543 us -> 110 us
  blocking collectives: 210 us -> 0 us
  matrix products: 154 us -> 0 us
  Pallas kernels: 0 us -> 136 us
  starting transfers between devices: 1.72 us -> 53.9 us
  other arithmetic: 54 us -> 25.1 us
  local copies, waits for them, and re-layouts: 49.4 us -> 23 us
  between operations: 19.2 us -> 1.1 us
    reduce_scatter x9 -> x0, waiting for transfers between devices: 439 us -> none  [the longest x1 72.5 us: body(): lax.psum_scatter(down_grad, 'dp', scatter_dimension=1, tiled=True)]
    dot_general x59 -> x0, matrix products: 149 us -> none  [the longest x5 26.1 us: weight_sum(): lax.dot_general(flat_left, flat_right, (((0,), (0,)), ((), ())), preferre...]
    pallas_call x0 -> x13, Pallas kernels: none -> 136 us  [the longest x2 32.6 us: attend_back(): call(attend_back_body, (3, chunks), [q_spec, k_spec, v_spec, e_spec, inv_...]
    all_gather x4 -> x0, blocking collectives: 127 us -> none  [the longest x1 33.4 us: body(): lax.all_gather(output_weight, 'dp', axis=1, tiled=True)]
    all_gather x6 -> x0, waiting for transfers between devices: 102 us -> none  [the longest x1 28.6 us: body(): seq_cot = lax.all_gather(cotangent, 'tensor', axis=1, tiled=True)]
    ppermute x0 -> x30, waiting for transfers between devices: none -> 98.7 us  [the longest x15 70.7 us: to_y(): return lax.ppermute(values, 'y', swap(2))]
    unnamed x2 -> x0, blocking collectives: 77.1 us -> none
    ppermute x0 -> x30, starting transfers between devices: none -> 30 us  [the longest x15 19.4 us: to_y(): return lax.ppermute(values, 'y', swap(2))]
  transfers between devices with their start and end apart: 16 -> 36, of which waited for: 13 -> 19; matrix products, arithmetic and copies ran while one was open for 15% -> 10% of each run, Pallas kernels for 0% -> 32%
where the time goes in v1:
time: 352 us; the launch traced here: 350 us
  Pallas kernels  136 us (39%)
  waiting for transfers between devices  110 us (31%)
  starting transfers between devices  53.9 us (15%)
  other arithmetic  25.1 us (7%)
  local copies, waits for them, and re-layouts  23 us (7%)
    ppermute x15, waiting for transfers between devices, to_y(): return lax.ppermute(values, 'y', swap(2))  70.7 us
    pallas_call x2, Pallas kernels, attend_back(): call(attend_back_body, (3, chunks), [q_spec, k_spec, v_spec, e_spec, inv_...  32.6 us
    ppermute x9, waiting for transfers between devices, to_x(): return lax.ppermute(values, 'b', swap(2))  27.9 us
    pallas_call x1, Pallas kernels, body(): call(functools.partial(mlp_body, rows=rows), (tiles,), [scalar(), by_tile...  24.7 us
    pallas_call x2, Pallas kernels, attend(): call(attend_body, (3, chunks), [q_spec, k_spec, v_spec], [(sds((3, seq, s...  24.4 us
    all_to_all x6, starting transfers between devices, spread_z(): return lax.all_to_all(values, 'a', 0, 0, tiled=True)  23.9 us
    ppermute x15, starting transfers between devices, to_y(): return lax.ppermute(values, 'y', swap(2))  19.4 us
    pallas_call x2, Pallas kernels, project_back(): call(functools.partial(project_back_body, rows=rows, more=more), (tiles,)...  18.4 us
  transfers between devices with their start and end apart: 36, of which 19 were waited for; matrix products, arithmetic and copies ran while one was open for 10% of the time, Pallas kernels for 32%

profile of v1, /device:TPU:0, one launch (start us, length us, event | category | flops | bytes accessed | tf_op | source)
XLA Modules:
  0.0 349.6 jit_solution(17071396966304608185)
XLA Ops:
  7.1 6.3 %all-to-all-start = ((bf16[4,104,768]{2,1,0:T(8,128)(2,1)}), bf16[4,104,768]{2,1,0:T(8,128)(2,1)}, u32[]{:S(2)}, u32[]{:S(2)}) async-start(bf16[4,104,768]{2,1,0:T(8,128)(2,1)} %broadcast_in_dim.22), calls=%async_computation | async-start | bytes 1277952 | tf_op jit(solution)/shard_map/all_to_all | solution.py:314
  13.4 1.6 collective-permute-start
  15.0 9.1 %collective-permute-done = bf16[256,768]{1,0:T(8,128)(2,1)S(1)} collective-permute-done((bf16[256,768]{1,0:T(8,128)(2,1)S(1)}, bf16[256,768]{1,0:T(8,128)(2,1)S(1)}, u32[]{:S(2)}, u32[]{:S(2)}) %collective-permute-start) | collective-permute-done | bytes 393248 | tf_op jit(solution)/shard_map/ppermute | solution.py:302
  24.2 6.2 %all-to-all-done.own_ref = bf16[4,104,768]{2,1,0:T(8,128)(2,1)} async-done(((bf16[4,104,768]{2,1,0:T(8,128)(2,1)}), bf16[4,104,768]{2,1,0:T(8,128)(2,1)}, u32[]{:S(2)}, u32[]{:S(2)}) %all-to-all-start) | async-done | bytes 639008 | tf_op jit(solution)/shard_map/all_to_all | solution.py:314
  30.4 1.5 collective-permute-start.2
  32.7 1.5 collective-permute-start.6
  36.0 3.5 %all-to-all-start.1 = ((bf16[4,192,768]{2,1,0:T(8,128)(2,1)}), bf16[4,192,768]{2,1,0:T(8,128)(2,1)S(1)}, u32[]{:S(2)}, u32[]{:S(2)}) async-start(bf16[4,192,768]{2,1,0:T(8,128)(2,1)} %broadcast_in_dim.23), calls=%async_computation.1 | async-start | bytes 2359296 | tf_op jit(solution)/shard_map/all_to_all | solution.py:314
  40.9 5.2 %collective-permute-done.2.oth_ref = bf16[4,104,768]{2,1,0:T(8,128)(2,1)} collective-permute-done((bf16[4,104,768]{2,1,0:T(8,128)(2,1)}, bf16[4,104,768]{2,1,0:T(8,128)(2,1)}, u32[]{:S(2)}, u32[]{:S(2)}) %collective-permute-start.2) | collective-permute-done | bytes 639008 | tf_op jit(solution)/shard_map/ppermute | solution.py:306
  46.1 1.5 collective-permute-start.4
  47.6 2.5 pad_maximum_fusion.start_ref
  50.8 7.4 %collective-permute-done.3.own_ref = bf16[4,104,768]{2,1,0:T(8,128)(2,1)S(1)} collective-permute-done((bf16[4,104,768]{2,1,0:T(8,128)(2,1)}, bf16[4,104,768]{2,1,0:T(8,128)(2,1)S(1)}, u32[]{:S(2)}, u32[]{:S(2)}) %collective-permute-start.3) | collective-permute-done | bytes 639008 | tf_op jit(solution)/shard_map/ppermute | solution.py:302
  58.2 12.0 %collective-permute-done.4.oth_ref = bf16[4,104,768]{2,1,0:T(8,128)(2,1)S(1)} collective-permute-done((bf16[4,104,768]{2,1,0:T(8,128)(2,1)}, bf16[4,104,768]{2,1,0:T(8,128)(2,1)S(1)}, u32[]{:S(2)}, u32[]{:S(2)}) %collective-permute-start.4) | collective-permute-done | bytes 639008 | tf_op jit(solution)/shard_map/ppermute | solution.py:302
  73.9 6.2 %shard_map.313 = (bf16[768,768]{1,0:T(8,128)(2,1)}, bf16[9,1024,64]{2,1,0:T(8,128)(2,1)}, bf16[1024,768]{1,0:T(8,128)(2,1)}, bf16[768,1024]{1,0:T(8,128)(2,1)}) custom-call(s32[1]{0:T(128)} %bitcast.x_ref, bf16[1024,768]{1,0:T(8,128)(2,1)} %pad_maximum_fusion.start_ref, bf16[1,768]{1,0:T(2,128)(2,1)} %constant_dynamic-slice_fusion.2.te_ref, ...), custom_call_target="tpu_custom_call" | custom-call | flops 905969664 | bytes 8000000 | tf_op jit(solution)/shard_map/pallas_call | solution.py:446
  80.1 5.5 %shard_map.315 = (bf16[768,768]{1,0:T(8,128)(2,1)}, bf16[9,1024,64]{2,1,0:T(8,128)(2,1)}) custom-call(s32[1]{0:T(128)} %bitcast.x_ref, bf16[1024,768]{1,0:T(8,128)(2,1)} %get-tuple-element.70.start_ref, bf16[1,768]{1,0:T(2,128)(2,1)} %constant_dynamic-slice_fusion.2.te_ref, f32[8,768]{1,0:T(8,128)} %reshape.103.vec_ref, ...), custom_call_target="tpu_custom_call" | custom-call | flops 905969664 | bytes 8000000 | tf_op jit(solution)/shard_map/pallas_call | solution.py:446
  85.6 12.2 %shard_map.316 = (bf16[3,1024,1024]{2,1,0:T(8,128)(2,1)}, f32[3,1,1024]{2,1,0:T(1,128)}, bf16[3,64,1024]{2,1,0:T(8,128)(2,1)}, f32[3,64,1024]{2,1,0:T(8,128)}) custom-call(bf16[9,1024,64]{2,1,0:T(8,128)(2,1)} %get-tuple-element.71.q_ref.k_ref.v_ref, bf16[9,1024,64]{2,1,0:T(8,128)(2,1)} %get-tuple-element.71.q_ref.k_ref.v_ref, ...), custom_call_target="tpu_custom_call" | custom-call | flops 3221225472 | bytes 8000000 | tf_op jit(solution)/shard_map/pallas_call | solution.py:464
  97.8 12.2 %shard_map.314 = (bf16[3,1024,1024]{2,1,0:T(8,128)(2,1)}, f32[3,1,1024]{2,1,0:T(1,128)}, bf16[3,64,1024]{2,1,0:T(8,128)(2,1)}, f32[3,64,1024]{2,1,0:T(8,128)}) custom-call(bf16[9,1024,64]{2,1,0:T(8,128)(2,1)} %get-tuple-element.68.q_ref.k_ref.v_ref, bf16[9,1024,64]{2,1,0:T(8,128)(2,1)} %get-tuple-element.68.q_ref.k_ref.v_ref, ...), custom_call_target="tpu_custom_call" | custom-call | flops 3221225472 | bytes 8000000 | tf_op jit(solution)/shard_map/pallas_call | solution.py:464
  110.0 5.2 %shard_map.317.a0_ref = bf16[1024,768]{1,0:T(8,128)(2,1)} custom-call(bf16[192,1024]{1,0:T(8,128)(2,1)} %bitcast.88, bf16[192,1024]{1,0:T(8,128)(2,1)} %bitcast.86, bf16[768,768]{1,0:T(8,128)(2,1)} %get-tuple-element.73.w0_ref.w_ref, bf16[768,768]{1,0:T(8,128)(2,1)} %get-tuple-element.74.w1_ref.w_ref), custom_call_target="tpu_custom_call" | custom-call | flops 603979776 | bytes 6000000 | tf_op jit(solution)/shard_map/pallas_call | solution.py:498
  117.5 1.5 collective-permute-start.12
  119.0 1.5 collective-permute-start.11
  121.3 12.1 %collective-permute-done.8.h_ox = bf16[4,96,768]{2,1,0:T(8,128)(2,1)S(1)} collective-permute-done((bf16[4,96,768]{2,1,0:T(8,128)(2,1)}, bf16[4,96,768]{2,1,0:T(8,128)(2,1)S(1)}, u32[]{:S(2)}, u32[]{:S(2)}) %collective-permute-start.8) | collective-permute-done | bytes 589856 | tf_op jit(solution)/shard_map/ppermute | solution.py:306
  133.4 1.5 collective-permute-start.10
  135.5 1.3 pad_maximum_fusion.1.cot_ref
  139.1 7.0 %collective-permute-done.11.d_ox = bf16[4,96,768]{2,1,0:T(8,128)(2,1)} collective-permute-done((bf16[4,96,768]{2,1,0:T(8,128)(2,1)}, bf16[4,96,768]{2,1,0:T(8,128)(2,1)}, u32[]{:S(2)}, u32[]{:S(2)}) %collective-permute-start.11) | collective-permute-done | bytes 589856 | tf_op jit(solution)/shard_map/ppermute | solution.py:306
  146.6 11.5 %collective-permute-done.10.h_yx = bf16[4,96,768]{2,1,0:T(8,128)(2,1)} collective-permute-done((bf16[4,96,768]{2,1,0:T(8,128)(2,1)S(1)}, bf16[4,96,768]{2,1,0:T(8,128)(2,1)}, u32[]{:S(2)}, u32[]{:S(2)}) %collective-permute-start.10) | collective-permute-done | bytes 589856 | tf_op jit(solution)/shard_map/ppermute | solution.py:302
  158.1 24.7 %shard_map.318 = (f32[1024,768]{1,0:T(8,128)}, bf16[1024,768]{1,0:T(8,128)(2,1)}, bf16[1024,768]{1,0:T(8,128)(2,1)}, f32[2,768]{1,0:T(2,128)}, bf16[4,96,768]{2,...) custom-call(s32[1]{0:T(128)} %bitcast.x_ref, ...), custom_call_target="tpu_custom_call" | custom-call | flops 14495514624 | bytes 24000000 | tf_op jit(solution)/shard_map/pallas_call | solution.py:510
  182.9 1.6 collective-permute-start.28
  185.0 1.5 collective-permute-start.25
  186.5 1.2 slice.171
  187.7 11.5 %collective-permute-done.28 = bf16[4,96,768]{2,1,0:T(8,128)(2,1)S(1)} collective-permute-done((bf16[4,96,768]{2,1,0:T(8,128)(2,1)}, bf16[4,96,768]{2,1,0:T(8,128)(2,1)S(1)}, u32[]{:S(2)}, u32[]{:S(2)}) %collective-permute-start.28) | collective-permute-done | bytes 589856 | tf_op jit(solution)/shard_map/ppermute | solution.py:302
  200.2 1.5 collective-permute-start.29
  201.7 1.1 copy-done.3
  202.9 10.1 %shard_map.320 = (f32[1024,768]{1,0:T(8,128)}, bf16[192,1024]{1,0:T(8,128)(2,1)}, bf16[192,1024]{1,0:T(8,128)(2,1)}, bf16[768,192]{1,0:T(8,128)(2,1)}, bf16[768,192]{1,0:T(8,128)(2,1)}, /*index=5*/f32[8,768]{1,0:T(8,128)}) custom-call(f32[1024,768]{1,0:T(8,128)} %get-tuple-element.77.mid_ref, bf16[1024,768]{1,0:T(8,128)(2,1)} %get-tuple-element.82.g0_ref, ...), custom_call_target="tpu_custom_call" | custom-call | flops 1207959552 | bytes 16000000 | tf_op jit(solution)/shard_map/pallas_call | solution.py:533
  213.0 16.3 %shard_map.322 = (bf16[3,1024,64]{2,1,0:T(8,128)(2,1)}, bf16[3,1024,64]{2,1,0:T(8,128)(2,1)}, bf16[3,1024,64]{2,1,0:T(8,128)(2,1)}) custom-call(bf16[9,1024,64]{2,1,0:T(8,128)(2,1)} %get-tuple-element.71.q_ref.k_ref.v_ref, bf16[9,1024,64]{2,1,0:T(8,128)(2,1)} %get-tuple-element.71.q_ref.k_ref.v_ref, ...), custom_call_target="tpu_custom_call" | custom-call | flops 8053063680 | bytes 9000000 | tf_op jit(solution)/shard_map/pallas_call | solution.py:481
  229.3 16.3 %shard_map.321 = (bf16[3,1024,64]{2,1,0:T(8,128)(2,1)}, bf16[3,1024,64]{2,1,0:T(8,128)(2,1)}, bf16[3,1024,64]{2,1,0:T(8,128)(2,1)}) custom-call(bf16[9,1024,64]{2,1,0:T(8,128)(2,1)} %get-tuple-element.68.q_ref.k_ref.v_ref, bf16[9,1024,64]{2,1,0:T(8,128)(2,1)} %get-tuple-element.68.q_ref.k_ref.v_ref, ...), custom_call_target="tpu_custom_call" | custom-call | flops 8053063680 | bytes 9000000 | tf_op jit(solution)/shard_map/pallas_call | solution.py:481
  245.6 9.1 %shard_map.323 = (bf16[4,96,768]{2,1,0:T(8,128)(2,1)}, bf16[4,96,768]{2,1,0:T(8,128)(2,1)}, f32[1024,768]{1,0:T(8,128)}, f32[1,576]{1,0:T(1,128)}) custom-call(s32[1]{0:T(128)} %bitcast.x_ref, bf16[3,1024,64]{2,1,0:T(8,128)(2,1)} %get-tuple-element.93.q_ref, bf16[3,1024,64]{2,1,0:T(8,128)(2,1)} %get-tuple-element.94.k_ref, ...), custom_call_target="tpu_custom_call" | custom-call | flops 1811939328 | bytes 10000000 | tf_op jit(solution)/shard_map/pallas_call | solution.py:555
  254.7 9.3 %shard_map.324 = (bf16[4,96,768]{2,1,0:T(8,128)(2,1)}, bf16[4,96,768]{2,1,0:T(8,128)(2,1)}, bf16[1024,768]{1,0:T(8,128)(2,1)}, f32[1,576]{1,0:T(1,128)}) custom-call(s32[1]{0:T(128)} %bitcast.x_ref, bf16[3,1024,64]{2,1,0:T(8,128)(2,1)} %get-tuple-element.84.q_ref, bf16[3,1024,64]{2,1,0:T(8,128)(2,1)} %get-tuple-element.85.k_ref, ...), custom_call_target="tpu_custom_call" | custom-call | flops 1811939328 | bytes 10000000 | tf_op jit(solution)/shard_map/pallas_call | solution.py:555
  264.6 2.2 add.71
  266.9 1.6 collective-permute-start.26
  268.5 2.7 shard_map.319
  271.2 2.3 add_add_fusion
  273.5 3.6 %all-to-all-start.5 = ((bf16[4,96,768]{2,1,0:T(8,128)(2,1)}), bf16[4,96,768]{2,1,0:T(8,128)(2,1)S(1)}, u32[]{:S(2)}, u32[]{:S(2)}) async-start(bf16[4,96,768]{2,1,0:T(8,128)(2,1)} %add_add_fusion), calls=%async_computation.5 | async-start | bytes 1179648 | tf_op jit(solution)/shard_map/all_to_all | solution.py:314
  278.9 1.2 collective-permute-done.24
  280.1 3.3 collective-permute-done.26
  283.4 2.4 add_add_fusion.1
  285.8 1.5 collective-permute-start.22
  287.3 4.5 %collective-permute-done.15 = bf16[256,768]{1,0:T(8,128)(2,1)} collective-permute-done((bf16[256,768]{1,0:T(8,128)(2,1)}, bf16[256,768]{1,0:T(8,128)(2,1)}, u32[]{:S(2)}, u32[]{:S(2)}) %collective-permute-start.15) | collective-permute-done | bytes 393248 | tf_op jit(solution)/shard_map/ppermute | solution.py:302
  291.8 2.2 maximum_select_fusion
  294.1 1.5 collective-permute-start.21
  296.3 3.5 all-to-all-start.4
  300.6 3.9 %collective-permute-done.22 = bf16[4,96,768]{2,1,0:T(8,128)(2,1)} collective-permute-done((bf16[4,96,768]{2,1,0:T(8,128)(2,1)}, bf16[4,96,768]{2,1,0:T(8,128)(2,1)}, u32[]{:S(2)}, u32[]{:S(2)}) %collective-permute-start.22) | collective-permute-done | bytes 589856 | tf_op jit(solution)/shard_map/ppermute | solution.py:302
  304.5 1.2 add.68
  305.7 1.6 collective-permute-start.23
  307.3 1.2 copy-done.4
  308.5 6.1 %shard_map.325 = (bf16[1024,768]{1,0:T(8,128)(2,1)}, f32[8,768]{1,0:T(8,128)}) custom-call(bf16[1024,768]{1,0:T(8,128)(2,1)} %pad_maximum_fusion.start_ref, bf16[1,768]{1,0:T(2,128)(2,1)} %constant_dynamic-slice_fusion.2.te_ref, f32[8,768]{1,0:T(8,128)} %reshape.103.vec_ref, bf16[1024,768]{1,0:T(8,128)(2,1)} %get-tuple-element.98.g0_ref, ...), custom_call_target="tpu_custom_call" | custom-call | flops 1000000 | bytes 12000000 | tf_op jit(solution)/shard_map/pallas_call | solution.py:577
  315.8 1.5 collective-permute-start.19
  317.4 2.3 collective-permute-done.19
  321.2 2.4 collective-permute-done.20
  324.3 3.5 %all-to-all-start.2 = ((f32[4,8,96]{2,1,0:T(8,128)}), f32[4,8,96]{2,1,0:T(8,128)S(1)}, u32[]{:S(2)}, u32[]{:S(2)}) async-start(f32[4,8,96]{2,1,0:T(8,128)} %fusion.2), calls=%async_computation.2 | async-start | bytes 32768 | tf_op jit(solution)/shard_map/all_to_all | solution.py:314
  327.8 2.2 add_add_fusion.2
  330.0 3.4 all-to-all-done.2
  333.4 3.5 all-to-all-start.3
  336.9 1.3 collective-permute-start.18
  340.1 4.7 %collective-permute-done.18 = bf16[256,768]{1,0:T(8,128)(2,1)S(1)} collective-permute-done((bf16[256,768]{1,0:T(8,128)(2,1)S(1)}, bf16[256,768]{1,0:T(8,128)(2,1)S(1)}, u32[]{:S(2)}, u32[]{:S(2)}) %collective-permute-start.18) | collective-permute-done | bytes 393248 | tf_op jit(solution)/shard_map/ppermute | solution.py:302
  345.8 2.2 all-to-all-done.3
  (175 shorter events, 34.5 us)
Async XLA Ops:
  0.7 33.7 %copy-start = (bf16[2,768]{1,0:T(2,128)(2,1)S(1)}, bf16[2,768]{1,0:T(2,128)(2,1)}, u32[]{:S(2)}) copy-start(bf16[2,768]{1,0:T(2,128)(2,1)} %param.19) | copy-start | bytes 9220
  1.6 11.8 %copy-start.6 = (bf16[2,256,768]{2,1,0:T(8,128)(2,1)S(1)}, bf16[2,256,768]{2,1,0:T(8,128)(2,1)}, u32[]{:S(2)}) copy-start(bf16[2,256,768]{2,1,0:T(8,128)(2,1)} %param.18) | copy-start | bytes 2359300
  7.1 23.4 %all-to-all-start = ((bf16[4,104,768]{2,1,0:T(8,128)(2,1)}), bf16[4,104,768]{2,1,0:T(8,128)(2,1)}, u32[]{:S(2)}, u32[]{:S(2)}) async-start(bf16[4,104,768]{2,1,0:T(8,128)(2,1)} %broadcast_in_dim.22), calls=%async_computation | async-start | bytes 1277952 | tf_op jit(solution)/shard_map/all_to_all | solution.py:314
  13.4 18.5 %copy-start.7 = (bf16[2,256,768]{2,1,0:T(8,128)(2,1)S(1)}, bf16[2,256,768]{2,1,0:T(8,128)(2,1)}, u32[]{:S(2)}) copy-start(bf16[2,256,768]{2,1,0:T(8,128)(2,1)} %param.35) | copy-start | bytes 2359300
  13.4 10.6 %collective-permute-start = (bf16[256,768]{1,0:T(8,128)(2,1)S(1)}, bf16[256,768]{1,0:T(8,128)(2,1)S(1)}, u32[]{:S(2)}, u32[]{:S(2)}) collective-permute-start(bf16[256,768]{1,0:T(8,128)(2,1)S(1)} %get-tuple-element.194), channel_id=1, source_target_pairs={{0,2},{2,0},{1,3},{3,1},{4,6},{6,4},{5,7},{7,5},{8,10},{10,8},{9,1... | collective-permute-start | bytes 1179656 | tf_op jit(solution)/shard_map/ppermute | solution.py:302
  24.1 10.8 %copy-start.14 = (bf16[768,96]{0,1:T(8,128)(2,1)S(1)}, bf16[768,96]{0,1:T(8,128)(2,1)}, u32[]{:S(2)}) copy-start(bf16[768,96]{0,1:T(8,128)(2,1)} %param.33) | copy-start | bytes 442372
  24.1 10.8 %copy-start.15 = (bf16[96,768]{1,0:T(8,128)(2,1)S(1)}, bf16[96,768]{1,0:T(8,128)(2,1)}, u32[]{:S(2)}) copy-start(bf16[96,768]{1,0:T(8,128)(2,1)} %param.31) | copy-start | bytes 442372
  24.1 23.5 %collective-permute-start.1 = (bf16[512,768]{1,0:T(8,128)(2,1)S(1)}, bf16[512,768]{1,0:T(8,128)(2,1)}, u32[]{:S(2)}, u32[]{:S(2)}) collective-permute-start(bf16[512,768]{1,0:T(8,128)(2,1)S(1)} %pad_maximum_fusion.2), channel_id=1, source_target_pairs={{0,1},{1,0},{2,3},{3,2},{4,5},{5,4},{6,7},{7,6},{8,9},{9,8},{10,11... | collective-permute-start | bytes 2359304 | tf_op jit(solution)/shard_map/ppermute | solution.py:310
  30.4 15.7 %collective-permute-start.2 = (bf16[4,104,768]{2,1,0:T(8,128)(2,1)}, bf16[4,104,768]{2,1,0:T(8,128)(2,1)}, u32[]{:S(2)}, u32[]{:S(2)}) collective-permute-start(bf16[4,104,768]{2,1,0:T(8,128)(2,1)} %all-to-all-done.own_ref), channel_id=1, source_target_pairs={{0,4},{4,0},{1,5},{5,1},{2,6},{6,2},{3,7},{7,3},{8,12},{12,8},{9,1... | collective-permute-start | bytes 1916936 | tf_op jit(solution)/shard_map/ppermute | solution.py:306
  32.7 82.5 %collective-permute-start.6 = (bf16[256,768]{1,0:T(8,128)(2,1)}, bf16[256,768]{1,0:T(8,128)(2,1)S(1)}, u32[]{:S(2)}, u32[]{:S(2)}) collective-permute-start(bf16[256,768]{1,0:T(8,128)(2,1)} %get-tuple-element.192), channel_id=1, source_target_pairs={{0,2},{2,0},{1,3},{3,1},{4,6},{6,4},{5,7},{7,5},{8,10},{10,8},{9,1... | collective-permute-start | bytes 1179656 | tf_op jit(solution)/shard_map/ppermute | solution.py:302
  36.0 79.8 %all-to-all-start.1 = ((bf16[4,192,768]{2,1,0:T(8,128)(2,1)}), bf16[4,192,768]{2,1,0:T(8,128)(2,1)S(1)}, u32[]{:S(2)}, u32[]{:S(2)}) async-start(bf16[4,192,768]{2,1,0:T(8,128)(2,1)} %broadcast_in_dim.23), calls=%async_computation.1 | async-start | bytes 2359296 | tf_op jit(solution)/shard_map/all_to_all | solution.py:314
  39.6 18.6 %collective-permute-start.3 = (bf16[4,104,768]{2,1,0:T(8,128)(2,1)}, bf16[4,104,768]{2,1,0:T(8,128)(2,1)S(1)}, u32[]{:S(2)}, u32[]{:S(2)}) collective-permute-start(bf16[4,104,768]{2,1,0:T(8,128)(2,1)} %all-to-all-done.own_ref), channel_id=1, source_target_pairs={{0,2},{2,0},{1,3},{3,1},{4,6},{6,4},{5,7},{7,5},{8,10},{10,8},{9,1... | collective-permute-start | bytes 1916936 | tf_op jit(solution)/shard_map/ppermute | solution.py:302
  46.1 24.0 %collective-permute-start.4 = (bf16[4,104,768]{2,1,0:T(8,128)(2,1)}, bf16[4,104,768]{2,1,0:T(8,128)(2,1)S(1)}, u32[]{:S(2)}, u32[]{:S(2)}) collective-permute-start(bf16[4,104,768]{2,1,0:T(8,128)(2,1)} %collective-permute-done.2.oth_ref), channel_id=1, source_target_pairs={{0,2},{2,0},{1,3},{3,1},{4,6},{6,4},{5,7},{7,5},{8,10},{10,8},{9,1... | collective-permute-start | bytes 1916936 | tf_op jit(solution)/shard_map/ppermute | solution.py:302
  58.2 12.1 %copy-start.21 = (bf16[4,104,768]{2,1,0:T(8,128)(2,1)}, bf16[4,104,768]{2,1,0:T(8,128)(2,1)S(1)}, u32[]{:S(2)}) copy-start(bf16[4,104,768]{2,1,0:T(8,128)(2,1)S(1)} %collective-permute-done.3.own_ref) | copy-start | bytes 1916932
  70.1 0.8 copy-start.22
  71.1 0.6 copy-start.16
  72.0 0.6 copy-start.13
  115.2 31.4 %collective-permute-start.5 = (bf16[1024,768]{1,0:T(8,128)(2,1)}, bf16[1024,768]{1,0:T(8,128)(2,1)}, u32[]{:S(2)}, u32[]{:S(2)}) collective-permute-start(bf16[1024,768]{1,0:T(8,128)(2,1)} %shard_map.317.a0_ref), channel_id=1, source_target_pairs={{0,1},{1,0},{2,3},{3,2},{4,5},{5,4},{6,7},{7,6},{8,9},{9,8},{10,11... | collective-permute-start | bytes 4718600 | tf_op jit(solution)/shard_map/ppermute | solution.py:310
  115.3 5.2 %collective-permute-start.7 = (bf16[512,768]{1,0:T(8,128)(2,1)S(1)}, bf16[512,768]{1,0:T(8,128)(2,1)S(1)}, u32[]{:S(2)}, u32[]{:S(2)}) collective-permute-start(bf16[512,768]{1,0:T(8,128)(2,1)S(1)} %pad_maximum_fusion.3), channel_id=1, source_target_pairs={{0,1},{1,0},{2,3},{3,2},{4,5},{5,4},{6,7},{7,6},{8,9},{9,8},{10,11... | collective-permute-start | bytes 2359304 | tf_op jit(solution)/shard_map/ppermute | solution.py:310
  117.0 16.4 %collective-permute-start.8 = (bf16[4,96,768]{2,1,0:T(8,128)(2,1)}, bf16[4,96,768]{2,1,0:T(8,128)(2,1)S(1)}, u32[]{:S(2)}, u32[]{:S(2)}) collective-permute-start(bf16[4,96,768]{2,1,0:T(8,128)(2,1)} %get-tuple-element.188.h_oo), channel_id=1, source_target_pairs={{0,4},{4,0},{1,5},{5,1},{2,6},{6,2},{3,7},{7,3},{8,12},{12,8},{9,1... | collective-permute-start | bytes 1769480 | tf_op jit(solution)/shard_map/ppermute | solution.py:306
  117.5 17.4 %collective-permute-start.12 = (bf16[4,96,768]{2,1,0:T(8,128)(2,1)}, bf16[4,96,768]{2,1,0:T(8,128)(2,1)S(1)}, u32[]{:S(2)}, u32[]{:S(2)}) collective-permute-start(bf16[4,96,768]{2,1,0:T(8,128)(2,1)} %get-tuple-element.187.d_oo), channel_id=1, source_target_pairs={{0,2},{2,0},{1,3},{3,1},{4,6},{6,4},{5,7},{7,5},{8,10},{10,8},{9,1... | collective-permute-start | bytes 1769480 | tf_op jit(solution)/shard_map/ppermute | solution.py:302
  119.0 27.1 %collective-permute-start.11 = (bf16[4,96,768]{2,1,0:T(8,128)(2,1)}, bf16[4,96,768]{2,1,0:T(8,128)(2,1)}, u32[]{:S(2)}, u32[]{:S(2)}) collective-permute-start(bf16[4,96,768]{2,1,0:T(8,128)(2,1)} %get-tuple-element.187.d_oo), channel_id=1, source_target_pairs={{0,4},{4,0},{1,5},{5,1},{2,6},{6,2},{3,7},{7,3},{8,12},{12,8},{9,1... | collective-permute-start | bytes 1769480 | tf_op jit(solution)/shard_map/ppermute | solution.py:306
  120.5 26.0 %collective-permute-start.9 = (bf16[4,96,768]{2,1,0:T(8,128)(2,1)}, bf16[4,96,768]{2,1,0:T(8,128)(2,1)S(1)}, u32[]{:S(2)}, u32[]{:S(2)}) collective-permute-start(bf16[4,96,768]{2,1,0:T(8,128)(2,1)} %get-tuple-element.188.h_oo), channel_id=1, source_target_pairs={{0,2},{2,0},{1,3},{3,1},{4,6},{6,4},{5,7},{7,5},{8,10},{10,8},{9,1... | collective-permute-start | bytes 1769480 | tf_op jit(solution)/shard_map/ppermute | solution.py:302
  133.4 3.4 copy-start.23
  133.4 24.7 %collective-permute-start.10 = (bf16[4,96,768]{2,1,0:T(8,128)(2,1)S(1)}, bf16[4,96,768]{2,1,0:T(8,128)(2,1)}, u32[]{:S(2)}, u32[]{:S(2)}) collective-permute-start(bf16[4,96,768]{2,1,0:T(8,128)(2,1)S(1)} %collective-permute-done.8.h_ox), channel_id=1, source_target_pairs={{0,2},{2,0},{1,3},{3,1},{4,6},{6,4},{5,7},{7,5},{8,10},{10,8},{9,1... | collective-permute-start | bytes 1769480 | tf_op jit(solution)/shard_map/ppermute | solution.py:302
  134.9 1.9 copy-start.24
  134.9 23.2 %collective-permute-start.13 = (bf16[4,96,768]{2,1,0:T(8,128)(2,1)S(1)}, bf16[4,96,768]{2,1,0:T(8,128)(2,1)}, u32[]{:S(2)}, u32[]{:S(2)}) collective-permute-start(bf16[4,96,768]{2,1,0:T(8,128)(2,1)S(1)} %collective-permute-done.12.d_yo), channel_id=1, source_target_pairs={{0,4},{4,0},{1,5},{5,1},{2,6},{6,2},{3,7},{7,3},{8,12},{12,8},{9,1... | collective-permute-start | bytes 1769480 | tf_op jit(solution)/shard_map/ppermute | solution.py:306
  146.6 11.5 %copy-start.25 = (bf16[4,96,768]{2,1,0:T(8,128)(2,1)}, bf16[4,96,768]{2,1,0:T(8,128)(2,1)S(1)}, u32[]{:S(2)}) copy-start(bf16[4,96,768]{2,1,0:T(8,128)(2,1)S(1)} %collective-permute-done.9.h_yo) | copy-start | bytes 1769476
  182.8 16.5 %copy-start.9 = (bf16[4,96,768]{2,1,0:T(8,128)(2,1)S(1)}, bf16[4,96,768]{2,1,0:T(8,128)(2,1)}, u32[]{:S(2)}) copy-start(bf16[4,96,768]{2,1,0:T(8,128)(2,1)} %get-tuple-element.116) | copy-start | bytes 1769476
  182.8 18.9 %collective-permute-start.16 = (bf16[1024,768]{1,0:T(8,128)(2,1)}, bf16[1024,768]{1,0:T(8,128)(2,1)S(1)}, u32[]{:S(2)}, u32[]{:S(2)}) collective-permute-start(bf16[1024,768]{1,0:T(8,128)(2,1)} %get-tuple-element.82.g0_ref), channel_id=1, source_target_pairs={{0,1},{1,0},{2,3},{3,2},{4,5},{5,4},{6,7},{7,6},{8,9},{9,8},{10,11... | collective-permute-start | bytes 4718600 | tf_op jit(solution)/shard_map/ppermute | solution.py:310
  182.9 16.4 %collective-permute-start.28 = (bf16[4,96,768]{2,1,0:T(8,128)(2,1)}, bf16[4,96,768]{2,1,0:T(8,128)(2,1)S(1)}, u32[]{:S(2)}, u32[]{:S(2)}) collective-permute-start(bf16[4,96,768]{2,1,0:T(8,128)(2,1)} %get-tuple-element.117), channel_id=1, source_target_pairs={{0,2},{2,0},{1,3},{3,1},{4,6},{6,4},{5,7},{7,5},{8,10},{10,8},{9,1... | collective-permute-start | bytes 1769480 | tf_op jit(solution)/shard_map/ppermute | solution.py:302
  184.5 86.7 %collective-permute-start.27 = (bf16[4,96,768]{2,1,0:T(8,128)(2,1)}, bf16[4,96,768]{2,1,0:T(8,128)(2,1)}, u32[]{:S(2)}, u32[]{:S(2)}) collective-permute-start(bf16[4,96,768]{2,1,0:T(8,128)(2,1)} %get-tuple-element.115), channel_id=1, source_target_pairs={{0,2},{2,0},{1,3},{3,1},{4,6},{6,4},{5,7},{7,5},{8,10},{10,8},{9,1... | collective-permute-start | bytes 1769480 | tf_op jit(solution)/shard_map/ppermute | solution.py:302
  185.0 79.1 %collective-permute-start.25 = (bf16[4,96,768]{2,1,0:T(8,128)(2,1)}, bf16[4,96,768]{2,1,0:T(8,128)(2,1)}, u32[]{:S(2)}, u32[]{:S(2)}) collective-permute-start(bf16[4,96,768]{2,1,0:T(8,128)(2,1)} %get-tuple-element.113), channel_id=1, source_target_pairs={{0,4},{4,0},{1,5},{5,1},{2,6},{6,2},{3,7},{7,3},{8,12},{12,8},{9,1... | collective-permute-start | bytes 1769480 | tf_op jit(solution)/shard_map/ppermute | solution.py:306
  187.7 79.2 %collective-permute-start.14 = (bf16[512,768]{1,0:T(8,128)(2,1)S(1)}, bf16[512,768]{1,0:T(8,128)(2,1)S(1)}, u32[]{:S(2)}, u32[]{:S(2)}) collective-permute-start(bf16[512,768]{1,0:T(8,128)(2,1)S(1)} %slice.171), channel_id=1, source_target_pairs={{0,1},{1,0},{2,3},{3,2},{4,5},{5,4},{6,7},{7,6},{8,9},{9,8},{10,11... | collective-permute-start | bytes 2359304 | tf_op jit(solution)/shard_map/ppermute | solution.py:310
  200.2 71.0 %collective-permute-start.29 = (bf16[4,96,768]{2,1,0:T(8,128)(2,1)}, bf16[4,96,768]{2,1,0:T(8,128)(2,1)}, u32[]{:S(2)}, u32[]{:S(2)}) collective-permute-start(bf16[4,96,768]{2,1,0:T(8,128)(2,1)} %add.74), channel_id=1, source_target_pairs={{0,4},{4,0},{1,5},{5,1},{2,6},{6,2},{3,7},{7,3},{8,12},{12,8},{9,1... | collective-permute-start | bytes 1769480 | tf_op jit(solution)/shard_map/ppermute | solution.py:306
  201.7 1.1 copy-start.3
  264.0 43.3 %collective-permute-start.17 = (bf16[1024,768]{1,0:T(8,128)(2,1)}, bf16[1024,768]{1,0:T(8,128)(2,1)S(1)}, u32[]{:S(2)}, u32[]{:S(2)}) collective-permute-start(bf16[1024,768]{1,0:T(8,128)(2,1)} %get-tuple-element.98.g0_ref), channel_id=1, source_target_pairs={{0,1},{1,0},{2,3},{3,2},{4,5},{5,4},{6,7},{7,6},{8,9},{9,8},{10,11... | collective-permute-start | bytes 4718600 | tf_op jit(solution)/shard_map/ppermute | solution.py:310
  264.0 16.0 %collective-permute-start.24 = (bf16[4,96,768]{2,1,0:T(8,128)(2,1)}, bf16[4,96,768]{2,1,0:T(8,128)(2,1)}, u32[]{:S(2)}, u32[]{:S(2)}) collective-permute-start(bf16[4,96,768]{2,1,0:T(8,128)(2,1)} %get-tuple-element.111), channel_id=1, source_target_pairs={{0,4},{4,0},{1,5},{5,1},{2,6},{6,2},{3,7},{7,3},{8,12},{12,8},{9,1... | collective-permute-start | bytes 1769480 | tf_op jit(solution)/shard_map/ppermute | solution.py:306
  266.8 4.4 %copy-start.11 = (bf16[4,96,768]{2,1,0:T(8,128)(2,1)S(1)}, bf16[4,96,768]{2,1,0:T(8,128)(2,1)}, u32[]{:S(2)}) copy-start(bf16[4,96,768]{2,1,0:T(8,128)(2,1)} %get-tuple-element.114) | copy-start | bytes 1769476
  266.9 1.6 copy-start.5
  266.9 16.6 %collective-permute-start.26 = (bf16[4,96,768]{2,1,0:T(8,128)(2,1)}, bf16[4,96,768]{2,1,0:T(8,128)(2,1)}, u32[]{:S(2)}, u32[]{:S(2)}) collective-permute-start(bf16[4,96,768]{2,1,0:T(8,128)(2,1)} %add.71), channel_id=1, source_target_pairs={{0,2},{2,0},{1,3},{3,1},{4,6},{6,4},{5,7},{7,5},{8,10},{10,8},{9,1... | collective-permute-start | bytes 1769480 | tf_op jit(solution)/shard_map/ppermute | solution.py:302
  271.2 5.9 %copy-start.2 = (bf16[512,768]{1,0:T(8,128)(2,1)S(1)}, bf16[512,768]{1,0:T(8,128)(2,1)}, u32[]{:S(2)}) copy-start(bf16[512,768]{1,0:T(8,128)(2,1)} %shard_map.319) | copy-start | bytes 2359300
  273.5 5.2 %copy-start.18 = (f32[2,768]{1,0:T(2,128)S(1)}, f32[2,768]{1,0:T(2,128)}, u32[]{:S(2)}) copy-start(f32[2,768]{1,0:T(2,128)} %get-tuple-element.103) | copy-start | bytes 18436
  273.5 22.8 %all-to-all-start.5 = ((bf16[4,96,768]{2,1,0:T(8,128)(2,1)}), bf16[4,96,768]{2,1,0:T(8,128)(2,1)S(1)}, u32[]{:S(2)}, u32[]{:S(2)}) async-start(bf16[4,96,768]{2,1,0:T(8,128)(2,1)} %add_add_fusion), calls=%async_computation.5 | async-start | bytes 1179648 | tf_op jit(solution)/shard_map/all_to_all | solution.py:314
  277.9 13.9 %collective-permute-start.15 = (bf16[256,768]{1,0:T(8,128)(2,1)}, bf16[256,768]{1,0:T(8,128)(2,1)}, u32[]{:S(2)}, u32[]{:S(2)}) collective-permute-start(bf16[256,768]{1,0:T(8,128)(2,1)} %get-tuple-element.190), channel_id=1, source_target_pairs={{0,2},{2,0},{1,3},{3,1},{4,6},{6,4},{5,7},{7,5},{8,10},{10,8},{9,1... | collective-permute-start | bytes 1179656 | tf_op jit(solution)/shard_map/ppermute | solution.py:302
  283.4 12.2 %copy-start.17 = (f32[8,768]{1,0:T(8,128)S(1)}, f32[8,768]{1,0:T(8,128)}, u32[]{:S(2)}) copy-start(f32[8,768]{1,0:T(8,128)} %get-tuple-element.102) | copy-start | bytes 73732
  283.4 12.5 %copy-start.20 = (f32[1,576]{1,0:T(1,128)S(1)}, f32[1,576]{1,0:T(1,128)}, u32[]{:S(2)}) copy-start(f32[1,576]{1,0:T(1,128)} %get-tuple-element.105) | copy-start | bytes 6916
  283.4 12.7 %copy-start.19 = (f32[1,576]{1,0:T(1,128)S(1)}, f32[1,576]{1,0:T(1,128)}, u32[]{:S(2)}) copy-start(f32[1,576]{1,0:T(1,128)} %get-tuple-element.104) | copy-start | bytes 6916
  285.8 18.7 %collective-permute-start.22 = (bf16[4,96,768]{2,1,0:T(8,128)(2,1)}, bf16[4,96,768]{2,1,0:T(8,128)(2,1)}, u32[]{:S(2)}, u32[]{:S(2)}) collective-permute-start(bf16[4,96,768]{2,1,0:T(8,128)(2,1)} %get-tuple-element.109), channel_id=1, source_target_pairs={{0,2},{2,0},{1,3},{3,1},{4,6},{6,4},{5,7},{7,5},{8,10},{10,8},{9,1... | collective-permute-start | bytes 1769480 | tf_op jit(solution)/shard_map/ppermute | solution.py:302
  291.8 12.6 %copy-start.8 = (bf16[4,96,768]{2,1,0:T(8,128)(2,1)S(1)}, bf16[4,96,768]{2,1,0:T(8,128)(2,1)}, u32[]{:S(2)}) copy-start(bf16[4,96,768]{2,1,0:T(8,128)(2,1)} %get-tuple-element.108) | copy-start | bytes 1769476
  294.1 33.7 %collective-permute-start.21 = (bf16[4,96,768]{2,1,0:T(8,128)(2,1)}, bf16[4,96,768]{2,1,0:T(8,128)(2,1)}, u32[]{:S(2)}, u32[]{:S(2)}) collective-permute-start(bf16[4,96,768]{2,1,0:T(8,128)(2,1)} %get-tuple-element.107), channel_id=1, source_target_pairs={{0,2},{2,0},{1,3},{3,1},{4,6},{6,4},{5,7},{7,5},{8,10},{10,8},{9,1... | collective-permute-start | bytes 1769480 | tf_op jit(solution)/shard_map/ppermute | solution.py:302
  296.3 24.2 %all-to-all-start.4 = ((bf16[4,96,768]{2,1,0:T(8,128)(2,1)}), bf16[4,96,768]{2,1,0:T(8,128)(2,1)S(1)}, u32[]{:S(2)}, u32[]{:S(2)}) async-start(bf16[4,96,768]{2,1,0:T(8,128)(2,1)} %add_add_fusion.1), calls=%async_computation.4 | async-start | bytes 1179648 | tf_op jit(solution)/shard_map/all_to_all | solution.py:314
  305.7 22.1 %collective-permute-start.23 = (bf16[4,96,768]{2,1,0:T(8,128)(2,1)S(1)}, bf16[4,96,768]{2,1,0:T(8,128)(2,1)S(1)}, u32[]{:S(2)}, u32[]{:S(2)}) collective-permute-start(bf16[4,96,768]{2,1,0:T(8,128)(2,1)S(1)} %add.68), channel_id=1, source_target_pairs={{0,4},{4,0},{1,5},{5,1},{2,6},{6,2},{3,7},{7,3},{8,12},{12,8},{9,1... | collective-permute-start | bytes 1769480 | tf_op jit(solution)/shard_map/ppermute | solution.py:306
  307.3 1.2 copy-start.4
  314.6 13.2 %copy-start.10 = (bf16[4,96,768]{2,1,0:T(8,128)(2,1)S(1)}, bf16[4,96,768]{2,1,0:T(8,128)(2,1)}, u32[]{:S(2)}) copy-start(bf16[4,96,768]{2,1,0:T(8,128)(2,1)} %get-tuple-element.106) | copy-start | bytes 1769476
  315.8 4.0 %collective-permute-start.19 = (f32[8,9,96]{2,0,1:T(8,128)S(1)}, f32[8,9,96]{2,0,1:T(8,128)S(1)}, u32[]{:S(2)}, u32[]{:S(2)}) collective-permute-start(f32[8,9,96]{2,0,1:T(8,128)S(1)} %constant_dynamic-update-slice_fusion), channel_id=1, source_target_pairs={{0,2},{2,0},{1,3},{3,1},{4,6},{6,4},{5,7},{7,5},{8,10},{10,8},{9,1... | collective-permute-start | bytes 82952 | tf_op jit(solution)/shard_map/ppermute | solution.py:302
  319.8 3.8 %collective-permute-start.20 = (f32[4,8,96]{2,1,0:T(8,128)S(1)}, f32[4,8,96]{2,1,0:T(8,128)S(1)}, u32[]{:S(2)}, u32[]{:S(2)}) collective-permute-start(f32[4,8,96]{2,1,0:T(8,128)S(1)} %bitcast.100), channel_id=1, source_target_pairs={{0,4},{4,0},{1,5},{5,1},{2,6},{6,2},{3,7},{7,3},{8,12},{12,8},{9,1... | collective-permute-start | bytes 36872 | tf_op jit(solution)/shard_map/ppermute | solution.py:306
  324.3 9.1 %all-to-all-start.2 = ((f32[4,8,96]{2,1,0:T(8,128)}), f32[4,8,96]{2,1,0:T(8,128)S(1)}, u32[]{:S(2)}, u32[]{:S(2)}) async-start(f32[4,8,96]{2,1,0:T(8,128)} %fusion.2), calls=%async_computation.2 | async-start | bytes 32768 | tf_op jit(solution)/shard_map/all_to_all | solution.py:314
  327.8 9.1 %copy-start.12 = (bf16[1024,768]{1,0:T(8,128)(2,1)S(1)}, bf16[1024,768]{1,0:T(8,128)(2,1)}, u32[]{:S(2)}) copy-start(bf16[1024,768]{1,0:T(8,128)(2,1)} %get-tuple-element.100) | copy-start | bytes 4718596
  333.4 14.6 %all-to-all-start.3 = ((bf16[4,96,768]{2,1,0:T(8,128)(2,1)}), bf16[4,96,768]{2,1,0:T(8,128)(2,1)S(1)}, u32[]{:S(2)}, u32[]{:S(2)}) async-start(bf16[4,96,768]{2,1,0:T(8,128)(2,1)} %add_add_fusion.2), calls=%async_computation.3 | async-start | bytes 1179648 | tf_op jit(solution)/shard_map/all_to_all | solution.py:314
  336.9 7.8 %collective-permute-start.18 = (bf16[256,768]{1,0:T(8,128)(2,1)S(1)}, bf16[256,768]{1,0:T(8,128)(2,1)S(1)}, u32[]{:S(2)}, u32[]{:S(2)}) collective-permute-start(bf16[256,768]{1,0:T(8,128)(2,1)S(1)} %get-tuple-element.186), channel_id=1, source_target_pairs={{0,2},{2,0},{1,3},{3,1},{4,6},{6,4},{5,7},{7,5},{8,10},{10,8},{9,1... | collective-permute-start | bytes 1179656 | tf_op jit(solution)/shard_map/ppermute | solution.py:302
  344.8 4.8 %copy-start.1 = (bf16[2,768]{1,0:T(2,128)(2,1)S(1)}, bf16[2,768]{1,0:T(2,128)(2,1)}, u32[]{:S(2)}) copy-start(bf16[2,768]{1,0:T(2,128)(2,1)} %param.19) | copy-start | bytes 9220

commit v2 on v1

--- a/solution.py
+++ b/solution.py
@@ -68,23 +68,65 @@
     return center * rate, rate
 
 
-def project_body(x_ref, start_ref, te_ref, vec_ref, bias_ref, own_ref, oth_ref, w_ref, qkv_ref, *norm_refs, rows, first):
+def pack_attn_body(q_ref, k_ref, v_ref, o_ref, fg, fs, ob, sg, ss, db, hb, qb, vb, out_ref):
+    shard = q_ref.shape[0]
+    low = jnp.concatenate([q_ref[...], k_ref[...], v_ref[...], o_ref[...].T], axis=1)
+    n = qb.shape[1]
+    bias = jnp.concatenate([qb[...], vb[...], jnp.zeros((1, shard - 2 * n), BF)], axis=1)
+    small = jnp.concatenate([r[...].astype(F32) for r in (fg, fs, ob, sg, ss, db, hb)] + [bias.astype(F32)], axis=0)
+    small = jnp.concatenate([small, jnp.zeros((KINDS, low.shape[1] - shard), F32)], axis=1).astype(BF)
+    for z in range(out_ref.shape[0]):
+        out_ref[z, :shard, :] = low
+        out_ref[z, shard:, :] = small
+
+
+def pack_mlp_body(h_ref, d_ref, out_ref):
+    shard = h_ref.shape[0]
+    high, low = h_ref[...], d_ref[...].T
+    for z in range(out_ref.shape[0]):
+        out_ref[z, :shard, :] = high
+        out_ref[z, shard:, :] = low
+
+
+def pick(mine_ref, mate_ref):
+    half = pl.num_programs(0) // 2
+    return jnp.where(pl.program_id(0) < half, mine_ref[...], mate_ref[...])
+
+
+def project_body(x_ref, *refs, rows, first):
+    refs = list(refs)
+    if first:
+        mine_ref, mate_ref, te_ref, own_ref, oth_ref, w_ref, vec_ref, qkv_ref, normed_ref, normed_t_ref, bias_ref = refs
+    else:
+        source_ref, own_ref, oth_ref, w_ref, vec_ref, qkv_ref, bias_ref = refs
+
     @pl.when(pl.program_id(0) == 0)
     def _():
         def store(at, value):
             w_ref[pl.ds(at, rows), :] = value
 
         assemble(store, own_ref, oth_ref, x_ref[0], rows)
+        own = [own_ref[z, rows:, :rows].astype(F32) for z in range(ZS)]
+        oth = [oth_ref[z, rows:, :rows].astype(F32) for z in range(ZS)]
+        even = jnp.concatenate([v for pair in zip(own, oth) for v in pair], axis=1)
+        odd = jnp.concatenate([v for pair in zip(oth, own) for v in pair], axis=1)
+        vec = jnp.where(x_ref[0] == 0, even, odd)
+        vec_ref[...] = vec
+        n = rows // 4
+        last = vec[7:8, :]
+        parts = [last[:, rows * k : rows * k + n] for k in range(ZS * XS)]
+        parts += [jnp.zeros((1, 3 * HD), F32)]
+        parts += [last[:, rows * k + n : rows * k + 2 * n] for k in range(ZS * XS)]
+        bias_ref[0:1, :] = jnp.concatenate(parts, axis=1)
 
     if first:
-        normed_ref, normed_t_ref = norm_refs
-        xhat, _ = normalize(start_ref[...].astype(F32) + te_ref[...].astype(F32))
+        xhat, _ = normalize(pick(mine_ref, mate_ref).astype(F32) + te_ref[...].astype(F32))
         normed = (xhat * vec_ref[0:1, :] + vec_ref[1:2, :]).astype(BF)
         normed_ref[...] = normed
         normed_t_ref[...] = normed.T
     else:
-        normed = start_ref[...]
-    made = dot(normed, w_ref[:, :640])[:, :576] + bias_ref[...]
+        normed = source_ref[...]
+    made = dot(normed, w_ref[:, :640])[:, :576] + bias_ref[0:1, :]
     made = made.astype(BF)
     for j in range(9):
         piece = made[:, 64 * j : 64 * j + 64]
@@ -142,9 +184,9 @@
 
 
 def mlp_body(
-    x_ref, start_ref, te_ref, a0_ref, a1_ref, cot_ref, vec_ref, hb_ref,
-    h_oo, h_ox, h_yo, h_yx, d_oo, d_ox, d_yo, d_yx,
-    mid_ref, ff_ref, gs_ref, hbg_ref, gh_oo, gh_ox, gh_yo, gh_yx, gd_oo, gd_ox, gd_yo, gd_yx,
+    x_ref, s0_ref, s1_ref, te_ref, a0_ref, a1_ref, c0_ref, c1_ref, vec_ref, vec_y_ref,
+    w_oo, w_ox, w_yo, h_yx, d_yx,
+    mid_ref, ff0_ref, ff1_ref, gs_ref, hbg_ref, gh_oo, gh_ox, gh_yo, gh_yx, gd_oo, gd_ox, gd_yo, gd_yx,
     wh, wd, acc_h, acc_d, *, rows,
 ):
     step, last = pl.program_id(0), pl.num_programs(0) - 1
@@ -152,16 +194,20 @@
 
     @pl.when(step == 0)
     def _():
-        for y, (own, oth) in enumerate(((h_oo, h_ox), (h_yo, h_yx))):
-            assemble(functools.partial(put, wh, y, rows), own, oth, x, rows)
-        for y, (own, oth) in enumerate(((d_oo, d_ox), (d_yo, d_yx))):
-            assemble(functools.partial(put, wd, y, rows), own, oth, x, rows)
+        for z in range(ZS):
+            own = pl.multiple_of((2 * z + x) * rows, 32)
+            oth = pl.multiple_of((2 * z + 1 - x) * rows, 32)
+            for y, first, second in ((0, w_oo, w_ox), (1, w_yo, None)):
+                wh[y, pl.ds(own, rows), :] = first[z, :rows, :]
+                wd[y, pl.ds(own, rows), :] = first[z, rows:, :]
+                wh[y, pl.ds(oth, rows), :] = h_yx[z] if second is None else second[z, :rows, :]
+                wd[y, pl.ds(oth, rows), :] = d_yx[z] if second is None else second[z, rows:, :]
         acc_h[...] = jnp.zeros_like(acc_h)
         acc_d[...] = jnp.zeros_like(acc_d)
         hbg_ref[...] = jnp.zeros_like(hbg_ref)
 
     middle = (
-        start_ref[...].astype(F32)
+        pick(s0_ref, s1_ref).astype(F32)
         + te_ref[...].astype(F32)
         + (a0_ref[...].astype(F32) + a1_ref[...].astype(F32))
         + vec_ref[2:3, :]
@@ -170,11 +216,11 @@
     xhat, _ = normalize(middle)
     normed = (xhat * vec_ref[3:4, :] + vec_ref[4:5, :]).astype(BF)
     normed_t = normed.T
-    cot = cot_ref[...]
+    cot = pick(c0_ref, c1_ref)
     cot_t = cot.T
     ff = gs = None
     for y in range(2):
-        pre = dot(normed, wh[y]) + hb_ref[y : y + 1, :]
+        pre = dot(normed, wh[y]) + (vec_y_ref if y else vec_ref)[6:7, :]
         below = 0.5 + 0.5 * lax.erf(pre * 0.7071067811865476)
         act = (pre * below).astype(BF)
         slope = below + pre * (jnp.exp(-0.5 * pre * pre) * 0.3989422804014327)
@@ -186,7 +232,15 @@
         acc_h[y] += dot(normed_t, grad)
         acc_d[y] += dot(cot_t, act)
         hbg_ref[y : y + 1, :] += jnp.sum(grad.astype(F32), axis=0, keepdims=True)
-    ff_ref[...] = ff.astype(BF)
+
+    @pl.when(step < pl.num_programs(0) // 2)
+    def _():
+        ff0_ref[...] = ff.astype(BF)
+
+    @pl.when(step >= pl.num_programs(0) // 2)
+    def _():
+        ff1_ref[...] = ff.astype(BF)
+
     gs_ref[...] = gs.astype(BF)
 
     @pl.when(step == last)
@@ -200,11 +254,7 @@
                     oth[z] = acc[y, pl.ds(at, rows), :].astype(BF)
 
 
-def put(ref, y, rows, at, value):
-    ref[y, pl.ds(at, rows), :] = value
-
-
-def second_back_body(mid_ref, g0_ref, g1_ref, cot_ref, vec_ref, w0_ref, w1_ref, m0_ref, m1_ref, gm_ref, x0_ref, x1_ref, wo0_ref, wo1_ref, sum_ref, wo_ref, acc):
+def second_back_body(mid_ref, g0_ref, g1_ref, c0_ref, c1_ref, vec_ref, w0_ref, w1_ref, m0_ref, m1_ref, gm_ref, x0_ref, x1_ref, wo0_ref, wo1_ref, sum_ref, wo_ref, acc):
     step, last = pl.program_id(0), pl.num_programs(0) - 1
 
     @pl.when(step == 0)
@@ -215,7 +265,7 @@
 
     xhat, rate = normalize(mid_ref[...])
     second = g0_ref[...].astype(F32) + g1_ref[...].astype(F32)
-    cot = cot_ref[...].astype(F32)
+    cot = pick(c0_ref, c1_ref).astype(F32)
     scaled = second * vec_ref[3:4, :]
     inner = jnp.mean(scaled * xhat, axis=-1, keepdims=True)
     grad = cot + rate * (scaled - jnp.mean(scaled, axis=-1, keepdims=True) - xhat * inner)
@@ -272,12 +322,12 @@
                 )
 
 
-def first_back_body(start_ref, te_ref, vec_ref, g0_ref, g1_ref, gm_ref, out_ref, sum_ref):
+def first_back_body(s0_ref, s1_ref, te_ref, vec_ref, g0_ref, g1_ref, gm_ref, out_ref, sum_ref):
     @pl.when(pl.program_id(0) == 0)
     def _():
         sum_ref[...] = jnp.zeros_like(sum_ref)
 
-    xhat, rate = normalize(start_ref[...].astype(F32) + te_ref[...].astype(F32))
+    xhat, rate = normalize(pick(s0_ref, s1_ref).astype(F32) + te_ref[...].astype(F32))
     first = g0_ref[...].astype(F32) + g1_ref[...].astype(F32)
     scaled = first * vec_ref[0:1, :]
     inner = jnp.mean(scaled * xhat, axis=-1, keepdims=True)
@@ -350,80 +400,63 @@
     xi = lax.axis_index("b") if fast else jnp.int32(0)
     x_arr = xi.astype(jnp.int32)[None]
 
-    def tokens(values):
-        mine = lax.dynamic_index_in_dim(values, yi, 0, keepdims=False)
-        sent = lax.dynamic_index_in_dim(values, 1 - yi, 0, keepdims=False)
-        pair = jnp.concatenate([mine, to_y(sent)], axis=0)
-        return jnp.concatenate([pair, to_core(pair)], axis=0)
-
-    start = tokens(inputs)
+    both = jnp.concatenate([inputs, cotangent], axis=1)
+    stays = lax.dynamic_index_in_dim(both, yi, 0, keepdims=False).reshape(2, 1, block, width)
+    comes = to_y(lax.dynamic_index_in_dim(both, 1 - yi, 0, keepdims=False)).reshape(2, 1, block, width)
+    pair = jnp.concatenate([stays, comes], axis=1).reshape(2, 2 * block, width)
+    pair_mate = to_core(pair)
     te = lax.dynamic_index_in_dim(time_embed, yi, 0, keepdims=True)
 
-    small = jnp.stack(
-        [first_gain, first_shift, output_bias, second_gain, second_shift, down_bias, hidden_bias,
-         jnp.pad(jnp.concatenate([query_bias, value_bias]), (0, shard - 2 * query_bias.shape[0]))]
+    n_copies = ZS if fast else 1
+    (attn_pack,) = call(
+        pack_attn_body,
+        (1,),
+        [kept((shard, hidden // 4))] * 3 + [kept((hidden // 4, shard))] + [kept((1, shard))] * 7 + [kept((1, query_bias.shape[0]))] * 2,
+        [(sds((n_copies, shard + KINDS, width), BF), kept((n_copies, shard + KINDS, width)))],
+        flops=1e6,
+        moved=1e6,
+    )(
+        query_weight, key_weight, value_weight, output_weight,
+        *(v[None] for v in (first_gain, first_shift, output_bias, second_gain, second_shift, down_bias, hidden_bias, query_bias, value_bias)),
     )
-    small = jnp.pad(small, ((0, 0), (0, width - shard)))
-    attn_pack = jnp.concatenate(
-        [jnp.concatenate([query_weight, key_weight, value_weight, output_weight.T], axis=1), small], axis=0
-    )
-    h_pack, d_pack = hidden_weight, down_weight.T
-
-    def vectors(own, oth):
-        both = jnp.stack([own, oth], axis=1)
-        both = jnp.where(xi == 0, both, both[:, ::-1])
-        return both.reshape(ZS * XS, KINDS, -1)
+    (mlp_pack,) = call(
+        pack_mlp_body,
+        (1,),
+        [kept((shard, hidden)), kept((hidden, shard))],
+        [(sds((n_copies, 2 * shard, width), BF), kept((n_copies, 2 * shard, width)))],
+        flops=1e6,
+        moved=2e6,
+    )(hidden_weight, down_weight)
 
     if fast:
-        def copies(values):
-            return jnp.broadcast_to(values[None], (ZS, *values.shape))
-
-        attn_oo = spread_z(copies(attn_pack))
-        h_pack, d_pack = lax.optimization_barrier((h_pack, d_pack, attn_oo))[:2]
+        attn_oo = spread_z(attn_pack)
         attn_ox = to_x(attn_oo)
         attn_yo = to_y(attn_oo)
         attn_yx = to_y(attn_ox)
-        mlp_z = spread_z(copies(jnp.concatenate([h_pack, d_pack], axis=0)))
-        h_oo, d_oo = mlp_z[:, :rows], mlp_z[:, rows:]
-        h_ox = to_x(h_oo)
-        h_yo = to_y(h_oo)
-        h_yx = to_y(h_ox)
-        d_yo = to_y(d_oo)
-        d_ox = to_x(d_oo)
-        d_yx = to_x(d_yo)
-        vec_o = vectors(attn_oo[:, rows:, :rows], attn_ox[:, rows:, :rows])
-        vec_y = vectors(attn_yo[:, rows:, :rows], attn_yx[:, rows:, :rows])
-        bias_of = vec_o.shape[-1] // 4
+        mlp_oo = spread_z(after(mlp_pack, attn_oo))
     else:
         def natural(values):
             full = lax.all_gather(values, ("a", "b"), axis=0, tiled=True)
             full = full.reshape(ZS, XS, rows, width)
             return full[:, 0], full[:, 1]
 
-        gathered = lax.all_gather(attn_pack, ("a", "b"), axis=0, tiled=False)
+        gathered = lax.all_gather(attn_pack[0], ("a", "b"), axis=0, tiled=False)
         matrix = gathered[:, :shard].reshape(ZS, XS, rows, width)
+        small = gathered[:, shard:, :shard]
+        flat = small[:, :7].transpose(1, 0, 2).reshape(7, width)
+        n = shard // 4
+        bias = [small[:, 7, k * n : k * n + n].reshape(ZS * XS, -1) for k in range(2)]
+        bias = jnp.concatenate([*bias, jnp.zeros((ZS * XS, rows - 2 * (rows // 4)), BF)], axis=1)
+        small = jnp.concatenate([flat, bias.reshape(1, width)], axis=0)
+        small = small.reshape(KINDS, ZS, XS, rows).transpose(1, 2, 0, 3)
+        small = jnp.pad(small, ((0, 0), (0, 0), (0, 0), (0, width - rows)))
+        matrix = jnp.concatenate([matrix, small], axis=2)
         attn_oo, attn_ox = matrix[:, 0], matrix[:, 1]
         attn_yo, attn_yx = to_y(attn_oo), to_y(attn_ox)
-        h_oo, h_ox = natural(h_pack)
-        d_oo, d_ox = natural(d_pack)
-        h_yo, h_yx, d_yo, d_yx = to_y(h_oo), to_y(h_ox), to_y(d_oo), to_y(d_ox)
-        vec_o = gathered[:, shard:, :shard]
-        vec_y = to_y(vec_o)
-        bias_of = shard // 4
-
-    def flat(values):
-        return values.astype(F32).transpose(1, 0, 2).reshape(KINDS, -1)
-
-    def qkv_bias(values):
-        part = values[:, 7, : 2 * bias_of].astype(F32)
-        q_part, v_part = part[:, :bias_of].reshape(1, -1), part[:, bias_of:].reshape(1, -1)
-        return jnp.concatenate([q_part, jnp.zeros_like(q_part), v_part], axis=1)
-
-    vec = flat(vec_o)
-    bias_o, bias_y = qkv_bias(vec_o), qkv_bias(vec_y)
-    hb = jnp.concatenate([vec[6:7], flat(vec_y)[6:7]], axis=0)
-
-    cot = tokens(cotangent)
+        h_oo, h_ox = natural(mlp_pack[0, :shard])
+        d_oo, d_ox = natural(mlp_pack[0, shard:])
+        mlp_oo = jnp.concatenate([h_oo, d_oo], axis=1)
+        mlp_ox = jnp.concatenate([h_ox, d_ox], axis=1)
 
     by_tile = pl.BlockSpec((tile, width), lambda i: (i, 0))
     by_mate = pl.BlockSpec((tile, width), lambda i: ((i + tiles // 2) % tiles, 0))
@@ -433,9 +466,16 @@
     part_rows = attn_oo.shape[1]
     heads9 = pl.BlockSpec((9, tile, HD), lambda i: (0, i, 0))
 
-    def project(first, source, bias, own, oth):
+    def mine(which):
+        return pl.BlockSpec((None, tile, width), lambda i: (which, jnp.minimum(i, tiles // 2 - 1), 0))
+
+    def mate(which):
+        return pl.BlockSpec((None, tile, width), lambda i: (which, jnp.maximum(i - tiles // 2, 0), 0))
+
+    def project(first, source, own, oth):
         outs = [
             (sds((width, width), BF), kept((width, width))),
+            (sds((KINDS, width), F32), vecs),
             (sds((9, seq, HD), BF), heads9),
         ]
         if first:
@@ -446,11 +486,12 @@
         return call(
             functools.partial(project_body, rows=rows, first=first),
             (tiles,),
-            [scalar(), by_tile, row, vecs, kept((1, 576)), whole((ZS, part_rows, width)), whole((ZS, part_rows, width))],
+            [scalar()] + ([mine(0), mate(0), row] if first else [by_tile]) + [whole((ZS, part_rows, width))] * 2,
             outs,
+            scratch=[pltpu.VMEM((8, 9 * HD), F32)],
             flops=2 * seq * width * 576,
             moved=8e6,
-        )(x_arr, source, te, vec, bias, own, oth)
+        )(x_arr, *source, own, oth)
 
     chunks = tiles
     q_spec = pl.BlockSpec((1, tile, HD), lambda h, i: (h, i, 0))
@@ -488,10 +529,18 @@
             moved=9e6,
         )(qkv, qkv, qkv, expon, inverse, mixed, grad_mixed)
 
-    w_o, qkv_o, normed, normed_t = project(True, start, bias_o, attn_oo, attn_ox)
+    w_o, vec, qkv_o, normed, normed_t = project(True, (pair, pair_mate, te), attn_oo, attn_ox)
     exp_o, inv_o, mixed_o, wide_o = attend(qkv_o)
-    w_y, qkv_y = project(False, normed, bias_y, attn_yo, attn_yx)
+    normed, exp_o, mlp_oo, attn_yo, attn_yx = lax.optimization_barrier((normed, exp_o, mlp_oo, attn_yo, attn_yx))
+    if fast:
+        mlp_ox, mlp_yo = to_x(mlp_oo), to_y(mlp_oo)
+    else:
+        mlp_yo = to_y(mlp_oo)
+    w_y, vec_y, qkv_y = project(False, (normed,), attn_yo, attn_yx)
     exp_y, inv_y, mixed_y, wide_y = attend(qkv_y)
+    mixed_y, mlp_ox, mlp_yo = lax.optimization_barrier((mixed_y, mlp_ox, mlp_yo))
+    h_yx = to_y(mlp_ox[:, :rows])
+    d_yx = to_x(mlp_yo[:, rows:]) if fast else to_y(mlp_ox[:, rows:])
 
     half_t = pl.BlockSpec((3 * HD, tile), lambda i: (0, i))
     flat_o, flat_y = mixed_o.reshape(3 * HD, seq), mixed_y.reshape(3 * HD, seq)
@@ -507,13 +556,14 @@
     attended_mate = to_core(attended)
 
     part = (ZS, rows, hidden)
-    middle, ff, gs, hb_sum, gh_oo, gh_ox, gh_yo, gh_yx, gd_oo, gd_ox, gd_yo, gd_yx = call(
+    middle, ff, ff_sent, gs, hb_sum, gh_oo, gh_ox, gh_yo, gh_yx, gd_oo, gd_ox, gd_yo, gd_yx = call(
         functools.partial(mlp_body, rows=rows),
         (tiles,),
-        [scalar(), by_tile, row, by_tile, by_mate, by_tile, vecs, kept((2, hidden))] + [whole(part)] * 8,
+        [scalar(), mine(0), mate(0), row, by_tile, by_mate, mine(1), mate(1), vecs, vecs] + [whole((ZS, 2 * rows, hidden))] * 3 + [whole(part)] * 2,
         [
             (sds((seq, width), F32), by_tile),
-            (sds((seq, width), BF), by_tile),
+            (sds((seq // 2, width), BF), pl.BlockSpec((tile, width), lambda i: (jnp.minimum(i, tiles // 2 - 1), 0))),
+            (sds((seq // 2, width), BF), pl.BlockSpec((tile, width), lambda i: (jnp.maximum(i - tiles // 2, 0), 0))),
             (sds((seq, width), BF), by_tile),
             (sds((2, hidden), F32), kept((2, hidden))),
         ]
@@ -527,13 +577,13 @@
         flops=12 * seq * width * hidden * 2,
         moved=24e6,
         trans=seq * hidden * 4,
-    )(x_arr, start, te, attended, attended_mate, cot, vec, hb, h_oo, h_ox, h_yo, h_yx, d_oo, d_ox, d_yo, d_yx)
+    )(x_arr, pair, pair_mate, te, attended, attended_mate, pair, pair_mate, vec, vec_y, mlp_oo, mlp_ox, mlp_yo, h_yx, d_yx)
     gs_mate = to_core(gs)
 
     grad_middle, gx_o, gx_y, wo_o, wo_y, second_sums = call(
         second_back_body,
         (tiles,),
-        [by_tile, by_tile, by_mate, by_tile, vecs, square, square, half_t, half_t],
+        [by_tile, by_tile, by_mate, mine(1), mate(1), vecs, square, square, half_t, half_t],
         [
             (sds((seq, width), F32), by_tile),
             (sds((3 * HD, seq), BF), half_t),
@@ -545,7 +595,7 @@
         scratch=[pltpu.VMEM((width, 6 * HD), BF), pltpu.VMEM((width, 6 * HD), F32)],
         flops=4 * seq * width * 384,
         moved=16e6,
-    )(middle, gs, gs_mate, cot, vec, w_o, w_y, flat_o, flat_y)
+    )(middle, gs, gs_mate, pair, pair_mate, vec, w_o, w_y, flat_o, flat_y)
 
     heads = pl.BlockSpec((3, tile, HD), lambda i: (0, i, 0))
     attn_part = (ZS, rows, width)
@@ -568,23 +618,8 @@
             moved=10e6,
         )(x_arr, *grads, normed_t, weights, wo, *((prev,) if more else ()))
 
-    grads_y = attend_back(qkv_y, exp_y, inv_y, wide_y, gx_y.reshape(3, HD, seq))
-    ga_yo, ga_yx, first_part, qkv_sum_y = project_back(grads_y, w_y, wo_y, None)
-    grads_o = attend_back(qkv_o, exp_o, inv_o, wide_o, gx_o.reshape(3, HD, seq))
-    ga_oo, ga_ox, first, qkv_sum_o = project_back(grads_o, w_o, wo_o, first_part)
-    first_mate = to_core(first)
-
-    input_grad, first_sums = call(
-        first_back_body,
-        (tiles,),
-        [by_tile, row, vecs, by_tile, by_mate, by_tile],
-        [(sds((seq, width), BF), by_tile), (sds((KINDS, width), F32), kept((KINDS, width)))],
-        flops=1e6,
-        moved=12e6,
-    )(start, te, vec, first, first_mate, grad_middle)
-
     half = tiles // 2
-    ff_mate = to_core(ff[seq // 2 :])
+    ff_mate = to_core(ff_sent)
     (out_tokens,) = call(
         output_body,
         (half,),
@@ -593,41 +628,48 @@
         flops=1e6,
         moved=5e6,
     )(middle, ff, ff_mate, vec)
-
-    def placed(values):
-        mine, sent = values[:block], values[block : 2 * block]
-        got = to_y(sent)
-        return jnp.where(yi == 0, jnp.stack([mine, got]), jnp.stack([got, mine]))
-
-    block_output = placed(out_tokens)
-    input_gradient = placed(input_grad)
+    if fast:
+        got_h, got_d = to_x(gh_yx), to_y(gd_yx)
+        gx_y, out_tokens, got_h, got_d, gh_ox, gd_yo = lax.optimization_barrier(
+            (gx_y, out_tokens, got_h, got_d, gh_ox, gd_yo)
+        )
+        got_ho, got_do = to_x(gh_ox), to_y(gd_yo)
+        got_hs, got_ds = to_y(gh_yo + got_h), to_x(gd_ox + got_d)
+    out_got = to_y(out_tokens[block:])
+    grads_y = attend_back(qkv_y, exp_y, inv_y, wide_y, gx_y.reshape(3, HD, seq))
+    ga_yo, ga_yx, first_part, qkv_sum_y = project_back(grads_y, w_y, wo_y, None)
+    if fast:
+        gx_o, first_part, out_got, got_ho, got_do, got_hs, got_ds, ga_yo, ga_yx = lax.optimization_barrier(
+            (gx_o, first_part, out_got, got_ho, got_do, got_hs, got_ds, ga_yo, ga_yx)
+        )
+        mlp_all = spread_z(jnp.concatenate([gh_oo + got_ho + got_hs, gd_oo + got_do + got_ds], axis=1))
+        ga_sx = to_y(ga_yx)
+    grads_o = attend_back(qkv_o, exp_o, inv_o, wide_o, gx_o.reshape(3, HD, seq))
+    if fast:
+        *grads_o, ga_sx, ga_yo = lax.optimization_barrier((*grads_o, ga_sx, ga_yo))
+        ga_so = to_y(ga_yo)
+    ga_oo, ga_ox, first, qkv_sum_o = project_back(grads_o, w_o, wo_o, first_part)
+    first_mate = to_core(first)
+    if fast:
+        ga_x = to_x(ga_ox + ga_sx)
+        first_mate, mlp_all, ga_so = lax.optimization_barrier((first_mate, mlp_all, ga_so))
+
+    input_grad, first_sums = call(
+        first_back_body,
+        (tiles,),
+        [mine(0), mate(0), row, vecs, by_tile, by_mate, by_tile],
+        [(sds((seq, width), BF), by_tile), (sds((KINDS, width), F32), kept((KINDS, width)))],
+        flops=1e6,
+        moved=12e6,
+    )(pair, pair_mate, te, vec, first, first_mate, grad_middle)
 
     def total(values):
         return jnp.sum(values.astype(F32), axis=0)
-
-    def scatter_xy(oo, ox, yo, yx):
-        got_o, got_y = to_x(ox), to_x(yx)
-        own, oth = oo + got_o, yo + got_y
-        return own + to_y(oth)
-
-    def scatter_yx(oo, ox, yo, yx):
-        got_y, got_x = to_y(yo), to_y(yx)
-        own, oth = oo + got_y, ox + got_x
-        return own + to_x(oth)
 
     def scatter_slow(oo, ox, yo, yx):
         own, oth = oo + to_y(yo), ox + to_y(yx)
         full = jnp.stack([own, oth], axis=1).reshape(width, -1).astype(F32)
         return lax.psum_scatter(full, ("a", "b"), scatter_dimension=0, tiled=True)
-
-    if fast:
-        gh = total(spread_z(scatter_xy(gh_oo, gh_ox, gh_yo, gh_yx)))
-        gd = total(spread_z(scatter_yx(gd_oo, gd_ox, gd_yo, gd_yx)))
-        ga = total(spread_z(scatter_yx(ga_oo, ga_ox, ga_yo, ga_yx)))
-    else:
-        gh = scatter_slow(gh_oo, gh_ox, gh_yo, gh_yx)
-        gd = scatter_slow(gd_oo, gd_ox, gd_yo, gd_yx)
-        ga = scatter_slow(ga_oo, ga_ox, ga_yo, ga_yx)
 
     owners = width // shard
 
@@ -647,15 +689,30 @@
     embed_got = got[:, KINDS].reshape(width)
     embed_gradient = jnp.where(yi == 0, jnp.stack([embed, embed_got]), jnp.stack([embed_got, embed]))
     small_sum = small_o + got[:, :KINDS]
+    n_head = query_weight.shape[1]
     if fast:
         by_x = small_sum.reshape(ZS, XS, KINDS, shard)
-        mine = lax.dynamic_index_in_dim(by_x, xi, 1, keepdims=False)
+        stays = lax.dynamic_index_in_dim(by_x, xi, 1, keepdims=False)
         other = lax.dynamic_index_in_dim(by_x, 1 - xi, 1, keepdims=False)
-        sums = total(spread_z(mine + to_x(other)))
+        small_x = to_x(other)
+        input_grad, small_x, ga_x = lax.optimization_barrier((input_grad, small_x, ga_x))
+        small_sum = jnp.pad((stays + small_x).astype(BF), ((0, 0), (0, 0), (0, width - shard)))
+        ga = total(spread_z(jnp.concatenate([ga_oo + ga_so + ga_x, small_sum], axis=1)))
+        ga, sums = ga[:shard], ga[shard:, :shard]
+        mlp_sum = total(mlp_all)
+        gh, gd = mlp_sum[:shard], mlp_sum[shard:]
     else:
         sums = lax.psum_scatter(small_sum, ("a", "b"), scatter_dimension=0, tiled=True)[0]
+        gh = scatter_slow(gh_oo, gh_ox, gh_yo, gh_yx)
+        gd = scatter_slow(gd_oo, gd_ox, gd_yo, gd_yx)
+        ga = scatter_slow(ga_oo, ga_ox, ga_yo, ga_yx)
+
+    def placed(mine, got):
+        return jnp.where(yi == 0, jnp.stack([mine, got]), jnp.stack([got, mine]))
+
+    block_output = placed(out_tokens[:block], out_got)
+    input_gradient = placed(input_grad[:block], to_y(input_grad[block : 2 * block]))
     n_bias = query_bias.shape[0]
-    n_head = query_weight.shape[1]
     return (
         block_output,
         input_gradient,

time: 352 us -> 303 us (0.86)
  waiting for transfers between devices: 110 us -> 77.2 us
  other arithmetic: 25.1 us -> 10.5 us
  starting transfers between devices: 53.9 us -> 42.8 us
  Pallas kernels: 136 us -> 142 us
  local copies, waits for them, and re-layouts: 23 us -> 26.6 us
    ppermute x15 -> x13, waiting for transfers between devices: 70.7 us -> 46.9 us  [to_y(): return lax.ppermute(values, 'y', swap(2))]
    add x7 -> x5, other arithmetic: 11.8 us -> 4.17 us  [the longest x1 2.2 us: body(): ga_x = to_x(ga_ox + ga_sx)]
    all_to_all x6 -> x4, waiting for transfers between devices: 11.8 us -> 4.74 us  [spread_z(): return lax.all_to_all(values, 'a', 0, 0, tiled=True)]
    unnamed x66, local copies, waits for them, and re-layouts: 7.99 us -> 13.9 us
    pallas_call x3 -> x5, Pallas kernels: 40.9 us -> 46.3 us  [the longest x1 25.6 us: body(): call(functools.partial(mlp_body, rows=rows), (tiles,), [scalar(), mine(0)...]
    all_to_all x6 -> x4, starting transfers between devices: 23.9 us -> 18.7 us  [spread_z(): return lax.all_to_all(values, 'a', 0, 0, tiled=True)]
    ppermute x15 -> x13, starting transfers between devices: 19.4 us -> 14.9 us  [to_y(): return lax.ppermute(values, 'y', swap(2))]
    ppermute x9 -> x8, waiting for transfers between devices: 27.9 us -> 23.7 us  [to_x(): return lax.ppermute(values, 'b', swap(2))]
  transfers between devices with their start and end apart: 36 -> 30, of which waited for: 19 -> 14; matrix products, arithmetic and copies ran while one was open for 10% -> 8% of each run, Pallas kernels for 32% -> 37%
where the time goes in v2:
time: 303 us; the launch traced here: 300 us
  Pallas kernels  142 us (47%)
  waiting for transfers between devices  77.2 us (25%)
  starting transfers between devices  42.8 us (14%)
  local copies, waits for them, and re-layouts  26.6 us (9%)
  other arithmetic  10.5 us (3%)
    ppermute x13, waiting for transfers between devices, to_y(): return lax.ppermute(values, 'y', swap(2))  46.9 us
    pallas_call x2, Pallas kernels, attend_back(): call(attend_back_body, (3, chunks), [q_spec, k_spec, v_spec, e_spec, inv_...  32.5 us
    pallas_call x1, Pallas kernels, body(): call(functools.partial(mlp_body, rows=rows), (tiles,), [scalar(), mine(0)...  25.6 us
    pallas_call x2, Pallas kernels, attend(): call(attend_body, (3, chunks), [q_spec, k_spec, v_spec], [(sds((3, seq, s...  24.4 us
    ppermute x8, waiting for transfers between devices, to_x(): return lax.ppermute(values, 'b', swap(2))  23.7 us
    all_to_all x4, starting transfers between devices, spread_z(): return lax.all_to_all(values, 'a', 0, 0, tiled=True)  18.7 us
    pallas_call x2, Pallas kernels, project_back(): call(functools.partial(project_back_body, rows=rows, more=more), (tiles,)...  18.6 us
    ppermute x13, starting transfers between devices, to_y(): return lax.ppermute(values, 'y', swap(2))  14.9 us
  transfers between devices with their start and end apart: 30, of which 14 were waited for; matrix products, arithmetic and copies ran while one was open for 8% of the time, Pallas kernels for 37%

profile of v2, /device:TPU:0, one launch (start us, length us, event | category | flops | bytes accessed | tf_op | source)
XLA Modules:
  0.0 300.0 jit_solution(12616690577128410948)
XLA Ops:
  0.7 1.3 constant_dynamic-update-slice_fusion.1
  2.2 3.0 %collective-permute-start = (bf16[512,768]{1,0:T(8,128)(2,1)S(1)}, bf16[512,768]{1,0:T(8,128)(2,1)}, u32[]{:S(2)}, u32[]{:S(2)}) collective-permute-start(bf16[512,768]{1,0:T(8,128)(2,1)S(1)} %get-tuple-element.260), channel_id=1, source_target_pairs={{0,2},{2,0},{1,3},{3,1},{4,6},{6,4},{5,7},{7,5},{8,10},{10,8},{9,1... | collective-permute-start | bytes 2359304 | tf_op jit(solution)/shard_map/ppermute | solution.py:352
  5.3 1.9 shard_map.313
  7.2 4.9 %all-to-all-start = ((bf16[4,104,768]{2,1,0:T(8,128)(2,1)}), bf16[4,104,768]{2,1,0:T(8,128)(2,1)}, u32[]{:S(2)}, u32[]{:S(2)}) async-start(bf16[4,104,768]{2,1,0:T(8,128)(2,1)} %shard_map.313), calls=%async_computation | async-start | bytes 1277952 | tf_op jit(solution)/shard_map/all_to_all | solution.py:364
  12.0 10.9 %collective-permute-done = bf16[512,768]{1,0:T(8,128)(2,1)} collective-permute-done((bf16[512,768]{1,0:T(8,128)(2,1)S(1)}, bf16[512,768]{1,0:T(8,128)(2,1)}, u32[]{:S(2)}, u32[]{:S(2)}) %collective-permute-start) | collective-permute-done | bytes 786464 | tf_op jit(solution)/shard_map/ppermute | solution.py:352
  22.9 1.3 pad_maximum_fusion
  24.3 1.1 copy.48.d_ref
  25.4 2.2 shard_map.316
  27.6 1.2 all-to-all-done.refs_3_
  28.8 4.3 %all-to-all-start.1 = ((bf16[4,192,768]{2,1,0:T(8,128)(2,1)}), bf16[4,192,768]{2,1,0:T(8,128)(2,1)}, u32[]{:S(2)}, u32[]{:S(2)}) async-start(bf16[4,192,768]{2,1,0:T(8,128)(2,1)} %shard_map.316), calls=%async_computation.1 | async-start | bytes 2359296 | tf_op jit(solution)/shard_map/all_to_all | solution.py:364
  33.1 1.6 collective-permute-start.2
  34.6 1.1 collective-permute-start.3
  35.7 13.5 %collective-permute-done.2.refs_4_ = bf16[4,104,768]{2,1,0:T(8,128)(2,1)} collective-permute-done((bf16[4,104,768]{2,1,0:T(8,128)(2,1)}, bf16[4,104,768]{2,1,0:T(8,128)(2,1)}, u32[]{:S(2)}, u32[]{:S(2)}) %collective-permute-start.2) | collective-permute-done | bytes 639008 | tf_op jit(solution)/shard_map/ppermute | solution.py:356
  49.2 1.5 collective-permute-start.4
  51.4 1.2 copy-done.3
  52.5 6.3 %shard_map.314 = (bf16[768,768]{1,0:T(8,128)(2,1)}, f32[8,768]{1,0:T(8,128)}, bf16[9,1024,64]{2,1,0:T(8,128)(2,1)}, bf16[1024,768]{1,0:T(8,128)(2,1)}, bf16[768,1024]{1,0:T(8,128)(2,1)}) custom-call(s32[1]{0:T(128)} %bitcast.x_ref, bf16[2,512,768]{2,1,0:T(8,128)(2,1)} %bitcast.68, bf16[2,512,768]{2,1,0:T(8,128)(2,1)} %copy-done.3, ...), custom_call_target="tpu_custom_call" | custom-call | flops 905969664 | bytes 8000000 | tf_op jit(solution)/shard_map/pallas_call | solution.py:486
  58.8 12.2 %shard_map.315 = (bf16[3,1024,1024]{2,1,0:T(8,128)(2,1)}, f32[3,1,1024]{2,1,0:T(1,128)}, bf16[3,64,1024]{2,1,0:T(8,128)(2,1)}, f32[3,64,1024]{2,1,0:T(8,128)}) custom-call(bf16[9,1024,64]{2,1,0:T(8,128)(2,1)} %get-tuple-element.104.q_ref.k_ref.v_ref, bf16[9,1024,64]{2,1,0:T(8,128)(2,1)} %get-tuple-element.104.q_ref.k_ref.v_ref, ...), custom_call_target="tpu_custom_call" | custom-call | flops 3221225472 | bytes 8000000 | tf_op jit(solution)/shard_map/pallas_call | solution.py:505
  71.1 1.6 collective-permute-start.5
  73.1 5.4 %shard_map.317 = (bf16[768,768]{1,0:T(8,128)(2,1)}, f32[8,768]{1,0:T(8,128)}, bf16[9,1024,64]{2,1,0:T(8,128)(2,1)}) custom-call(s32[1]{0:T(128)} %bitcast.x_ref, bf16[1024,768]{1,0:T(8,128)(2,1)} %get-tuple-element.109.refs_0_, bf16[4,104,768]{2,1,0:T(8,128)(2,1)} %collective-permute-done.3.refs_1_, bf16[4,104,768]{2,1,0:T(8,128)(2,1)} %collective-permute-done.4.refs_2_), custom_call_target="tpu_custom_call" | custom-call | flops 905969664 | bytes 8000000 | tf_op jit(solution)/shard_map/pallas_call | solution.py:486
  78.6 12.2 %shard_map.318 = (bf16[3,1024,1024]{2,1,0:T(8,128)(2,1)}, f32[3,1,1024]{2,1,0:T(1,128)}, bf16[3,64,1024]{2,1,0:T(8,128)(2,1)}, f32[3,64,1024]{2,1,0:T(8,128)}) custom-call(bf16[9,1024,64]{2,1,0:T(8,128)(2,1)} %get-tuple-element.112.q_ref.k_ref.v_ref, bf16[9,1024,64]{2,1,0:T(8,128)(2,1)} %get-tuple-element.112.q_ref.k_ref.v_ref, ...), custom_call_target="tpu_custom_call" | custom-call | flops 3221225472 | bytes 8000000 | tf_op jit(solution)/shard_map/pallas_call | solution.py:505
  90.8 7.2 %collective-permute-done.5.w_ox = bf16[4,192,768]{2,1,0:T(8,128)(2,1)S(1)} collective-permute-done((bf16[4,192,768]{2,1,0:T(8,128)(2,1)}, bf16[4,192,768]{2,1,0:T(8,128)(2,1)S(1)}, u32[]{:S(2)}, u32[]{:S(2)}) %collective-permute-start.5) | collective-permute-done | bytes 1179680 | tf_op jit(solution)/shard_map/ppermute | solution.py:356
  98.0 1.2 collective-permute-done.6.w_yo
  99.2 5.6 %shard_map.319.a0_ref = bf16[1024,768]{1,0:T(8,128)(2,1)} custom-call(bf16[192,1024]{1,0:T(8,128)(2,1)} %bitcast.74, bf16[192,1024]{1,0:T(8,128)(2,1)} %bitcast.76, bf16[768,768]{1,0:T(8,128)(2,1)} %get-tuple-element.116.w0_ref.w_ref, bf16[768,768]{1,0:T(8,128)(2,1)} %get-tuple-element.117.w1_ref.w_ref), custom_call_target="tpu_custom_call" | custom-call | flops 603979776 | bytes 6000000 | tf_op jit(solution)/shard_map/pallas_call | solution.py:547
  106.0 14.6 %collective-permute-done.8.h_yx = bf16[4,96,768]{2,1,0:T(8,128)(2,1)S(1)} collective-permute-done((bf16[4,96,768]{2,1,0:T(8,128)(2,1)S(1)}, bf16[4,96,768]{2,1,0:T(8,128)(2,1)S(1)}, u32[]{:S(2)}, u32[]{:S(2)}) %collective-permute-start.8) | collective-permute-done | bytes 589856 | tf_op jit(solution)/shard_map/ppermute | solution.py:352
  122.2 25.6 %shard_map.320 = (f32[1024,768]{1,0:T(8,128)}, bf16[512,768]{1,0:T(8,128)(2,1)}, bf16[512,768]{1,0:T(8,128)(2,1)}, bf16[1024,768]{1,0:T(8,128)(2,1)}, f32[2,768]...) custom-call(s32[1]{0:T(128)} %bitcast.x_ref, ...), custom_call_target="tpu_custom_call" | custom-call | flops 14495514624 | bytes 24000000 | tf_op jit(solution)/shard_map/pallas_call | solution.py:559
  149.1 1.7 collective-permute-start.13
  150.8 1.9 collective-permute-done.11.f1_ref
  152.6 0.9 copy-done.8
  153.5 2.7 shard_map.322
  156.3 1.1 copy-done.6
  157.4 10.3 %shard_map.321 = (f32[1024,768]{1,0:T(8,128)}, bf16[192,1024]{1,0:T(8,128)(2,1)}, bf16[192,1024]{1,0:T(8,128)(2,1)}, bf16[768,192]{1,0:T(8,128)(2,1)}, bf16[768,192]{1,0:T(8,128)(2,1)}, /*index=5*/f32[8,768]{1,0:T(8,128)}) custom-call(f32[1024,768]{1,0:T(8,128)} %get-tuple-element.122.mid_ref, bf16[1024,768]{1,0:T(8,128)(2,1)} %get-tuple-element.123.g0_ref, ...), custom_call_target="tpu_custom_call" | custom-call | flops 1207959552 | bytes 16000000 | tf_op jit(solution)/shard_map/pallas_call | solution.py:583
  167.9 0.8 collective-permute-start.18
  168.9 1.8 collective-permute-start.17
  171.1 1.2 collective-permute-start.15
  172.4 1.7 collective-permute-start.16
  174.1 16.2 %shard_map.323 = (bf16[3,1024,64]{2,1,0:T(8,128)(2,1)}, bf16[3,1024,64]{2,1,0:T(8,128)(2,1)}, bf16[3,1024,64]{2,1,0:T(8,128)(2,1)}) custom-call(bf16[9,1024,64]{2,1,0:T(8,128)(2,1)} %get-tuple-element.112.q_ref.k_ref.v_ref, bf16[9,1024,64]{2,1,0:T(8,128)(2,1)} %get-tuple-element.112.q_ref.k_ref.v_ref, ...), custom_call_target="tpu_custom_call" | custom-call | flops 8053063680 | bytes 9000000 | tf_op jit(solution)/shard_map/pallas_call | solution.py:522
  190.3 9.1 %shard_map.324 = (bf16[4,96,768]{2,1,0:T(8,128)(2,1)}, bf16[4,96,768]{2,1,0:T(8,128)(2,1)}, f32[1024,768]{1,0:T(8,128)}, f32[1,576]{1,0:T(1,128)}) custom-call(s32[1]{0:T(128)} %bitcast.x_ref, bf16[3,1024,64]{2,1,0:T(8,128)(2,1)} %get-tuple-element.137.q_ref, bf16[3,1024,64]{2,1,0:T(8,128)(2,1)} %get-tuple-element.138.k_ref, ...), custom_call_target="tpu_custom_call" | custom-call | flops 1811939328 | bytes 10000000 | tf_op jit(solution)/shard_map/pallas_call | solution.py:605
  199.5 5.9 %collective-permute-done.16 = bf16[4,96,768]{2,1,0:T(8,128)(2,1)S(1)} collective-permute-done((bf16[4,96,768]{2,1,0:T(8,128)(2,1)S(1)}, bf16[4,96,768]{2,1,0:T(8,128)(2,1)S(1)}, u32[]{:S(2)}, u32[]{:S(2)}) %collective-permute-start.16) | collective-permute-done | bytes 589856 | tf_op jit(solution)/shard_map/ppermute | solution.py:352
  205.4 1.7 collective-permute-start.19
  207.3 1.1 pad_maximum_fusion.1
  208.4 4.5 %all-to-all-start.2 = ((bf16[4,192,768]{2,1,0:T(8,128)(2,1)}), bf16[4,192,768]{2,1,0:T(8,128)(2,1)S(1)}, u32[]{:S(2)}, u32[]{:S(2)}) async-start(bf16[4,192,768]{2,1,0:T(8,128)(2,1)} %pad_maximum_fusion.1), calls=%async_computation.2 | async-start | bytes 2359296 | tf_op jit(solution)/shard_map/all_to_all | solution.py:364
  212.9 16.3 %shard_map.325 = (bf16[3,1024,64]{2,1,0:T(8,128)(2,1)}, bf16[3,1024,64]{2,1,0:T(8,128)(2,1)}, bf16[3,1024,64]{2,1,0:T(8,128)(2,1)}) custom-call(bf16[9,1024,64]{2,1,0:T(8,128)(2,1)} %get-tuple-element.104.q_ref.k_ref.v_ref, bf16[9,1024,64]{2,1,0:T(8,128)(2,1)} %get-tuple-element.104.q_ref.k_ref.v_ref, ...), custom_call_target="tpu_custom_call" | custom-call | flops 8053063680 | bytes 9000000 | tf_op jit(solution)/shard_map/pallas_call | solution.py:522
  229.2 9.5 %shard_map.326 = (bf16[4,96,768]{2,1,0:T(8,128)(2,1)}, bf16[4,96,768]{2,1,0:T(8,128)(2,1)}, bf16[1024,768]{1,0:T(8,128)(2,1)}, f32[1,576]{1,0:T(1,128)}) custom-call(s32[1]{0:T(128)} %bitcast.x_ref, bf16[3,1024,64]{2,1,0:T(8,128)(2,1)} %get-tuple-element.161.q_ref, bf16[3,1024,64]{2,1,0:T(8,128)(2,1)} %get-tuple-element.162.k_ref, ...), custom_call_target="tpu_custom_call" | custom-call | flops 1811939328 | bytes 10000000 | tf_op jit(solution)/shard_map/pallas_call | solution.py:605
  240.5 0.9 slice_reduce_fusion.2
  245.0 2.2 add.67
  247.2 0.9 collective-permute-start.24
  248.8 0.8 reshape.89
  249.5 5.3 %collective-permute-done.21 = bf16[4,96,768]{2,1,0:T(8,128)(2,1)} collective-permute-done((bf16[4,96,768]{2,1,0:T(8,128)(2,1)}, bf16[4,96,768]{2,1,0:T(8,128)(2,1)}, u32[]{:S(2)}, u32[]{:S(2)}) %collective-permute-start.21) | collective-permute-done | bytes 589856 | tf_op jit(solution)/shard_map/ppermute | solution.py:352
  254.8 1.1 copy-done.5
  256.0 6.3 %shard_map.327 = (bf16[1024,768]{1,0:T(8,128)(2,1)}, f32[8,768]{1,0:T(8,128)}) custom-call(bf16[2,512,768]{2,1,0:T(8,128)(2,1)} %bitcast.72, bf16[2,512,768]{2,1,0:T(8,128)(2,1)} %copy-done.3, bf16[1,768]{1,0:T(2,128)(2,1)} %constant_dynamic-slice_fusion.2.refs_2_.te_ref, f32[8,768]{1,0:T(8,128)} %get-tuple-element.118.vec_ref, ...), custom_call_target="tpu_custom_call" | custom-call | flops 1000000 | bytes 12000000 | tf_op jit(solution)/shard_map/pallas_call | solution.py:657
  262.3 1.4 slice_reduce_fusion.12
  268.6 2.9 collective-permute-done.22
  271.5 1.0 collective-permute-start.23
  272.5 2.8 collective-permute-done.23
  275.3 1.5 add_add_fusion
  276.8 0.9 fusion.1
  277.7 5.1 %all-to-all-start.3 = ((bf16[4,104,768]{2,1,0:T(8,128)(2,1)}), bf16[4,104,768]{2,1,0:T(8,128)(2,1)S(1)}, u32[]{:S(2)}, u32[]{:S(2)}) async-start(bf16[4,104,768]{2,1,0:T(8,128)(2,1)} %fusion.1), calls=%async_computation.3 | async-start | bytes 1277952 | tf_op jit(solution)/shard_map/all_to_all | solution.py:364
  282.8 1.0 maximum_select_fusion
  285.1 0.8 slice_bitcast_fusion.2
  286.7 6.0 %collective-permute-done.25 = bf16[256,768]{1,0:T(8,128)(2,1)S(1)} collective-permute-done((bf16[256,768]{1,0:T(8,128)(2,1)S(1)}, bf16[256,768]{1,0:T(8,128)(2,1)S(1)}, u32[]{:S(2)}, u32[]{:S(2)}) %collective-permute-start.25) | collective-permute-done | bytes 393248 | tf_op jit(solution)/shard_map/ppermute | solution.py:352
  292.7 1.0 maximum_select_fusion.1
  293.7 3.5 %all-to-all-done.3 = bf16[4,104,768]{2,1,0:T(8,128)(2,1)S(1)} async-done(((bf16[4,104,768]{2,1,0:T(8,128)(2,1)}), bf16[4,104,768]{2,1,0:T(8,128)(2,1)S(1)}, u32[]{:S(2)}, u32[]{:S(2)}) %all-to-all-start.3) | async-done | bytes 639008 | tf_op jit(solution)/shard_map/all_to_all | solution.py:364
  297.4 0.8 slice_bitcast_fusion.3
  299.2 0.7 copy.51
  (128 shorter events, 20.7 us)
Async XLA Ops:
  0.7 50.1 %copy-start = (bf16[2,768]{1,0:T(2,128)(2,1)S(1)}, bf16[2,768]{1,0:T(2,128)(2,1)}, u32[]{:S(2)}) copy-start(bf16[2,768]{1,0:T(2,128)(2,1)} %param.19) | copy-start | bytes 9220
  0.7 1.4 copy-start.7
  2.2 20.7 %collective-permute-start = (bf16[512,768]{1,0:T(8,128)(2,1)S(1)}, bf16[512,768]{1,0:T(8,128)(2,1)}, u32[]{:S(2)}, u32[]{:S(2)}) collective-permute-start(bf16[512,768]{1,0:T(8,128)(2,1)S(1)} %get-tuple-element.260), channel_id=1, source_target_pairs={{0,2},{2,0},{1,3},{3,1},{4,6},{6,4},{5,7},{7,5},{8,10},{10,8},{9,1... | collective-permute-start | bytes 2359304 | tf_op jit(solution)/shard_map/ppermute | solution.py:352
  7.2 21.6 %all-to-all-start = ((bf16[4,104,768]{2,1,0:T(8,128)(2,1)}), bf16[4,104,768]{2,1,0:T(8,128)(2,1)}, u32[]{:S(2)}, u32[]{:S(2)}) async-start(bf16[4,104,768]{2,1,0:T(8,128)(2,1)} %shard_map.313), calls=%async_computation | async-start | bytes 1277952 | tf_op jit(solution)/shard_map/all_to_all | solution.py:364
  22.9 1.4 copy-start.17
  24.2 4.6 %copy-start.2 = (bf16[2,2,256,768]{3,2,1,0:T(8,128)(2,1)}, bf16[2,2,256,768]{3,2,1,0:T(8,128)(2,1)S(1)}, u32[]{:S(2)}) copy-start(bf16[2,2,256,768]{3,2,1,0:T(8,128)(2,1)S(1)} %pad_maximum_fusion) | copy-start | bytes 4718596
  24.2 27.1 %collective-permute-start.1 = (bf16[2,512,768]{2,1,0:T(8,128)(2,1)S(1)}, bf16[2,512,768]{2,1,0:T(8,128)(2,1)S(1)}, u32[]{:S(2)}, u32[]{:S(2)}) collective-permute-start(bf16[2,512,768]{2,1,0:T(8,128)(2,1)S(1)} %bitcast.67), channel_id=1, source_target_pairs={{0,1},{1,0},{2,3},{3,2},{4,5},{5,4},{6,7},{7,6},{8,9},{9,8},{10,11... | collective-permute-start | bytes 4718600 | tf_op jit(solution)/shard_map/ppermute | solution.py:360
  28.8 42.2 %all-to-all-start.1 = ((bf16[4,192,768]{2,1,0:T(8,128)(2,1)}), bf16[4,192,768]{2,1,0:T(8,128)(2,1)}, u32[]{:S(2)}, u32[]{:S(2)}) async-start(bf16[4,192,768]{2,1,0:T(8,128)(2,1)} %shard_map.316), calls=%async_computation.1 | async-start | bytes 2359296 | tf_op jit(solution)/shard_map/all_to_all | solution.py:364
  33.1 16.1 %collective-permute-start.2 = (bf16[4,104,768]{2,1,0:T(8,128)(2,1)}, bf16[4,104,768]{2,1,0:T(8,128)(2,1)}, u32[]{:S(2)}, u32[]{:S(2)}) collective-permute-start(bf16[4,104,768]{2,1,0:T(8,128)(2,1)} %all-to-all-done.refs_3_), channel_id=1, source_target_pairs={{0,4},{4,0},{1,5},{5,1},{2,6},{6,2},{3,7},{7,3},{8,12},{12,8},{9,1... | collective-permute-start | bytes 1916936 | tf_op jit(solution)/shard_map/ppermute | solution.py:356
  34.6 36.4 %collective-permute-start.3 = (bf16[4,104,768]{2,1,0:T(8,128)(2,1)}, bf16[4,104,768]{2,1,0:T(8,128)(2,1)}, u32[]{:S(2)}, u32[]{:S(2)}) collective-permute-start(bf16[4,104,768]{2,1,0:T(8,128)(2,1)} %all-to-all-done.refs_3_), channel_id=1, source_target_pairs={{0,2},{2,0},{1,3},{3,1},{4,6},{6,4},{5,7},{7,5},{8,10},{10,8},{9,1... | collective-permute-start | bytes 1916936 | tf_op jit(solution)/shard_map/ppermute | solution.py:352
  49.2 21.8 %collective-permute-start.4 = (bf16[4,104,768]{2,1,0:T(8,128)(2,1)}, bf16[4,104,768]{2,1,0:T(8,128)(2,1)}, u32[]{:S(2)}, u32[]{:S(2)}) collective-permute-start(bf16[4,104,768]{2,1,0:T(8,128)(2,1)} %collective-permute-done.2.refs_4_), channel_id=1, source_target_pairs={{0,2},{2,0},{1,3},{3,1},{4,6},{6,4},{5,7},{7,5},{8,10},{10,8},{9,1... | collective-permute-start | bytes 1916936 | tf_op jit(solution)/shard_map/ppermute | solution.py:352
  51.4 1.2 copy-start.3
  71.1 26.9 %collective-permute-start.5 = (bf16[4,192,768]{2,1,0:T(8,128)(2,1)}, bf16[4,192,768]{2,1,0:T(8,128)(2,1)S(1)}, u32[]{:S(2)}, u32[]{:S(2)}) collective-permute-start(bf16[4,192,768]{2,1,0:T(8,128)(2,1)} %all-to-all-done.1.w_oo), channel_id=1, source_target_pairs={{0,4},{4,0},{1,5},{5,1},{2,6},{6,2},{3,7},{7,3},{8,12},{12,8},{9,1... | collective-permute-start | bytes 3538952 | tf_op jit(solution)/shard_map/ppermute | solution.py:356
  72.6 26.6 %collective-permute-start.6 = (bf16[4,192,768]{2,1,0:T(8,128)(2,1)}, bf16[4,192,768]{2,1,0:T(8,128)(2,1)S(1)}, u32[]{:S(2)}, u32[]{:S(2)}) collective-permute-start(bf16[4,192,768]{2,1,0:T(8,128)(2,1)} %all-to-all-done.1.w_oo), channel_id=1, source_target_pairs={{0,2},{2,0},{1,3},{3,1},{4,6},{6,4},{5,7},{7,5},{8,10},{10,8},{9,1... | collective-permute-start | bytes 3538952 | tf_op jit(solution)/shard_map/ppermute | solution.py:352
  98.0 6.8 %copy-start.15 = (bf16[4,192,768]{2,1,0:T(8,128)(2,1)}, bf16[4,192,768]{2,1,0:T(8,128)(2,1)S(1)}, u32[]{:S(2)}) copy-start(bf16[4,192,768]{2,1,0:T(8,128)(2,1)S(1)} %collective-permute-done.5.w_ox) | copy-start | bytes 3538948
  99.2 6.0 %copy-start.16 = (bf16[4,192,768]{2,1,0:T(8,128)(2,1)}, bf16[4,192,768]{2,1,0:T(8,128)(2,1)S(1)}, u32[]{:S(2)}) copy-start(bf16[4,192,768]{2,1,0:T(8,128)(2,1)S(1)} %collective-permute-done.6.w_yo) | copy-start | bytes 3538948
  104.8 16.0 %collective-permute-start.7 = (bf16[1024,768]{1,0:T(8,128)(2,1)}, bf16[1024,768]{1,0:T(8,128)(2,1)S(1)}, u32[]{:S(2)}, u32[]{:S(2)}) collective-permute-start(bf16[1024,768]{1,0:T(8,128)(2,1)} %shard_map.319.a0_ref), channel_id=1, source_target_pairs={{0,1},{1,0},{2,3},{3,2},{4,5},{5,4},{6,7},{7,6},{8,9},{9,8},{10,11... | collective-permute-start | bytes 4718600 | tf_op jit(solution)/shard_map/ppermute | solution.py:360
  104.9 15.8 %collective-permute-start.8 = (bf16[4,96,768]{2,1,0:T(8,128)(2,1)S(1)}, bf16[4,96,768]{2,1,0:T(8,128)(2,1)S(1)}, u32[]{:S(2)}, u32[]{:S(2)}) collective-permute-start(bf16[4,96,768]{2,1,0:T(8,128)(2,1)S(1)} %slice.127), channel_id=1, source_target_pairs={{0,2},{2,0},{1,3},{3,1},{4,6},{6,4},{5,7},{7,5},{8,10},{10,8},{9,1... | collective-permute-start | bytes 1769480 | tf_op jit(solution)/shard_map/ppermute | solution.py:352
  105.3 15.5 %collective-permute-start.9 = (bf16[4,96,768]{2,1,0:T(8,128)(2,1)S(1)}, bf16[4,96,768]{2,1,0:T(8,128)(2,1)S(1)}, u32[]{:S(2)}, u32[]{:S(2)}) collective-permute-start(bf16[4,96,768]{2,1,0:T(8,128)(2,1)S(1)} %slice.128), channel_id=1, source_target_pairs={{0,4},{4,0},{1,5},{5,1},{2,6},{6,2},{3,7},{7,3},{8,12},{12,8},{9,1... | collective-permute-start | bytes 1769480 | tf_op jit(solution)/shard_map/ppermute | solution.py:356
  120.7 0.8 copy-start.25
  120.8 0.9 copy-start.26
  120.8 1.4 copy-start.22
  147.8 8.4 %collective-permute-start.10 = (bf16[1024,768]{1,0:T(8,128)(2,1)}, bf16[1024,768]{1,0:T(8,128)(2,1)S(1)}, u32[]{:S(2)}, u32[]{:S(2)}) collective-permute-start(bf16[1024,768]{1,0:T(8,128)(2,1)} %get-tuple-element.123.g0_ref), channel_id=1, source_target_pairs={{0,1},{1,0},{2,3},{3,2},{4,5},{5,4},{6,7},{7,6},{8,9},{9,8},{10,11... | collective-permute-start | bytes 4718600 | tf_op jit(solution)/shard_map/ppermute | solution.py:360
  147.9 4.7 %collective-permute-start.11 = (bf16[512,768]{1,0:T(8,128)(2,1)}, bf16[512,768]{1,0:T(8,128)(2,1)S(1)}, u32[]{:S(2)}, u32[]{:S(2)}) collective-permute-start(bf16[512,768]{1,0:T(8,128)(2,1)} %get-tuple-element.126), channel_id=1, source_target_pairs={{0,1},{1,0},{2,3},{3,2},{4,5},{5,4},{6,7},{7,6},{8,9},{9,8},{10,11... | collective-permute-start | bytes 2359304 | tf_op jit(solution)/shard_map/ppermute | solution.py:360
  148.4 19.3 %collective-permute-start.12 = (bf16[4,96,768]{2,1,0:T(8,128)(2,1)}, bf16[4,96,768]{2,1,0:T(8,128)(2,1)S(1)}, u32[]{:S(2)}, u32[]{:S(2)}) collective-permute-start(bf16[4,96,768]{2,1,0:T(8,128)(2,1)} %get-tuple-element.127), channel_id=1, source_target_pairs={{0,4},{4,0},{1,5},{5,1},{2,6},{6,2},{3,7},{7,3},{8,12},{12,8},{9,1... | collective-permute-start | bytes 1769480 | tf_op jit(solution)/shard_map/ppermute | solution.py:356
  149.1 18.6 %collective-permute-start.13 = (bf16[4,96,768]{2,1,0:T(8,128)(2,1)}, bf16[4,96,768]{2,1,0:T(8,128)(2,1)S(1)}, u32[]{:S(2)}, u32[]{:S(2)}) collective-permute-start(bf16[4,96,768]{2,1,0:T(8,128)(2,1)} %get-tuple-element.128), channel_id=1, source_target_pairs={{0,2},{2,0},{1,3},{3,1},{4,6},{6,4},{5,7},{7,5},{8,10},{10,8},{9,1... | collective-permute-start | bytes 1769480 | tf_op jit(solution)/shard_map/ppermute | solution.py:352
  152.6 0.9 copy-start.8
  156.3 11.5 %copy-start.13 = (bf16[4,96,768]{2,1,0:T(8,128)(2,1)S(1)}, bf16[4,96,768]{2,1,0:T(8,128)(2,1)}, u32[]{:S(2)}) copy-start(bf16[4,96,768]{2,1,0:T(8,128)(2,1)} %get-tuple-element.147) | copy-start | bytes 1769476
  156.3 1.1 copy-start.6
  167.7 1.1 copy-start.12
  167.7 2.9 copy-start.4
  167.9 31.6 %collective-permute-start.18 = (bf16[4,96,768]{2,1,0:T(8,128)(2,1)S(1)}, bf16[4,96,768]{2,1,0:T(8,128)(2,1)S(1)}, u32[]{:S(2)}, u32[]{:S(2)}) collective-permute-start(bf16[4,96,768]{2,1,0:T(8,128)(2,1)S(1)} %add.60), channel_id=1, source_target_pairs={{0,4},{4,0},{1,5},{5,1},{2,6},{6,2},{3,7},{7,3},{8,12},{12,8},{9,1... | collective-permute-start | bytes 1769480 | tf_op jit(solution)/shard_map/ppermute | solution.py:356
  168.8 2.4 copy-start.24
  168.8 3.6 %copy-start.23 = (bf16[4,96,768]{2,1,0:T(8,128)(2,1)S(1)}, bf16[4,96,768]{2,1,0:T(8,128)(2,1)}, u32[]{:S(2)}) copy-start(bf16[4,96,768]{2,1,0:T(8,128)(2,1)} %get-tuple-element.144) | copy-start | bytes 1769476
  168.9 30.6 %collective-permute-start.17 = (bf16[4,96,768]{2,1,0:T(8,128)(2,1)S(1)}, bf16[4,96,768]{2,1,0:T(8,128)(2,1)S(1)}, u32[]{:S(2)}, u32[]{:S(2)}) collective-permute-start(bf16[4,96,768]{2,1,0:T(8,128)(2,1)S(1)} %add.59), channel_id=1, source_target_pairs={{0,2},{2,0},{1,3},{3,1},{4,6},{6,4},{5,7},{7,5},{8,10},{10,8},{9,1... | collective-permute-start | bytes 1769480 | tf_op jit(solution)/shard_map/ppermute | solution.py:352
  170.7 28.7 %collective-permute-start.14 = (bf16[256,768]{1,0:T(8,128)(2,1)S(1)}, bf16[256,768]{1,0:T(8,128)(2,1)S(1)}, u32[]{:S(2)}, u32[]{:S(2)}) collective-permute-start(bf16[256,768]{1,0:T(8,128)(2,1)S(1)} %get-tuple-element.262), channel_id=1, source_target_pairs={{0,2},{2,0},{1,3},{3,1},{4,6},{6,4},{5,7},{7,5},{8,10},{10,8},{9,1... | collective-permute-start | bytes 1179656 | tf_op jit(solution)/shard_map/ppermute | solution.py:352
  171.1 28.3 %collective-permute-start.15 = (bf16[4,96,768]{2,1,0:T(8,128)(2,1)S(1)}, bf16[4,96,768]{2,1,0:T(8,128)(2,1)S(1)}, u32[]{:S(2)}, u32[]{:S(2)}) collective-permute-start(bf16[4,96,768]{2,1,0:T(8,128)(2,1)S(1)} %copy-done.24), channel_id=1, source_target_pairs={{0,4},{4,0},{1,5},{5,1},{2,6},{6,2},{3,7},{7,3},{8,12},{12,8},{9,1... | collective-permute-start | bytes 1769480 | tf_op jit(solution)/shard_map/ppermute | solution.py:356
  172.4 33.0 %collective-permute-start.16 = (bf16[4,96,768]{2,1,0:T(8,128)(2,1)S(1)}, bf16[4,96,768]{2,1,0:T(8,128)(2,1)S(1)}, u32[]{:S(2)}, u32[]{:S(2)}) collective-permute-start(bf16[4,96,768]{2,1,0:T(8,128)(2,1)S(1)} %copy-done.23), channel_id=1, source_target_pairs={{0,2},{2,0},{1,3},{3,1},{4,6},{6,4},{5,7},{7,5},{8,10},{10,8},{9,1... | collective-permute-start | bytes 1769480 | tf_op jit(solution)/shard_map/ppermute | solution.py:352
  190.3 16.8 %copy-start.9 = (bf16[4,96,768]{2,1,0:T(8,128)(2,1)S(1)}, bf16[4,96,768]{2,1,0:T(8,128)(2,1)}, u32[]{:S(2)}) copy-start(bf16[4,96,768]{2,1,0:T(8,128)(2,1)} %get-tuple-element.167) | copy-start | bytes 1769476
  190.3 16.8 %copy-start.10 = (bf16[4,96,768]{2,1,0:T(8,128)(2,1)S(1)}, bf16[4,96,768]{2,1,0:T(8,128)(2,1)}, u32[]{:S(2)}) copy-start(bf16[4,96,768]{2,1,0:T(8,128)(2,1)} %get-tuple-element.170) | copy-start | bytes 1769476
  205.4 23.8 %collective-permute-start.19 = (bf16[4,96,768]{2,1,0:T(8,128)(2,1)}, bf16[4,96,768]{2,1,0:T(8,128)(2,1)S(1)}, u32[]{:S(2)}, u32[]{:S(2)}) collective-permute-start(bf16[4,96,768]{2,1,0:T(8,128)(2,1)} %get-tuple-element.159), channel_id=1, source_target_pairs={{0,2},{2,0},{1,3},{3,1},{4,6},{6,4},{5,7},{7,5},{8,10},{10,8},{9,1... | collective-permute-start | bytes 1769480 | tf_op jit(solution)/shard_map/ppermute | solution.py:352
  208.4 46.4 %all-to-all-start.2 = ((bf16[4,192,768]{2,1,0:T(8,128)(2,1)}), bf16[4,192,768]{2,1,0:T(8,128)(2,1)S(1)}, u32[]{:S(2)}, u32[]{:S(2)}) async-start(bf16[4,192,768]{2,1,0:T(8,128)(2,1)} %pad_maximum_fusion.1), calls=%async_computation.2 | async-start | bytes 2359296 | tf_op jit(solution)/shard_map/all_to_all | solution.py:364
  229.2 9.5 %copy-start.11 = (bf16[4,96,768]{2,1,0:T(8,128)(2,1)}, bf16[4,96,768]{2,1,0:T(8,128)(2,1)S(1)}, u32[]{:S(2)}) copy-start(bf16[4,96,768]{2,1,0:T(8,128)(2,1)S(1)} %collective-permute-done.19) | copy-start | bytes 1769476
  229.2 10.0 %copy-start.20 = (f32[2,768]{1,0:T(2,128)S(1)}, f32[2,768]{1,0:T(2,128)}, u32[]{:S(2)}) copy-start(f32[2,768]{1,0:T(2,128)} %get-tuple-element.179) | copy-start | bytes 18436
  238.7 16.1 %collective-permute-start.20 = (bf16[1024,768]{1,0:T(8,128)(2,1)}, bf16[1024,768]{1,0:T(8,128)(2,1)S(1)}, u32[]{:S(2)}, u32[]{:S(2)}) collective-permute-start(bf16[1024,768]{1,0:T(8,128)(2,1)} %get-tuple-element.166.g0_ref), channel_id=1, source_target_pairs={{0,1},{1,0},{2,3},{3,2},{4,5},{5,4},{6,7},{7,6},{8,9},{9,8},{10,11... | collective-permute-start | bytes 4718600 | tf_op jit(solution)/shard_map/ppermute | solution.py:360
  238.8 16.1 %collective-permute-start.21 = (bf16[4,96,768]{2,1,0:T(8,128)(2,1)}, bf16[4,96,768]{2,1,0:T(8,128)(2,1)}, u32[]{:S(2)}, u32[]{:S(2)}) collective-permute-start(bf16[4,96,768]{2,1,0:T(8,128)(2,1)} %get-tuple-element.173), channel_id=1, source_target_pairs={{0,2},{2,0},{1,3},{3,1},{4,6},{6,4},{5,7},{7,5},{8,10},{10,8},{9,1... | collective-permute-start | bytes 1769480 | tf_op jit(solution)/shard_map/ppermute | solution.py:352
  245.0 3.1 %copy-start.21 = (f32[1,576]{1,0:T(1,128)S(1)}, f32[1,576]{1,0:T(1,128)}, u32[]{:S(2)}) copy-start(f32[1,576]{1,0:T(1,128)} %get-tuple-element.180) | copy-start | bytes 6916
  247.2 25.4 %collective-permute-start.24 = (bf16[4,96,768]{2,1,0:T(8,128)(2,1)}, bf16[4,96,768]{2,1,0:T(8,128)(2,1)}, u32[]{:S(2)}, u32[]{:S(2)}) collective-permute-start(bf16[4,96,768]{2,1,0:T(8,128)(2,1)} %add.67), channel_id=1, source_target_pairs={{0,4},{4,0},{1,5},{5,1},{2,6},{6,2},{3,7},{7,3},{8,12},{12,8},{9,1... | collective-permute-start | bytes 1769480 | tf_op jit(solution)/shard_map/ppermute | solution.py:356
  254.8 1.2 copy-start.5
  267.5 4.0 %collective-permute-start.22 = (f32[8,9,96]{2,0,1:T(8,128)S(1)}, f32[8,9,96]{2,0,1:T(8,128)S(1)}, u32[]{:S(2)}, u32[]{:S(2)}) collective-permute-start(f32[8,9,96]{2,0,1:T(8,128)S(1)} %constant_dynamic-update-slice_fusion.10), channel_id=1, source_target_pairs={{0,2},{2,0},{1,3},{3,1},{4,6},{6,4},{5,7},{7,5},{8,10},{10,8},{9,1... | collective-permute-start | bytes 82952 | tf_op jit(solution)/shard_map/ppermute | solution.py:352
  271.4 6.3 %copy-start.18 = (f32[8,9,96]{2,0,1:T(8,128)}, f32[8,9,96]{2,0,1:T(8,128)S(1)}, u32[]{:S(2)}) copy-start(f32[8,9,96]{2,0,1:T(8,128)S(1)} %collective-permute-done.22) | copy-start | bytes 82948
  271.5 3.8 %collective-permute-start.23 = (f32[4,8,96]{2,1,0:T(8,128)S(1)}, f32[4,8,96]{2,1,0:T(8,128)S(1)}, u32[]{:S(2)}, u32[]{:S(2)}) collective-permute-start(f32[4,8,96]{2,1,0:T(8,128)S(1)} %bitcast.81), channel_id=1, source_target_pairs={{0,4},{4,0},{1,5},{5,1},{2,6},{6,2},{3,7},{7,3},{8,12},{12,8},{9,1... | collective-permute-start | bytes 36872 | tf_op jit(solution)/shard_map/ppermute | solution.py:356
  277.7 19.5 %all-to-all-start.3 = ((bf16[4,104,768]{2,1,0:T(8,128)(2,1)}), bf16[4,104,768]{2,1,0:T(8,128)(2,1)S(1)}, u32[]{:S(2)}, u32[]{:S(2)}) async-start(bf16[4,104,768]{2,1,0:T(8,128)(2,1)} %fusion.1), calls=%async_computation.3 | async-start | bytes 1277952 | tf_op jit(solution)/shard_map/all_to_all | solution.py:364
  282.8 1.7 copy-start.14
  284.5 1.5 slice-start
  284.5 1.5 copy-start.19
  284.6 8.2 %collective-permute-start.25 = (bf16[256,768]{1,0:T(8,128)(2,1)S(1)}, bf16[256,768]{1,0:T(8,128)(2,1)S(1)}, u32[]{:S(2)}, u32[]{:S(2)}) collective-permute-start(bf16[256,768]{1,0:T(8,128)(2,1)S(1)} %get-tuple-element.258), channel_id=1, source_target_pairs={{0,2},{2,0},{1,3},{3,1},{4,6},{6,4},{5,7},{7,5},{8,10},{10,8},{9,1... | collective-permute-start | bytes 1179656 | tf_op jit(solution)/shard_map/ppermute | solution.py:352
  292.7 7.3 %copy-start.1 = (bf16[2,768]{1,0:T(2,128)(2,1)S(1)}, bf16[2,768]{1,0:T(2,128)(2,1)}, u32[]{:S(2)}) copy-start(bf16[2,768]{1,0:T(2,128)(2,1)} %param.19) | copy-start | bytes 9220

commit v3 on v2

v3 whole, which is shorter than its diff:
```python
import functools

import jax
import jax.numpy as jnp
from jax import lax
from jax.experimental import pallas as pl
from jax.experimental.pallas import tpu as pltpu
from jax.sharding import Mesh
from jax.sharding import PartitionSpec as P

HD = 64
EPSILON = 1e-05
SCALE = 0.125
BF = jnp.bfloat16
F32 = jnp.float32
ZS, XS = 4, 2
KINDS = 8
HINT = 1.0
TILE_PROJECT = 256
TILE_OUT = 256
TILE_MLP = 256
TILE_SECOND = 256
TILE_BACK = 256
TILE_FIRST = 256

NN = (((1,), (0,)), ((), ()))
NT = (((1,), (1,)), ((), ()))


def dot(left, right, dims=NN):
    return lax.dot_general(left, right, dims, preferred_element_type=F32)


def call(body, grid, ins, outs, scratch=(), flops=0, moved=0, trans=0, vmem=16):
    return pl.pallas_call(
        body,
        grid=grid,
        in_specs=[s for s in ins],
        out_specs=[s for _, s in outs],
        out_shape=[o for o, _ in outs],
        scratch_shapes=list(scratch),
        compiler_params=pltpu.CompilerParams(vmem_limit_bytes=vmem << 20),
        cost_estimate=pl.CostEstimate(flops=int(flops * HINT), bytes_accessed=int(moved * HINT), transcendentals=int(trans * HINT)),
    )


def whole(shape, n=1):
    zeros = (0,) * len(shape)
    return pl.BlockSpec(shape, lambda *_: zeros, pipeline_mode=pl.Buffered(1))


def kept(shape):
    zeros = (0,) * len(shape)
    return pl.BlockSpec(shape, lambda *_: zeros)


def far(values):
    return pltpu.with_memory_space_constraint(values, pltpu.HBM)


def scalar():
    return pl.BlockSpec(memory_space=pltpu.SMEM)


def sds(shape, dtype):
    return jax.ShapeDtypeStruct(shape, dtype)


def shard_of(refs, z, rows):
    parts = [r[z] for r in refs]
    value = parts[0] if len(parts) == 1 else jnp.concatenate(parts, axis=0)
    return value[:rows], value[rows:]


def normalize(values):
    center = values - jnp.mean(values, axis=-1, keepdims=True)
    spread = jnp.mean(center * center, axis=-1, keepdims=True)
    rate = lax.rsqrt(spread + EPSILON)
    return center * rate, rate


def pack_attn_body(q_ref, k_ref, v_ref, o_ref, fg, fs, ob, sg, ss, db, hb, qb, vb, out_ref):
    shard = q_ref.shape[0]
    low = jnp.concatenate([q_ref[...], k_ref[...], v_ref[...], o_ref[...].T], axis=1)
    n = qb.shape[1]
    bias = jnp.concatenate([qb[...], vb[...], jnp.zeros((1, shard - 2 * n), BF)], axis=1)
    small = jnp.concatenate([r[...].astype(F32) for r in (fg, fs, ob, sg, ss, db, hb)] + [bias.astype(F32)], axis=0)
    small = jnp.concatenate([small, jnp.zeros((KINDS, low.shape[1] - shard), F32)], axis=1).astype(BF)
    for z in range(out_ref.shape[0]):
        out_ref[z, :shard, :] = low
        out_ref[z, shard:, :] = small


def pack_mlp_body(h_ref, d_ref, out_ref):
    shard = h_ref.shape[0]
    high, low = h_ref[...], d_ref[...].T
    for z in range(out_ref.shape[0]):
        out_ref[z, :shard, :] = high
        out_ref[z, shard:, :] = low


def pick(refs):
    step, each = pl.program_id(0), len(refs) // pl.num_programs(0)
    blocks = [r[...] for r in refs]
    tiles = [blocks[k : k + each] for k in range(0, len(blocks), each)]
    tiles = [t[0] if each == 1 else jnp.concatenate(t, axis=0) for t in tiles]
    value = tiles[0]
    for k in range(1, len(tiles)):
        value = jnp.where(step == k, tiles[k], value)
    return value


def project_body(x_ref, *refs, rows, first):
    refs = list(refs)
    if first:
        *tokens, te_ref, own_ref, oth_ref, w_ref, vec_ref, qkv_ref, normed_ref, normed_t_ref, bias_ref = refs
        oth_refs = (oth_ref,)
    else:
        source_ref, own_ref, *oth_refs, w_ref, vec_ref, qkv_ref, bias_ref = refs

    @pl.when(pl.program_id(0) == 0)
    def _():
        x = x_ref[0]
        own, oth = [], []
        for z in range(ZS):
            weight, small = shard_of((own_ref,), z, rows)
            w_ref[pl.ds(pl.multiple_of((2 * z + x) * rows, 32), rows), :] = weight
            own.append(small[:, :rows].astype(F32))
            weight, small = shard_of(oth_refs, z, rows)
            w_ref[pl.ds(pl.multiple_of((2 * z + 1 - x) * rows, 32), rows), :] = weight
            oth.append(small[:, :rows].astype(F32))
        even = jnp.concatenate([v for pair in zip(own, oth) for v in pair], axis=1)
        odd = jnp.concatenate([v for pair in zip(oth, own) for v in pair], axis=1)
        vec = jnp.where(x == 0, even, odd)
        vec_ref[...] = vec
        n = rows // 4
        last = vec[7:8, :]
        parts = [last[:, rows * k : rows * k + n] for k in range(ZS * XS)]
        parts += [jnp.zeros((1, 3 * HD), F32)]
        parts += [last[:, rows * k + n : rows * k + 2 * n] for k in range(ZS * XS)]
        bias_ref[0:1, :] = jnp.concatenate(parts, axis=1)

    if first:
        xhat, _ = normalize(pick(tokens).astype(F32) + te_ref[...].astype(F32))
        normed = (xhat * vec_ref[0:1, :] + vec_ref[1:2, :]).astype(BF)
        normed_ref[...] = normed
        normed_t_ref[...] = normed.T
    else:
        normed = source_ref[...]
    made = dot(normed, w_ref[:, :640])[:, :576] + bias_ref[0:1, :]
    made = made.astype(BF)
    for j in range(9):
        piece = made[:, 64 * j : 64 * j + 64]
        qkv_ref[j] = piece * BF(SCALE) if j < 3 else piece


def attend_body(q_ref, k_ref, v_ref, e_ref, inv_ref, mixed_ref, wide_ref):
    scores = dot(k_ref[0], q_ref[0], NT)
    expon = jnp.exp(scores - jnp.max(scores, axis=0, keepdims=True))
    inverse = 1.0 / jnp.sum(expon, axis=0, keepdims=True)
    low = expon.astype(BF)
    e_ref[0] = low
    inv_ref[0] = inverse
    wide = dot(v_ref[0].T, low) * inverse
    mixed_ref[0] = wide.astype(BF)
    wide_ref[0] = wide


def attend_back_body(q_ref, k_ref, v_ref, e_ref, inv_ref, mixed_ref, gm_ref, dq_ref, dk_ref, dv_ref):
    low = (gm_ref[0].astype(F32) * inv_ref[0]).astype(BF)
    inner = jnp.sum(low.astype(F32) * mixed_ref[0], axis=0, keepdims=True)
    expon = e_ref[0]
    grad_scores = (expon.astype(F32) * (dot(v_ref[0], low) - inner)).astype(BF)
    dv_ref[0] = dot(expon, low, NT).astype(BF)
    dk_ref[0] = dot(grad_scores, q_ref[0]).astype(BF)
    dq_ref[0] = (dot(k_ref[0].T, grad_scores) * SCALE).T.astype(BF)


def outproj_body(m0_ref, m1_ref, w0_ref, w1_ref, out_ref, wo_ref):
    @pl.when(pl.program_id(0) == 0)
    def _():
        wo_ref[...] = jnp.concatenate([w0_ref[:, 576:], w1_ref[:, 576:]], axis=1)

    mixed = jnp.concatenate([m0_ref[...], m1_ref[...]], axis=0).T
    out_ref[...] = dot(mixed, wo_ref[...], NT).astype(BF)


def feed(normed, cot, wh, wd, bias, acc_h, acc_d, hbg_ref):
    pre = dot(normed, wh[...]) + bias
    below = 0.5 + 0.5 * lax.erf(pre * 0.7071067811865476)
    act = (pre * below).astype(BF)
    slope = below + pre * (jnp.exp(-0.5 * pre * pre) * 0.3989422804014327)
    grad = (dot(cot, wd[...]) * slope).astype(BF)
    acc_h[...] += dot(normed.T, grad)
    acc_d[...] += dot(cot.T, act)
    hbg_ref[...] += jnp.sum(grad.astype(F32), axis=0, keepdims=True)
    return dot(act, wd[...], NT), dot(grad, wh[...], NT)


def fill(x, rows, own, oth, wh, wd, acc_h, acc_d, hbg_ref):
    for z in range(ZS):
        for refs, side in ((own, x), (oth, 1 - x)):
            at = pl.multiple_of((2 * z + side) * rows, 32)
            wh[pl.ds(at, rows), :], wd[pl.ds(at, rows), :] = shard_of(refs, z, rows)
    for ref in (acc_h, acc_d, hbg_ref):
        ref[...] = jnp.zeros_like(ref)


def drain(x, rows, acc, own, oth):
    for z in range(ZS):
        own[z] = acc[pl.ds(pl.multiple_of((2 * z + x) * rows, 32), rows), :].astype(BF)
        oth[z] = acc[pl.ds(pl.multiple_of((2 * z + 1 - x) * rows, 32), rows), :].astype(BF)


def mlp_first_body(
    x_ref, s0, s1, s2, s3, te_ref, a0_ref, a1_ref, c0, c1, c2, c3, vec_ref, w_oo, w_ox,
    mid_ref, normed_ref, ff_ref, gs_ref, hbg_ref, gh_o, gh_x, gd_o, gd_x,
    wh, wd, acc_h, acc_d, *, rows,
):
    x = x_ref[0]

    @pl.when(pl.program_id(0) == 0)
    def _():
        fill(x, rows, (w_oo,), (w_ox,), wh, wd, acc_h, acc_d, hbg_ref)

    middle = (
        pick((s0, s1, s2, s3)).astype(F32)
        + te_ref[...].astype(F32)
        + (a0_ref[...].astype(F32) + a1_ref[...].astype(F32))
        + vec_ref[2:3, :]
    )
    mid_ref[...] = middle
    xhat, _ = normalize(middle)
    normed = (xhat * vec_ref[3:4, :] + vec_ref[4:5, :]).astype(BF)
    normed_ref[...] = normed
    ff_ref[...], gs_ref[...] = feed(normed, pick((c0, c1, c2, c3)), wh, wd, vec_ref[6:7, :], acc_h, acc_d, hbg_ref)

    @pl.when(pl.program_id(0) == pl.num_programs(0) - 1)
    def _():
        drain(x, rows, acc_h, gh_o, gh_x)
        drain(x, rows, acc_d, gd_o, gd_x)


def mlp_second_body(
    x_ref, normed_ref, c0, c1, c2, c3, vec_ref, f_ref, g_ref, w_yo, h_yx, d_yx,
    ff0_ref, ff1_ref, gs_ref, hbg_ref, gh_o, gh_x, gd_o, gd_x,
    wh, wd, acc_h, acc_d, *, rows,
):
    x = x_ref[0]

    @pl.when(pl.program_id(0) == 0)
    def _():
        fill(x, rows, (w_yo,), (h_yx, d_yx), wh, wd, acc_h, acc_d, hbg_ref)

    ff, gs = feed(normed_ref[...], pick((c0, c1, c2, c3)), wh, wd, vec_ref[6:7, :], acc_h, acc_d, hbg_ref)
    gs_ref[...] = (g_ref[...] + gs).astype(BF)
    ff = (f_ref[...] + ff).astype(BF)
    half = pl.num_programs(0) // 2

    @pl.when(pl.program_id(0) < half)
    def _():
        ff0_ref[...] = ff

    @pl.when(pl.program_id(0) >= half)
    def _():
        ff1_ref[...] = ff

    @pl.when(pl.program_id(0) == pl.num_programs(0) - 1)
    def _():
        drain(x, rows, acc_h, gh_o, gh_x)
        drain(x, rows, acc_d, gd_o, gd_x)


def second_back_body(mid_ref, g0_ref, g1_ref, c0, c1, c2, c3, vec_ref, w0_ref, w1_ref, m0_ref, m1_ref, gm_ref, x0_ref, x1_ref, wo0_ref, wo1_ref, sum_ref, wo_ref, acc):
    step, last = pl.program_id(0), pl.num_programs(0) - 1

    @pl.when(step == 0)
    def _():
        wo_ref[...] = jnp.concatenate([w0_ref[:, 576:], w1_ref[:, 576:]], axis=1)
        acc[...] = jnp.zeros_like(acc)
        sum_ref[...] = jnp.zeros_like(sum_ref)

    xhat, rate = normalize(mid_ref[...])
    second = g0_ref[...].astype(F32) + g1_ref[...].astype(F32)
    cot = pick((c0, c1, c2, c3)).astype(F32)
    scaled = second * vec_ref[3:4, :]
    inner = jnp.mean(scaled * xhat, axis=-1, keepdims=True)
    grad = cot + rate * (scaled - jnp.mean(scaled, axis=-1, keepdims=True) - xhat * inner)
    gm_ref[...] = grad
    sum_ref[0:1, :] += jnp.sum(second * xhat, axis=0, keepdims=True)
    sum_ref[1:2, :] += jnp.sum(second, axis=0, keepdims=True)
    sum_ref[2:3, :] += jnp.sum(grad, axis=0, keepdims=True)
    sum_ref[3:4, :] += jnp.sum(cot, axis=0, keepdims=True)
    low = grad.astype(BF)
    back = dot(low, wo_ref[...]).astype(BF).T
    x0_ref[...] = back[:192]
    x1_ref[...] = back[192:]
    mixed = jnp.concatenate([m0_ref[...], m1_ref[...]], axis=0)
    acc[...] += dot(low.T, mixed, NT)

    @pl.when(step == last)
    def _():
        wo0_ref[...] = acc[:, :192].astype(BF)
        wo1_ref[...] = acc[:, 192:].astype(BF)


def project_back_body(x_ref, q_ref, k_ref, v_ref, nt_ref, w_ref, wo_ref, *refs, rows, more):
    refs = list(refs)
    prev_ref = refs.pop(0) if more else None
    own_ref, oth_ref, first_ref, sum_ref, acc = refs
    step, last = pl.program_id(0), pl.num_programs(0) - 1
    x = x_ref[0]
    grads = jnp.concatenate([r[h] for r in (q_ref, k_ref, v_ref) for h in range(3)], axis=1)
    made = dot(nt_ref[...], grads)
    total = jnp.sum(grads.astype(F32), axis=0, keepdims=True)

    @pl.when(step == 0)
    def _():
        acc[...] = made
        sum_ref[...] = total

    @pl.when(step > 0)
    def _():
        acc[...] += made
        sum_ref[...] += total

    back = dot(grads, w_ref[:, :576], NT)
    if more:
        back = back + prev_ref[...]
    first_ref[...] = back.astype(first_ref.dtype)

    @pl.when(step == last)
    def _():
        for z in range(ZS):
            for ref, side in ((own_ref, x), (oth_ref, 1 - x)):
                at = pl.multiple_of((2 * z + side) * rows, 32)
                ref[z] = jnp.concatenate(
                    [acc[pl.ds(at, rows), :].astype(BF), wo_ref[pl.ds(at, rows), :]], axis=1
                )


def first_back_body(
    x_ref, s0, s1, s2, s3, te_ref, vec_ref, g0_ref, g1_ref, gm_ref, second_ref, ho_ref, hy_ref, qo_ref, qy_ref,
    out_ref, own_ref, oth_ref, sum_ref, *, rows,
):
    @pl.when(pl.program_id(0) == 0)
    def _():
        sum_ref[...] = jnp.zeros_like(sum_ref)

    xhat, rate = normalize(pick((s0, s1, s2, s3)).astype(F32) + te_ref[...].astype(F32))
    first = g0_ref[...].astype(F32) + g1_ref[...].astype(F32)
    scaled = first * vec_ref[0:1, :]
    inner = jnp.mean(scaled * xhat, axis=-1, keepdims=True)
    grad = gm_ref[...] + rate * (scaled - jnp.mean(scaled, axis=-1, keepdims=True) - xhat * inner)
    out_ref[...] = grad.astype(BF)
    sum_ref[0:1, :] += jnp.sum(first * xhat, axis=0, keepdims=True)
    sum_ref[1:2, :] += jnp.sum(first, axis=0, keepdims=True)
    sum_ref[2:3, :] += jnp.sum(grad, axis=0, keepdims=True)

    @pl.when(pl.program_id(0) == pl.num_programs(0) - 1)
    def _():
        n = rows // 4
        sums = sum_ref[0:3, :]
        shared = [sums[0:2], second_ref[2:3, :], second_ref[0:2, :], second_ref[3:4, :]]
        blank = jnp.zeros((1, rows - 2 * n), F32)
        for hidden, bias, ref, more in ((ho_ref, qo_ref, own_ref, []), (hy_ref, qy_ref, oth_ref, [sums[2:3]])):
            made = []
            kinds = jnp.concatenate(shared + [hidden[...]], axis=0)
            extra = jnp.concatenate(more + [jnp.zeros((KINDS - 1, kinds.shape[1]), F32)], axis=0) if more else None
            for k in range(ZS * XS):
                part = slice(k * rows, k * rows + rows)
                last = [bias[0:1, k * n : k * n + n], bias[0:1, 6 * HD + k * n : 6 * HD + k * n + n], blank]
                piece = [kinds[:, part], jnp.concatenate(last, axis=1)]
                made.append(jnp.concatenate(piece + ([extra[:, part]] if more else []), axis=0))
            for z in range(ZS):
                even, odd = made[2 * z], made[2 * z + 1]
                ref[0, z] = jnp.where(x_ref[0] == 0, even, odd)
                ref[1, z] = jnp.where(x_ref[0] == 0, odd, even)


def final_body(got_ref, p0_ref, p1_ref, p2_ref, p3_ref, q_ref, k_ref, v_ref, o_ref, *small, rows):
    total = got_ref[0].astype(F32)
    for z in range(1, got_ref.shape[0]):
        total = total + got_ref[z].astype(F32)
    width = 3 * HD
    q_ref[...] = total[:, :width]
    k_ref[...] = total[:, width : 2 * width]
    v_ref[...] = total[:, 2 * width : 3 * width]
    o_ref[...] = total[:, 3 * width :].T
    sums = (p0_ref[...] + p1_ref[...]) + (p2_ref[...] + p3_ref[...])
    n = rows // 4
    for k, ref in enumerate(small[:7]):
        ref[...] = sums[k : k + 1]
    small[7][...] = sums[7:8, :n]
    small[8][...] = sums[7:8, n : 2 * n]


def output_body(mid_ref, f0_ref, f1_ref, vec_ref, out_ref):
    out_ref[...] = (
        mid_ref[...] + (f0_ref[...].astype(F32) + f1_ref[...].astype(F32)) + vec_ref[5:6, :]
    ).astype(BF)


def swap(size):
    return [(i, size - 1 - i) for i in range(size)]


def to_y(values):
    return lax.ppermute(values, "y", swap(2))


def to_x(values):
    return lax.ppermute(values, "b", swap(2))


def to_core(values):
    return lax.ppermute(values, "c", swap(2))


def spread_z(values):
    return lax.all_to_all(values, "a", 0, 0, tiled=True)


def after(value, *others):
    return lax.optimization_barrier((value, *others))[0]


def body(
    fast,
    inputs,
    time_embed,
    first_gain,
    first_shift,
    query_weight,
    query_bias,
    key_weight,
    value_weight,
    value_bias,
    output_weight,
    output_bias,
    second_gain,
    second_shift,
    hidden_weight,
    hidden_bias,
    down_weight,
    down_bias,
    cotangent,
):
    _, block, width = inputs.shape
    shard = query_weight.shape[0]
    rows = width // (ZS * XS)
    seq = 4 * block
    hidden = hidden_weight.shape[1]
    yi = lax.axis_index("y")
    xi = lax.axis_index("b") if fast else jnp.int32(0)
    x_arr = xi.astype(jnp.int32)[None]

    n_copies = ZS if fast else 1
    (attn_pack,) = call(
        pack_attn_body,
        (1,),
        [kept((shard, hidden // 4))] * 3 + [kept((hidden // 4, shard))] + [kept((1, shard))] * 7 + [kept((1, query_bias.shape[0]))] * 2,
        [(sds((n_copies, shard + KINDS, width), BF), kept((n_copies, shard + KINDS, width)))],
        flops=1e6,
        moved=1e6,
        vmem=56,
    )(
        query_weight, key_weight, value_weight, output_weight,
        *(v[None] for v in (first_gain, first_shift, output_bias, second_gain, second_shift, down_bias, hidden_bias, query_bias, value_bias)),
    )
    (mlp_pack,) = call(
        pack_mlp_body,
        (1,),
        [kept((shard, hidden)), kept((hidden, shard))],
        [(sds((n_copies, 2 * shard, width), BF), kept((n_copies, 2 * shard, width)))],
        flops=1e6,
        moved=2e6,
        vmem=56,
    )(hidden_weight, down_weight)

    def tokens(values):
        stays = lax.dynamic_index_in_dim(values, yi, 0, keepdims=False)
        comes = to_y(lax.dynamic_index_in_dim(values, 1 - yi, 0, keepdims=False))
        return stays, comes

    def with_mate(stays, comes):
        return stays, comes, to_core(stays), to_core(comes)

    inputs, cotangent = lax.optimization_barrier((inputs, cotangent, attn_pack))[:2]
    start, cot = tokens(inputs), tokens(cotangent)
    te = lax.dynamic_index_in_dim(time_embed, yi, 0, keepdims=True)

    if fast:
        attn_oo = spread_z(attn_pack)
        attn_oo, *comes = lax.optimization_barrier((attn_oo, start[1], cot[1]))
        start, cot = with_mate(start[0], comes[0]), with_mate(cot[0], comes[1])
        attn_ox, attn_yo = to_x(attn_oo), to_y(attn_oo)
        mlp_oo = spread_z(mlp_pack)
        attn_yx = to_y(attn_ox)
    else:
        def natural(values):
            full = lax.all_gather(values, ("a", "b"), axis=0, tiled=True)
            full = full.reshape(ZS, XS, rows, width)
            return full[:, 0], full[:, 1]

        gathered = lax.all_gather(attn_pack[0], ("a", "b"), axis=0, tiled=False)
        matrix = gathered[:, :shard].reshape(ZS, XS, rows, width)
        small = gathered[:, shard:, :shard]
        flat = small[:, :7].transpose(1, 0, 2).reshape(7, width)
        n = shard // 4
        bias = [small[:, 7, k * n : k * n + n].reshape(ZS * XS, -1) for k in range(2)]
        bias = jnp.concatenate([*bias, jnp.zeros((ZS * XS, rows - 2 * (rows // 4)), BF)], axis=1)
        small = jnp.concatenate([flat, bias.reshape(1, width)], axis=0)
        small = small.reshape(KINDS, ZS, XS, rows).transpose(1, 2, 0, 3)
        small = jnp.pad(small, ((0, 0), (0, 0), (0, 0), (0, width - rows)))
        matrix = jnp.concatenate([matrix, small], axis=2)
        attn_oo, attn_ox = matrix[:, 0], matrix[:, 1]
        attn_yo, attn_yx = to_y(attn_oo), to_y(attn_ox)
        start, cot = with_mate(*start), with_mate(*cot)
        h_oo, h_ox = natural(mlp_pack[0, :shard])
        d_oo, d_ox = natural(mlp_pack[0, shard:])
        mlp_oo = jnp.concatenate([h_oo, d_oo], axis=1)
        mlp_ox = jnp.concatenate([h_ox, d_ox], axis=1)

    def by(tile):
        return pl.BlockSpec((tile, width), lambda i: (i, 0))

    def by_mate(tile):
        tiles = seq // tile
        return pl.BlockSpec((tile, width), lambda i: ((i + tiles // 2) % tiles, 0))

    def low_half(tile):
        last = seq // tile // 2 - 1
        return pl.BlockSpec((tile, width), lambda i: (jnp.minimum(i, last), 0))

    def high_half(tile):
        first = seq // tile // 2
        return pl.BlockSpec((tile, width), lambda i: (jnp.maximum(i - first, 0), 0))

    blocks = [whole((block, width))] * 4
    row = kept((1, width))
    vecs = kept((KINDS, width))
    square = whole((width, width))
    n_qkv = 9 * HD

    def project(first, source, *shards):
        tile = TILE_PROJECT
        outs = [
            (sds((width, width), BF), kept((width, width))),
            (sds((KINDS, width), F32), vecs),
            (sds((9, seq, HD), BF), pl.BlockSpec((9, tile, HD), lambda i: (0, i, 0))),
        ]
        if first:
            outs += [
                (sds((seq, width), BF), by(tile)),
                (pltpu.HBM((width, seq), BF), pl.BlockSpec((width, tile), lambda i: (0, i))),
            ]
        return call(
            functools.partial(project_body, rows=rows, first=first),
            (seq // tile,),
            [scalar()] + (blocks + [row] if first else [by(tile)]) + [whole(v.shape) for v in shards],
            outs,
            scratch=[pltpu.VMEM((8, n_qkv), F32)],
            flops=2 * seq * width * n_qkv,
            moved=8e6,
        )(x_arr, *source, *shards)

    q_spec = pl.BlockSpec((1, seq, HD), lambda h: (h, 0, 0))
    k_spec = pl.BlockSpec((1, seq, HD), lambda h: (3 + h, 0, 0))
    v_spec = pl.BlockSpec((1, seq, HD), lambda h: (6 + h, 0, 0))
    e_spec = pl.BlockSpec((1, seq, seq), lambda h: (h, 0, 0))
    inv_spec = pl.BlockSpec((1, 1, seq), lambda h: (h, 0, 0))
    t_spec = pl.BlockSpec((1, HD, seq), lambda h: (h, 0, 0))

    def attend(qkv):
        return call(
            attend_body,
            (3,),
            [q_spec, k_spec, v_spec],
            [
                (pltpu.HBM((3, seq, seq), BF), e_spec),
                (sds((3, 1, seq), F32), inv_spec),
                (sds((3, HD, seq), BF), t_spec),
                (pltpu.HBM((3, HD, seq), F32), t_spec),
            ],
            flops=3 * 16 * seq * seq * HD,
            moved=8e6,
            trans=3 * seq * seq,
        )(qkv, qkv, qkv)

    def attend_back(qkv, expon, inverse, mixed, grad_mixed):
        return call(
            attend_back_body,
            (3,),
            [q_spec, k_spec, v_spec, e_spec, inv_spec, t_spec, t_spec],
            [(sds((3, seq, HD), BF), q_spec)] * 3,
            flops=3 * 40 * seq * seq * HD,
            moved=9e6,
        )(qkv, qkv, qkv, far(expon), inverse, far(mixed), grad_mixed)

    w_o, vec, qkv_o, normed, normed_t = project(True, (*start, te), attn_oo, attn_ox)
    exp_o, inv_o, mixed_o, wide_o = attend(qkv_o)
    normed, exp_o, attn_yo, attn_yx, mlp_oo = lax.optimization_barrier(
        (normed, exp_o, attn_yo, attn_yx, mlp_oo)
    )
    mlp_yo = to_y(mlp_oo)
    if fast:
        mlp_ox = to_x(mlp_oo)
    w_y, vec_y, qkv_y = project(False, (normed,), attn_yo, attn_yx)
    exp_y, inv_y, mixed_y, wide_y = attend(qkv_y)
    mixed_y, mlp_ox, mlp_yo = lax.optimization_barrier((mixed_y, mlp_ox, mlp_yo))
    h_yx = to_y(mlp_ox[:, :rows])
    d_yx = to_x(mlp_yo[:, rows:]) if fast else to_y(mlp_ox[:, rows:])

    tile = TILE_OUT
    half_t = pl.BlockSpec((3 * HD, tile), lambda i: (0, i))
    flat_o, flat_y = mixed_o.reshape(3 * HD, seq), mixed_y.reshape(3 * HD, seq)
    (attended,) = call(
        outproj_body,
        (seq // tile,),
        [half_t, half_t, square, square],
        [(sds((seq, width), BF), by(tile))],
        scratch=[pltpu.VMEM((width, 6 * HD), BF)],
        flops=2 * seq * width * 384,
        moved=6e6,
    )(flat_o, flat_y, w_o, w_y)
    attended_mate = to_core(attended)

    tile = TILE_MLP
    part = (ZS, rows, hidden)
    grad_parts = [(sds((1, hidden), F32), kept((1, hidden)))] + [(sds(part, BF), kept(part))] * 4
    mlp_scratch = [pltpu.VMEM((width, hidden), t) for t in (BF, BF, F32, F32)]
    mlp_cost = dict(flops=12 * seq * width * hidden, moved=16e6, trans=seq * hidden * 2)
    middle, normed_second, ff_part, gs_part, hb_o, gh_oo, gh_ox, gd_oo, gd_ox = call(
        functools.partial(mlp_first_body, rows=rows),
        (seq // tile,),
        [scalar(), *blocks, row, by(tile), by_mate(tile), *blocks, vecs]
        + [whole((ZS, 2 * rows, hidden))] * 2,
        [
            (sds((seq, width), F32), by(tile)),
            (sds((seq, width), BF), by(tile)),
            (sds((seq, width), F32), by(tile)),
            (sds((seq, width), F32), by(tile)),
        ]
        + grad_parts,
        scratch=mlp_scratch,
        **mlp_cost,
    )(x_arr, *start, te, attended, attended_mate, *cot, vec, mlp_oo, mlp_ox)
    if fast:
        got_ho = to_x(gh_ox)
        normed_second, h_yx, d_yx = lax.optimization_barrier((normed_second, h_yx, d_yx))
    ff, ff_sent, gs, hb_y, gh_yo, gh_yx, gd_yo, gd_yx = call(
        functools.partial(mlp_second_body, rows=rows),
        (seq // tile,),
        [scalar(), by(tile), *blocks, vecs, by(tile), by(tile)]
        + [whole((ZS, 2 * rows, hidden)), whole(part), whole(part)],
        [
            (sds((seq // 2, width), BF), low_half(tile)),
            (sds((seq // 2, width), BF), high_half(tile)),
            (sds((seq, width), BF), by(tile)),
        ]
        + grad_parts,
        scratch=mlp_scratch,
        **mlp_cost,
    )(x_arr, normed_second, *cot, vec_y, ff_part, gs_part, mlp_yo, h_yx, d_yx)
    if fast:
        gs, got_ho = lax.optimization_barrier((gs, got_ho))
    gs_mate = to_core(gs)
    ff_mate = to_core(ff_sent)

    tile = TILE_SECOND
    half_t = pl.BlockSpec((3 * HD, tile), lambda i: (0, i))
    grad_middle, gx_o, gx_y, wo_o, wo_y, second_sums = call(
        second_back_body,
        (seq // tile,),
        [by(tile), by(tile), by_mate(tile), *blocks, vecs, square, square, half_t, half_t],
        [
            (pltpu.HBM((seq, width), F32), by(tile)),
            (sds((3 * HD, seq), BF), half_t),
            (sds((3 * HD, seq), BF), half_t),
            (sds((width, 3 * HD), BF), kept((width, 3 * HD))),
            (sds((width, 3 * HD), BF), kept((width, 3 * HD))),
            (sds((KINDS, width), F32), vecs),
        ],
        scratch=[pltpu.VMEM((width, 6 * HD), BF), pltpu.VMEM((width, 6 * HD), F32)],
        flops=4 * seq * width * 384,
        moved=16e6,
    )(middle, gs, gs_mate, *cot, vec, w_o, w_y, flat_o, flat_y)
    if fast:
        got_h, got_d = to_x(gh_yx), to_y(gd_yx)
        gx_y, got_h, got_d, gd_yo = lax.optimization_barrier((gx_y, got_h, got_d, gd_yo))
        got_hs, got_ds = to_y(gh_yo + got_h), to_x(gd_ox + got_d)

    def project_back(grads, weights, wo, prev):
        tile = TILE_BACK
        more = prev is not None
        heads = pl.BlockSpec((3, tile, HD), lambda i: (0, i, 0))
        attn_part = (ZS, rows, width)
        return call(
            functools.partial(project_back_body, rows=rows, more=more),
            (seq // tile,),
            [scalar(), heads, heads, heads, pl.BlockSpec((width, tile), lambda i: (0, i)), square, whole((width, 3 * HD))]
            + ([by(tile)] if more else []),
            [
                (sds(attn_part, BF), kept(attn_part)),
                (sds(attn_part, BF), kept(attn_part)),
                ((sds((seq, width), BF) if more else pltpu.HBM((seq, width), F32)), by(tile)),
                (sds((1, n_qkv), F32), kept((1, n_qkv))),
            ],
            scratch=[pltpu.VMEM((width, n_qkv), F32)],
            flops=4 * seq * width * n_qkv,
            moved=10e6,
        )(x_arr, *grads, far(normed_t), weights, wo, *((far(prev),) if more else ()))

    grads_y = attend_back(qkv_y, exp_y, inv_y, wide_y, gx_y.reshape(3, HD, seq))
    if fast:
        *grads_y, gd_yo = lax.optimization_barrier((*grads_y, gd_yo))
        got_do = to_y(gd_yo)
    ga_yo, ga_yx, first_part, qkv_sum_y = project_back(grads_y, w_y, wo_y, None)
    tile = TILE_OUT
    (out_tokens,) = call(
        output_body,
        (seq // tile // 2,),
        [by(tile), by(tile), by(tile), vecs],
        [(sds((seq // 2, width), BF), by(tile))],
        flops=1e6,
        moved=5e6,
    )(middle, ff, ff_mate, vec)
    gx_o, first_part, out_tokens = lax.optimization_barrier((gx_o, first_part, out_tokens))
    out_got = to_y(out_tokens[block:])
    if fast:
        gx_o, ga_yx, got_hs = lax.optimization_barrier((gx_o, ga_yx, got_hs))
        ga_d = to_x(ga_yx)
    grads_o = attend_back(qkv_o, exp_o, inv_o, wide_o, gx_o.reshape(3, HD, seq))
    if fast:
        *grads_o, got_ds, got_do, ga_d, out_got = lax.optimization_barrier(
            (*grads_o, got_ds, got_do, ga_d, out_got)
        )
        mlp_all = spread_z(jnp.concatenate([gh_oo + got_ho + got_hs, gd_oo + got_do + got_ds], axis=1))
        ga_s = to_y(ga_yo + ga_d)
    ga_oo, ga_ox, first, qkv_sum_o = project_back(grads_o, w_o, wo_o, first_part)
    if fast:
        ga_x = to_x(ga_ox)
        first, ga_s = lax.optimization_barrier((first, ga_s))
    first_mate = to_core(first)

    tile = TILE_FIRST
    hb_spec, qkv_spec = kept((1, hidden)), kept((1, n_qkv))
    small_o_shape, small_y_shape = (XS, ZS, KINDS, rows), (XS, ZS, 2 * KINDS, rows)
    input_grad, small_o, small_y, first_sums = call(
        functools.partial(first_back_body, rows=rows),
        (seq // tile,),
        [scalar(), *blocks, row, vecs, by(tile), by_mate(tile), by(tile), vecs, hb_spec, hb_spec, qkv_spec, qkv_spec],
        [
            (sds((seq, width), BF), by(tile)),
            (sds(small_o_shape, F32), kept(small_o_shape)),
            (sds(small_y_shape, F32), kept(small_y_shape)),
            (sds((KINDS, width), F32), vecs),
        ],
        flops=1e6,
        moved=12e6,
    )(x_arr, *start, te, vec, first, first_mate, far(grad_middle), second_sums, hb_o, hb_y, qkv_sum_o, qkv_sum_y)

    if fast:
        small_o, small_y, input_grad, ga_x = lax.optimization_barrier((small_o, small_y, input_grad, ga_x))
        ga_all = spread_z(ga_oo + ga_s + ga_x)
    small_got = to_y(small_y)
    small_sum = small_o + small_got[:, :, :KINDS]
    embed = first_sums[2]
    embed_got = jnp.where(xi == 0, small_got, small_got[::-1])[:, :, KINDS].transpose(1, 0, 2).reshape(width)
    embed_gradient = jnp.where(yi == 0, jnp.stack([embed, embed_got]), jnp.stack([embed_got, embed]))
    n_bias = query_bias.shape[0]
    n_head = query_weight.shape[1]
    if fast:
        small_sum = small_sum[0] + to_x(small_sum[1])
        zi = lax.axis_index("a")
        pieces = [lax.dynamic_index_in_dim(small_sum, (zi + k) % ZS, 0, keepdims=False) for k in range(ZS)]
        pieces = [lax.ppermute(v, "a", [(i, (i + k) % ZS) for i in range(ZS)]) if k else v for k, v in enumerate(pieces)]
        *weights, fg, fs, ob, sg, ss, db, hb, qb, vb = call(
            functools.partial(final_body, rows=rows),
            (1,),
            [kept(ga_all.shape)] + [kept((KINDS, rows))] * ZS,
            [(sds((shard, n_head), F32), kept((shard, n_head)))] * 3
            + [(sds((n_head, shard), F32), kept((n_head, shard)))]
            + [(sds((1, shard), F32), kept((1, shard)))] * 7
            + [(sds((1, n_bias), F32), kept((1, n_bias)))] * 2,
            flops=1e6,
            moved=2e6,
        )(ga_all, *pieces)
        vectors = [v[0] for v in (fg, fs, ob, sg, ss, db, hb, qb, vb)]
        mlp_sum = jnp.sum(mlp_all.astype(F32), axis=0)
        gh, gd = mlp_sum[:shard], mlp_sum[shard:].T
    else:

        def scatter(values):
            return lax.psum_scatter(values, ("a", "b"), scatter_dimension=0, tiled=True)

        def scatter_slow(oo, ox, yo, yx):
            own, oth = oo + to_y(yo), ox + to_y(yx)
            return scatter(jnp.stack([own, oth], axis=1).reshape(width, -1).astype(F32))

        kinds = small_sum.transpose(2, 1, 0, 3)
        bias = kinds[7].reshape(ZS * XS, rows)
        split = rows // 4
        vectors = [scatter(v) for v in kinds[:7].reshape(7, width)]
        vectors += [scatter(bias[:, k * split : k * split + split].reshape(-1)) for k in range(2)]
        gh = scatter_slow(gh_oo, gh_ox, gh_yo, gh_yx)
        gd = scatter_slow(gd_oo, gd_ox, gd_yo, gd_yx).T
        ga = scatter_slow(ga_oo, ga_ox, ga_yo, ga_yx)
        weights = [ga[:, k * n_head : k * n_head + n_head] for k in range(4)]
        weights[3] = weights[3].T

    def placed(stays, got):
        return jnp.where(yi == 0, jnp.stack([stays, got]), jnp.stack([got, stays]))

    block_output = placed(out_tokens[:block], out_got)
    input_gradient = placed(input_grad[:block], to_y(input_grad[block : 2 * block]))

    fg, fs, ob, sg, ss, db, hb, qb, vb = vectors
    return (
        block_output, input_gradient, embed_gradient, fg, fs, weights[0], qb, weights[1], weights[2], vb,
        weights[3], ob, sg, ss, gh, hb, gd, db,
    )


def solution(mesh):
    dp, tensor = mesh.shape["dp"], mesh.shape["tensor"]
    fine = Mesh(mesh.devices.reshape(dp // 2, 2, tensor // 2, 2), ("a", "b", "y", "c"))
    by_dp, by_tensor = ("a", "b"), ("y", "c")
    both = by_tensor + by_dp
    column, matrix, turned = P(by_dp), P(by_dp, by_tensor), P(by_tensor, by_dp)
    seqs = P(by_dp, by_tensor, None)
    return jax.shard_map(
        functools.partial(body, dp == ZS * XS),
        mesh=fine,
        in_specs=(
            seqs, P(by_dp, None), column, column, matrix, P(both), matrix, matrix, P(both), turned,
            column, column, column, matrix, P(both), turned, column, seqs,
        ),
        out_specs=(
            seqs, seqs, P(by_dp, None), column, column, matrix, P(both), matrix, matrix, P(both), turned,
            column, column, column, matrix, P(both), turned, column,
        ),
        check_vma=False,
    )
```

time: 303 us -> 261 us (0.86)
  Pallas kernels: 142 us -> 96.1 us
  local copies, waits for them, and re-layouts: 26.6 us -> 13.9 us
  waiting for transfers between devices: 77.2 us -> 88.8 us
  starting transfers between devices: 42.8 us -> 49.5 us
    pallas_call x13 -> x15, Pallas kernels: 138 us -> 91.9 us  [the longest x2 16.5 us: attend_back(): call(attend_back_body, (3,), [q_spec, k_spec, v_spec, e_spec, inv_spec, t...]
    ppermute x13, waiting for transfers between devices: 46.9 us -> 24.3 us  [to_y(): return lax.ppermute(values, 'y', swap(2))]
    all_to_all x4, waiting for transfers between devices: 4.74 us -> 21.4 us  [spread_z(): return lax.all_to_all(values, 'a', 0, 0, tiled=True)]
    ppermute x8 -> x9, waiting for transfers between devices: 23.7 us -> 38.3 us  [to_x(): return lax.ppermute(values, 'b', swap(2))]
    ppermute x0 -> x3, starting transfers between devices: none -> 3.87 us  [body(): lax.ppermute(v, 'a', [(i, (i + k) % ZS) for i in range(ZS)])]
    another operation x11 -> x2, local copies, waits for them, and re-layouts: 4.31 us -> 0.88 us  [placed(): return jnp.where(yi == 0, jnp.stack([stays, got]), jnp.stack([got, stays]))]
    unnamed x66 -> x95, local copies, waits for them, and re-layouts: 13.9 us -> 11.1 us
    ppermute x8 -> x9, starting transfers between devices: 8.48 us -> 10.6 us  [to_x(): return lax.ppermute(values, 'b', swap(2))]
  transfers between devices with their start and end apart: 30 -> 37, of which waited for: 14 -> 21; matrix products, arithmetic and copies ran while one was open for 8% -> 5% of each run, Pallas kernels for 37% -> 35%
where the time goes in v3:
time: 261 us; the launch traced here: 260 us
  Pallas kernels  96.1 us (37%)
  waiting for transfers between devices  88.8 us (34%)
  starting transfers between devices  49.5 us (19%)
  local copies, waits for them, and re-layouts  13.9 us (5%)
  other arithmetic  10 us (4%)
    ppermute x9, waiting for transfers between devices, to_x(): return lax.ppermute(values, 'b', swap(2))  38.3 us
    ppermute x13, waiting for transfers between devices, to_y(): return lax.ppermute(values, 'y', swap(2))  24.3 us
    all_to_all x4, waiting for transfers between devices, spread_z(): return lax.all_to_all(values, 'a', 0, 0, tiled=True)  21.4 us
    all_to_all x4, starting transfers between devices, spread_z(): return lax.all_to_all(values, 'a', 0, 0, tiled=True)  18.4 us
    pallas_call x2, Pallas kernels, attend_back(): call(attend_back_body, (3,), [q_spec, k_spec, v_spec, e_spec, inv_spec, t...  16.5 us
    pallas_call x2, Pallas kernels, project_back(): call(functools.partial(project_back_body, rows=rows, more=more), (seq //...  16.1 us
    ppermute x13, starting transfers between devices, to_y(): return lax.ppermute(values, 'y', swap(2))  15 us
    pallas_call x2, Pallas kernels, attend(): call(attend_body, (3,), [q_spec, k_spec, v_spec], [(pltpu.HBM((3, seq, se...  13.8 us
  transfers between devices with their start and end apart: 37, of which 21 were waited for; matrix products, arithmetic and copies ran while one was open for 5% of the time, Pallas kernels for 35%

profile of v3, /device:TPU:0, one launch (start us, length us, event | category | flops | bytes accessed | tf_op | source)
XLA Modules:
  0.0 259.7 jit_solution(13521282259479237269)
XLA Ops:
  0.7 2.0 shard_map.313
  2.7 6.4 %all-to-all-start = ((bf16[4,104,768]{2,1,0:T(8,128)(2,1)}), bf16[4,104,768]{2,1,0:T(8,128)(2,1)}, u32[]{:S(2)}, u32[]{:S(2)}) async-start(bf16[4,104,768]{2,1,0:T(8,128)(2,1)} %shard_map.313), calls=%async_computation | async-start | bytes 1277952 | tf_op jit(solution)/shard_map/all_to_all | solution.py:421
  9.9 1.5 collective-permute-start
  11.4 0.8 copy.36.d_ref
  12.3 2.2 shard_map.316
  14.5 11.7 %all-to-all-done.refs_5_ = bf16[4,104,768]{2,1,0:T(8,128)(2,1)} async-done(((bf16[4,104,768]{2,1,0:T(8,128)(2,1)}), bf16[4,104,768]{2,1,0:T(8,128)(2,1)}, u32[]{:S(2)}, u32[]{:S(2)}) %all-to-all-start) | async-done | bytes 639008 | tf_op jit(solution)/shard_map/all_to_all | solution.py:421
  26.2 3.5 %all-to-all-start.1 = ((bf16[4,192,768]{2,1,0:T(8,128)(2,1)}), bf16[4,192,768]{2,1,0:T(8,128)(2,1)S(1)}, u32[]{:S(2)}, u32[]{:S(2)}) async-start(bf16[4,192,768]{2,1,0:T(8,128)(2,1)} %shard_map.316), calls=%async_computation.1 | async-start | bytes 2359296 | tf_op jit(solution)/shard_map/all_to_all | solution.py:421
  29.8 1.6 collective-permute-start.1
  31.4 8.6 %collective-permute-done.1.c1 = bf16[256,768]{1,0:T(8,128)(2,1)S(1)} collective-permute-done((bf16[256,768]{1,0:T(8,128)(2,1)S(1)}, bf16[256,768]{1,0:T(8,128)(2,1)S(1)}, u32[]{:S(2)}, u32[]{:S(2)}) %collective-permute-start.1) | collective-permute-done | bytes 393248 | tf_op jit(solution)/shard_map/ppermute | solution.py:409
  39.9 1.5 collective-permute-start.4
  42.0 1.5 collective-permute-start.5
  43.5 11.2 %collective-permute-done.4.refs_6_ = bf16[4,104,768]{2,1,0:T(8,128)(2,1)} collective-permute-done((bf16[4,104,768]{2,1,0:T(8,128)(2,1)}, bf16[4,104,768]{2,1,0:T(8,128)(2,1)}, u32[]{:S(2)}, u32[]{:S(2)}) %collective-permute-start.4) | collective-permute-done | bytes 639008 | tf_op jit(solution)/shard_map/ppermute | solution.py:413
  54.7 1.5 collective-permute-start.6
  57.7 1.0 copy-done.14
  58.7 1.0 copy-done.18
  59.7 5.3 %shard_map.314 = (bf16[768,768]{1,0:T(8,128)(2,1)S(1)}, f32[8,768]{1,0:T(8,128)S(1)}, bf16[9,1024,64]{2,1,0:T(8,128)(2,1)S(1)}, bf16[1024,768]{1,0:T(8,128)(2,1)S(1)}, bf16[768,1024]{1,0:T(8,128)(2,1)}) custom-call(s32[1]{0:T(128)} %bitcast.x_ref, bf16[256,768]{1,0:T(8,128)(2,1)S(1)} %get-tuple-element.255.refs_0_.s0, ...), custom_call_target="tpu_custom_call" | custom-call | flops 905969664 | bytes 8000000 | tf_op jit(solution)/shard_map/pallas_call | solution.py:558
  65.7 6.9 %shard_map.315 = (bf16[3,1024,1024]{2,1,0:T(8,128)(2,1)}, f32[3,1,1024]{2,1,0:T(1,128)S(1)}, bf16[3,64,1024]{2,1,0:T(8,128)(2,1)S(1)}, f32[3,64,1024]{2,1,0:T(8,128)}) custom-call(bf16[9,1024,64]{2,1,0:T(8,128)(2,1)S(1)} %get-tuple-element.137.q_ref.k_ref.v_ref, bf16[9,1024,64]{2,1,0:T(8,128)(2,1)S(1)} %get-tuple-element.137.q_ref.k_ref.v_ref, ...), custom_call_target="tpu_custom_call" | custom-call | flops 3221225472 | bytes 8000000 | tf_op jit(solution)/shard_map/pallas_call | solution.py:576
  73.2 1.6 collective-permute-start.7
  75.3 1.4 copy-done.36
  76.7 3.6 %shard_map.317 = (bf16[768,768]{1,0:T(8,128)(2,1)S(1)}, f32[8,768]{1,0:T(8,128)S(1)}, bf16[9,1024,64]{2,1,0:T(8,128)(2,1)S(1)}) custom-call(s32[1]{0:T(128)} %bitcast.x_ref, bf16[1024,768]{1,0:T(8,128)(2,1)S(1)} %copy-done.36, bf16[4,104,768]{2,1,0:T(8,128)(2,1)} %collective-permute-done.5.refs_1_, bf16[4,104,768]{2,1,0:T(8,128)(2,1)} %collective-permute-done.6.refs_2_), custom_call_target="tpu_custom_call" | custom-call | flops 905969664 | bytes 8000000 | tf_op jit(solution)/shard_map/pallas_call | solution.py:558
  80.2 6.9 %shard_map.318 = (bf16[3,1024,1024]{2,1,0:T(8,128)(2,1)}, f32[3,1,1024]{2,1,0:T(1,128)S(1)}, bf16[3,64,1024]{2,1,0:T(8,128)(2,1)S(1)}, f32[3,64,1024]{2,1,0:T(8,128)}) custom-call(bf16[9,1024,64]{2,1,0:T(8,128)(2,1)S(1)} %get-tuple-element.144.q_ref.k_ref.v_ref, bf16[9,1024,64]{2,1,0:T(8,128)(2,1)S(1)} %get-tuple-element.144.q_ref.k_ref.v_ref, ...), custom_call_target="tpu_custom_call" | custom-call | flops 3221225472 | bytes 8000000 | tf_op jit(solution)/shard_map/pallas_call | solution.py:576
  87.2 12.1 %collective-permute-done.7.w_ox = bf16[4,192,768]{2,1,0:T(8,128)(2,1)S(1)} collective-permute-done((bf16[4,192,768]{2,1,0:T(8,128)(2,1)S(1)}, bf16[4,192,768]{2,1,0:T(8,128)(2,1)S(1)}, u32[]{:S(2)}, u32[]{:S(2)}) %collective-permute-start.7) | collective-permute-done | bytes 1179680 | tf_op jit(solution)/shard_map/ppermute | solution.py:413
  99.7 2.0 shard_map.319.a0_ref
  102.4 1.6 collective-permute-start.12
  104.1 1.3 collective-permute-start.13
  106.4 11.3 %shard_map.320 = (f32[1024,768]{1,0:T(8,128)S(1)}, bf16[1024,768]{1,0:T(8,128)(2,1)S(1)}, f32[1024,768]{1,0:T(8,128)S(1)}, f32[1024,768]{1,0:T(8,128)S(1)}, f32[...) custom-call(s32[1]{0:T(128)} %bitcast.x_ref, ...), custom_call_target="tpu_custom_call" | custom-call | flops 7247757312 | bytes 16000000 | tf_op jit(solution)/shard_map/pallas_call | solution.py:634
  118.2 1.3 collective-permute-done.13.d_yx
  119.5 1.3 collective-permute-start.14
  120.8 9.9 %shard_map.321 = (bf16[512,768]{1,0:T(8,128)(2,1)S(1)}, bf16[512,768]{1,0:T(8,128)(2,1)S(1)}, bf16[1024,768]{1,0:T(8,128)(2,1)S(1)}, f32[1,768]{1,0:T(1,128)S(1)...) custom-call(s32[1]{0:T(128)} %bitcast.x_ref, ...), custom_call_target="tpu_custom_call" | custom-call | flops 7247757312 | bytes 16000000 | tf_op jit(solution)/shard_map/pallas_call | solution.py:652
  130.7 3.4 %collective-permute-done.14 = bf16[4,96,768]{2,1,0:T(8,128)(2,1)S(1)} collective-permute-done((bf16[4,96,768]{2,1,0:T(8,128)(2,1)S(1)}, bf16[4,96,768]{2,1,0:T(8,128)(2,1)S(1)}, u32[]{:S(2)}, u32[]{:S(2)}) %collective-permute-start.14) | collective-permute-done | bytes 589856 | tf_op jit(solution)/shard_map/ppermute | solution.py:413
  134.6 1.3 collective-permute-start.16
  136.4 2.2 collective-permute-done.18.f1_ref
  139.0 6.8 %shard_map.322 = (f32[1024,768]{1,0:T(8,128)}, bf16[192,1024]{1,0:T(8,128)(2,1)S(1)}, bf16[192,1024]{1,0:T(8,128)(2,1)S(1)}, bf16[768,192]{1,0:T(8,128)(2,1)S(1)...) custom-call(f32[1024,768]{1,0:T(8,128)S(1)} %get-tuple-element.153.mid_ref, ...), custom_call_target="tpu_custom_call" | custom-call | flops 1207959552 | bytes 16000000 | tf_op jit(solution)/shard_map/pallas_call | solution.py:673
  145.8 4.0 %collective-permute-done.16 = bf16[4,96,768]{2,1,0:T(8,128)(2,1)S(1)} collective-permute-done((bf16[4,96,768]{2,1,0:T(8,128)(2,1)S(1)}, bf16[4,96,768]{2,1,0:T(8,128)(2,1)S(1)}, u32[]{:S(2)}, u32[]{:S(2)}) %collective-permute-start.16) | collective-permute-done | bytes 589856 | tf_op jit(solution)/shard_map/ppermute | solution.py:413
  149.9 1.0 collective-permute-done.17
  151.6 8.2 %shard_map.323 = (bf16[3,1024,64]{2,1,0:T(8,128)(2,1)S(1)}, bf16[3,1024,64]{2,1,0:T(8,128)(2,1)S(1)}, bf16[3,1024,64]{2,1,0:T(8,128)(2,1)S(1)}) custom-call(bf16[9,1024,64]{2,1,0:T(8,128)(2,1)S(1)} %get-tuple-element.144.q_ref.k_ref.v_ref, bf16[9,1024,64]{2,1,0:T(8,128)(2,1)S(1)} %get-tuple-element.144.q_ref.k_ref.v_ref, ...), custom_call_target="tpu_custom_call" | custom-call | flops 8053063680 | bytes 9000000 | tf_op jit(solution)/shard_map/pallas_call | solution.py:592
  159.9 8.0 %shard_map.324 = (bf16[4,96,768]{2,1,0:T(8,128)(2,1)S(1)}, bf16[4,96,768]{2,1,0:T(8,128)(2,1)S(1)}, f32[1024,768]{1,0:T(8,128)}, f32[1,576]{1,0:T(1,128)S(1)}) custom-call(s32[1]{0:T(128)} %bitcast.x_ref, bf16[3,1024,64]{2,1,0:T(8,128)(2,1)S(1)} %get-tuple-element.178.q_ref, bf16[3,1024,64]{2,1,0:T(8,128)(2,1)S(1)} %get-tuple-element.179.k_ref, ...), custom_call_target="tpu_custom_call" | custom-call | flops 1811939328 | bytes 10000000 | tf_op jit(solution)/shard_map/pallas_call | solution.py:699
  168.8 1.5 collective-permute-start.21
  170.3 0.8 slice_bitcast_fusion.1
  171.7 1.3 collective-permute-start.22
  172.9 8.2 %shard_map.326 = (bf16[3,1024,64]{2,1,0:T(8,128)(2,1)S(1)}, bf16[3,1024,64]{2,1,0:T(8,128)(2,1)S(1)}, bf16[3,1024,64]{2,1,0:T(8,128)(2,1)S(1)}) custom-call(bf16[9,1024,64]{2,1,0:T(8,128)(2,1)S(1)} %copy-done.34, bf16[9,1024,64]{2,1,0:T(8,128)(2,1)S(1)} %copy-done.34, bf16[9,1024,64]{2,1,0:T(8,128)(2,1)S(1)} %copy-done.34, ...), custom_call_target="tpu_custom_call" | custom-call | flops 8053063680 | bytes 9000000 | tf_op jit(solution)/shard_map/pallas_call | solution.py:592
  181.3 9.4 %collective-permute-done.23 = bf16[256,768]{1,0:T(8,128)(2,1)S(1)} collective-permute-done((bf16[256,768]{1,0:T(8,128)(2,1)S(1)}, bf16[256,768]{1,0:T(8,128)(2,1)S(1)}, u32[]{:S(2)}, u32[]{:S(2)}) %collective-permute-start.23) | collective-permute-done | bytes 393248 | tf_op jit(solution)/shard_map/ppermute | solution.py:409
  190.7 3.7 %collective-permute-done.22 = bf16[4,96,768]{2,1,0:T(8,128)(2,1)S(1)} collective-permute-done((bf16[4,96,768]{2,1,0:T(8,128)(2,1)S(1)}, bf16[4,96,768]{2,1,0:T(8,128)(2,1)S(1)}, u32[]{:S(2)}, u32[]{:S(2)}) %collective-permute-start.22) | collective-permute-done | bytes 589856 | tf_op jit(solution)/shard_map/ppermute | solution.py:413
  195.3 1.1 pad_maximum_fusion
  196.4 4.9 %all-to-all-start.3 = ((bf16[4,192,768]{2,1,0:T(8,128)(2,1)}), bf16[4,192,768]{2,1,0:T(8,128)(2,1)}, u32[]{:S(2)}, u32[]{:S(2)}) async-start(bf16[4,192,768]{2,1,0:T(8,128)(2,1)} %pad_maximum_fusion), calls=%async_computation.3 | async-start | bytes 2359296 | tf_op jit(solution)/shard_map/all_to_all | solution.py:421
  201.4 1.6 collective-permute-start.24
  203.0 1.1 copy-done.7
  204.2 8.1 %shard_map.327 = (bf16[4,96,768]{2,1,0:T(8,128)(2,1)S(1)}, bf16[4,96,768]{2,1,0:T(8,128)(2,1)}, bf16[1024,768]{1,0:T(8,128)(2,1)S(1)}, f32[1,576]{1,0:T(1,128)S(1)}) custom-call(s32[1]{0:T(128)} %bitcast.x_ref, bf16[3,1024,64]{2,1,0:T(8,128)(2,1)S(1)} %copy-done.3, bf16[3,1024,64]{2,1,0:T(8,128)(2,1)S(1)} %copy-done.5, bf16[3,1024,64]{2,1,0:T(8,128)(2,1)S(1)} %copy-done.7, ...), custom_call_target="tpu_custom_call" | custom-call | flops 1811939328 | bytes 10000000 | tf_op jit(solution)/shard_map/pallas_call | solution.py:699
  212.3 0.8 copy-done.8
  214.1 0.8 copy-done.43
  215.7 2.4 maximum_select_fusion
  218.1 9.6 %all-to-all-done.3 = bf16[4,192,768]{2,1,0:T(8,128)(2,1)} async-done(((bf16[4,192,768]{2,1,0:T(8,128)(2,1)}), bf16[4,192,768]{2,1,0:T(8,128)(2,1)}, u32[]{:S(2)}, u32[]{:S(2)}) %all-to-all-start.3) | async-done | bytes 1179680 | tf_op jit(solution)/shard_map/all_to_all | solution.py:421
  227.7 1.6 convert_reduce_fusion
  229.3 0.8 slice_bitcast_fusion.2
  230.2 5.6 %shard_map.328 = (bf16[1024,768]{1,0:T(8,128)(2,1)S(1)}, f32[2,4,8,96]{3,2,1,0:T(8,128)S(1)}, f32[2,4,16,96]{3,2,1,0:T(8,128)}, f32[8,768]{1,0:T(8,128)S(1)}) custom-call(s32[1]{0:T(128)} %bitcast.x_ref, bf16[256,768]{1,0:T(8,128)(2,1)S(1)} %get-tuple-element.255.refs_0_.s0, bf16[256,768]{1,0:T(8,128)(2,1)S(1)} %copy-done.12, ...), custom_call_target="tpu_custom_call" | custom-call | flops 1000000 | bytes 12000000 | tf_op jit(solution)/shard_map/pallas_call | solution.py:750
  235.9 1.6 collective-permute-start.27
  238.0 2.0 add_add_fusion.2
  240.0 3.5 %all-to-all-start.2 = ((bf16[4,96,768]{2,1,0:T(8,128)(2,1)}), bf16[4,96,768]{2,1,0:T(8,128)(2,1)S(1)}, u32[]{:S(2)}, u32[]{:S(2)}) async-start(bf16[4,96,768]{2,1,0:T(8,128)(2,1)} %add_add_fusion.2), calls=%async_computation.2 | async-start | bytes 1179648 | tf_op jit(solution)/shard_map/all_to_all | solution.py:421
  243.5 3.9 %collective-permute-done.28 = f32[2,4,16,96]{3,2,1,0:T(8,128)S(1)} collective-permute-done((f32[2,4,16,96]{3,2,1,0:T(8,128)}, f32[2,4,16,96]{3,2,1,0:T(8,128)S(1)}, u32[]{:S(2)}, u32[]{:S(2)}) %collective-permute-start.28) | collective-permute-done | bytes 49184 | tf_op jit(solution)/shard_map/ppermute | solution.py:409
  249.7 2.4 collective-permute-done.29
  252.6 3.4 %collective-permute-start.32 = (f32[8,96]{1,0:T(8,128)S(1)}, f32[8,96]{1,0:T(8,128)S(1)}, u32[]{:S(2)}, u32[]{:S(2)}) collective-permute-start(f32[8,96]{1,0:T(8,128)S(1)} %get-tuple-element.258), channel_id=1, source_target_pairs={{0,24},{8,0},{16,8},{24,16},{1,25},{9,1},{17,9},{25,17},{2,26},{10... | collective-permute-start | bytes 9224 | tf_op jit(solution)/shard_map/ppermute | solution.py:778
  256.0 1.0 maximum_select_fusion.1
  257.7 0.9 collective-permute-done.31.p2_ref
  258.6 0.9 shard_map.329
  (150 shorter events, 17.8 us)
Async XLA Ops:
  0.7 55.5 %copy-start = (bf16[2,768]{1,0:T(2,128)(2,1)S(1)}, bf16[2,768]{1,0:T(2,128)(2,1)}, u32[]{:S(2)}) copy-start(bf16[2,768]{1,0:T(2,128)(2,1)} %param.19) | copy-start | bytes 9220
  0.7 8.5 %copy-start.39 = (bf16[2,256,768]{2,1,0:T(8,128)(2,1)S(1)}, bf16[2,256,768]{2,1,0:T(8,128)(2,1)}, u32[]{:S(2)}) copy-start(bf16[2,256,768]{2,1,0:T(8,128)(2,1)} %param.18) | copy-start | bytes 2359300
  2.7 8.8 %copy-start.46 = (bf16[768,96]{0,1:T(8,128)(2,1)S(1)}, bf16[768,96]{0,1:T(8,128)(2,1)}, u32[]{:S(2)}) copy-start(bf16[768,96]{0,1:T(8,128)(2,1)} %param.33) | copy-start | bytes 442372
  2.7 23.5 %all-to-all-start = ((bf16[4,104,768]{2,1,0:T(8,128)(2,1)}), bf16[4,104,768]{2,1,0:T(8,128)(2,1)}, u32[]{:S(2)}, u32[]{:S(2)}) async-start(bf16[4,104,768]{2,1,0:T(8,128)(2,1)} %shard_map.313), calls=%async_computation | async-start | bytes 1277952 | tf_op jit(solution)/shard_map/all_to_all | solution.py:421
  9.9 21.5 %collective-permute-start = (bf16[256,768]{1,0:T(8,128)(2,1)}, bf16[256,768]{1,0:T(8,128)(2,1)S(1)}, u32[]{:S(2)}, u32[]{:S(2)}) collective-permute-start(bf16[256,768]{1,0:T(8,128)(2,1)} %get-tuple-element.254), channel_id=1, source_target_pairs={{0,2},{2,0},{1,3},{3,1},{4,6},{6,4},{5,7},{7,5},{8,10},{10,8},{9,1... | collective-permute-start | bytes 1179656 | tf_op jit(solution)/shard_map/ppermute | solution.py:409
  12.3 17.5 %copy-start.40 = (bf16[2,256,768]{2,1,0:T(8,128)(2,1)S(1)}, bf16[2,256,768]{2,1,0:T(8,128)(2,1)}, u32[]{:S(2)}) copy-start(bf16[2,256,768]{2,1,0:T(8,128)(2,1)} %param.35) | copy-start | bytes 2359300
  26.2 47.0 %all-to-all-start.1 = ((bf16[4,192,768]{2,1,0:T(8,128)(2,1)}), bf16[4,192,768]{2,1,0:T(8,128)(2,1)S(1)}, u32[]{:S(2)}, u32[]{:S(2)}) async-start(bf16[4,192,768]{2,1,0:T(8,128)(2,1)} %shard_map.316), calls=%async_computation.1 | async-start | bytes 2359296 | tf_op jit(solution)/shard_map/all_to_all | solution.py:421
  29.8 10.1 %collective-permute-start.1 = (bf16[256,768]{1,0:T(8,128)(2,1)S(1)}, bf16[256,768]{1,0:T(8,128)(2,1)S(1)}, u32[]{:S(2)}, u32[]{:S(2)}) collective-permute-start(bf16[256,768]{1,0:T(8,128)(2,1)S(1)} %get-tuple-element.253), channel_id=1, source_target_pairs={{0,2},{2,0},{1,3},{3,1},{4,6},{6,4},{5,7},{7,5},{8,10},{10,8},{9,1... | collective-permute-start | bytes 1179656 | tf_op jit(solution)/shard_map/ppermute | solution.py:409
  31.4 33.7 %copy-start.10 = (bf16[256,768]{1,0:T(8,128)(2,1)}, bf16[256,768]{1,0:T(8,128)(2,1)S(1)}, u32[]{:S(2)}) copy-start(bf16[256,768]{1,0:T(8,128)(2,1)S(1)} %collective-permute-done.refs_1_.s1) | copy-start | bytes 1179652
  39.9 14.7 %collective-permute-start.4 = (bf16[4,104,768]{2,1,0:T(8,128)(2,1)}, bf16[4,104,768]{2,1,0:T(8,128)(2,1)}, u32[]{:S(2)}, u32[]{:S(2)}) collective-permute-start(bf16[4,104,768]{2,1,0:T(8,128)(2,1)} %all-to-all-done.refs_5_), channel_id=1, source_target_pairs={{0,4},{4,0},{1,5},{5,1},{2,6},{6,2},{3,7},{7,3},{8,12},{12,8},{9,1... | collective-permute-start | bytes 1916936 | tf_op jit(solution)/shard_map/ppermute | solution.py:413
  41.4 14.8 %collective-permute-start.2 = (bf16[256,768]{1,0:T(8,128)(2,1)S(1)}, bf16[256,768]{1,0:T(8,128)(2,1)S(1)}, u32[]{:S(2)}, u32[]{:S(2)}) collective-permute-start(bf16[256,768]{1,0:T(8,128)(2,1)S(1)} %get-tuple-element.255.refs_0_.s0), channel_id=1, source_target_pairs={{0,1},{1,0},{2,3},{3,2},{4,5},{5,4},{6,7},{7,6},{8,9},{9,8},{10,11... | collective-permute-start | bytes 1179656 | tf_op jit(solution)/shard_map/ppermute | solution.py:417
  41.4 15.5 %collective-permute-start.3 = (bf16[256,768]{1,0:T(8,128)(2,1)S(1)}, bf16[256,768]{1,0:T(8,128)(2,1)S(1)}, u32[]{:S(2)}, u32[]{:S(2)}) collective-permute-start(bf16[256,768]{1,0:T(8,128)(2,1)S(1)} %collective-permute-done.refs_1_.s1), channel_id=1, source_target_pairs={{0,1},{1,0},{2,3},{3,2},{4,5},{5,4},{6,7},{7,6},{8,9},{9,8},{10,11... | collective-permute-start | bytes 1179656 | tf_op jit(solution)/shard_map/ppermute | solution.py:417
  42.0 31.2 %collective-permute-start.5 = (bf16[4,104,768]{2,1,0:T(8,128)(2,1)}, bf16[4,104,768]{2,1,0:T(8,128)(2,1)}, u32[]{:S(2)}, u32[]{:S(2)}) collective-permute-start(bf16[4,104,768]{2,1,0:T(8,128)(2,1)} %all-to-all-done.refs_5_), channel_id=1, source_target_pairs={{0,2},{2,0},{1,3},{3,1},{4,6},{6,4},{5,7},{7,5},{8,10},{10,8},{9,1... | collective-permute-start | bytes 1916936 | tf_op jit(solution)/shard_map/ppermute | solution.py:409
  54.7 18.5 %collective-permute-start.6 = (bf16[4,104,768]{2,1,0:T(8,128)(2,1)}, bf16[4,104,768]{2,1,0:T(8,128)(2,1)}, u32[]{:S(2)}, u32[]{:S(2)}) collective-permute-start(bf16[4,104,768]{2,1,0:T(8,128)(2,1)} %collective-permute-done.4.refs_6_), channel_id=1, source_target_pairs={{0,2},{2,0},{1,3},{3,1},{4,6},{6,4},{5,7},{7,5},{8,10},{10,8},{9,1... | collective-permute-start | bytes 1916936 | tf_op jit(solution)/shard_map/ppermute | solution.py:409
  65.7 6.9 %copy-start.33 = (bf16[9,1024,64]{2,1,0:T(8,128)(2,1)}, bf16[9,1024,64]{2,1,0:T(8,128)(2,1)S(1)}, u32[]{:S(2)}) copy-start(bf16[9,1024,64]{2,1,0:T(8,128)(2,1)S(1)} %get-tuple-element.137.q_ref.k_ref.v_ref) | copy-start | bytes 3538948
  65.7 6.9 %copy-start.35 = (bf16[1024,768]{1,0:T(8,128)(2,1)}, bf16[1024,768]{1,0:T(8,128)(2,1)S(1)}, u32[]{:S(2)}) copy-start(bf16[1024,768]{1,0:T(8,128)(2,1)S(1)} %get-tuple-element.141.refs_0_) | copy-start | bytes 4718596
  73.2 26.1 %collective-permute-start.7 = (bf16[4,192,768]{2,1,0:T(8,128)(2,1)S(1)}, bf16[4,192,768]{2,1,0:T(8,128)(2,1)S(1)}, u32[]{:S(2)}, u32[]{:S(2)}) collective-permute-start(bf16[4,192,768]{2,1,0:T(8,128)(2,1)S(1)} %all-to-all-done.1.w_oo), channel_id=1, source_target_pairs={{0,4},{4,0},{1,5},{5,1},{2,6},{6,2},{3,7},{7,3},{8,12},{12,8},{9,1... | collective-permute-start | bytes 3538952 | tf_op jit(solution)/shard_map/ppermute | solution.py:413
  74.7 25.0 %collective-permute-start.8 = (bf16[4,192,768]{2,1,0:T(8,128)(2,1)S(1)}, bf16[4,192,768]{2,1,0:T(8,128)(2,1)S(1)}, u32[]{:S(2)}, u32[]{:S(2)}) collective-permute-start(bf16[4,192,768]{2,1,0:T(8,128)(2,1)S(1)} %all-to-all-done.1.w_oo), channel_id=1, source_target_pairs={{0,2},{2,0},{1,3},{3,1},{4,6},{6,4},{5,7},{7,5},{8,10},{10,8},{9,1... | collective-permute-start | bytes 3538952 | tf_op jit(solution)/shard_map/ppermute | solution.py:409
  99.7 2.6 copy-start.22
  101.7 4.6 %copy-start.11 = (bf16[256,768]{1,0:T(8,128)(2,1)S(1)}, bf16[256,768]{1,0:T(8,128)(2,1)}, u32[]{:S(2)}) copy-start(bf16[256,768]{1,0:T(8,128)(2,1)} %copy-done.10) | copy-start | bytes 1179652
  101.7 4.6 %copy-start.15 = (bf16[256,768]{1,0:T(8,128)(2,1)S(1)}, bf16[256,768]{1,0:T(8,128)(2,1)}, u32[]{:S(2)}) copy-start(bf16[256,768]{1,0:T(8,128)(2,1)} %copy-done.13) | copy-start | bytes 1179652
  101.7 4.6 %copy-start.19 = (bf16[256,768]{1,0:T(8,128)(2,1)S(1)}, bf16[256,768]{1,0:T(8,128)(2,1)}, u32[]{:S(2)}) copy-start(bf16[256,768]{1,0:T(8,128)(2,1)} %copy-done.17) | copy-start | bytes 1179652
  101.7 4.6 %copy-start.26 = (f32[8,768]{1,0:T(8,128)S(1)}, f32[8,768]{1,0:T(8,128)}, u32[]{:S(2)}) copy-start(f32[8,768]{1,0:T(8,128)} %copy-done.25) | copy-start | bytes 73732
  101.7 4.6 %collective-permute-start.9 = (bf16[1024,768]{1,0:T(8,128)(2,1)S(1)}, bf16[1024,768]{1,0:T(8,128)(2,1)S(1)}, u32[]{:S(2)}, u32[]{:S(2)}) collective-permute-start(bf16[1024,768]{1,0:T(8,128)(2,1)S(1)} %shard_map.319.a0_ref), channel_id=1, source_target_pairs={{0,1},{1,0},{2,3},{3,2},{4,5},{5,4},{6,7},{7,6},{8,9},{9,8},{10,11... | collective-permute-start | bytes 4718600 | tf_op jit(solution)/shard_map/ppermute | solution.py:417
  101.8 4.0 %collective-permute-start.10 = (bf16[256,768]{1,0:T(8,128)(2,1)S(1)}, bf16[256,768]{1,0:T(8,128)(2,1)S(1)}, u32[]{:S(2)}, u32[]{:S(2)}) collective-permute-start(bf16[256,768]{1,0:T(8,128)(2,1)S(1)} %get-tuple-element.252.c0), channel_id=1, source_target_pairs={{0,1},{1,0},{2,3},{3,2},{4,5},{5,4},{6,7},{7,6},{8,9},{9,8},{10,11... | collective-permute-start | bytes 1179656 | tf_op jit(solution)/shard_map/ppermute | solution.py:417
  102.3 4.0 %collective-permute-start.11 = (bf16[256,768]{1,0:T(8,128)(2,1)S(1)}, bf16[256,768]{1,0:T(8,128)(2,1)S(1)}, u32[]{:S(2)}, u32[]{:S(2)}) collective-permute-start(bf16[256,768]{1,0:T(8,128)(2,1)S(1)} %copy-done.22), channel_id=1, source_target_pairs={{0,1},{1,0},{2,3},{3,2},{4,5},{5,4},{6,7},{7,6},{8,9},{9,8},{10,11... | collective-permute-start | bytes 1179656 | tf_op jit(solution)/shard_map/ppermute | solution.py:417
  102.4 15.7 %collective-permute-start.12 = (bf16[4,96,768]{2,1,0:T(8,128)(2,1)S(1)}, bf16[4,96,768]{2,1,0:T(8,128)(2,1)S(1)}, u32[]{:S(2)}, u32[]{:S(2)}) collective-permute-start(bf16[4,96,768]{2,1,0:T(8,128)(2,1)S(1)} %slice.39), channel_id=1, source_target_pairs={{0,2},{2,0},{1,3},{3,1},{4,6},{6,4},{5,7},{7,5},{8,10},{10,8},{9,1... | collective-permute-start | bytes 1769480 | tf_op jit(solution)/shard_map/ppermute | solution.py:409
  104.1 15.5 %collective-permute-start.13 = (bf16[4,96,768]{2,1,0:T(8,128)(2,1)S(1)}, bf16[4,96,768]{2,1,0:T(8,128)(2,1)S(1)}, u32[]{:S(2)}, u32[]{:S(2)}) collective-permute-start(bf16[4,96,768]{2,1,0:T(8,128)(2,1)S(1)} %slice.40), channel_id=1, source_target_pairs={{0,4},{4,0},{1,5},{5,1},{2,6},{6,2},{3,7},{7,3},{8,12},{12,8},{9,1... | collective-permute-start | bytes 1769480 | tf_op jit(solution)/shard_map/ppermute | solution.py:413
  119.5 14.6 %collective-permute-start.14 = (bf16[4,96,768]{2,1,0:T(8,128)(2,1)S(1)}, bf16[4,96,768]{2,1,0:T(8,128)(2,1)S(1)}, u32[]{:S(2)}, u32[]{:S(2)}) collective-permute-start(bf16[4,96,768]{2,1,0:T(8,128)(2,1)S(1)} %get-tuple-element.163), channel_id=1, source_target_pairs={{0,4},{4,0},{1,5},{5,1},{2,6},{6,2},{3,7},{7,3},{8,12},{12,8},{9,1... | collective-permute-start | bytes 1769480 | tf_op jit(solution)/shard_map/ppermute | solution.py:413
  134.1 4.9 %collective-permute-start.15 = (bf16[1024,768]{1,0:T(8,128)(2,1)S(1)}, bf16[1024,768]{1,0:T(8,128)(2,1)S(1)}, u32[]{:S(2)}, u32[]{:S(2)}) collective-permute-start(bf16[1024,768]{1,0:T(8,128)(2,1)S(1)} %get-tuple-element.164.g0_ref), channel_id=1, source_target_pairs={{0,1},{1,0},{2,3},{3,2},{4,5},{5,4},{6,7},{7,6},{8,9},{9,8},{10,11... | collective-permute-start | bytes 4718600 | tf_op jit(solution)/shard_map/ppermute | solution.py:417
  134.1 4.5 %collective-permute-start.18 = (bf16[512,768]{1,0:T(8,128)(2,1)S(1)}, bf16[512,768]{1,0:T(8,128)(2,1)S(1)}, u32[]{:S(2)}, u32[]{:S(2)}) collective-permute-start(bf16[512,768]{1,0:T(8,128)(2,1)S(1)} %get-tuple-element.185), channel_id=1, source_target_pairs={{0,1},{1,0},{2,3},{3,2},{4,5},{5,4},{6,7},{7,6},{8,9},{9,8},{10,11... | collective-permute-start | bytes 2359304 | tf_op jit(solution)/shard_map/ppermute | solution.py:417
  134.6 15.2 %collective-permute-start.16 = (bf16[4,96,768]{2,1,0:T(8,128)(2,1)S(1)}, bf16[4,96,768]{2,1,0:T(8,128)(2,1)S(1)}, u32[]{:S(2)}, u32[]{:S(2)}) collective-permute-start(bf16[4,96,768]{2,1,0:T(8,128)(2,1)S(1)} %get-tuple-element.170), channel_id=1, source_target_pairs={{0,4},{4,0},{1,5},{5,1},{2,6},{6,2},{3,7},{7,3},{8,12},{12,8},{9,1... | collective-permute-start | bytes 1769480 | tf_op jit(solution)/shard_map/ppermute | solution.py:413
  135.9 15.0 %collective-permute-start.17 = (bf16[4,96,768]{2,1,0:T(8,128)(2,1)S(1)}, bf16[4,96,768]{2,1,0:T(8,128)(2,1)S(1)}, u32[]{:S(2)}, u32[]{:S(2)}) collective-permute-start(bf16[4,96,768]{2,1,0:T(8,128)(2,1)S(1)} %get-tuple-element.171), channel_id=1, source_target_pairs={{0,2},{2,0},{1,3},{3,1},{4,6},{6,4},{5,7},{7,5},{8,10},{10,8},{9,1... | collective-permute-start | bytes 1769480 | tf_op jit(solution)/shard_map/ppermute | solution.py:409
  145.8 5.2 %copy-start.29 = (f32[8,768]{1,0:T(8,128)}, f32[8,768]{1,0:T(8,128)S(1)}, u32[]{:S(2)}) copy-start(f32[8,768]{1,0:T(8,128)S(1)} %get-tuple-element.213.second_ref) | copy-start | bytes 73732
  145.8 14.1 %copy-start.23 = (bf16[768,192]{1,0:T(8,128)(2,1)}, bf16[768,192]{1,0:T(8,128)(2,1)S(1)}, u32[]{:S(2)}) copy-start(bf16[768,192]{1,0:T(8,128)(2,1)S(1)} %get-tuple-element.206.wo_ref) | copy-start | bytes 884740
  151.0 20.6 %collective-permute-start.19 = (bf16[4,96,768]{2,1,0:T(8,128)(2,1)S(1)}, bf16[4,96,768]{2,1,0:T(8,128)(2,1)S(1)}, u32[]{:S(2)}, u32[]{:S(2)}) collective-permute-start(bf16[4,96,768]{2,1,0:T(8,128)(2,1)S(1)} %add.82), channel_id=1, source_target_pairs={{0,2},{2,0},{1,3},{3,1},{4,6},{6,4},{5,7},{7,5},{8,10},{10,8},{9,1... | collective-permute-start | bytes 1769480 | tf_op jit(solution)/shard_map/ppermute | solution.py:409
  167.8 5.1 %copy-start.34 = (bf16[9,1024,64]{2,1,0:T(8,128)(2,1)S(1)}, bf16[9,1024,64]{2,1,0:T(8,128)(2,1)}, u32[]{:S(2)}) copy-start(bf16[9,1024,64]{2,1,0:T(8,128)(2,1)} %copy-done.33) | copy-start | bytes 3538948
  167.8 5.1 %copy-start.38 = (f32[3,1,1024]{2,1,0:T(1,128)S(1)}, f32[3,1,1024]{2,1,0:T(1,128)}, u32[]{:S(2)}) copy-start(f32[3,1,1024]{2,1,0:T(1,128)} %copy-done.37) | copy-start | bytes 36868
  168.0 22.7 %collective-permute-start.20 = (bf16[4,96,768]{2,1,0:T(8,128)(2,1)S(1)}, bf16[4,96,768]{2,1,0:T(8,128)(2,1)S(1)}, u32[]{:S(2)}, u32[]{:S(2)}) collective-permute-start(bf16[4,96,768]{2,1,0:T(8,128)(2,1)S(1)} %add.83), channel_id=1, source_target_pairs={{0,4},{4,0},{1,5},{5,1},{2,6},{6,2},{3,7},{7,3},{8,12},{12,8},{9,1... | collective-permute-start | bytes 1769480 | tf_op jit(solution)/shard_map/ppermute | solution.py:413
  168.8 21.9 %collective-permute-start.21 = (bf16[4,96,768]{2,1,0:T(8,128)(2,1)S(1)}, bf16[4,96,768]{2,1,0:T(8,128)(2,1)S(1)}, u32[]{:S(2)}, u32[]{:S(2)}) collective-permute-start(bf16[4,96,768]{2,1,0:T(8,128)(2,1)S(1)} %get-tuple-element.200), channel_id=1, source_target_pairs={{0,2},{2,0},{1,3},{3,1},{4,6},{6,4},{5,7},{7,5},{8,10},{10,8},{9,1... | collective-permute-start | bytes 1769480 | tf_op jit(solution)/shard_map/ppermute | solution.py:409
  171.1 19.6 %collective-permute-start.23 = (bf16[256,768]{1,0:T(8,128)(2,1)S(1)}, bf16[256,768]{1,0:T(8,128)(2,1)S(1)}, u32[]{:S(2)}, u32[]{:S(2)}) collective-permute-start(bf16[256,768]{1,0:T(8,128)(2,1)S(1)} %get-tuple-element.251), channel_id=1, source_target_pairs={{0,2},{2,0},{1,3},{3,1},{4,6},{6,4},{5,7},{7,5},{8,10},{10,8},{9,1... | collective-permute-start | bytes 1179656 | tf_op jit(solution)/shard_map/ppermute | solution.py:409
  171.7 22.8 %collective-permute-start.22 = (bf16[4,96,768]{2,1,0:T(8,128)(2,1)S(1)}, bf16[4,96,768]{2,1,0:T(8,128)(2,1)S(1)}, u32[]{:S(2)}, u32[]{:S(2)}) collective-permute-start(bf16[4,96,768]{2,1,0:T(8,128)(2,1)S(1)} %get-tuple-element.201), channel_id=1, source_target_pairs={{0,4},{4,0},{1,5},{5,1},{2,6},{6,2},{3,7},{7,3},{8,12},{12,8},{9,1... | collective-permute-start | bytes 1769480 | tf_op jit(solution)/shard_map/ppermute | solution.py:413
  181.2 13.4 %copy-start.2 = (bf16[3,1024,64]{2,1,0:T(8,128)(2,1)}, bf16[3,1024,64]{2,1,0:T(8,128)(2,1)S(1)}, u32[]{:S(2)}) copy-start(bf16[3,1024,64]{2,1,0:T(8,128)(2,1)S(1)} %get-tuple-element.203.q_ref) | copy-start | bytes 1179652
  181.2 13.4 %copy-start.4 = (bf16[3,1024,64]{2,1,0:T(8,128)(2,1)}, bf16[3,1024,64]{2,1,0:T(8,128)(2,1)S(1)}, u32[]{:S(2)}) copy-start(bf16[3,1024,64]{2,1,0:T(8,128)(2,1)S(1)} %get-tuple-element.204.k_ref) | copy-start | bytes 1179652
  181.2 13.4 %copy-start.6 = (bf16[3,1024,64]{2,1,0:T(8,128)(2,1)}, bf16[3,1024,64]{2,1,0:T(8,128)(2,1)S(1)}, u32[]{:S(2)}) copy-start(bf16[3,1024,64]{2,1,0:T(8,128)(2,1)S(1)} %get-tuple-element.205.v_ref) | copy-start | bytes 1179652
  190.7 5.7 %copy-start.45 = (bf16[256,768]{1,0:T(8,128)(2,1)}, bf16[256,768]{1,0:T(8,128)(2,1)S(1)}, u32[]{:S(2)}) copy-start(bf16[256,768]{1,0:T(8,128)(2,1)S(1)} %collective-permute-done.23) | copy-start | bytes 1179652
  196.4 4.9 %copy-start.42 = (bf16[4,96,768]{2,1,0:T(8,128)(2,1)S(1)}, bf16[4,96,768]{2,1,0:T(8,128)(2,1)}, u32[]{:S(2)}) copy-start(bf16[4,96,768]{2,1,0:T(8,128)(2,1)} %copy-done.41) | copy-start | bytes 1769476
  196.4 6.6 %copy-start.24 = (bf16[768,192]{1,0:T(8,128)(2,1)S(1)}, bf16[768,192]{1,0:T(8,128)(2,1)}, u32[]{:S(2)}) copy-start(bf16[768,192]{1,0:T(8,128)(2,1)} %copy-done.23) | copy-start | bytes 884740
  196.4 31.3 %all-to-all-start.3 = ((bf16[4,192,768]{2,1,0:T(8,128)(2,1)}), bf16[4,192,768]{2,1,0:T(8,128)(2,1)}, u32[]{:S(2)}, u32[]{:S(2)}) async-start(bf16[4,192,768]{2,1,0:T(8,128)(2,1)} %pad_maximum_fusion), calls=%async_computation.3 | async-start | bytes 2359296 | tf_op jit(solution)/shard_map/all_to_all | solution.py:421
  201.4 12.7 %collective-permute-start.24 = (bf16[4,96,768]{2,1,0:T(8,128)(2,1)S(1)}, bf16[4,96,768]{2,1,0:T(8,128)(2,1)S(1)}, u32[]{:S(2)}, u32[]{:S(2)}) collective-permute-start(bf16[4,96,768]{2,1,0:T(8,128)(2,1)S(1)} %add.84), channel_id=1, source_target_pairs={{0,2},{2,0},{1,3},{3,1},{4,6},{6,4},{5,7},{7,5},{8,10},{10,8},{9,1... | collective-permute-start | bytes 1769480 | tf_op jit(solution)/shard_map/ppermute | solution.py:409
  214.9 15.2 %collective-permute-start.25 = (bf16[1024,768]{1,0:T(8,128)(2,1)S(1)}, bf16[1024,768]{1,0:T(8,128)(2,1)S(1)}, u32[]{:S(2)}, u32[]{:S(2)}) collective-permute-start(bf16[1024,768]{1,0:T(8,128)(2,1)S(1)} %get-tuple-element.211.g0_ref), channel_id=1, source_target_pairs={{0,1},{1,0},{2,3},{3,2},{4,5},{5,4},{6,7},{7,6},{8,9},{9,8},{10,11... | collective-permute-start | bytes 4718600 | tf_op jit(solution)/shard_map/ppermute | solution.py:417
  215.0 20.9 %collective-permute-start.26 = (bf16[4,96,768]{2,1,0:T(8,128)(2,1)}, bf16[4,96,768]{2,1,0:T(8,128)(2,1)}, u32[]{:S(2)}, u32[]{:S(2)}) collective-permute-start(bf16[4,96,768]{2,1,0:T(8,128)(2,1)} %get-tuple-element.221), channel_id=1, source_target_pairs={{0,4},{4,0},{1,5},{5,1},{2,6},{6,2},{3,7},{7,3},{8,12},{12,8},{9,1... | collective-permute-start | bytes 1769480 | tf_op jit(solution)/shard_map/ppermute | solution.py:413
  227.7 2.5 copy-start.27
  227.7 2.5 copy-start.30
  227.7 2.5 copy-start.32
  235.8 4.2 %copy-start.28 = (f32[2,4,8,96]{3,2,1,0:T(8,128)}, f32[2,4,8,96]{3,2,1,0:T(8,128)S(1)}, u32[]{:S(2)}) copy-start(f32[2,4,8,96]{3,2,1,0:T(8,128)S(1)} %get-tuple-element.228) | copy-start | bytes 73732
  235.9 20.1 %collective-permute-start.27 = (bf16[256,768]{1,0:T(8,128)(2,1)S(1)}, bf16[256,768]{1,0:T(8,128)(2,1)S(1)}, u32[]{:S(2)}, u32[]{:S(2)}) collective-permute-start(bf16[256,768]{1,0:T(8,128)(2,1)S(1)} %get-tuple-element.249), channel_id=1, source_target_pairs={{0,2},{2,0},{1,3},{3,1},{4,6},{6,4},{5,7},{7,5},{8,10},{10,8},{9,1... | collective-permute-start | bytes 1179656 | tf_op jit(solution)/shard_map/ppermute | solution.py:409
  237.5 10.0 %collective-permute-start.28 = (f32[2,4,16,96]{3,2,1,0:T(8,128)}, f32[2,4,16,96]{3,2,1,0:T(8,128)S(1)}, u32[]{:S(2)}, u32[]{:S(2)}) collective-permute-start(f32[2,4,16,96]{3,2,1,0:T(8,128)} %get-tuple-element.224), channel_id=1, source_target_pairs={{0,2},{2,0},{1,3},{3,1},{4,6},{6,4},{5,7},{7,5},{8,10},{10,8},{9,1... | collective-permute-start | bytes 147464 | tf_op jit(solution)/shard_map/ppermute | solution.py:409
  240.0 18.6 %all-to-all-start.2 = ((bf16[4,96,768]{2,1,0:T(8,128)(2,1)}), bf16[4,96,768]{2,1,0:T(8,128)(2,1)S(1)}, u32[]{:S(2)}, u32[]{:S(2)}) async-start(bf16[4,96,768]{2,1,0:T(8,128)(2,1)} %add_add_fusion.2), calls=%async_computation.2 | async-start | bytes 1179648 | tf_op jit(solution)/shard_map/all_to_all | solution.py:421
  243.5 16.0 %copy-start.1 = (bf16[2,768]{1,0:T(2,128)(2,1)S(1)}, bf16[2,768]{1,0:T(2,128)(2,1)}, u32[]{:S(2)}) copy-start(bf16[2,768]{1,0:T(2,128)(2,1)} %param.19) | copy-start | bytes 9220
  248.3 3.8 %collective-permute-start.29 = (f32[4,8,96]{2,1,0:T(8,128)S(1)}, f32[4,8,96]{2,1,0:T(8,128)S(1)}, u32[]{:S(2)}, u32[]{:S(2)}) collective-permute-start(f32[4,8,96]{2,1,0:T(8,128)S(1)} %slice_bitcast_fusion.3), channel_id=1, source_target_pairs={{0,4},{4,0},{1,5},{5,1},{2,6},{6,2},{3,7},{7,3},{8,12},{12,8},{9,1... | collective-permute-start | bytes 36872 | tf_op jit(solution)/shard_map/ppermute | solution.py:413
  252.1 5.6 %collective-permute-start.30 = (f32[8,96]{1,0:T(8,128)S(1)}, f32[8,96]{1,0:T(8,128)S(1)}, u32[]{:S(2)}, u32[]{:S(2)}) collective-permute-start(f32[8,96]{1,0:T(8,128)S(1)} %get-tuple-element.260), channel_id=1, source_target_pairs={{0,8},{8,16},{16,24},{24,0},{1,9},{9,17},{17,25},{25,1},{2,10},{10... | collective-permute-start | bytes 9224 | tf_op jit(solution)/shard_map/ppermute | solution.py:778
  252.2 6.4 %collective-permute-start.31 = (f32[8,96]{1,0:T(8,128)S(1)}, f32[8,96]{1,0:T(8,128)S(1)}, u32[]{:S(2)}, u32[]{:S(2)}) collective-permute-start(f32[8,96]{1,0:T(8,128)S(1)} %get-tuple-element.259), channel_id=1, source_target_pairs={{0,16},{8,24},{16,0},{24,8},{1,17},{9,25},{17,1},{25,9},{2,18},{10... | collective-permute-start | bytes 9224 | tf_op jit(solution)/shard_map/ppermute | solution.py:778
  252.6 6.0 %collective-permute-start.32 = (f32[8,96]{1,0:T(8,128)S(1)}, f32[8,96]{1,0:T(8,128)S(1)}, u32[]{:S(2)}, u32[]{:S(2)}) collective-permute-start(f32[8,96]{1,0:T(8,128)S(1)} %get-tuple-element.258), channel_id=1, source_target_pairs={{0,24},{8,0},{16,8},{24,16},{1,25},{9,1},{17,9},{25,17},{2,26},{10... | collective-permute-start | bytes 9224 | tf_op jit(solution)/shard_map/ppermute | solution.py:778
  (20 other events, 27.0 us)

commit v4 on v3

--- a/solution.py
+++ b/solution.py
@@ -79,24 +79,19 @@
     return center * rate, rate
 
 
-def pack_attn_body(q_ref, k_ref, v_ref, o_ref, fg, fs, ob, sg, ss, db, hb, qb, vb, out_ref):
+def pack_body(q_ref, k_ref, v_ref, o_ref, h_ref, d_ref, fg, fs, ob, sg, ss, db, hb, qb, vb, attn_ref, mlp_ref):
     shard = q_ref.shape[0]
     low = jnp.concatenate([q_ref[...], k_ref[...], v_ref[...], o_ref[...].T], axis=1)
     n = qb.shape[1]
     bias = jnp.concatenate([qb[...], vb[...], jnp.zeros((1, shard - 2 * n), BF)], axis=1)
     small = jnp.concatenate([r[...].astype(F32) for r in (fg, fs, ob, sg, ss, db, hb)] + [bias.astype(F32)], axis=0)
     small = jnp.concatenate([small, jnp.zeros((KINDS, low.shape[1] - shard), F32)], axis=1).astype(BF)
-    for z in range(out_ref.shape[0]):
-        out_ref[z, :shard, :] = low
-        out_ref[z, shard:, :] = small
-
-
-def pack_mlp_body(h_ref, d_ref, out_ref):
-    shard = h_ref.shape[0]
-    high, low = h_ref[...], d_ref[...].T
-    for z in range(out_ref.shape[0]):
-        out_ref[z, :shard, :] = high
-        out_ref[z, shard:, :] = low
+    high, down = h_ref[...], d_ref[...].T
+    for z in range(attn_ref.shape[0]):
+        attn_ref[z, :shard, :] = low
+        attn_ref[z, shard:, :] = small
+        mlp_ref[z, :shard, :] = high
+        mlp_ref[z, shard:, :] = down
 
 
 def pick(refs):
@@ -419,10 +414,6 @@
 
 def spread_z(values):
     return lax.all_to_all(values, "a", 0, 0, tiled=True)
-
-
-def after(value, *others):
-    return lax.optimization_barrier((value, *others))[0]
 
 
 def body(
@@ -456,47 +447,40 @@
     x_arr = xi.astype(jnp.int32)[None]
 
     n_copies = ZS if fast else 1
-    (attn_pack,) = call(
-        pack_attn_body,
+    attn_pack, mlp_pack = call(
+        pack_body,
         (1,),
-        [kept((shard, hidden // 4))] * 3 + [kept((hidden // 4, shard))] + [kept((1, shard))] * 7 + [kept((1, query_bias.shape[0]))] * 2,
-        [(sds((n_copies, shard + KINDS, width), BF), kept((n_copies, shard + KINDS, width)))],
-        flops=1e6,
-        moved=1e6,
-        vmem=56,
-    )(
-        query_weight, key_weight, value_weight, output_weight,
-        *(v[None] for v in (first_gain, first_shift, output_bias, second_gain, second_shift, down_bias, hidden_bias, query_bias, value_bias)),
-    )
-    (mlp_pack,) = call(
-        pack_mlp_body,
-        (1,),
-        [kept((shard, hidden)), kept((hidden, shard))],
-        [(sds((n_copies, 2 * shard, width), BF), kept((n_copies, 2 * shard, width)))],
+        [kept((shard, hidden // 4))] * 3
+        + [kept((hidden // 4, shard)), kept((shard, hidden)), kept((hidden, shard))]
+        + [kept((1, shard))] * 7
+        + [kept((1, query_bias.shape[0]))] * 2,
+        [
+            (sds((n_copies, shard + KINDS, width), BF), kept((n_copies, shard + KINDS, width))),
+            (sds((n_copies, 2 * shard, width), BF), kept((n_copies, 2 * shard, width))),
+        ],
         flops=1e6,
         moved=2e6,
         vmem=56,
-    )(hidden_weight, down_weight)
-
-    def tokens(values):
-        stays = lax.dynamic_index_in_dim(values, yi, 0, keepdims=False)
-        comes = to_y(lax.dynamic_index_in_dim(values, 1 - yi, 0, keepdims=False))
-        return stays, comes
-
-    def with_mate(stays, comes):
-        return stays, comes, to_core(stays), to_core(comes)
-
-    inputs, cotangent = lax.optimization_barrier((inputs, cotangent, attn_pack))[:2]
-    start, cot = tokens(inputs), tokens(cotangent)
+    )(
+        query_weight, key_weight, value_weight, output_weight, hidden_weight, down_weight,
+        *(v[None] for v in (first_gain, first_shift, output_bias, second_gain, second_shift, down_bias, hidden_bias, query_bias, value_bias)),
+    )
+
+    inputs, cotangent, attn_pack = lax.optimization_barrier((inputs, cotangent, attn_pack))
+    both = jnp.concatenate([inputs, cotangent], axis=1)
+    stays = lax.dynamic_index_in_dim(both, yi, 0, keepdims=False)
+    comes = to_y(lax.dynamic_index_in_dim(both, 1 - yi, 0, keepdims=False))
+    stays_mate = to_core(stays)
     te = lax.dynamic_index_in_dim(time_embed, yi, 0, keepdims=True)
 
     if fast:
         attn_oo = spread_z(attn_pack)
-        attn_oo, *comes = lax.optimization_barrier((attn_oo, start[1], cot[1]))
-        start, cot = with_mate(start[0], comes[0]), with_mate(cot[0], comes[1])
+        attn_oo, comes, stays_mate = lax.optimization_barrier((attn_oo, comes, stays_mate))
+        comes_mate = to_core(comes)
         attn_ox, attn_yo = to_x(attn_oo), to_y(attn_oo)
+        attn_ox, attn_yo = lax.optimization_barrier((attn_ox, attn_yo))
         mlp_oo = spread_z(mlp_pack)
-        attn_yx = to_y(attn_ox)
+        attn_yx = (to_y(attn_ox[:, : rows // 2]), to_x(attn_yo[:, rows // 2 :]))
     else:
         def natural(values):
             full = lax.all_gather(values, ("a", "b"), axis=0, tiled=True)
@@ -515,8 +499,8 @@
         small = jnp.pad(small, ((0, 0), (0, 0), (0, 0), (0, width - rows)))
         matrix = jnp.concatenate([matrix, small], axis=2)
         attn_oo, attn_ox = matrix[:, 0], matrix[:, 1]
-        attn_yo, attn_yx = to_y(attn_oo), to_y(attn_ox)
-        start, cot = with_mate(*start), with_mate(*cot)
+        attn_yo, attn_yx = to_y(attn_oo), (to_y(attn_ox),)
+        comes_mate = to_core(comes)
         h_oo, h_ox = natural(mlp_pack[0, :shard])
         d_oo, d_ox = natural(mlp_pack[0, shard:])
         mlp_oo = jnp.concatenate([h_oo, d_oo], axis=1)
@@ -537,7 +521,9 @@
         first = seq // tile // 2
         return pl.BlockSpec((tile, width), lambda i: (jnp.maximum(i - first, 0), 0))
 
-    blocks = [whole((block, width))] * 4
+    tokens = tuple(far(v) for v in (stays, comes, stays_mate, comes_mate))
+    start_blocks = [pl.BlockSpec((block, width), lambda *_: (0, 0), pipeline_mode=pl.Buffered(1))] * 4
+    cot_blocks = [pl.BlockSpec((block, width), lambda *_: (1, 0), pipeline_mode=pl.Buffered(1))] * 4
     row = kept((1, width))
     vecs = kept((KINDS, width))
     square = whole((width, width))
@@ -548,17 +534,17 @@
         outs = [
             (sds((width, width), BF), kept((width, width))),
             (sds((KINDS, width), F32), vecs),
-            (sds((9, seq, HD), BF), pl.BlockSpec((9, tile, HD), lambda i: (0, i, 0))),
+            (pltpu.HBM((9, seq, HD), BF), pl.BlockSpec((9, tile, HD), lambda i: (0, i, 0))),
         ]
         if first:
             outs += [
-                (sds((seq, width), BF), by(tile)),
+                (pltpu.HBM((seq, width), BF), by(tile)),
                 (pltpu.HBM((width, seq), BF), pl.BlockSpec((width, tile), lambda i: (0, i))),
             ]
         return call(
             functools.partial(project_body, rows=rows, first=first),
             (seq // tile,),
-            [scalar()] + (blocks + [row] if first else [by(tile)]) + [whole(v.shape) for v in shards],
+            [scalar()] + (start_blocks + [row] if first else [by(tile)]) + [whole(v.shape) for v in shards],
             outs,
             scratch=[pltpu.VMEM((8, n_qkv), F32)],
             flops=2 * seq * width * n_qkv,
@@ -586,27 +572,26 @@
             flops=3 * 16 * seq * seq * HD,
             moved=8e6,
             trans=3 * seq * seq,
-        )(qkv, qkv, qkv)
+        )(*[far(qkv)] * 3)
 
     def attend_back(qkv, expon, inverse, mixed, grad_mixed):
         return call(
             attend_back_body,
             (3,),
             [q_spec, k_spec, v_spec, e_spec, inv_spec, t_spec, t_spec],
-            [(sds((3, seq, HD), BF), q_spec)] * 3,
+            [(pltpu.HBM((3, seq, HD), BF), q_spec)] * 3,
             flops=3 * 40 * seq * seq * HD,
             moved=9e6,
-        )(qkv, qkv, qkv, far(expon), inverse, far(mixed), grad_mixed)
-
-    w_o, vec, qkv_o, normed, normed_t = project(True, (*start, te), attn_oo, attn_ox)
+        )(*[far(qkv)] * 3, far(expon), inverse, far(mixed), grad_mixed)
+
+    w_o, vec, qkv_o, normed, normed_t = project(True, (*tokens, te), attn_oo, attn_ox)
+    qkv_o, attn_yx, mlp_oo = lax.optimization_barrier((qkv_o, attn_yx, mlp_oo))
+    mlp_yo = to_y(mlp_oo)
+    if fast:
+        mlp_ox = to_x(mlp_oo)
     exp_o, inv_o, mixed_o, wide_o = attend(qkv_o)
-    normed, exp_o, attn_yo, attn_yx, mlp_oo = lax.optimization_barrier(
-        (normed, exp_o, attn_yo, attn_yx, mlp_oo)
-    )
-    mlp_yo = to_y(mlp_oo)
-    if fast:
-        mlp_ox = to_x(mlp_oo)
-    w_y, vec_y, qkv_y = project(False, (normed,), attn_yo, attn_yx)
+    normed, exp_o = lax.optimization_barrier((normed, exp_o))
+    w_y, vec_y, qkv_y = project(False, (far(normed),), attn_yo, *attn_yx)
     exp_y, inv_y, mixed_y, wide_y = attend(qkv_y)
     mixed_y, mlp_ox, mlp_yo = lax.optimization_barrier((mixed_y, mlp_ox, mlp_yo))
     h_yx = to_y(mlp_ox[:, :rows])
@@ -634,7 +619,7 @@
     middle, normed_second, ff_part, gs_part, hb_o, gh_oo, gh_ox, gd_oo, gd_ox = call(
         functools.partial(mlp_first_body, rows=rows),
         (seq // tile,),
-        [scalar(), *blocks, row, by(tile), by_mate(tile), *blocks, vecs]
+        [scalar(), *start_blocks, row, by(tile), by_mate(tile), *cot_blocks, vecs]
         + [whole((ZS, 2 * rows, hidden))] * 2,
         [
             (sds((seq, width), F32), by(tile)),
@@ -645,14 +630,14 @@
         + grad_parts,
         scratch=mlp_scratch,
         **mlp_cost,
-    )(x_arr, *start, te, attended, attended_mate, *cot, vec, mlp_oo, mlp_ox)
+    )(x_arr, *tokens, te, attended, attended_mate, *tokens, vec, mlp_oo, mlp_ox)
     if fast:
         got_ho = to_x(gh_ox)
         normed_second, h_yx, d_yx = lax.optimization_barrier((normed_second, h_yx, d_yx))
     ff, ff_sent, gs, hb_y, gh_yo, gh_yx, gd_yo, gd_yx = call(
         functools.partial(mlp_second_body, rows=rows),
         (seq // tile,),
-        [scalar(), by(tile), *blocks, vecs, by(tile), by(tile)]
+        [scalar(), by(tile), *cot_blocks, vecs, by(tile), by(tile)]
         + [whole((ZS, 2 * rows, hidden)), whole(part), whole(part)],
         [
             (sds((seq // 2, width), BF), low_half(tile)),
@@ -662,7 +647,7 @@
         + grad_parts,
         scratch=mlp_scratch,
         **mlp_cost,
-    )(x_arr, normed_second, *cot, vec_y, ff_part, gs_part, mlp_yo, h_yx, d_yx)
+    )(x_arr, normed_second, *tokens, vec_y, ff_part, gs_part, mlp_yo, h_yx, d_yx)
     if fast:
         gs, got_ho = lax.optimization_barrier((gs, got_ho))
     gs_mate = to_core(gs)
@@ -673,22 +658,22 @@
     grad_middle, gx_o, gx_y, wo_o, wo_y, second_sums = call(
         second_back_body,
         (seq // tile,),
-        [by(tile), by(tile), by_mate(tile), *blocks, vecs, square, square, half_t, half_t],
+        [by(tile), by(tile), by_mate(tile), *cot_blocks, vecs, square, square, half_t, half_t],
         [
             (pltpu.HBM((seq, width), F32), by(tile)),
             (sds((3 * HD, seq), BF), half_t),
             (sds((3 * HD, seq), BF), half_t),
-            (sds((width, 3 * HD), BF), kept((width, 3 * HD))),
-            (sds((width, 3 * HD), BF), kept((width, 3 * HD))),
+            (pltpu.HBM((width, 3 * HD), BF), kept((width, 3 * HD))),
+            (pltpu.HBM((width, 3 * HD), BF), kept((width, 3 * HD))),
             (sds((KINDS, width), F32), vecs),
         ],
         scratch=[pltpu.VMEM((width, 6 * HD), BF), pltpu.VMEM((width, 6 * HD), F32)],
         flops=4 * seq * width * 384,
         moved=16e6,
-    )(middle, gs, gs_mate, *cot, vec, w_o, w_y, flat_o, flat_y)
+    )(middle, gs, gs_mate, *tokens, vec, w_o, w_y, flat_o, flat_y)
     if fast:
         got_h, got_d = to_x(gh_yx), to_y(gd_yx)
-        gx_y, got_h, got_d, gd_yo = lax.optimization_barrier((gx_y, got_h, got_d, gd_yo))
+        gx_y, got_h, got_d = lax.optimization_barrier((gx_y, got_h, got_d))
         got_hs, got_ds = to_y(gh_yo + got_h), to_x(gd_ox + got_d)
 
     def project_back(grads, weights, wo, prev):
@@ -702,20 +687,17 @@
             [scalar(), heads, heads, heads, pl.BlockSpec((width, tile), lambda i: (0, i)), square, whole((width, 3 * HD))]
             + ([by(tile)] if more else []),
             [
-                (sds(attn_part, BF), kept(attn_part)),
-                (sds(attn_part, BF), kept(attn_part)),
+                (pltpu.HBM(attn_part, BF), kept(attn_part)),
+                (pltpu.HBM(attn_part, BF), kept(attn_part)),
                 ((sds((seq, width), BF) if more else pltpu.HBM((seq, width), F32)), by(tile)),
                 (sds((1, n_qkv), F32), kept((1, n_qkv))),
             ],
             scratch=[pltpu.VMEM((width, n_qkv), F32)],
             flops=4 * seq * width * n_qkv,
             moved=10e6,
-        )(x_arr, *grads, far(normed_t), weights, wo, *((far(prev),) if more else ()))
+        )(x_arr, *(far(v) for v in grads), far(normed_t), weights, far(wo), *((far(prev),) if more else ()))
 
     grads_y = attend_back(qkv_y, exp_y, inv_y, wide_y, gx_y.reshape(3, HD, seq))
-    if fast:
-        *grads_y, gd_yo = lax.optimization_barrier((*grads_y, gd_yo))
-        got_do = to_y(gd_yo)
     ga_yo, ga_yx, first_part, qkv_sum_y = project_back(grads_y, w_y, wo_y, None)
     tile = TILE_OUT
     (out_tokens,) = call(
@@ -729,19 +711,17 @@
     gx_o, first_part, out_tokens = lax.optimization_barrier((gx_o, first_part, out_tokens))
     out_got = to_y(out_tokens[block:])
     if fast:
-        gx_o, ga_yx, got_hs = lax.optimization_barrier((gx_o, ga_yx, got_hs))
+        gx_o, ga_yx, got_hs, got_ds, gd_yo = lax.optimization_barrier((gx_o, ga_yx, got_hs, got_ds, gd_yo))
+        got_do = to_y(gd_yo)
         ga_d = to_x(ga_yx)
     grads_o = attend_back(qkv_o, exp_o, inv_o, wide_o, gx_o.reshape(3, HD, seq))
     if fast:
-        *grads_o, got_ds, got_do, ga_d, out_got = lax.optimization_barrier(
-            (*grads_o, got_ds, got_do, ga_d, out_got)
-        )
+        *grads_o, got_do, ga_d = lax.optimization_barrier((*grads_o, got_do, ga_d))
         mlp_all = spread_z(jnp.concatenate([gh_oo + got_ho + got_hs, gd_oo + got_do + got_ds], axis=1))
         ga_s = to_y(ga_yo + ga_d)
     ga_oo, ga_ox, first, qkv_sum_o = project_back(grads_o, w_o, wo_o, first_part)
     if fast:
         ga_x = to_x(ga_ox)
-        first, ga_s = lax.optimization_barrier((first, ga_s))
     first_mate = to_core(first)
 
     tile = TILE_FIRST
@@ -750,7 +730,7 @@
     input_grad, small_o, small_y, first_sums = call(
         functools.partial(first_back_body, rows=rows),
         (seq // tile,),
-        [scalar(), *blocks, row, vecs, by(tile), by_mate(tile), by(tile), vecs, hb_spec, hb_spec, qkv_spec, qkv_spec],
+        [scalar(), *start_blocks, row, vecs, by(tile), by_mate(tile), by(tile), vecs, hb_spec, hb_spec, qkv_spec, qkv_spec],
         [
             (sds((seq, width), BF), by(tile)),
             (sds(small_o_shape, F32), kept(small_o_shape)),
@@ -759,10 +739,10 @@
         ],
         flops=1e6,
         moved=12e6,
-    )(x_arr, *start, te, vec, first, first_mate, far(grad_middle), second_sums, hb_o, hb_y, qkv_sum_o, qkv_sum_y)
-
-    if fast:
-        small_o, small_y, input_grad, ga_x = lax.optimization_barrier((small_o, small_y, input_grad, ga_x))
+    )(x_arr, *tokens, te, vec, first, first_mate, far(grad_middle), second_sums, hb_o, hb_y, qkv_sum_o, qkv_sum_y)
+
+    if fast:
+        input_grad, ga_x, ga_s, mlp_all = lax.optimization_barrier((input_grad, ga_x, ga_s, mlp_all))
         ga_all = spread_z(ga_oo + ga_s + ga_x)
     small_got = to_y(small_y)
     small_sum = small_o + small_got[:, :, :KINDS]

time: 261 us -> 243 us (0.931)
  waiting for transfers between devices: 88.8 us -> 67.8 us
  Pallas kernels: 96.1 us -> 107 us
  local copies, waits for them, and re-layouts: 13.9 us -> 7.22 us
    ppermute x13 -> x12, waiting for transfers between devices: 24.3 us -> 14.9 us  [to_y(): return lax.ppermute(values, 'y', swap(2))]
    unnamed x95 -> x42, local copies, waits for them, and re-layouts: 11.1 us -> 4.41 us
    all_to_all x4, waiting for transfers between devices: 21.4 us -> 16.5 us  [spread_z(): return lax.all_to_all(values, 'a', 0, 0, tiled=True)]
    ppermute x9 -> x10, waiting for transfers between devices: 38.3 us -> 33.4 us  [to_x(): return lax.ppermute(values, 'b', swap(2))]
    ppermute x9 -> x10, starting transfers between devices: 10.6 us -> 9.38 us  [to_x(): return lax.ppermute(values, 'b', swap(2))]
    ppermute x13 -> x12, starting transfers between devices: 15 us -> 15.7 us  [to_y(): return lax.ppermute(values, 'y', swap(2))]
  transfers between devices with their start and end apart: 37 -> 35, of which waited for: 21 -> 18; matrix products, arithmetic and copies ran while one was open for 5% -> 4% of each run, Pallas kernels for 35% -> 38%
where the time goes in v4:
time: 243 us
  Pallas kernels  107 us (44%)
  waiting for transfers between devices  67.8 us (28%)
  starting transfers between devices  51.2 us (21%)
  other arithmetic  7.94 us (3%)
  local copies, waits for them, and re-layouts  7.22 us (3%)
    ppermute x10, waiting for transfers between devices, to_x(): return lax.ppermute(values, 'b', swap(2))  33.4 us
    all_to_all x4, starting transfers between devices, spread_z(): return lax.all_to_all(values, 'a', 0, 0, tiled=True)  19.6 us
    pallas_call x2, Pallas kernels, attend_back(): call(attend_back_body, (3,), [q_spec, k_spec, v_spec, e_spec, inv_spec, t...  18.4 us
    pallas_call x2, Pallas kernels, project_back(): call(functools.partial(project_back_body, rows=rows, more=more), (seq //...  17.5 us
    all_to_all x4, waiting for transfers between devices, spread_z(): return lax.all_to_all(values, 'a', 0, 0, tiled=True)  16.5 us
    pallas_call x2, Pallas kernels, attend(): call(attend_body, (3,), [q_spec, k_spec, v_spec], [(pltpu.HBM((3, seq, se...  16.2 us
    ppermute x12, starting transfers between devices, to_y(): return lax.ppermute(values, 'y', swap(2))  15.7 us
    ppermute x12, waiting for transfers between devices, to_y(): return lax.ppermute(values, 'y', swap(2))  14.9 us
  transfers between devices with their start and end apart: 35, of which 18 were waited for; matrix products, arithmetic and copies ran while one was open for 4% of the time, Pallas kernels for 38%

profile of v4, /device:TPU:0, one launch (start us, length us, event | category | flops | bytes accessed | tf_op | source)
XLA Modules:
  0.0 242.5 jit_solution(3309001886935466506)
XLA Ops:
  0.7 1.8 copy.36.d_ref
  2.5 2.6 %shard_map.313 = (bf16[4,104,768]{2,1,0:T(8,128)(2,1)}, bf16[4,192,768]{2,1,0:T(8,128)(2,1)}) custom-call(bf16[96,192]{1,0:T(8,128)(2,1)} %q_ref.1, bf16[96,192]{1,0:T(8,128)(2,1)} %k_ref.1, bf16[96,192]{1,0:T(8,128)(2,1)} %v_ref.1, bf16[192,96]{1,0:T(8,128)(2,1)} %o_ref.1, bf16[96,768]{1,0:T(8,128)(2,1)} %h_ref.1, bf16[768,96]{1,0:T(8,128)(2,1)} %copy.36.d_ref, ...), custom_call_target="tpu_custom_call" | custom-call | flops 1000000 | bytes 2000000 | tf_op jit(solution)/shard_map/pallas_call | solution.py:450
  5.1 6.4 %all-to-all-start = ((bf16[4,104,768]{2,1,0:T(8,128)(2,1)}), bf16[4,104,768]{2,1,0:T(8,128)(2,1)S(1)}, u32[]{:S(2)}, u32[]{:S(2)}) async-start(bf16[4,104,768]{2,1,0:T(8,128)(2,1)} %get-tuple-element.135), calls=%async_computation | async-start | bytes 1277952 | tf_op jit(solution)/shard_map/all_to_all | solution.py:416
  11.9 1.6 collective-permute-start
  13.5 15.0 %all-to-all-done.refs_5_ = bf16[4,104,768]{2,1,0:T(8,128)(2,1)S(1)} async-done(((bf16[4,104,768]{2,1,0:T(8,128)(2,1)}), bf16[4,104,768]{2,1,0:T(8,128)(2,1)S(1)}, u32[]{:S(2)}, u32[]{:S(2)}) %all-to-all-start) | async-done | bytes 639008 | tf_op jit(solution)/shard_map/all_to_all | solution.py:416
  28.5 4.3 %all-to-all-start.1 = ((bf16[4,192,768]{2,1,0:T(8,128)(2,1)}), bf16[4,192,768]{2,1,0:T(8,128)(2,1)}, u32[]{:S(2)}, u32[]{:S(2)}) async-start(bf16[4,192,768]{2,1,0:T(8,128)(2,1)} %get-tuple-element.142), calls=%async_computation.1 | async-start | bytes 2359296 | tf_op jit(solution)/shard_map/all_to_all | solution.py:416
  32.8 0.9 copy-done.11
  33.6 1.5 collective-permute-start.3
  35.1 1.5 collective-permute-start.4
  36.7 12.3 %collective-permute-done.3.refs_6_ = bf16[4,104,768]{2,1,0:T(8,128)(2,1)S(1)} collective-permute-done((bf16[4,104,768]{2,1,0:T(8,128)(2,1)S(1)}, bf16[4,104,768]{2,1,0:T(8,128)(2,1)S(1)}, u32[]{:S(2)}, u32[]{:S(2)}) %collective-permute-start.3) | collective-permute-done | bytes 639008 | tf_op jit(solution)/shard_map/ppermute | solution.py:408
  49.0 1.2 collective-permute-done.4.refs_1_
  50.2 0.8 slice.46
  51.5 0.7 slice.45
  52.2 1.5 collective-permute-start.5
  53.8 6.0 %shard_map.314 = (bf16[768,768]{1,0:T(8,128)(2,1)S(1)}, f32[8,768]{1,0:T(8,128)S(1)}, bf16[9,1024,64]{2,1,0:T(8,128)(2,1)}, bf16[1024,768]{1,0:T(8,128)(2,1)}, bf16[768,1024]{1,0:T(8,128)(2,1)}) custom-call(s32[1]{0:T(128)} %bitcast.x_ref, bf16[512,768]{1,0:T(8,128)(2,1)} %copy-done.10, bf16[512,768]{1,0:T(8,128)(2,1)} %collective-permute-done.refs_1_.s1.c1, ...), custom_call_target="tpu_custom_call" | custom-call | flops 905969664 | bytes 8000000 | tf_op jit(solution)/shard_map/pallas_call | solution.py:544
  59.8 1.1 all-to-all-done.1.w_oo
  60.9 1.5 collective-permute-start.7
  62.3 1.5 collective-permute-start.8
  63.9 8.1 %shard_map.315 = (bf16[3,1024,1024]{2,1,0:T(8,128)(2,1)}, f32[3,1,1024]{2,1,0:T(1,128)S(1)}, bf16[3,64,1024]{2,1,0:T(8,128)(2,1)S(1)}, f32[3,64,1024]{2,1,0:T(8,128)}) custom-call(bf16[9,1024,64]{2,1,0:T(8,128)(2,1)} %get-tuple-element.143.q_ref.k_ref.v_ref, bf16[9,1024,64]{2,1,0:T(8,128)(2,1)} %get-tuple-element.143.q_ref.k_ref.v_ref, ...), custom_call_target="tpu_custom_call" | custom-call | flops 3221225472 | bytes 8000000 | tf_op jit(solution)/shard_map/pallas_call | solution.py:562
  71.9 4.9 %shard_map.316 = (bf16[768,768]{1,0:T(8,128)(2,1)S(1)}, f32[8,768]{1,0:T(8,128)S(1)}, bf16[9,1024,64]{2,1,0:T(8,128)(2,1)}) custom-call(s32[1]{0:T(128)} %bitcast.x_ref, bf16[1024,768]{1,0:T(8,128)(2,1)} %get-tuple-element.147.refs_0_, bf16[4,104,768]{2,1,0:T(8,128)(2,1)S(1)} %collective-permute-done.4.refs_1_, ...), custom_call_target="tpu_custom_call" | custom-call | flops 905969664 | bytes 8000000 | tf_op jit(solution)/shard_map/pallas_call | solution.py:544
  76.8 8.1 %shard_map.317 = (bf16[3,1024,1024]{2,1,0:T(8,128)(2,1)}, f32[3,1,1024]{2,1,0:T(1,128)S(1)}, bf16[3,64,1024]{2,1,0:T(8,128)(2,1)S(1)}, f32[3,64,1024]{2,1,0:T(8,128)}) custom-call(bf16[9,1024,64]{2,1,0:T(8,128)(2,1)} %get-tuple-element.150.q_ref.k_ref.v_ref, bf16[9,1024,64]{2,1,0:T(8,128)(2,1)} %get-tuple-element.150.q_ref.k_ref.v_ref, ...), custom_call_target="tpu_custom_call" | custom-call | flops 3221225472 | bytes 8000000 | tf_op jit(solution)/shard_map/pallas_call | solution.py:562
  84.9 3.1 %collective-permute-done.7.w_ox = bf16[4,192,768]{2,1,0:T(8,128)(2,1)S(1)} collective-permute-done((bf16[4,192,768]{2,1,0:T(8,128)(2,1)}, bf16[4,192,768]{2,1,0:T(8,128)(2,1)S(1)}, u32[]{:S(2)}, u32[]{:S(2)}) %collective-permute-start.7) | collective-permute-done | bytes 1179680 | tf_op jit(solution)/shard_map/ppermute | solution.py:408
  88.0 1.2 collective-permute-done.8.w_yo
  89.2 2.0 shard_map.318.a0_ref
  91.3 1.6 collective-permute-start.10
  92.9 0.6 collective-permute-start.11
  93.5 1.1 collective-permute-done.9.a1_ref
  94.6 13.4 %shard_map.319 = (f32[1024,768]{1,0:T(8,128)S(1)}, bf16[1024,768]{1,0:T(8,128)(2,1)S(1)}, f32[1024,768]{1,0:T(8,128)S(1)}, f32[1024,768]{1,0:T(8,128)S(1)}, f32[...) custom-call(s32[1]{0:T(128)} %bitcast.x_ref, ...), custom_call_target="tpu_custom_call" | custom-call | flops 7247757312 | bytes 16000000 | tf_op jit(solution)/shard_map/pallas_call | solution.py:619
  109.0 11.1 %shard_map.320 = (bf16[512,768]{1,0:T(8,128)(2,1)S(1)}, bf16[512,768]{1,0:T(8,128)(2,1)S(1)}, bf16[1024,768]{1,0:T(8,128)(2,1)S(1)}, f32[1,768]{1,0:T(1,128)S(1)...) custom-call(s32[1]{0:T(128)} %bitcast.x_ref, ...), custom_call_target="tpu_custom_call" | custom-call | flops 7247757312 | bytes 16000000 | tf_op jit(solution)/shard_map/pallas_call | solution.py:637
  120.1 3.4 %collective-permute-done.12 = bf16[4,96,768]{2,1,0:T(8,128)(2,1)S(1)} collective-permute-done((bf16[4,96,768]{2,1,0:T(8,128)(2,1)S(1)}, bf16[4,96,768]{2,1,0:T(8,128)(2,1)S(1)}, u32[]{:S(2)}, u32[]{:S(2)}) %collective-permute-start.12) | collective-permute-done | bytes 589856 | tf_op jit(solution)/shard_map/ppermute | solution.py:408
  124.5 1.5 collective-permute-start.15
  126.0 2.0 collective-permute-done.16.f1_ref
  128.3 8.2 %shard_map.321 = (f32[1024,768]{1,0:T(8,128)}, bf16[192,1024]{1,0:T(8,128)(2,1)S(1)}, bf16[192,1024]{1,0:T(8,128)(2,1)S(1)}, bf16[768,192]{1,0:T(8,128)(2,1)}, b...) custom-call(f32[1024,768]{1,0:T(8,128)S(1)} %get-tuple-element.158.mid_ref, ...), custom_call_target="tpu_custom_call" | custom-call | flops 1207959552 | bytes 16000000 | tf_op jit(solution)/shard_map/pallas_call | solution.py:658
  136.6 2.6 %collective-permute-done.14 = bf16[4,96,768]{2,1,0:T(8,128)(2,1)S(1)} collective-permute-done((bf16[4,96,768]{2,1,0:T(8,128)(2,1)S(1)}, bf16[4,96,768]{2,1,0:T(8,128)(2,1)S(1)}, u32[]{:S(2)}, u32[]{:S(2)}) %collective-permute-start.14) | collective-permute-done | bytes 589856 | tf_op jit(solution)/shard_map/ppermute | solution.py:408
  139.6 1.5 collective-permute-start.19
  141.3 1.6 collective-permute-start.18
  142.9 9.2 %shard_map.322 = (bf16[3,1024,64]{2,1,0:T(8,128)(2,1)}, bf16[3,1024,64]{2,1,0:T(8,128)(2,1)}, bf16[3,1024,64]{2,1,0:T(8,128)(2,1)}) custom-call(bf16[9,1024,64]{2,1,0:T(8,128)(2,1)} %get-tuple-element.150.q_ref.k_ref.v_ref, bf16[9,1024,64]{2,1,0:T(8,128)(2,1)} %get-tuple-element.150.q_ref.k_ref.v_ref, ...), custom_call_target="tpu_custom_call" | custom-call | flops 8053063680 | bytes 9000000 | tf_op jit(solution)/shard_map/pallas_call | solution.py:578
  152.1 8.7 %shard_map.323 = (bf16[4,96,768]{2,1,0:T(8,128)(2,1)}, bf16[4,96,768]{2,1,0:T(8,128)(2,1)}, f32[1024,768]{1,0:T(8,128)}, f32[1,576]{1,0:T(1,128)S(1)}) custom-call(s32[1]{0:T(128)} %bitcast.x_ref, bf16[3,1024,64]{2,1,0:T(8,128)(2,1)} %get-tuple-element.178.q_ref, bf16[3,1024,64]{2,1,0:T(8,128)(2,1)} %get-tuple-element.179.k_ref, ...), custom_call_target="tpu_custom_call" | custom-call | flops 1811939328 | bytes 10000000 | tf_op jit(solution)/shard_map/pallas_call | solution.py:684
  162.0 9.2 %shard_map.325 = (bf16[3,1024,64]{2,1,0:T(8,128)(2,1)}, bf16[3,1024,64]{2,1,0:T(8,128)(2,1)}, bf16[3,1024,64]{2,1,0:T(8,128)(2,1)}) custom-call(bf16[9,1024,64]{2,1,0:T(8,128)(2,1)} %get-tuple-element.143.q_ref.k_ref.v_ref, bf16[9,1024,64]{2,1,0:T(8,128)(2,1)} %get-tuple-element.143.q_ref.k_ref.v_ref, ...), custom_call_target="tpu_custom_call" | custom-call | flops 8053063680 | bytes 9000000 | tf_op jit(solution)/shard_map/pallas_call | solution.py:578
  171.2 3.2 %collective-permute-done.20 = bf16[4,96,768]{2,1,0:T(8,128)(2,1)S(1)} collective-permute-done((bf16[4,96,768]{2,1,0:T(8,128)(2,1)S(1)}, bf16[4,96,768]{2,1,0:T(8,128)(2,1)S(1)}, u32[]{:S(2)}, u32[]{:S(2)}) %collective-permute-start.20) | collective-permute-done | bytes 589856 | tf_op jit(solution)/shard_map/ppermute | solution.py:404
  174.9 0.8 copy-done.15
  175.7 8.8 %shard_map.326 = (bf16[4,96,768]{2,1,0:T(8,128)(2,1)}, bf16[4,96,768]{2,1,0:T(8,128)(2,1)}, bf16[1024,768]{1,0:T(8,128)(2,1)S(1)}, f32[1,576]{1,0:T(1,128)S(1)}) custom-call(s32[1]{0:T(128)} %bitcast.x_ref, bf16[3,1024,64]{2,1,0:T(8,128)(2,1)} %get-tuple-element.203.q_ref, bf16[3,1024,64]{2,1,0:T(8,128)(2,1)} %get-tuple-element.204.k_ref, ...), custom_call_target="tpu_custom_call" | custom-call | flops 1811939328 | bytes 10000000 | tf_op jit(solution)/shard_map/pallas_call | solution.py:684
  185.0 1.1 pad_maximum_fusion
  186.1 4.4 %all-to-all-start.2 = ((bf16[4,192,768]{2,1,0:T(8,128)(2,1)}), bf16[4,192,768]{2,1,0:T(8,128)(2,1)}, u32[]{:S(2)}, u32[]{:S(2)}) async-start(bf16[4,192,768]{2,1,0:T(8,128)(2,1)} %pad_maximum_fusion), calls=%async_computation.2 | async-start | bytes 2359296 | tf_op jit(solution)/shard_map/all_to_all | solution.py:416
  190.6 1.6 collective-permute-start.17
  192.2 5.7 %shard_map.327 = (bf16[1024,768]{1,0:T(8,128)(2,1)S(1)}, f32[2,4,8,96]{3,2,1,0:T(8,128)S(1)}, f32[2,4,16,96]{3,2,1,0:T(8,128)S(1)}, f32[8,768]{1,0:T(8,128)S(1)}) custom-call(s32[1]{0:T(128)} %bitcast.x_ref, bf16[512,768]{1,0:T(8,128)(2,1)} %copy-done.10, bf16[512,768]{1,0:T(8,128)(2,1)} %collective-permute-done.refs_1_.s1.c1, bf16[512,768]{1,0:T(8,128)(2,1)} %copy-done.11, ...), custom_call_target="tpu_custom_call" | custom-call | flops 1000000 | bytes 12000000 | tf_op jit(solution)/shard_map/pallas_call | solution.py:730
  198.5 4.0 %collective-permute-done.17 = bf16[256,768]{1,0:T(8,128)(2,1)S(1)} collective-permute-done((bf16[256,768]{1,0:T(8,128)(2,1)S(1)}, bf16[256,768]{1,0:T(8,128)(2,1)S(1)}, u32[]{:S(2)}, u32[]{:S(2)}) %collective-permute-start.17) | collective-permute-done | bytes 393248 | tf_op jit(solution)/shard_map/ppermute | solution.py:404
  202.5 1.0 maximum_select_fusion
  203.7 1.6 collective-permute-start.24
  205.3 0.6 collective-permute-start.23
  205.9 1.5 collective-permute-start.27
  207.5 0.6 maximum_select_fusion.2
  208.2 11.2 %collective-permute-done.27 = f32[4,8,96]{2,1,0:T(8,128)S(1)} collective-permute-done((f32[4,8,96]{2,1,0:T(8,128)S(1)}, f32[4,8,96]{2,1,0:T(8,128)S(1)}, u32[]{:S(2)}, u32[]{:S(2)}) %collective-permute-start.27) | collective-permute-done | bytes 12320 | tf_op jit(solution)/shard_map/ppermute | solution.py:408
  220.2 2.1 add_add_fusion
  222.2 4.4 %all-to-all-start.3 = ((bf16[4,96,768]{2,1,0:T(8,128)(2,1)}), bf16[4,96,768]{2,1,0:T(8,128)(2,1)S(1)}, u32[]{:S(2)}, u32[]{:S(2)}) async-start(bf16[4,96,768]{2,1,0:T(8,128)(2,1)} %add_add_fusion), calls=%async_computation.3 | async-start | bytes 1179648 | tf_op jit(solution)/shard_map/all_to_all | solution.py:416
  226.7 2.0 collective-permute-start.28
  228.7 2.4 collective-permute-start.29
  231.1 1.5 collective-permute-start.30
  232.6 0.6 collective-permute-start.25
  233.2 1.5 convert_reduce_fusion
  234.7 0.8 slice_bitcast_fusion.2
  235.5 4.9 %collective-permute-done.25 = bf16[256,768]{1,0:T(8,128)(2,1)S(1)} collective-permute-done((bf16[256,768]{1,0:T(8,128)(2,1)S(1)}, bf16[256,768]{1,0:T(8,128)(2,1)S(1)}, u32[]{:S(2)}, u32[]{:S(2)}) %collective-permute-start.25) | collective-permute-done | bytes 393248 | tf_op jit(solution)/shard_map/ppermute | solution.py:404
  240.4 1.0 maximum_select_fusion.1
  241.5 0.9 shard_map.328
  (94 shorter events, 7.9 us)
Async XLA Ops:
  0.7 53.1 %copy-start = (bf16[2,768]{1,0:T(2,128)(2,1)S(1)}, bf16[2,768]{1,0:T(2,128)(2,1)}, u32[]{:S(2)}) copy-start(bf16[2,768]{1,0:T(2,128)(2,1)} %param.19) | copy-start | bytes 9220
  0.7 10.9 %copy-start.12 = (bf16[2,256,768]{2,1,0:T(8,128)(2,1)S(1)}, bf16[2,256,768]{2,1,0:T(8,128)(2,1)}, u32[]{:S(2)}) copy-start(bf16[2,256,768]{2,1,0:T(8,128)(2,1)} %param.18) | copy-start | bytes 2359300
  5.1 6.5 %copy-start.13 = (bf16[2,256,768]{2,1,0:T(8,128)(2,1)S(1)}, bf16[2,256,768]{2,1,0:T(8,128)(2,1)}, u32[]{:S(2)}) copy-start(bf16[2,256,768]{2,1,0:T(8,128)(2,1)} %param.35) | copy-start | bytes 2359300
  5.1 23.4 %all-to-all-start = ((bf16[4,104,768]{2,1,0:T(8,128)(2,1)}), bf16[4,104,768]{2,1,0:T(8,128)(2,1)S(1)}, u32[]{:S(2)}, u32[]{:S(2)}) async-start(bf16[4,104,768]{2,1,0:T(8,128)(2,1)} %get-tuple-element.135), calls=%async_computation | async-start | bytes 1277952 | tf_op jit(solution)/shard_map/all_to_all | solution.py:416
  11.8 40.5 %copy-start.10 = (bf16[512,768]{1,0:T(8,128)(2,1)}, bf16[512,768]{1,0:T(8,128)(2,1)S(1)}, u32[]{:S(2)}) copy-start(bf16[512,768]{1,0:T(8,128)(2,1)S(1)} %get-tuple-element.249.refs_0_.s0.c0) | copy-start | bytes 2359300
  11.8 21.0 %collective-permute-start.1 = (bf16[512,768]{1,0:T(8,128)(2,1)S(1)}, bf16[512,768]{1,0:T(8,128)(2,1)S(1)}, u32[]{:S(2)}, u32[]{:S(2)}) collective-permute-start(bf16[512,768]{1,0:T(8,128)(2,1)S(1)} %get-tuple-element.249.refs_0_.s0.c0), channel_id=1, source_target_pairs={{0,1},{1,0},{2,3},{3,2},{4,5},{5,4},{6,7},{7,6},{8,9},{9,8},{10,11... | collective-permute-start | bytes 2359304 | tf_op jit(solution)/shard_map/ppermute | solution.py:412
  11.9 21.8 %collective-permute-start = (bf16[512,768]{1,0:T(8,128)(2,1)S(1)}, bf16[512,768]{1,0:T(8,128)(2,1)}, u32[]{:S(2)}, u32[]{:S(2)}) collective-permute-start(bf16[512,768]{1,0:T(8,128)(2,1)S(1)} %get-tuple-element.248), channel_id=1, source_target_pairs={{0,2},{2,0},{1,3},{3,1},{4,6},{6,4},{5,7},{7,5},{8,10},{10,8},{9,1... | collective-permute-start | bytes 2359304 | tf_op jit(solution)/shard_map/ppermute | solution.py:404
  28.5 32.4 %all-to-all-start.1 = ((bf16[4,192,768]{2,1,0:T(8,128)(2,1)}), bf16[4,192,768]{2,1,0:T(8,128)(2,1)}, u32[]{:S(2)}, u32[]{:S(2)}) async-start(bf16[4,192,768]{2,1,0:T(8,128)(2,1)} %get-tuple-element.142), calls=%async_computation.1 | async-start | bytes 2359296 | tf_op jit(solution)/shard_map/all_to_all | solution.py:416
  32.8 0.9 copy-start.11
  33.6 15.3 %collective-permute-start.3 = (bf16[4,104,768]{2,1,0:T(8,128)(2,1)S(1)}, bf16[4,104,768]{2,1,0:T(8,128)(2,1)S(1)}, u32[]{:S(2)}, u32[]{:S(2)}) collective-permute-start(bf16[4,104,768]{2,1,0:T(8,128)(2,1)S(1)} %all-to-all-done.refs_5_), channel_id=1, source_target_pairs={{0,4},{4,0},{1,5},{5,1},{2,6},{6,2},{3,7},{7,3},{8,12},{12,8},{9,1... | collective-permute-start | bytes 1916936 | tf_op jit(solution)/shard_map/ppermute | solution.py:408
  35.1 15.1 %collective-permute-start.4 = (bf16[4,104,768]{2,1,0:T(8,128)(2,1)S(1)}, bf16[4,104,768]{2,1,0:T(8,128)(2,1)S(1)}, u32[]{:S(2)}, u32[]{:S(2)}) collective-permute-start(bf16[4,104,768]{2,1,0:T(8,128)(2,1)S(1)} %all-to-all-done.refs_5_), channel_id=1, source_target_pairs={{0,2},{2,0},{1,3},{3,1},{4,6},{6,4},{5,7},{7,5},{8,10},{10,8},{9,1... | collective-permute-start | bytes 1916936 | tf_op jit(solution)/shard_map/ppermute | solution.py:404
  36.7 17.1 %collective-permute-start.2 = (bf16[512,768]{1,0:T(8,128)(2,1)}, bf16[512,768]{1,0:T(8,128)(2,1)}, u32[]{:S(2)}, u32[]{:S(2)}) collective-permute-start(bf16[512,768]{1,0:T(8,128)(2,1)} %collective-permute-done.refs_1_.s1.c1), channel_id=1, source_target_pairs={{0,1},{1,0},{2,3},{3,2},{4,5},{5,4},{6,7},{7,6},{8,9},{9,8},{10,11... | collective-permute-start | bytes 2359304 | tf_op jit(solution)/shard_map/ppermute | solution.py:412
  51.0 9.9 %collective-permute-start.6 = (bf16[4,56,768]{2,1,0:T(8,128)(2,1)}, bf16[4,56,768]{2,1,0:T(8,128)(2,1)S(1)}, u32[]{:S(2)}, u32[]{:S(2)}) collective-permute-start(bf16[4,56,768]{2,1,0:T(8,128)(2,1)} %slice.46), channel_id=1, source_target_pairs={{0,4},{4,0},{1,5},{5,1},{2,6},{6,2},{3,7},{7,3},{8,12},{12,8},{9,1... | collective-permute-start | bytes 1032200 | tf_op jit(solution)/shard_map/ppermute | solution.py:408
  52.2 8.6 %collective-permute-start.5 = (bf16[4,48,768]{2,1,0:T(8,128)(2,1)}, bf16[4,48,768]{2,1,0:T(8,128)(2,1)}, u32[]{:S(2)}, u32[]{:S(2)}) collective-permute-start(bf16[4,48,768]{2,1,0:T(8,128)(2,1)} %slice.45), channel_id=1, source_target_pairs={{0,2},{2,0},{1,3},{3,1},{4,6},{6,4},{5,7},{7,5},{8,10},{10,8},{9,1... | collective-permute-start | bytes 884744 | tf_op jit(solution)/shard_map/ppermute | solution.py:404
  59.8 68.5 %copy-start.4 = (f32[8,768]{1,0:T(8,128)}, f32[8,768]{1,0:T(8,128)S(1)}, u32[]{:S(2)}) copy-start(f32[8,768]{1,0:T(8,128)S(1)} %get-tuple-element.156.vec_ref) | copy-start | bytes 73732
  60.9 27.1 %collective-permute-start.7 = (bf16[4,192,768]{2,1,0:T(8,128)(2,1)}, bf16[4,192,768]{2,1,0:T(8,128)(2,1)S(1)}, u32[]{:S(2)}, u32[]{:S(2)}) collective-permute-start(bf16[4,192,768]{2,1,0:T(8,128)(2,1)} %all-to-all-done.1.w_oo), channel_id=1, source_target_pairs={{0,4},{4,0},{1,5},{5,1},{2,6},{6,2},{3,7},{7,3},{8,12},{12,8},{9,1... | collective-permute-start | bytes 3538952 | tf_op jit(solution)/shard_map/ppermute | solution.py:408
  62.3 26.8 %collective-permute-start.8 = (bf16[4,192,768]{2,1,0:T(8,128)(2,1)}, bf16[4,192,768]{2,1,0:T(8,128)(2,1)S(1)}, u32[]{:S(2)}, u32[]{:S(2)}) collective-permute-start(bf16[4,192,768]{2,1,0:T(8,128)(2,1)} %all-to-all-done.1.w_oo), channel_id=1, source_target_pairs={{0,2},{2,0},{1,3},{3,1},{4,6},{6,4},{5,7},{7,5},{8,10},{10,8},{9,1... | collective-permute-start | bytes 3538952 | tf_op jit(solution)/shard_map/ppermute | solution.py:404
  91.2 3.5 %collective-permute-start.9 = (bf16[1024,768]{1,0:T(8,128)(2,1)S(1)}, bf16[1024,768]{1,0:T(8,128)(2,1)S(1)}, u32[]{:S(2)}, u32[]{:S(2)}) collective-permute-start(bf16[1024,768]{1,0:T(8,128)(2,1)S(1)} %shard_map.318.a0_ref), channel_id=1, source_target_pairs={{0,1},{1,0},{2,3},{3,2},{4,5},{5,4},{6,7},{7,6},{8,9},{9,8},{10,11... | collective-permute-start | bytes 4718600 | tf_op jit(solution)/shard_map/ppermute | solution.py:412
  91.3 16.7 %collective-permute-start.10 = (bf16[4,96,768]{2,1,0:T(8,128)(2,1)S(1)}, bf16[4,96,768]{2,1,0:T(8,128)(2,1)S(1)}, u32[]{:S(2)}, u32[]{:S(2)}) collective-permute-start(bf16[4,96,768]{2,1,0:T(8,128)(2,1)S(1)} %slice.47), channel_id=1, source_target_pairs={{0,2},{2,0},{1,3},{3,1},{4,6},{6,4},{5,7},{7,5},{8,10},{10,8},{9,1... | collective-permute-start | bytes 1769480 | tf_op jit(solution)/shard_map/ppermute | solution.py:404
  92.9 15.5 %collective-permute-start.11 = (bf16[4,96,768]{2,1,0:T(8,128)(2,1)S(1)}, bf16[4,96,768]{2,1,0:T(8,128)(2,1)S(1)}, u32[]{:S(2)}, u32[]{:S(2)}) collective-permute-start(bf16[4,96,768]{2,1,0:T(8,128)(2,1)S(1)} %slice.48), channel_id=1, source_target_pairs={{0,4},{4,0},{1,5},{5,1},{2,6},{6,2},{3,7},{7,3},{8,12},{12,8},{9,1... | collective-permute-start | bytes 1769480 | tf_op jit(solution)/shard_map/ppermute | solution.py:408
  108.4 15.0 %collective-permute-start.12 = (bf16[4,96,768]{2,1,0:T(8,128)(2,1)S(1)}, bf16[4,96,768]{2,1,0:T(8,128)(2,1)S(1)}, u32[]{:S(2)}, u32[]{:S(2)}) collective-permute-start(bf16[4,96,768]{2,1,0:T(8,128)(2,1)S(1)} %get-tuple-element.168), channel_id=1, source_target_pairs={{0,4},{4,0},{1,5},{5,1},{2,6},{6,2},{3,7},{7,3},{8,12},{12,8},{9,1... | collective-permute-start | bytes 1769480 | tf_op jit(solution)/shard_map/ppermute | solution.py:408
  123.4 4.9 %collective-permute-start.13 = (bf16[1024,768]{1,0:T(8,128)(2,1)S(1)}, bf16[1024,768]{1,0:T(8,128)(2,1)S(1)}, u32[]{:S(2)}, u32[]{:S(2)}) collective-permute-start(bf16[1024,768]{1,0:T(8,128)(2,1)S(1)} %get-tuple-element.169.g0_ref), channel_id=1, source_target_pairs={{0,1},{1,0},{2,3},{3,2},{4,5},{5,4},{6,7},{7,6},{8,9},{9,8},{10,11... | collective-permute-start | bytes 4718600 | tf_op jit(solution)/shard_map/ppermute | solution.py:412
  123.4 4.5 %collective-permute-start.16 = (bf16[512,768]{1,0:T(8,128)(2,1)S(1)}, bf16[512,768]{1,0:T(8,128)(2,1)S(1)}, u32[]{:S(2)}, u32[]{:S(2)}) collective-permute-start(bf16[512,768]{1,0:T(8,128)(2,1)S(1)} %get-tuple-element.185), channel_id=1, source_target_pairs={{0,1},{1,0},{2,3},{3,2},{4,5},{5,4},{6,7},{7,6},{8,9},{9,8},{10,11... | collective-permute-start | bytes 2359304 | tf_op jit(solution)/shard_map/ppermute | solution.py:412
  124.0 15.2 %collective-permute-start.14 = (bf16[4,96,768]{2,1,0:T(8,128)(2,1)S(1)}, bf16[4,96,768]{2,1,0:T(8,128)(2,1)S(1)}, u32[]{:S(2)}, u32[]{:S(2)}) collective-permute-start(bf16[4,96,768]{2,1,0:T(8,128)(2,1)S(1)} %get-tuple-element.175), channel_id=1, source_target_pairs={{0,4},{4,0},{1,5},{5,1},{2,6},{6,2},{3,7},{7,3},{8,12},{12,8},{9,1... | collective-permute-start | bytes 1769480 | tf_op jit(solution)/shard_map/ppermute | solution.py:408
  124.5 15.0 %collective-permute-start.15 = (bf16[4,96,768]{2,1,0:T(8,128)(2,1)S(1)}, bf16[4,96,768]{2,1,0:T(8,128)(2,1)S(1)}, u32[]{:S(2)}, u32[]{:S(2)}) collective-permute-start(bf16[4,96,768]{2,1,0:T(8,128)(2,1)S(1)} %get-tuple-element.176), channel_id=1, source_target_pairs={{0,2},{2,0},{1,3},{3,1},{4,6},{6,4},{5,7},{7,5},{8,10},{10,8},{9,1... | collective-permute-start | bytes 1769480 | tf_op jit(solution)/shard_map/ppermute | solution.py:404
  136.6 4.7 %copy-start.6 = (f32[8,768]{1,0:T(8,128)}, f32[8,768]{1,0:T(8,128)S(1)}, u32[]{:S(2)}) copy-start(f32[8,768]{1,0:T(8,128)S(1)} %get-tuple-element.210.second_ref) | copy-start | bytes 73732
  139.6 21.2 %collective-permute-start.19 = (bf16[4,96,768]{2,1,0:T(8,128)(2,1)S(1)}, bf16[4,96,768]{2,1,0:T(8,128)(2,1)S(1)}, u32[]{:S(2)}, u32[]{:S(2)}) collective-permute-start(bf16[4,96,768]{2,1,0:T(8,128)(2,1)S(1)} %add.81), channel_id=1, source_target_pairs={{0,4},{4,0},{1,5},{5,1},{2,6},{6,2},{3,7},{7,3},{8,12},{12,8},{9,1... | collective-permute-start | bytes 1769480 | tf_op jit(solution)/shard_map/ppermute | solution.py:408
  141.3 19.6 %collective-permute-start.18 = (bf16[4,96,768]{2,1,0:T(8,128)(2,1)S(1)}, bf16[4,96,768]{2,1,0:T(8,128)(2,1)S(1)}, u32[]{:S(2)}, u32[]{:S(2)}) collective-permute-start(bf16[4,96,768]{2,1,0:T(8,128)(2,1)S(1)} %add.80), channel_id=1, source_target_pairs={{0,2},{2,0},{1,3},{3,1},{4,6},{6,4},{5,7},{7,5},{8,10},{10,8},{9,1... | collective-permute-start | bytes 1769480 | tf_op jit(solution)/shard_map/ppermute | solution.py:404
  160.9 13.6 %collective-permute-start.20 = (bf16[4,96,768]{2,1,0:T(8,128)(2,1)S(1)}, bf16[4,96,768]{2,1,0:T(8,128)(2,1)S(1)}, u32[]{:S(2)}, u32[]{:S(2)}) collective-permute-start(bf16[4,96,768]{2,1,0:T(8,128)(2,1)S(1)} %get-tuple-element.201), channel_id=1, source_target_pairs={{0,2},{2,0},{1,3},{3,1},{4,6},{6,4},{5,7},{7,5},{8,10},{10,8},{9,1... | collective-permute-start | bytes 1769480 | tf_op jit(solution)/shard_map/ppermute | solution.py:404
  161.4 13.4 %collective-permute-start.21 = (bf16[4,96,768]{2,1,0:T(8,128)(2,1)}, bf16[4,96,768]{2,1,0:T(8,128)(2,1)S(1)}, u32[]{:S(2)}, u32[]{:S(2)}) collective-permute-start(bf16[4,96,768]{2,1,0:T(8,128)(2,1)} %get-tuple-element.202), channel_id=1, source_target_pairs={{0,4},{4,0},{1,5},{5,1},{2,6},{6,2},{3,7},{7,3},{8,12},{12,8},{9,1... | collective-permute-start | bytes 1769480 | tf_op jit(solution)/shard_map/ppermute | solution.py:408
  174.9 0.8 copy-start.15
  184.4 0.6 copy-start.8
  184.4 7.8 %collective-permute-start.22 = (bf16[1024,768]{1,0:T(8,128)(2,1)S(1)}, bf16[1024,768]{1,0:T(8,128)(2,1)}, u32[]{:S(2)}, u32[]{:S(2)}) collective-permute-start(bf16[1024,768]{1,0:T(8,128)(2,1)S(1)} %get-tuple-element.208.g0_ref), channel_id=1, source_target_pairs={{0,1},{1,0},{2,3},{3,2},{4,5},{5,4},{6,7},{7,6},{8,9},{9,8},{10,11... | collective-permute-start | bytes 4718600 | tf_op jit(solution)/shard_map/ppermute | solution.py:412
  186.1 6.1 %copy-start.5 = (f32[8,768]{1,0:T(8,128)S(1)}, f32[8,768]{1,0:T(8,128)}, u32[]{:S(2)}) copy-start(f32[8,768]{1,0:T(8,128)} %copy-done.4) | copy-start | bytes 73732
  186.1 6.1 %copy-start.7 = (f32[8,768]{1,0:T(8,128)S(1)}, f32[8,768]{1,0:T(8,128)}, u32[]{:S(2)}) copy-start(f32[8,768]{1,0:T(8,128)} %copy-done.6) | copy-start | bytes 73732
  186.1 6.1 %copy-start.9 = (f32[1,576]{1,0:T(1,128)S(1)}, f32[1,576]{1,0:T(1,128)}, u32[]{:S(2)}) copy-start(f32[1,576]{1,0:T(1,128)} %copy-done.8) | copy-start | bytes 6916
  186.1 33.6 %all-to-all-start.2 = ((bf16[4,192,768]{2,1,0:T(8,128)(2,1)}), bf16[4,192,768]{2,1,0:T(8,128)(2,1)}, u32[]{:S(2)}, u32[]{:S(2)}) async-start(bf16[4,192,768]{2,1,0:T(8,128)(2,1)} %pad_maximum_fusion), calls=%async_computation.2 | async-start | bytes 2359296 | tf_op jit(solution)/shard_map/all_to_all | solution.py:416
  190.6 11.9 %collective-permute-start.17 = (bf16[256,768]{1,0:T(8,128)(2,1)S(1)}, bf16[256,768]{1,0:T(8,128)(2,1)S(1)}, u32[]{:S(2)}, u32[]{:S(2)}) collective-permute-start(bf16[256,768]{1,0:T(8,128)(2,1)S(1)} %get-tuple-element.251), channel_id=1, source_target_pairs={{0,2},{2,0},{1,3},{3,1},{4,6},{6,4},{5,7},{7,5},{8,10},{10,8},{9,1... | collective-permute-start | bytes 1179656 | tf_op jit(solution)/shard_map/ppermute | solution.py:404
  197.9 5.8 %copy-start.2 = (bf16[1024,768]{1,0:T(8,128)(2,1)}, bf16[1024,768]{1,0:T(8,128)(2,1)S(1)}, u32[]{:S(2)}) copy-start(bf16[1024,768]{1,0:T(8,128)(2,1)S(1)} %get-tuple-element.225) | copy-start | bytes 4718596
  197.9 5.6 %copy-start.14 = (bf16[4,96,768]{2,1,0:T(8,128)(2,1)S(1)}, bf16[4,96,768]{2,1,0:T(8,128)(2,1)}, u32[]{:S(2)}) copy-start(bf16[4,96,768]{2,1,0:T(8,128)(2,1)} %get-tuple-element.217) | copy-start | bytes 1769476
  197.9 5.6 %copy-start.16 = (bf16[4,96,768]{2,1,0:T(8,128)(2,1)S(1)}, bf16[4,96,768]{2,1,0:T(8,128)(2,1)}, u32[]{:S(2)}) copy-start(bf16[4,96,768]{2,1,0:T(8,128)(2,1)} %copy-done.15) | copy-start | bytes 1769476
  197.9 8.0 %collective-permute-start.26 = (f32[2,4,16,96]{3,2,1,0:T(8,128)S(1)}, f32[2,4,16,96]{3,2,1,0:T(8,128)S(1)}, u32[]{:S(2)}, u32[]{:S(2)}) collective-permute-start(f32[2,4,16,96]{3,2,1,0:T(8,128)S(1)} %get-tuple-element.227), channel_id=1, source_target_pairs={{0,2},{2,0},{1,3},{3,1},{4,6},{6,4},{5,7},{7,5},{8,10},{10,8},{9,1... | collective-permute-start | bytes 147464 | tf_op jit(solution)/shard_map/ppermute | solution.py:404
  202.5 2.8 %copy-start.19 = (bf16[4,96,768]{2,1,0:T(8,128)(2,1)S(1)}, bf16[4,96,768]{2,1,0:T(8,128)(2,1)}, u32[]{:S(2)}) copy-start(bf16[4,96,768]{2,1,0:T(8,128)(2,1)} %get-tuple-element.216) | copy-start | bytes 1769476
  202.5 17.6 %copy-start.17 = (bf16[4,96,768]{2,1,0:T(8,128)(2,1)S(1)}, bf16[4,96,768]{2,1,0:T(8,128)(2,1)}, u32[]{:S(2)}) copy-start(bf16[4,96,768]{2,1,0:T(8,128)(2,1)} %get-tuple-element.228) | copy-start | bytes 1769476
  203.7 15.6 %collective-permute-start.24 = (bf16[4,96,768]{2,1,0:T(8,128)(2,1)S(1)}, bf16[4,96,768]{2,1,0:T(8,128)(2,1)S(1)}, u32[]{:S(2)}, u32[]{:S(2)}) collective-permute-start(bf16[4,96,768]{2,1,0:T(8,128)(2,1)S(1)} %add.82), channel_id=1, source_target_pairs={{0,2},{2,0},{1,3},{3,1},{4,6},{6,4},{5,7},{7,5},{8,10},{10,8},{9,1... | collective-permute-start | bytes 1769480 | tf_op jit(solution)/shard_map/ppermute | solution.py:404
  205.3 14.0 %collective-permute-start.23 = (bf16[4,96,768]{2,1,0:T(8,128)(2,1)S(1)}, bf16[4,96,768]{2,1,0:T(8,128)(2,1)S(1)}, u32[]{:S(2)}, u32[]{:S(2)}) collective-permute-start(bf16[4,96,768]{2,1,0:T(8,128)(2,1)S(1)} %copy-done.19), channel_id=1, source_target_pairs={{0,4},{4,0},{1,5},{5,1},{2,6},{6,2},{3,7},{7,3},{8,12},{12,8},{9,1... | collective-permute-start | bytes 1769480 | tf_op jit(solution)/shard_map/ppermute | solution.py:408
  205.9 13.4 %collective-permute-start.27 = (f32[4,8,96]{2,1,0:T(8,128)S(1)}, f32[4,8,96]{2,1,0:T(8,128)S(1)}, u32[]{:S(2)}, u32[]{:S(2)}) collective-permute-start(f32[4,8,96]{2,1,0:T(8,128)S(1)} %slice_bitcast_fusion.3), channel_id=1, source_target_pairs={{0,4},{4,0},{1,5},{5,1},{2,6},{6,2},{3,7},{7,3},{8,12},{12,8},{9,1... | collective-permute-start | bytes 36872 | tf_op jit(solution)/shard_map/ppermute | solution.py:408
  219.3 0.8 copy-start.18
  220.2 12.4 %copy-start.3 = (bf16[1024,768]{1,0:T(8,128)(2,1)S(1)}, bf16[1024,768]{1,0:T(8,128)(2,1)}, u32[]{:S(2)}) copy-start(bf16[1024,768]{1,0:T(8,128)(2,1)} %copy-done.2) | copy-start | bytes 4718596
  222.2 19.2 %all-to-all-start.3 = ((bf16[4,96,768]{2,1,0:T(8,128)(2,1)}), bf16[4,96,768]{2,1,0:T(8,128)(2,1)S(1)}, u32[]{:S(2)}, u32[]{:S(2)}) async-start(bf16[4,96,768]{2,1,0:T(8,128)(2,1)} %add_add_fusion), calls=%async_computation.3 | async-start | bytes 1179648 | tf_op jit(solution)/shard_map/all_to_all | solution.py:416
  226.7 14.8 %collective-permute-start.28 = (f32[8,96]{1,0:T(8,128)S(1)}, f32[8,96]{1,0:T(8,128)S(1)}, u32[]{:S(2)}, u32[]{:S(2)}) collective-permute-start(f32[8,96]{1,0:T(8,128)S(1)} %get-tuple-element.256), channel_id=1, source_target_pairs={{0,8},{8,16},{16,24},{24,0},{1,9},{9,17},{17,25},{25,1},{2,10},{10... | collective-permute-start | bytes 9224 | tf_op jit(solution)/shard_map/ppermute | solution.py:758
  228.7 12.8 %collective-permute-start.29 = (f32[8,96]{1,0:T(8,128)S(1)}, f32[8,96]{1,0:T(8,128)S(1)}, u32[]{:S(2)}, u32[]{:S(2)}) collective-permute-start(f32[8,96]{1,0:T(8,128)S(1)} %get-tuple-element.255), channel_id=1, source_target_pairs={{0,16},{8,24},{16,0},{24,8},{1,17},{9,25},{17,1},{25,9},{2,18},{10... | collective-permute-start | bytes 9224 | tf_op jit(solution)/shard_map/ppermute | solution.py:758
  231.1 10.4 %collective-permute-start.30 = (f32[8,96]{1,0:T(8,128)S(1)}, f32[8,96]{1,0:T(8,128)S(1)}, u32[]{:S(2)}, u32[]{:S(2)}) collective-permute-start(f32[8,96]{1,0:T(8,128)S(1)} %get-tuple-element.254), channel_id=1, source_target_pairs={{0,24},{8,0},{16,8},{24,16},{1,25},{9,1},{17,9},{25,17},{2,26},{10... | collective-permute-start | bytes 9224 | tf_op jit(solution)/shard_map/ppermute | solution.py:758
  232.6 7.9 %collective-permute-start.25 = (bf16[256,768]{1,0:T(8,128)(2,1)S(1)}, bf16[256,768]{1,0:T(8,128)(2,1)S(1)}, u32[]{:S(2)}, u32[]{:S(2)}) collective-permute-start(bf16[256,768]{1,0:T(8,128)(2,1)S(1)} %get-tuple-element.247), channel_id=1, source_target_pairs={{0,2},{2,0},{1,3},{3,1},{4,6},{6,4},{5,7},{7,5},{8,10},{10,8},{9,1... | collective-permute-start | bytes 1179656 | tf_op jit(solution)/shard_map/ppermute | solution.py:404
  233.2 9.2 %copy-start.1 = (bf16[2,768]{1,0:T(2,128)(2,1)S(1)}, bf16[2,768]{1,0:T(2,128)(2,1)}, u32[]{:S(2)}) copy-start(bf16[2,768]{1,0:T(2,128)(2,1)} %param.19) | copy-start | bytes 9220

commit v5 on v4

--- a/solution.py
+++ b/solution.py
@@ -16,12 +16,12 @@
 ZS, XS = 4, 2
 KINDS = 8
 HINT = 1.0
-TILE_PROJECT = 256
+TILE_PROJECT = 512
 TILE_OUT = 256
-TILE_MLP = 256
-TILE_SECOND = 256
-TILE_BACK = 256
-TILE_FIRST = 256
+TILE_MLP = 512
+TILE_SECOND = 512
+TILE_BACK = 1024
+TILE_FIRST = 512
 
 NN = (((1,), (0,)), ((), ()))
 NT = (((1,), (1,)), ((), ()))
@@ -574,12 +574,13 @@
             trans=3 * seq * seq,
         )(*[far(qkv)] * 3)
 
-    def attend_back(qkv, expon, inverse, mixed, grad_mixed):
+    def attend_back(qkv, expon, inverse, mixed, grad_mixed, keep):
+        made = keep((3, seq, HD), BF)
         return call(
             attend_back_body,
             (3,),
             [q_spec, k_spec, v_spec, e_spec, inv_spec, t_spec, t_spec],
-            [(pltpu.HBM((3, seq, HD), BF), q_spec)] * 3,
+            [(made, q_spec)] * 3,
             flops=3 * 40 * seq * seq * HD,
             moved=9e6,
         )(*[far(qkv)] * 3, far(expon), inverse, far(mixed), grad_mixed)
@@ -615,7 +616,7 @@
     part = (ZS, rows, hidden)
     grad_parts = [(sds((1, hidden), F32), kept((1, hidden)))] + [(sds(part, BF), kept(part))] * 4
     mlp_scratch = [pltpu.VMEM((width, hidden), t) for t in (BF, BF, F32, F32)]
-    mlp_cost = dict(flops=12 * seq * width * hidden, moved=16e6, trans=seq * hidden * 2)
+    mlp_cost = dict(flops=12 * seq * width * hidden, moved=16e6, trans=seq * hidden * 2, vmem=24)
     middle, normed_second, ff_part, gs_part, hb_o, gh_oo, gh_ox, gd_oo, gd_ox = call(
         functools.partial(mlp_first_body, rows=rows),
         (seq // tile,),
@@ -695,9 +696,9 @@
             scratch=[pltpu.VMEM((width, n_qkv), F32)],
             flops=4 * seq * width * n_qkv,
             moved=10e6,
-        )(x_arr, *(far(v) for v in grads), far(normed_t), weights, far(wo), *((far(prev),) if more else ()))
-
-    grads_y = attend_back(qkv_y, exp_y, inv_y, wide_y, gx_y.reshape(3, HD, seq))
+        )(x_arr, *(far(v) if more else v for v in grads), far(normed_t), weights, far(wo), *((far(prev),) if more else ()))
+
+    grads_y = attend_back(qkv_y, exp_y, inv_y, wide_y, gx_y.reshape(3, HD, seq), sds)
     ga_yo, ga_yx, first_part, qkv_sum_y = project_back(grads_y, w_y, wo_y, None)
     tile = TILE_OUT
     (out_tokens,) = call(
@@ -709,19 +710,20 @@
         moved=5e6,
     )(middle, ff, ff_mate, vec)
     gx_o, first_part, out_tokens = lax.optimization_barrier((gx_o, first_part, out_tokens))
-    out_got = to_y(out_tokens[block:])
     if fast:
         gx_o, ga_yx, got_hs, got_ds, gd_yo = lax.optimization_barrier((gx_o, ga_yx, got_hs, got_ds, gd_yo))
         got_do = to_y(gd_yo)
         ga_d = to_x(ga_yx)
-    grads_o = attend_back(qkv_o, exp_o, inv_o, wide_o, gx_o.reshape(3, HD, seq))
-    if fast:
-        *grads_o, got_do, ga_d = lax.optimization_barrier((*grads_o, got_do, ga_d))
+    grads_o = attend_back(qkv_o, exp_o, inv_o, wide_o, gx_o.reshape(3, HD, seq), pltpu.HBM)
+    if fast:
+        *grads_o, got_do, ga_d, out_tokens = lax.optimization_barrier((*grads_o, got_do, ga_d, out_tokens))
+        out_got = to_y(out_tokens[block:])
         mlp_all = spread_z(jnp.concatenate([gh_oo + got_ho + got_hs, gd_oo + got_do + got_ds], axis=1))
         ga_s = to_y(ga_yo + ga_d)
     ga_oo, ga_ox, first, qkv_sum_o = project_back(grads_o, w_o, wo_o, first_part)
     if fast:
         ga_x = to_x(ga_ox)
+        first, out_got = lax.optimization_barrier((first, out_got))
     first_mate = to_core(first)
 
     tile = TILE_FIRST
@@ -737,14 +739,16 @@
             (sds(small_y_shape, F32), kept(small_y_shape)),
             (sds((KINDS, width), F32), vecs),
         ],
-        flops=1e6,
-        moved=12e6,
+        flops=0,
+        moved=0,
     )(x_arr, *tokens, te, vec, first, first_mate, far(grad_middle), second_sums, hb_o, hb_y, qkv_sum_o, qkv_sum_y)
 
-    if fast:
-        input_grad, ga_x, ga_s, mlp_all = lax.optimization_barrier((input_grad, ga_x, ga_s, mlp_all))
+    small_got = to_y(small_y)
+    if fast:
+        small_got, input_grad, ga_x, ga_s, mlp_all = lax.optimization_barrier(
+            (small_got, input_grad, ga_x, ga_s, mlp_all)
+        )
         ga_all = spread_z(ga_oo + ga_s + ga_x)
-    small_got = to_y(small_y)
     small_sum = small_o + small_got[:, :, :KINDS]
     embed = first_sums[2]
     embed_got = jnp.where(xi == 0, small_got, small_got[::-1])[:, :, KINDS].transpose(1, 0, 2).reshape(width)
@@ -793,6 +797,8 @@
     def placed(stays, got):
         return jnp.where(yi == 0, jnp.stack([stays, got]), jnp.stack([got, stays]))
 
+    if not fast:
+        out_got = to_y(out_tokens[block:])
     block_output = placed(out_tokens[:block], out_got)
     input_gradient = placed(input_grad[:block], to_y(input_grad[block : 2 * block]))
 

time: 243 us -> 229 us (0.942)
  Pallas kernels: 107 us -> 97.5 us
  waiting for transfers between devices: 67.8 us -> 62.7 us
    ppermute x12, waiting for transfers between devices: 14.9 us -> 6.1 us  [to_y(): return lax.ppermute(values, 'y', swap(2))]
    pallas_call x2, Pallas kernels: 17.5 us -> 12.5 us  [project_back(): call(functools.partial(project_back_body, rows=rows, more=more), (seq //...]
    ppermute x10, waiting for transfers between devices: 33.4 us -> 28.5 us  [to_x(): return lax.ppermute(values, 'b', swap(2))]
    ppermute x3, waiting for transfers between devices: 0.01 us -> 4.14 us  [body(): lax.ppermute(v, 'a', [(i, (i + k) % ZS) for i in range(ZS)])]
  transfers between devices with their start and end apart: 35 -> 35, of which waited for: 18 -> 21; matrix products, arithmetic and copies ran while one was open for 4% -> 5% of each run, Pallas kernels for 38% -> 40%
where the time goes in v5:
time: 229 us; the launch traced here: 228 us
  Pallas kernels  97.5 us (43%)
  waiting for transfers between devices  62.7 us (27%)
  starting transfers between devices  49.5 us (22%)
  other arithmetic  9.17 us (4%)
  local copies, waits for them, and re-layouts  8.34 us (4%)
    ppermute x10, waiting for transfers between devices, to_x(): return lax.ppermute(values, 'b', swap(2))  28.5 us
    all_to_all x4, waiting for transfers between devices, spread_z(): return lax.all_to_all(values, 'a', 0, 0, tiled=True)  18.7 us
    all_to_all x4, starting transfers between devices, spread_z(): return lax.all_to_all(values, 'a', 0, 0, tiled=True)  18.5 us
    pallas_call x2, Pallas kernels, attend_back(): call(attend_back_body, (3,), [q_spec, k_spec, v_spec, e_spec, inv_spec, t...  18 us
    pallas_call x2, Pallas kernels, attend(): call(attend_body, (3,), [q_spec, k_spec, v_spec], [(pltpu.HBM((3, seq, se...  16.2 us
    ppermute x12, starting transfers between devices, to_y(): return lax.ppermute(values, 'y', swap(2))  15.2 us
    pallas_call x2, Pallas kernels, project_back(): call(functools.partial(project_back_body, rows=rows, more=more), (seq //...  12.5 us
    pallas_call x1, Pallas kernels, body(): call(functools.partial(mlp_first_body, rows=rows), (seq // tile,), [scala...  12.2 us
  transfers between devices with their start and end apart: 35, of which 21 were waited for; matrix products, arithmetic and copies ran while one was open for 5% of the time, Pallas kernels for 40%

profile of v5, /device:TPU:0, one launch (start us, length us, event | category | flops | bytes accessed | tf_op | source)
XLA Modules:
  0.0 228.4 jit_solution(11911116885953248163)
XLA Ops:
  0.7 1.8 copy.36.d_ref
  2.5 2.6 %shard_map.313 = (bf16[4,104,768]{2,1,0:T(8,128)(2,1)}, bf16[4,192,768]{2,1,0:T(8,128)(2,1)}) custom-call(bf16[96,192]{1,0:T(8,128)(2,1)} %q_ref.1, bf16[96,192]{1,0:T(8,128)(2,1)} %k_ref.1, bf16[96,192]{1,0:T(8,128)(2,1)} %v_ref.1, bf16[192,96]{1,0:T(8,128)(2,1)} %o_ref.1, bf16[96,768]{1,0:T(8,128)(2,1)} %h_ref.1, bf16[768,96]{1,0:T(8,128)(2,1)} %copy.36.d_ref, ...), custom_call_target="tpu_custom_call" | custom-call | flops 1000000 | bytes 2000000 | tf_op jit(solution)/shard_map/pallas_call | solution.py:450
  5.1 6.4 %all-to-all-start = ((bf16[4,104,768]{2,1,0:T(8,128)(2,1)}), bf16[4,104,768]{2,1,0:T(8,128)(2,1)S(1)}, u32[]{:S(2)}, u32[]{:S(2)}) async-start(bf16[4,104,768]{2,1,0:T(8,128)(2,1)} %get-tuple-element.139), calls=%async_computation | async-start | bytes 1277952 | tf_op jit(solution)/shard_map/all_to_all | solution.py:416
  11.8 1.6 collective-permute-start
  13.4 15.1 %all-to-all-done.refs_5_ = bf16[4,104,768]{2,1,0:T(8,128)(2,1)S(1)} async-done(((bf16[4,104,768]{2,1,0:T(8,128)(2,1)}), bf16[4,104,768]{2,1,0:T(8,128)(2,1)S(1)}, u32[]{:S(2)}, u32[]{:S(2)}) %all-to-all-start) | async-done | bytes 639008 | tf_op jit(solution)/shard_map/all_to_all | solution.py:416
  28.5 4.3 %all-to-all-start.1 = ((bf16[4,192,768]{2,1,0:T(8,128)(2,1)}), bf16[4,192,768]{2,1,0:T(8,128)(2,1)}, u32[]{:S(2)}, u32[]{:S(2)}) async-start(bf16[4,192,768]{2,1,0:T(8,128)(2,1)} %get-tuple-element.146), calls=%async_computation.1 | async-start | bytes 2359296 | tf_op jit(solution)/shard_map/all_to_all | solution.py:416
  32.8 0.9 copy-done.5
  33.6 1.5 collective-permute-start.3
  35.1 1.5 collective-permute-start.4
  36.6 12.3 %collective-permute-done.3.refs_6_ = bf16[4,104,768]{2,1,0:T(8,128)(2,1)S(1)} collective-permute-done((bf16[4,104,768]{2,1,0:T(8,128)(2,1)S(1)}, bf16[4,104,768]{2,1,0:T(8,128)(2,1)S(1)}, u32[]{:S(2)}, u32[]{:S(2)}) %collective-permute-start.3) | collective-permute-done | bytes 639008 | tf_op jit(solution)/shard_map/ppermute | solution.py:408
  49.0 1.2 collective-permute-done.4.refs_1_
  52.2 1.5 collective-permute-start.5
  53.8 5.7 %shard_map.314 = (bf16[768,768]{1,0:T(8,128)(2,1)S(1)}, f32[8,768]{1,0:T(8,128)S(1)}, bf16[9,1024,64]{2,1,0:T(8,128)(2,1)}, bf16[1024,768]{1,0:T(8,128)(2,1)}, bf16[768,1024]{1,0:T(8,128)(2,1)}) custom-call(s32[1]{0:T(128)} %bitcast.x_ref, bf16[512,768]{1,0:T(8,128)(2,1)} %copy-done.4, bf16[512,768]{1,0:T(8,128)(2,1)} %copy-done.5, ...), custom_call_target="tpu_custom_call" | custom-call | flops 905969664 | bytes 8000000 | tf_op jit(solution)/shard_map/pallas_call | solution.py:544
  59.4 1.4 all-to-all-done.1.w_oo
  60.8 1.5 collective-permute-start.7
  62.3 1.5 collective-permute-start.8
  63.8 8.1 %shard_map.315 = (bf16[3,1024,1024]{2,1,0:T(8,128)(2,1)}, f32[3,1,1024]{2,1,0:T(1,128)S(1)}, bf16[3,64,1024]{2,1,0:T(8,128)(2,1)S(1)}, f32[3,64,1024]{2,1,0:T(8,128)}) custom-call(bf16[9,1024,64]{2,1,0:T(8,128)(2,1)} %get-tuple-element.147.q_ref.k_ref.v_ref, bf16[9,1024,64]{2,1,0:T(8,128)(2,1)} %get-tuple-element.147.q_ref.k_ref.v_ref, ...), custom_call_target="tpu_custom_call" | custom-call | flops 3221225472 | bytes 8000000 | tf_op jit(solution)/shard_map/pallas_call | solution.py:562
  71.9 4.0 %shard_map.316 = (bf16[768,768]{1,0:T(8,128)(2,1)S(1)}, f32[8,768]{1,0:T(8,128)S(1)}, bf16[9,1024,64]{2,1,0:T(8,128)(2,1)}) custom-call(s32[1]{0:T(128)} %bitcast.x_ref, bf16[1024,768]{1,0:T(8,128)(2,1)} %get-tuple-element.154.refs_0_, bf16[4,104,768]{2,1,0:T(8,128)(2,1)S(1)} %collective-permute-done.4.refs_1_, ...), custom_call_target="tpu_custom_call" | custom-call | flops 905969664 | bytes 8000000 | tf_op jit(solution)/shard_map/pallas_call | solution.py:544
  75.9 8.1 %shard_map.317 = (bf16[3,1024,1024]{2,1,0:T(8,128)(2,1)}, f32[3,1,1024]{2,1,0:T(1,128)S(1)}, bf16[3,64,1024]{2,1,0:T(8,128)(2,1)S(1)}, f32[3,64,1024]{2,1,0:T(8,128)}) custom-call(bf16[9,1024,64]{2,1,0:T(8,128)(2,1)} %get-tuple-element.157.q_ref.k_ref.v_ref, bf16[9,1024,64]{2,1,0:T(8,128)(2,1)} %get-tuple-element.157.q_ref.k_ref.v_ref, ...), custom_call_target="tpu_custom_call" | custom-call | flops 3221225472 | bytes 8000000 | tf_op jit(solution)/shard_map/pallas_call | solution.py:562
  84.0 4.0 %collective-permute-done.7.w_ox = bf16[4,192,768]{2,1,0:T(8,128)(2,1)S(1)} collective-permute-done((bf16[4,192,768]{2,1,0:T(8,128)(2,1)}, bf16[4,192,768]{2,1,0:T(8,128)(2,1)S(1)}, u32[]{:S(2)}, u32[]{:S(2)}) %collective-permute-start.7) | collective-permute-done | bytes 1179680 | tf_op jit(solution)/shard_map/ppermute | solution.py:408
  88.0 1.2 collective-permute-done.8.w_yo
  89.2 2.0 shard_map.318.a0_ref
  91.3 1.6 collective-permute-start.10
  93.5 1.1 collective-permute-done.9.a1_ref
  94.6 12.2 %shard_map.319 = (f32[1024,768]{1,0:T(8,128)S(1)}, bf16[1024,768]{1,0:T(8,128)(2,1)S(1)}, f32[1024,768]{1,0:T(8,128)S(1)}, f32[1024,768]{1,0:T(8,128)S(1)}, f32[...) custom-call(s32[1]{0:T(128)} %bitcast.x_ref, ...), custom_call_target="tpu_custom_call" | custom-call | flops 7247757312 | bytes 16000000 | tf_op jit(solution)/shard_map/pallas_call | solution.py:620
  107.1 1.3 collective-permute-done.11.d_yx
  108.9 10.3 %shard_map.320 = (bf16[512,768]{1,0:T(8,128)(2,1)S(1)}, bf16[512,768]{1,0:T(8,128)(2,1)S(1)}, bf16[1024,768]{1,0:T(8,128)(2,1)S(1)}, f32[1,768]{1,0:T(1,128)S(1)...) custom-call(s32[1]{0:T(128)} %bitcast.x_ref, ...), custom_call_target="tpu_custom_call" | custom-call | flops 7247757312 | bytes 16000000 | tf_op jit(solution)/shard_map/pallas_call | solution.py:638
  119.3 3.8 %collective-permute-done.12 = bf16[4,96,768]{2,1,0:T(8,128)(2,1)S(1)} collective-permute-done((bf16[4,96,768]{2,1,0:T(8,128)(2,1)S(1)}, bf16[4,96,768]{2,1,0:T(8,128)(2,1)S(1)}, u32[]{:S(2)}, u32[]{:S(2)}) %collective-permute-start.12) | collective-permute-done | bytes 589856 | tf_op jit(solution)/shard_map/ppermute | solution.py:408
  124.9 2.7 %collective-permute-done.16.f1_ref = bf16[512,768]{1,0:T(8,128)(2,1)S(1)} collective-permute-done((bf16[512,768]{1,0:T(8,128)(2,1)S(1)}, bf16[512,768]{1,0:T(8,128)(2,1)S(1)}, u32[]{:S(2)}, u32[]{:S(2)}) %collective-permute-start.16) | collective-permute-done | bytes 786464 | tf_op jit(solution)/shard_map/ppermute | solution.py:412
  127.9 7.8 %shard_map.321 = (f32[1024,768]{1,0:T(8,128)}, bf16[192,1024]{1,0:T(8,128)(2,1)S(1)}, bf16[192,1024]{1,0:T(8,128)(2,1)S(1)}, bf16[768,192]{1,0:T(8,128)(2,1)}, b...) custom-call(f32[1024,768]{1,0:T(8,128)S(1)} %get-tuple-element.165.mid_ref, ...), custom_call_target="tpu_custom_call" | custom-call | flops 1207959552 | bytes 16000000 | tf_op jit(solution)/shard_map/pallas_call | solution.py:659
  135.7 3.1 %collective-permute-done.14 = bf16[4,96,768]{2,1,0:T(8,128)(2,1)S(1)} collective-permute-done((bf16[4,96,768]{2,1,0:T(8,128)(2,1)S(1)}, bf16[4,96,768]{2,1,0:T(8,128)(2,1)S(1)}, u32[]{:S(2)}, u32[]{:S(2)}) %collective-permute-start.14) | collective-permute-done | bytes 589856 | tf_op jit(solution)/shard_map/ppermute | solution.py:408
  139.2 0.9 collective-permute-start.17
  140.2 1.6 collective-permute-start.18
  141.8 8.5 %shard_map.322 = (bf16[3,1024,64]{2,1,0:T(8,128)(2,1)S(1)}, bf16[3,1024,64]{2,1,0:T(8,128)(2,1)S(1)}, bf16[3,1024,64]{2,1,0:T(8,128)(2,1)S(1)}) custom-call(bf16[9,1024,64]{2,1,0:T(8,128)(2,1)} %get-tuple-element.157.q_ref.k_ref.v_ref, bf16[9,1024,64]{2,1,0:T(8,128)(2,1)} %get-tuple-element.157.q_ref.k_ref.v_ref, ...), custom_call_target="tpu_custom_call" | custom-call | flops 8053063680 | bytes 9000000 | tf_op jit(solution)/shard_map/pallas_call | solution.py:579
  150.3 6.1 %shard_map.323 = (bf16[4,96,768]{2,1,0:T(8,128)(2,1)}, bf16[4,96,768]{2,1,0:T(8,128)(2,1)}, f32[1024,768]{1,0:T(8,128)}, f32[1,576]{1,0:T(1,128)S(1)}) custom-call(s32[1]{0:T(128)} %bitcast.x_ref, bf16[3,1024,64]{2,1,0:T(8,128)(2,1)S(1)} %get-tuple-element.185.q_ref, bf16[3,1024,64]{2,1,0:T(8,128)(2,1)S(1)} %get-tuple-element.186.k_ref, ...), custom_call_target="tpu_custom_call" | custom-call | flops 1811939328 | bytes 10000000 | tf_op jit(solution)/shard_map/pallas_call | solution.py:685
  156.4 1.3 collective-permute-start.19
  158.3 9.5 %shard_map.325 = (bf16[3,1024,64]{2,1,0:T(8,128)(2,1)}, bf16[3,1024,64]{2,1,0:T(8,128)(2,1)}, bf16[3,1024,64]{2,1,0:T(8,128)(2,1)}) custom-call(bf16[9,1024,64]{2,1,0:T(8,128)(2,1)} %get-tuple-element.147.q_ref.k_ref.v_ref, bf16[9,1024,64]{2,1,0:T(8,128)(2,1)} %get-tuple-element.147.q_ref.k_ref.v_ref, ...), custom_call_target="tpu_custom_call" | custom-call | flops 8053063680 | bytes 9000000 | tf_op jit(solution)/shard_map/pallas_call | solution.py:579
  167.8 2.2 collective-permute-done.19
  169.9 1.2 collective-permute-done.20
  171.1 0.9 slice_bitcast_fusion.1
  172.9 1.1 pad_maximum_fusion
  174.0 4.3 %all-to-all-start.2 = ((bf16[4,192,768]{2,1,0:T(8,128)(2,1)}), bf16[4,192,768]{2,1,0:T(8,128)(2,1)}, u32[]{:S(2)}, u32[]{:S(2)}) async-start(bf16[4,192,768]{2,1,0:T(8,128)(2,1)} %pad_maximum_fusion), calls=%async_computation.2 | async-start | bytes 2359296 | tf_op jit(solution)/shard_map/all_to_all | solution.py:416
  178.4 6.5 %shard_map.326 = (bf16[4,96,768]{2,1,0:T(8,128)(2,1)}, bf16[4,96,768]{2,1,0:T(8,128)(2,1)}, bf16[1024,768]{1,0:T(8,128)(2,1)S(1)}, f32[1,576]{1,0:T(1,128)S(1)}) custom-call(s32[1]{0:T(128)} %bitcast.x_ref, bf16[3,1024,64]{2,1,0:T(8,128)(2,1)} %get-tuple-element.208.q_ref, bf16[3,1024,64]{2,1,0:T(8,128)(2,1)} %get-tuple-element.209.k_ref, ...), custom_call_target="tpu_custom_call" | custom-call | flops 1811939328 | bytes 10000000 | tf_op jit(solution)/shard_map/pallas_call | solution.py:685
  185.6 1.3 collective-permute-start.25
  186.9 1.4 collective-permute-done.22.g1_ref
  188.4 5.2 %shard_map.327 = (bf16[1024,768]{1,0:T(8,128)(2,1)S(1)}, f32[2,4,8,96]{3,2,1,0:T(8,128)S(1)}, f32[2,4,16,96]{3,2,1,0:T(8,128)S(1)}, f32[8,768]{1,0:T(8,128)S(1)}) custom-call(s32[1]{0:T(128)} %bitcast.x_ref, bf16[512,768]{1,0:T(8,128)(2,1)} %copy-done.4, bf16[512,768]{1,0:T(8,128)(2,1)} %copy-done.5, bf16[512,768]{1,0:T(8,128)(2,1)} %collective-permute-done.1.refs_2_.s2.c2, ...), custom_call_target="tpu_custom_call" | custom-call | tf_op jit(solution)/shard_map/pallas_call | solution.py:732
  193.6 1.2 copy-done.2
  194.7 1.2 collective-permute-start.23
  195.9 2.1 maximum_select_fusion
  198.1 2.8 %collective-permute-done.24 = bf16[4,96,768]{2,1,0:T(8,128)(2,1)} collective-permute-done((bf16[4,96,768]{2,1,0:T(8,128)(2,1)}, bf16[4,96,768]{2,1,0:T(8,128)(2,1)}, u32[]{:S(2)}, u32[]{:S(2)}) %collective-permute-start.24) | collective-permute-done | bytes 589856 | tf_op jit(solution)/shard_map/ppermute | solution.py:408
  200.9 1.0 collective-permute-done.25
  201.9 2.3 all-to-all-done.2
  205.0 1.2 collective-permute-start.26
  206.3 2.2 add_add_fusion
  208.5 3.5 %all-to-all-start.3 = ((bf16[4,96,768]{2,1,0:T(8,128)(2,1)}), bf16[4,96,768]{2,1,0:T(8,128)(2,1)S(1)}, u32[]{:S(2)}, u32[]{:S(2)}) async-start(bf16[4,96,768]{2,1,0:T(8,128)(2,1)} %add_add_fusion), calls=%async_computation.3 | async-start | bytes 1179648 | tf_op jit(solution)/shard_map/all_to_all | solution.py:416
  212.0 1.4 collective-permute-start.27
  213.3 1.5 convert_reduce_fusion
  216.3 2.1 collective-permute-start.28
  218.4 2.4 %collective-permute-start.29 = (f32[8,96]{1,0:T(8,128)S(1)}, f32[8,96]{1,0:T(8,128)S(1)}, u32[]{:S(2)}, u32[]{:S(2)}) collective-permute-start(f32[8,96]{1,0:T(8,128)S(1)} %get-tuple-element.263), channel_id=1, source_target_pairs={{0,16},{8,24},{16,0},{24,8},{1,17},{9,25},{17,1},{25,9},{2,18},{10... | collective-permute-start | bytes 9224 | tf_op jit(solution)/shard_map/ppermute | solution.py:762
  220.7 1.5 collective-permute-start.30
  222.2 1.0 maximum_select_fusion.1
  223.2 1.9 collective-permute-done.28.p1_ref
  225.1 2.2 collective-permute-done.29.p2_ref
  227.4 0.9 shard_map.328
  (78 shorter events, 11.3 us)
Async XLA Ops:
  0.7 53.1 %copy-start = (bf16[2,768]{1,0:T(2,128)(2,1)S(1)}, bf16[2,768]{1,0:T(2,128)(2,1)}, u32[]{:S(2)}) copy-start(bf16[2,768]{1,0:T(2,128)(2,1)} %param.19) | copy-start | bytes 9220
  0.7 10.8 %copy-start.6 = (bf16[2,256,768]{2,1,0:T(8,128)(2,1)S(1)}, bf16[2,256,768]{2,1,0:T(8,128)(2,1)}, u32[]{:S(2)}) copy-start(bf16[2,256,768]{2,1,0:T(8,128)(2,1)} %param.18) | copy-start | bytes 2359300
  5.1 6.5 %copy-start.7 = (bf16[2,256,768]{2,1,0:T(8,128)(2,1)S(1)}, bf16[2,256,768]{2,1,0:T(8,128)(2,1)}, u32[]{:S(2)}) copy-start(bf16[2,256,768]{2,1,0:T(8,128)(2,1)} %param.35) | copy-start | bytes 2359300
  5.1 23.4 %all-to-all-start = ((bf16[4,104,768]{2,1,0:T(8,128)(2,1)}), bf16[4,104,768]{2,1,0:T(8,128)(2,1)S(1)}, u32[]{:S(2)}, u32[]{:S(2)}) async-start(bf16[4,104,768]{2,1,0:T(8,128)(2,1)} %get-tuple-element.139), calls=%async_computation | async-start | bytes 1277952 | tf_op jit(solution)/shard_map/all_to_all | solution.py:416
  11.8 40.5 %copy-start.4 = (bf16[512,768]{1,0:T(8,128)(2,1)}, bf16[512,768]{1,0:T(8,128)(2,1)S(1)}, u32[]{:S(2)}) copy-start(bf16[512,768]{1,0:T(8,128)(2,1)S(1)} %get-tuple-element.257.refs_0_.s0.c0) | copy-start | bytes 2359300
  11.8 21.0 %collective-permute-start = (bf16[512,768]{1,0:T(8,128)(2,1)S(1)}, bf16[512,768]{1,0:T(8,128)(2,1)S(1)}, u32[]{:S(2)}, u32[]{:S(2)}) collective-permute-start(bf16[512,768]{1,0:T(8,128)(2,1)S(1)} %get-tuple-element.256), channel_id=1, source_target_pairs={{0,2},{2,0},{1,3},{3,1},{4,6},{6,4},{5,7},{7,5},{8,10},{10,8},{9,1... | collective-permute-start | bytes 2359304 | tf_op jit(solution)/shard_map/ppermute | solution.py:404
  13.3 19.4 %collective-permute-start.1 = (bf16[512,768]{1,0:T(8,128)(2,1)S(1)}, bf16[512,768]{1,0:T(8,128)(2,1)}, u32[]{:S(2)}, u32[]{:S(2)}) collective-permute-start(bf16[512,768]{1,0:T(8,128)(2,1)S(1)} %get-tuple-element.257.refs_0_.s0.c0), channel_id=1, source_target_pairs={{0,1},{1,0},{2,3},{3,2},{4,5},{5,4},{6,7},{7,6},{8,9},{9,8},{10,11... | collective-permute-start | bytes 2359304 | tf_op jit(solution)/shard_map/ppermute | solution.py:412
  28.5 32.4 %all-to-all-start.1 = ((bf16[4,192,768]{2,1,0:T(8,128)(2,1)}), bf16[4,192,768]{2,1,0:T(8,128)(2,1)}, u32[]{:S(2)}, u32[]{:S(2)}) async-start(bf16[4,192,768]{2,1,0:T(8,128)(2,1)} %get-tuple-element.146), calls=%async_computation.1 | async-start | bytes 2359296 | tf_op jit(solution)/shard_map/all_to_all | solution.py:416
  32.7 0.9 copy-start.5
  33.6 15.3 %collective-permute-start.3 = (bf16[4,104,768]{2,1,0:T(8,128)(2,1)S(1)}, bf16[4,104,768]{2,1,0:T(8,128)(2,1)S(1)}, u32[]{:S(2)}, u32[]{:S(2)}) collective-permute-start(bf16[4,104,768]{2,1,0:T(8,128)(2,1)S(1)} %all-to-all-done.refs_5_), channel_id=1, source_target_pairs={{0,4},{4,0},{1,5},{5,1},{2,6},{6,2},{3,7},{7,3},{8,12},{12,8},{9,1... | collective-permute-start | bytes 1916936 | tf_op jit(solution)/shard_map/ppermute | solution.py:408
  35.1 15.1 %collective-permute-start.4 = (bf16[4,104,768]{2,1,0:T(8,128)(2,1)S(1)}, bf16[4,104,768]{2,1,0:T(8,128)(2,1)S(1)}, u32[]{:S(2)}, u32[]{:S(2)}) collective-permute-start(bf16[4,104,768]{2,1,0:T(8,128)(2,1)S(1)} %all-to-all-done.refs_5_), channel_id=1, source_target_pairs={{0,2},{2,0},{1,3},{3,1},{4,6},{6,4},{5,7},{7,5},{8,10},{10,8},{9,1... | collective-permute-start | bytes 1916936 | tf_op jit(solution)/shard_map/ppermute | solution.py:404
  36.6 17.1 %collective-permute-start.2 = (bf16[512,768]{1,0:T(8,128)(2,1)}, bf16[512,768]{1,0:T(8,128)(2,1)}, u32[]{:S(2)}, u32[]{:S(2)}) collective-permute-start(bf16[512,768]{1,0:T(8,128)(2,1)} %copy-done.5), channel_id=1, source_target_pairs={{0,1},{1,0},{2,3},{3,2},{4,5},{5,4},{6,7},{7,6},{8,9},{9,8},{10,11... | collective-permute-start | bytes 2359304 | tf_op jit(solution)/shard_map/ppermute | solution.py:412
  50.9 9.9 %collective-permute-start.6 = (bf16[4,56,768]{2,1,0:T(8,128)(2,1)}, bf16[4,56,768]{2,1,0:T(8,128)(2,1)}, u32[]{:S(2)}, u32[]{:S(2)}) collective-permute-start(bf16[4,56,768]{2,1,0:T(8,128)(2,1)} %slice.46), channel_id=1, source_target_pairs={{0,4},{4,0},{1,5},{5,1},{2,6},{6,2},{3,7},{7,3},{8,12},{12,8},{9,1... | collective-permute-start | bytes 1032200 | tf_op jit(solution)/shard_map/ppermute | solution.py:408
  52.2 8.6 %collective-permute-start.5 = (bf16[4,48,768]{2,1,0:T(8,128)(2,1)}, bf16[4,48,768]{2,1,0:T(8,128)(2,1)S(1)}, u32[]{:S(2)}, u32[]{:S(2)}) collective-permute-start(bf16[4,48,768]{2,1,0:T(8,128)(2,1)} %slice.45), channel_id=1, source_target_pairs={{0,2},{2,0},{1,3},{3,1},{4,6},{6,4},{5,7},{7,5},{8,10},{10,8},{9,1... | collective-permute-start | bytes 884744 | tf_op jit(solution)/shard_map/ppermute | solution.py:404
  60.8 27.1 %collective-permute-start.7 = (bf16[4,192,768]{2,1,0:T(8,128)(2,1)}, bf16[4,192,768]{2,1,0:T(8,128)(2,1)S(1)}, u32[]{:S(2)}, u32[]{:S(2)}) collective-permute-start(bf16[4,192,768]{2,1,0:T(8,128)(2,1)} %all-to-all-done.1.w_oo), channel_id=1, source_target_pairs={{0,4},{4,0},{1,5},{5,1},{2,6},{6,2},{3,7},{7,3},{8,12},{12,8},{9,1... | collective-permute-start | bytes 3538952 | tf_op jit(solution)/shard_map/ppermute | solution.py:408
  62.3 26.8 %collective-permute-start.8 = (bf16[4,192,768]{2,1,0:T(8,128)(2,1)}, bf16[4,192,768]{2,1,0:T(8,128)(2,1)S(1)}, u32[]{:S(2)}, u32[]{:S(2)}) collective-permute-start(bf16[4,192,768]{2,1,0:T(8,128)(2,1)} %all-to-all-done.1.w_oo), channel_id=1, source_target_pairs={{0,2},{2,0},{1,3},{3,1},{4,6},{6,4},{5,7},{7,5},{8,10},{10,8},{9,1... | collective-permute-start | bytes 3538952 | tf_op jit(solution)/shard_map/ppermute | solution.py:404
  91.1 3.5 %collective-permute-start.9 = (bf16[1024,768]{1,0:T(8,128)(2,1)S(1)}, bf16[1024,768]{1,0:T(8,128)(2,1)S(1)}, u32[]{:S(2)}, u32[]{:S(2)}) collective-permute-start(bf16[1024,768]{1,0:T(8,128)(2,1)S(1)} %shard_map.318.a0_ref), channel_id=1, source_target_pairs={{0,1},{1,0},{2,3},{3,2},{4,5},{5,4},{6,7},{7,6},{8,9},{9,8},{10,11... | collective-permute-start | bytes 4718600 | tf_op jit(solution)/shard_map/ppermute | solution.py:412
  91.3 15.8 %collective-permute-start.10 = (bf16[4,96,768]{2,1,0:T(8,128)(2,1)S(1)}, bf16[4,96,768]{2,1,0:T(8,128)(2,1)S(1)}, u32[]{:S(2)}, u32[]{:S(2)}) collective-permute-start(bf16[4,96,768]{2,1,0:T(8,128)(2,1)S(1)} %slice.47), channel_id=1, source_target_pairs={{0,2},{2,0},{1,3},{3,1},{4,6},{6,4},{5,7},{7,5},{8,10},{10,8},{9,1... | collective-permute-start | bytes 1769480 | tf_op jit(solution)/shard_map/ppermute | solution.py:404
  92.9 15.5 %collective-permute-start.11 = (bf16[4,96,768]{2,1,0:T(8,128)(2,1)S(1)}, bf16[4,96,768]{2,1,0:T(8,128)(2,1)S(1)}, u32[]{:S(2)}, u32[]{:S(2)}) collective-permute-start(bf16[4,96,768]{2,1,0:T(8,128)(2,1)S(1)} %slice.48), channel_id=1, source_target_pairs={{0,4},{4,0},{1,5},{5,1},{2,6},{6,2},{3,7},{7,3},{8,12},{12,8},{9,1... | collective-permute-start | bytes 1769480 | tf_op jit(solution)/shard_map/ppermute | solution.py:408
  108.4 14.6 %collective-permute-start.12 = (bf16[4,96,768]{2,1,0:T(8,128)(2,1)S(1)}, bf16[4,96,768]{2,1,0:T(8,128)(2,1)S(1)}, u32[]{:S(2)}, u32[]{:S(2)}) collective-permute-start(bf16[4,96,768]{2,1,0:T(8,128)(2,1)S(1)} %get-tuple-element.175), channel_id=1, source_target_pairs={{0,4},{4,0},{1,5},{5,1},{2,6},{6,2},{3,7},{7,3},{8,12},{12,8},{9,1... | collective-permute-start | bytes 1769480 | tf_op jit(solution)/shard_map/ppermute | solution.py:408
  123.0 4.9 %collective-permute-start.13 = (bf16[1024,768]{1,0:T(8,128)(2,1)S(1)}, bf16[1024,768]{1,0:T(8,128)(2,1)S(1)}, u32[]{:S(2)}, u32[]{:S(2)}) collective-permute-start(bf16[1024,768]{1,0:T(8,128)(2,1)S(1)} %get-tuple-element.176.g0_ref), channel_id=1, source_target_pairs={{0,1},{1,0},{2,3},{3,2},{4,5},{5,4},{6,7},{7,6},{8,9},{9,8},{10,11... | collective-permute-start | bytes 4718600 | tf_op jit(solution)/shard_map/ppermute | solution.py:412
  123.0 4.5 %collective-permute-start.16 = (bf16[512,768]{1,0:T(8,128)(2,1)S(1)}, bf16[512,768]{1,0:T(8,128)(2,1)S(1)}, u32[]{:S(2)}, u32[]{:S(2)}) collective-permute-start(bf16[512,768]{1,0:T(8,128)(2,1)S(1)} %get-tuple-element.192), channel_id=1, source_target_pairs={{0,1},{1,0},{2,3},{3,2},{4,5},{5,4},{6,7},{7,6},{8,9},{9,8},{10,11... | collective-permute-start | bytes 2359304 | tf_op jit(solution)/shard_map/ppermute | solution.py:412
  123.5 15.2 %collective-permute-start.14 = (bf16[4,96,768]{2,1,0:T(8,128)(2,1)S(1)}, bf16[4,96,768]{2,1,0:T(8,128)(2,1)S(1)}, u32[]{:S(2)}, u32[]{:S(2)}) collective-permute-start(bf16[4,96,768]{2,1,0:T(8,128)(2,1)S(1)} %get-tuple-element.182), channel_id=1, source_target_pairs={{0,4},{4,0},{1,5},{5,1},{2,6},{6,2},{3,7},{7,3},{8,12},{12,8},{9,1... | collective-permute-start | bytes 1769480 | tf_op jit(solution)/shard_map/ppermute | solution.py:408
  124.1 15.0 %collective-permute-start.15 = (bf16[4,96,768]{2,1,0:T(8,128)(2,1)S(1)}, bf16[4,96,768]{2,1,0:T(8,128)(2,1)S(1)}, u32[]{:S(2)}, u32[]{:S(2)}) collective-permute-start(bf16[4,96,768]{2,1,0:T(8,128)(2,1)S(1)} %get-tuple-element.183), channel_id=1, source_target_pairs={{0,2},{2,0},{1,3},{3,1},{4,6},{6,4},{5,7},{7,5},{8,10},{10,8},{9,1... | collective-permute-start | bytes 1769480 | tf_op jit(solution)/shard_map/ppermute | solution.py:404
  139.2 17.2 %collective-permute-start.17 = (bf16[4,96,768]{2,1,0:T(8,128)(2,1)S(1)}, bf16[4,96,768]{2,1,0:T(8,128)(2,1)S(1)}, u32[]{:S(2)}, u32[]{:S(2)}) collective-permute-start(bf16[4,96,768]{2,1,0:T(8,128)(2,1)S(1)} %add.80), channel_id=1, source_target_pairs={{0,2},{2,0},{1,3},{3,1},{4,6},{6,4},{5,7},{7,5},{8,10},{10,8},{9,1... | collective-permute-start | bytes 1769480 | tf_op jit(solution)/shard_map/ppermute | solution.py:404
  140.2 16.2 %collective-permute-start.18 = (bf16[4,96,768]{2,1,0:T(8,128)(2,1)S(1)}, bf16[4,96,768]{2,1,0:T(8,128)(2,1)S(1)}, u32[]{:S(2)}, u32[]{:S(2)}) collective-permute-start(bf16[4,96,768]{2,1,0:T(8,128)(2,1)S(1)} %add.81), channel_id=1, source_target_pairs={{0,4},{4,0},{1,5},{5,1},{2,6},{6,2},{3,7},{7,3},{8,12},{12,8},{9,1... | collective-permute-start | bytes 1769480 | tf_op jit(solution)/shard_map/ppermute | solution.py:408
  156.4 13.6 %collective-permute-start.19 = (bf16[4,96,768]{2,1,0:T(8,128)(2,1)S(1)}, bf16[4,96,768]{2,1,0:T(8,128)(2,1)S(1)}, u32[]{:S(2)}, u32[]{:S(2)}) collective-permute-start(bf16[4,96,768]{2,1,0:T(8,128)(2,1)S(1)} %get-tuple-element.204), channel_id=1, source_target_pairs={{0,2},{2,0},{1,3},{3,1},{4,6},{6,4},{5,7},{7,5},{8,10},{10,8},{9,1... | collective-permute-start | bytes 1769480 | tf_op jit(solution)/shard_map/ppermute | solution.py:404
  157.7 13.4 %collective-permute-start.20 = (bf16[4,96,768]{2,1,0:T(8,128)(2,1)}, bf16[4,96,768]{2,1,0:T(8,128)(2,1)S(1)}, u32[]{:S(2)}, u32[]{:S(2)}) collective-permute-start(bf16[4,96,768]{2,1,0:T(8,128)(2,1)} %get-tuple-element.205), channel_id=1, source_target_pairs={{0,4},{4,0},{1,5},{5,1},{2,6},{6,2},{3,7},{7,3},{8,12},{12,8},{9,1... | collective-permute-start | bytes 1769480 | tf_op jit(solution)/shard_map/ppermute | solution.py:408
  171.1 1.8 copy-start.9
  172.0 12.8 %collective-permute-start.21 = (bf16[256,768]{1,0:T(8,128)(2,1)}, bf16[256,768]{1,0:T(8,128)(2,1)}, u32[]{:S(2)}, u32[]{:S(2)}) collective-permute-start(bf16[256,768]{1,0:T(8,128)(2,1)} %get-tuple-element.259), channel_id=1, source_target_pairs={{0,2},{2,0},{1,3},{3,1},{4,6},{6,4},{5,7},{7,5},{8,10},{10,8},{9,1... | collective-permute-start | bytes 1179656 | tf_op jit(solution)/shard_map/ppermute | solution.py:404
  174.0 30.1 %all-to-all-start.2 = ((bf16[4,192,768]{2,1,0:T(8,128)(2,1)}), bf16[4,192,768]{2,1,0:T(8,128)(2,1)}, u32[]{:S(2)}, u32[]{:S(2)}) async-start(bf16[4,192,768]{2,1,0:T(8,128)(2,1)} %pad_maximum_fusion), calls=%async_computation.2 | async-start | bytes 2359296 | tf_op jit(solution)/shard_map/all_to_all | solution.py:416
  178.3 7.2 %copy-start.8 = (bf16[4,96,768]{2,1,0:T(8,128)(2,1)S(1)}, bf16[4,96,768]{2,1,0:T(8,128)(2,1)}, u32[]{:S(2)}) copy-start(bf16[4,96,768]{2,1,0:T(8,128)(2,1)} %get-tuple-element.225) | copy-start | bytes 1769476
  178.3 7.1 %copy-start.10 = (bf16[4,96,768]{2,1,0:T(8,128)(2,1)S(1)}, bf16[4,96,768]{2,1,0:T(8,128)(2,1)}, u32[]{:S(2)}) copy-start(bf16[4,96,768]{2,1,0:T(8,128)(2,1)} %copy-done.9) | copy-start | bytes 1769476
  184.8 3.5 %collective-permute-start.22 = (bf16[1024,768]{1,0:T(8,128)(2,1)S(1)}, bf16[1024,768]{1,0:T(8,128)(2,1)}, u32[]{:S(2)}, u32[]{:S(2)}) collective-permute-start(bf16[1024,768]{1,0:T(8,128)(2,1)S(1)} %get-tuple-element.215.g0_ref), channel_id=1, source_target_pairs={{0,1},{1,0},{2,3},{3,2},{4,5},{5,4},{6,7},{7,6},{8,9},{9,8},{10,11... | collective-permute-start | bytes 4718600 | tf_op jit(solution)/shard_map/ppermute | solution.py:412
  184.8 16.1 %collective-permute-start.24 = (bf16[4,96,768]{2,1,0:T(8,128)(2,1)}, bf16[4,96,768]{2,1,0:T(8,128)(2,1)}, u32[]{:S(2)}, u32[]{:S(2)}) collective-permute-start(bf16[4,96,768]{2,1,0:T(8,128)(2,1)} %get-tuple-element.224), channel_id=1, source_target_pairs={{0,4},{4,0},{1,5},{5,1},{2,6},{6,2},{3,7},{7,3},{8,12},{12,8},{9,1... | collective-permute-start | bytes 1769480 | tf_op jit(solution)/shard_map/ppermute | solution.py:408
  185.6 16.3 %collective-permute-start.25 = (bf16[4,96,768]{2,1,0:T(8,128)(2,1)S(1)}, bf16[4,96,768]{2,1,0:T(8,128)(2,1)}, u32[]{:S(2)}, u32[]{:S(2)}) collective-permute-start(bf16[4,96,768]{2,1,0:T(8,128)(2,1)S(1)} %add.82), channel_id=1, source_target_pairs={{0,2},{2,0},{1,3},{3,1},{4,6},{6,4},{5,7},{7,5},{8,10},{10,8},{9,1... | collective-permute-start | bytes 1769480 | tf_op jit(solution)/shard_map/ppermute | solution.py:404
  193.5 1.2 copy-start.2
  194.7 9.5 %copy-start.3 = (bf16[1024,768]{1,0:T(8,128)(2,1)S(1)}, bf16[1024,768]{1,0:T(8,128)(2,1)}, u32[]{:S(2)}) copy-start(bf16[1024,768]{1,0:T(8,128)(2,1)} %copy-done.2) | copy-start | bytes 4718596
  194.7 9.4 %collective-permute-start.23 = (f32[2,4,16,96]{3,2,1,0:T(8,128)S(1)}, f32[2,4,16,96]{3,2,1,0:T(8,128)S(1)}, u32[]{:S(2)}, u32[]{:S(2)}) collective-permute-start(f32[2,4,16,96]{3,2,1,0:T(8,128)S(1)} %get-tuple-element.222), channel_id=1, source_target_pairs={{0,2},{2,0},{1,3},{3,1},{4,6},{6,4},{5,7},{7,5},{8,10},{10,8},{9,1... | collective-permute-start | bytes 147464 | tf_op jit(solution)/shard_map/ppermute | solution.py:404
  198.1 8.2 %copy-start.11 = (bf16[4,96,768]{2,1,0:T(8,128)(2,1)S(1)}, bf16[4,96,768]{2,1,0:T(8,128)(2,1)}, u32[]{:S(2)}) copy-start(bf16[4,96,768]{2,1,0:T(8,128)(2,1)} %get-tuple-element.236) | copy-start | bytes 1769476
  205.0 17.2 %collective-permute-start.26 = (bf16[256,768]{1,0:T(8,128)(2,1)}, bf16[256,768]{1,0:T(8,128)(2,1)S(1)}, u32[]{:S(2)}, u32[]{:S(2)}) collective-permute-start(bf16[256,768]{1,0:T(8,128)(2,1)} %get-tuple-element.255), channel_id=1, source_target_pairs={{0,2},{2,0},{1,3},{3,1},{4,6},{6,4},{5,7},{7,5},{8,10},{10,8},{9,1... | collective-permute-start | bytes 1179656 | tf_op jit(solution)/shard_map/ppermute | solution.py:404
  208.5 18.9 %all-to-all-start.3 = ((bf16[4,96,768]{2,1,0:T(8,128)(2,1)}), bf16[4,96,768]{2,1,0:T(8,128)(2,1)S(1)}, u32[]{:S(2)}, u32[]{:S(2)}) async-start(bf16[4,96,768]{2,1,0:T(8,128)(2,1)} %add_add_fusion), calls=%async_computation.3 | async-start | bytes 1179648 | tf_op jit(solution)/shard_map/all_to_all | solution.py:416
  212.0 4.3 %collective-permute-start.27 = (f32[4,8,96]{2,1,0:T(8,128)S(1)}, f32[4,8,96]{2,1,0:T(8,128)S(1)}, u32[]{:S(2)}, u32[]{:S(2)}) collective-permute-start(f32[4,8,96]{2,1,0:T(8,128)S(1)} %slice_bitcast_fusion.3), channel_id=1, source_target_pairs={{0,4},{4,0},{1,5},{5,1},{2,6},{6,2},{3,7},{7,3},{8,12},{12,8},{9,1... | collective-permute-start | bytes 36872 | tf_op jit(solution)/shard_map/ppermute | solution.py:408
  213.3 14.9 %copy-start.1 = (bf16[2,768]{1,0:T(2,128)(2,1)S(1)}, bf16[2,768]{1,0:T(2,128)(2,1)}, u32[]{:S(2)}) copy-start(bf16[2,768]{1,0:T(2,128)(2,1)} %param.19) | copy-start | bytes 9220
  216.3 8.8 %collective-permute-start.28 = (f32[8,96]{1,0:T(8,128)S(1)}, f32[8,96]{1,0:T(8,128)S(1)}, u32[]{:S(2)}, u32[]{:S(2)}) collective-permute-start(f32[8,96]{1,0:T(8,128)S(1)} %get-tuple-element.264), channel_id=1, source_target_pairs={{0,8},{8,16},{16,24},{24,0},{1,9},{9,17},{17,25},{25,1},{2,10},{10... | collective-permute-start | bytes 9224 | tf_op jit(solution)/shard_map/ppermute | solution.py:762
  218.4 9.0 %collective-permute-start.29 = (f32[8,96]{1,0:T(8,128)S(1)}, f32[8,96]{1,0:T(8,128)S(1)}, u32[]{:S(2)}, u32[]{:S(2)}) collective-permute-start(f32[8,96]{1,0:T(8,128)S(1)} %get-tuple-element.263), channel_id=1, source_target_pairs={{0,16},{8,24},{16,0},{24,8},{1,17},{9,25},{17,1},{25,9},{2,18},{10... | collective-permute-start | bytes 9224 | tf_op jit(solution)/shard_map/ppermute | solution.py:762
  220.7 6.6 %collective-permute-start.30 = (f32[8,96]{1,0:T(8,128)S(1)}, f32[8,96]{1,0:T(8,128)S(1)}, u32[]{:S(2)}, u32[]{:S(2)}) collective-permute-start(f32[8,96]{1,0:T(8,128)S(1)} %get-tuple-element.262), channel_id=1, source_target_pairs={{0,24},{8,0},{16,8},{24,16},{1,25},{9,1},{17,9},{25,17},{2,26},{10... | collective-permute-start | bytes 9224 | tf_op jit(solution)/shard_map/ppermute | solution.py:762

commit v6 on v5

--- a/solution.py
+++ b/solution.py
@@ -66,6 +66,11 @@
     return jax.ShapeDtypeStruct(shape, dtype)
 
 
+def place(x_ref, k, side, rows):
+    x = x_ref[0] if side == 0 else 1 - x_ref[0]
+    return pl.multiple_of((2 * lax.rem(x_ref[1] + k, ZS) + x) * rows, 32)
+
+
 def shard_of(refs, z, rows):
     parts = [r[z] for r in refs]
     value = parts[0] if len(parts) == 1 else jnp.concatenate(parts, axis=0)
@@ -86,10 +91,10 @@
     bias = jnp.concatenate([qb[...], vb[...], jnp.zeros((1, shard - 2 * n), BF)], axis=1)
     small = jnp.concatenate([r[...].astype(F32) for r in (fg, fs, ob, sg, ss, db, hb)] + [bias.astype(F32)], axis=0)
     small = jnp.concatenate([small, jnp.zeros((KINDS, low.shape[1] - shard), F32)], axis=1).astype(BF)
-    high, down = h_ref[...], d_ref[...].T
-    for z in range(attn_ref.shape[0]):
-        attn_ref[z, :shard, :] = low
-        attn_ref[z, shard:, :] = small
+    high, down = h_ref[...], d_ref[...]
+    attn_ref[:shard, :] = low
+    attn_ref[shard:, :] = small
+    for z in range(mlp_ref.shape[0]):
         mlp_ref[z, :shard, :] = high
         mlp_ref[z, shard:, :] = down
 
@@ -115,18 +120,18 @@
 
     @pl.when(pl.program_id(0) == 0)
     def _():
-        x = x_ref[0]
         own, oth = [], []
-        for z in range(ZS):
-            weight, small = shard_of((own_ref,), z, rows)
-            w_ref[pl.ds(pl.multiple_of((2 * z + x) * rows, 32), rows), :] = weight
+        for k in range(ZS):
+            weight, small = shard_of((own_ref,), k, rows)
+            w_ref[pl.ds(place(x_ref, k, 0, rows), rows), :] = weight
             own.append(small[:, :rows].astype(F32))
-            weight, small = shard_of(oth_refs, z, rows)
-            w_ref[pl.ds(pl.multiple_of((2 * z + 1 - x) * rows, 32), rows), :] = weight
+            weight, small = shard_of(oth_refs, k, rows)
+            w_ref[pl.ds(place(x_ref, k, 1, rows), rows), :] = weight
             oth.append(small[:, :rows].astype(F32))
         even = jnp.concatenate([v for pair in zip(own, oth) for v in pair], axis=1)
         odd = jnp.concatenate([v for pair in zip(oth, own) for v in pair], axis=1)
-        vec = jnp.where(x == 0, even, odd)
+        vec = jnp.where(x_ref[0] == 0, even, odd)
+        vec = pltpu.roll(vec, x_ref[1] * (2 * rows), 1)
         vec_ref[...] = vec
         n = rows // 4
         last = vec[7:8, :]
@@ -336,7 +341,7 @@
 
 def first_back_body(
     x_ref, s0, s1, s2, s3, te_ref, vec_ref, g0_ref, g1_ref, gm_ref, second_ref, ho_ref, hy_ref, qo_ref, qy_ref,
-    out_ref, own_ref, oth_ref, sum_ref, *, rows,
+    stays_ref, sent_ref, own_ref, oth_ref, sum_ref, *, rows,
 ):
     @pl.when(pl.program_id(0) == 0)
     def _():
@@ -347,7 +352,13 @@
     scaled = first * vec_ref[0:1, :]
     inner = jnp.mean(scaled * xhat, axis=-1, keepdims=True)
     grad = gm_ref[...] + rate * (scaled - jnp.mean(scaled, axis=-1, keepdims=True) - xhat * inner)
-    out_ref[...] = grad.astype(BF)
+
+    @pl.when(pl.program_id(0) == 0)
+    def _():
+        half = grad.shape[0] // 2
+        stays_ref[...] = grad[:half].astype(BF)
+        sent_ref[...] = grad[half:].astype(BF)
+
     sum_ref[0:1, :] += jnp.sum(first * xhat, axis=0, keepdims=True)
     sum_ref[1:2, :] += jnp.sum(first, axis=0, keepdims=True)
     sum_ref[2:3, :] += jnp.sum(grad, axis=0, keepdims=True)
@@ -390,10 +401,16 @@
     small[8][...] = sums[7:8, n : 2 * n]
 
 
-def output_body(mid_ref, f0_ref, f1_ref, vec_ref, out_ref):
-    out_ref[...] = (
-        mid_ref[...] + (f0_ref[...].astype(F32) + f1_ref[...].astype(F32)) + vec_ref[5:6, :]
-    ).astype(BF)
+def output_body(mid_ref, f0_ref, f1_ref, vec_ref, stays_ref, sent_ref):
+    made = (mid_ref[...] + (f0_ref[...].astype(F32) + f1_ref[...].astype(F32)) + vec_ref[5:6, :]).astype(BF)
+
+    @pl.when(pl.program_id(0) == 0)
+    def _():
+        stays_ref[...] = made
+
+    @pl.when(pl.program_id(0) == 1)
+    def _():
+        sent_ref[...] = made
 
 
 def swap(size):
@@ -410,6 +427,11 @@
 
 def to_core(values):
     return lax.ppermute(values, "c", swap(2))
+
+
+def gather_z(values):
+    got = [lax.ppermute(values, "a", [((i + k) % ZS, i) for i in range(ZS)]) for k in range(1, ZS)]
+    return jnp.stack([values] + got)
 
 
 def spread_z(values):
@@ -444,25 +466,26 @@
     hidden = hidden_weight.shape[1]
     yi = lax.axis_index("y")
     xi = lax.axis_index("b") if fast else jnp.int32(0)
-    x_arr = xi.astype(jnp.int32)[None]
+    zi = lax.axis_index("a") if fast else jnp.int32(0)
+    x_arr = jnp.stack([xi.astype(jnp.int32), zi.astype(jnp.int32)])
 
     n_copies = ZS if fast else 1
     attn_pack, mlp_pack = call(
         pack_body,
         (1,),
         [kept((shard, hidden // 4))] * 3
-        + [kept((hidden // 4, shard)), kept((shard, hidden)), kept((hidden, shard))]
+        + [kept((hidden // 4, shard)), kept((shard, hidden)), kept((shard, hidden))]
         + [kept((1, shard))] * 7
         + [kept((1, query_bias.shape[0]))] * 2,
         [
-            (sds((n_copies, shard + KINDS, width), BF), kept((n_copies, shard + KINDS, width))),
+            (sds((shard + KINDS, width), BF), kept((shard + KINDS, width))),
             (sds((n_copies, 2 * shard, width), BF), kept((n_copies, 2 * shard, width))),
         ],
         flops=1e6,
         moved=2e6,
         vmem=56,
     )(
-        query_weight, key_weight, value_weight, output_weight, hidden_weight, down_weight,
+        query_weight, key_weight, value_weight, output_weight, hidden_weight, down_weight.T,
         *(v[None] for v in (first_gain, first_shift, output_bias, second_gain, second_shift, down_bias, hidden_bias, query_bias, value_bias)),
     )
 
@@ -474,7 +497,8 @@
     te = lax.dynamic_index_in_dim(time_embed, yi, 0, keepdims=True)
 
     if fast:
-        attn_oo = spread_z(attn_pack)
+        attn_oo = gather_z(attn_pack)
+        attn_oo, mlp_pack = lax.optimization_barrier((attn_oo, mlp_pack))
         attn_oo, comes, stays_mate = lax.optimization_barrier((attn_oo, comes, stays_mate))
         comes_mate = to_core(comes)
         attn_ox, attn_yo = to_x(attn_oo), to_y(attn_oo)
@@ -487,7 +511,7 @@
             full = full.reshape(ZS, XS, rows, width)
             return full[:, 0], full[:, 1]
 
-        gathered = lax.all_gather(attn_pack[0], ("a", "b"), axis=0, tiled=False)
+        gathered = lax.all_gather(attn_pack, ("a", "b"), axis=0, tiled=False)
         matrix = gathered[:, :shard].reshape(ZS, XS, rows, width)
         small = gathered[:, shard:, :shard]
         flat = small[:, :7].transpose(1, 0, 2).reshape(7, width)
@@ -700,12 +724,12 @@
 
     grads_y = attend_back(qkv_y, exp_y, inv_y, wide_y, gx_y.reshape(3, HD, seq), sds)
     ga_yo, ga_yx, first_part, qkv_sum_y = project_back(grads_y, w_y, wo_y, None)
-    tile = TILE_OUT
-    (out_tokens,) = call(
+    tile = block
+    out_stays, out_tokens = call(
         output_body,
-        (seq // tile // 2,),
+        (2,),
         [by(tile), by(tile), by(tile), vecs],
-        [(sds((seq // 2, width), BF), by(tile))],
+        [(sds((block, width), BF), kept((block, width)))] * 2,
         flops=1e6,
         moved=5e6,
     )(middle, ff, ff_mate, vec)
@@ -717,7 +741,7 @@
     grads_o = attend_back(qkv_o, exp_o, inv_o, wide_o, gx_o.reshape(3, HD, seq), pltpu.HBM)
     if fast:
         *grads_o, got_do, ga_d, out_tokens = lax.optimization_barrier((*grads_o, got_do, ga_d, out_tokens))
-        out_got = to_y(out_tokens[block:])
+        out_got = to_y(out_tokens)
         mlp_all = spread_z(jnp.concatenate([gh_oo + got_ho + got_hs, gd_oo + got_do + got_ds], axis=1))
         ga_s = to_y(ga_yo + ga_d)
     ga_oo, ga_ox, first, qkv_sum_o = project_back(grads_o, w_o, wo_o, first_part)
@@ -729,12 +753,12 @@
     tile = TILE_FIRST
     hb_spec, qkv_spec = kept((1, hidden)), kept((1, n_qkv))
     small_o_shape, small_y_shape = (XS, ZS, KINDS, rows), (XS, ZS, 2 * KINDS, rows)
-    input_grad, small_o, small_y, first_sums = call(
+    in_stays, input_grad, small_o, small_y, first_sums = call(
         functools.partial(first_back_body, rows=rows),
         (seq // tile,),
         [scalar(), *start_blocks, row, vecs, by(tile), by_mate(tile), by(tile), vecs, hb_spec, hb_spec, qkv_spec, qkv_spec],
-        [
-            (sds((seq, width), BF), by(tile)),
+        [(sds((seq // 4, width), BF), kept((seq // 4, width)))] * 2
+        + [
             (sds(small_o_shape, F32), kept(small_o_shape)),
             (sds(small_y_shape, F32), kept(small_y_shape)),
             (sds((KINDS, width), F32), vecs),
@@ -798,9 +822,9 @@
         return jnp.where(yi == 0, jnp.stack([stays, got]), jnp.stack([got, stays]))
 
     if not fast:
-        out_got = to_y(out_tokens[block:])
-    block_output = placed(out_tokens[:block], out_got)
-    input_gradient = placed(input_grad[:block], to_y(input_grad[block : 2 * block]))
+        out_got = to_y(out_tokens)
+    block_output = placed(out_stays, out_got)
+    input_gradient = placed(in_stays, to_y(input_grad))
 
     fg, fs, ob, sg, ss, db, hb, qb, vb = vectors
     return (

time: 229 us -> 222 us (0.969)
  waiting for transfers between devices: 62.7 us -> 54.1 us
  local copies, waits for them, and re-layouts: 8.34 us -> 3.93 us
  starting transfers between devices: 49.5 us -> 51.9 us
    all_to_all x4 -> x3, waiting for transfers between devices: 18.7 us -> 2.09 us  [spread_z(): return lax.all_to_all(values, 'a', 0, 0, tiled=True)]
    ppermute x0 -> x3, starting transfers between devices: none -> 6.96 us  [gather_z(): lax.ppermute(values, 'a', [((i + k) % ZS, i) for i in range(ZS)])]
    ppermute x0 -> x3, waiting for transfers between devices: none -> 6.35 us  [gather_z(): lax.ppermute(values, 'a', [((i + k) % ZS, i) for i in range(ZS)])]
    all_to_all x4 -> x3, starting transfers between devices: 18.5 us -> 14.5 us  [spread_z(): return lax.all_to_all(values, 'a', 0, 0, tiled=True)]
    ppermute x12, waiting for transfers between devices: 6.1 us -> 9.72 us  [to_y(): return lax.ppermute(values, 'y', swap(2))]
  transfers between devices with their start and end apart: 35 -> 37, of which waited for: 21 -> 22; matrix products, arithmetic and copies ran while one was open for 5% -> 6% of each run, Pallas kernels for 40% -> 43%
where the time goes in v6:
time: 222 us; the launch traced here: 221 us
  Pallas kernels  99.7 us (45%)
  waiting for transfers between devices  54.1 us (24%)
  starting transfers between devices  51.9 us (23%)
  other arithmetic  10.2 us (5%)
  local copies, waits for them, and re-layouts  3.93 us (2%)
    ppermute x10, waiting for transfers between devices, to_x(): return lax.ppermute(values, 'b', swap(2))  26.5 us
    pallas_call x2, Pallas kernels, attend_back(): call(attend_back_body, (3,), [q_spec, k_spec, v_spec, e_spec, inv_spec, t...  18 us
    pallas_call x2, Pallas kernels, attend(): call(attend_body, (3,), [q_spec, k_spec, v_spec], [(pltpu.HBM((3, seq, se...  16.1 us
    all_to_all x3, starting transfers between devices, spread_z(): return lax.all_to_all(values, 'a', 0, 0, tiled=True)  14.5 us
    ppermute x12, starting transfers between devices, to_y(): return lax.ppermute(values, 'y', swap(2))  14.4 us
    pallas_call x2, Pallas kernels, project_back(): call(functools.partial(project_back_body, rows=rows, more=more), (seq //...  12.5 us
    pallas_call x1, Pallas kernels, body(): call(functools.partial(mlp_first_body, rows=rows), (seq // tile,), [scala...  12.4 us
    pallas_call x1, Pallas kernels, body(): call(functools.partial(mlp_second_body, rows=rows), (seq // tile,), [scal...  10.2 us
  transfers between devices with their start and end apart: 37, of which 22 were waited for; matrix products, arithmetic and copies ran while one was open for 6% of the time, Pallas kernels for 43%

profile of v6, /device:TPU:0, one launch (start us, length us, event | category | flops | bytes accessed | tf_op | source)
XLA Modules:
  0.0 220.9 jit_solution(7084368375785099659)
XLA Ops:
  0.7 2.3 %shard_map.313 = (bf16[104,768]{1,0:T(8,128)(2,1)}, bf16[4,192,768]{2,1,0:T(8,128)(2,1)}) custom-call(bf16[96,192]{1,0:T(8,128)(2,1)} %q_ref.1, bf16[96,192]{1,0:T(8,128)(2,1)} %k_ref.1, bf16[96,192]{1,0:T(8,128)(2,1)} %v_ref.1, bf16[192,96]{1,0:T(8,128)(2,1)} %o_ref.1, bf16[96,768]{1,0:T(8,128)(2,1)} %h_ref.1, bf16[96,768]{1,0:T(8,128)(2,1)} %bitcast.68, ...), custom_call_target="tpu_custom_call" | custom-call | flops 1000000 | bytes 2000000 | tf_op jit(solution)/shard_map/pallas_call | solution.py:473
  3.0 3.0 %collective-permute-start.2 = (bf16[104,768]{1,0:T(8,128)(2,1)}, bf16[104,768]{1,0:T(8,128)(2,1)S(1)}, u32[]{:S(2)}, u32[]{:S(2)}) collective-permute-start(bf16[104,768]{1,0:T(8,128)(2,1)} %get-tuple-element.144), channel_id=1, source_target_pairs={{24,0},{0,8},{8,16},{16,24},{25,1},{1,9},{9,17},{17,25},{26,2},{2,... | collective-permute-start | bytes 479240 | tf_op jit(solution)/shard_map/ppermute | solution.py:433
  6.1 2.6 %collective-permute-start.1 = (bf16[104,768]{1,0:T(8,128)(2,1)}, bf16[104,768]{1,0:T(8,128)(2,1)S(1)}, u32[]{:S(2)}, u32[]{:S(2)}) collective-permute-start(bf16[104,768]{1,0:T(8,128)(2,1)} %get-tuple-element.144), channel_id=1, source_target_pairs={{16,0},{24,8},{0,16},{8,24},{17,1},{25,9},{1,17},{9,25},{18,2},{26... | collective-permute-start | bytes 479240 | tf_op jit(solution)/shard_map/ppermute | solution.py:433
  8.6 1.3 collective-permute-start
  10.0 1.2 constant_dynamic-update-slice_fusion.1
  11.4 1.6 collective-permute-start.3
  13.3 6.0 %collective-permute-done.1 = bf16[104,768]{1,0:T(8,128)(2,1)S(1)} collective-permute-done((bf16[104,768]{1,0:T(8,128)(2,1)}, bf16[104,768]{1,0:T(8,128)(2,1)S(1)}, u32[]{:S(2)}, u32[]{:S(2)}) %collective-permute-start.1) | collective-permute-done | bytes 159776 | tf_op jit(solution)/shard_map/ppermute | solution.py:433
  19.3 1.0 pad_maximum_fusion.1.refs_5_
  20.4 6.2 %all-to-all-start = ((bf16[4,192,768]{2,1,0:T(8,128)(2,1)}), bf16[4,192,768]{2,1,0:T(8,128)(2,1)}, u32[]{:S(2)}, u32[]{:S(2)}) async-start(bf16[4,192,768]{2,1,0:T(8,128)(2,1)} %get-tuple-element.153), calls=%async_computation | async-start | bytes 2359296 | tf_op jit(solution)/shard_map/all_to_all | solution.py:438
  26.6 3.4 %collective-permute-done.3.refs_1_.s1.c1 = bf16[512,768]{1,0:T(8,128)(2,1)} collective-permute-done((bf16[512,768]{1,0:T(8,128)(2,1)S(1)}, bf16[512,768]{1,0:T(8,128)(2,1)}, u32[]{:S(2)}, u32[]{:S(2)}) %collective-permute-start.3) | collective-permute-done | bytes 786464 | tf_op jit(solution)/shard_map/ppermute | solution.py:421
  30.0 1.5 collective-permute-start.6
  31.5 1.5 collective-permute-start.7
  33.0 11.3 %collective-permute-done.6.refs_6_ = bf16[4,104,768]{2,1,0:T(8,128)(2,1)S(1)} collective-permute-done((bf16[4,104,768]{2,1,0:T(8,128)(2,1)S(1)}, bf16[4,104,768]{2,1,0:T(8,128)(2,1)S(1)}, u32[]{:S(2)}, u32[]{:S(2)}) %collective-permute-start.6) | collective-permute-done | bytes 639008 | tf_op jit(solution)/shard_map/ppermute | solution.py:425
  44.4 1.2 collective-permute-done.7.refs_1_
  46.9 1.6 collective-permute-start.8
  48.6 5.8 %shard_map.314 = (bf16[768,768]{1,0:T(8,128)(2,1)S(1)}, f32[8,768]{1,0:T(8,128)S(1)}, bf16[9,1024,64]{2,1,0:T(8,128)(2,1)}, bf16[1024,768]{1,0:T(8,128)(2,1)}, bf16[768,1024]{1,0:T(8,128)(2,1)}) custom-call(s32[2]{0:T(128)S(1)} %pad_add_fusion.x_ref, bf16[512,768]{1,0:T(8,128)(2,1)} %copy-done.4, bf16[512,768]{1,0:T(8,128)(2,1)} %collective-permute-done.3.refs_1_.s1.c1, ...), custom_call_target="tpu_custom_call" | custom-call | flops 905969664 | bytes 8000000 | tf_op jit(solution)/shard_map/pallas_call | solution.py:568
  55.1 1.6 collective-permute-start.10
  57.5 8.0 %shard_map.315 = (bf16[3,1024,1024]{2,1,0:T(8,128)(2,1)}, f32[3,1,1024]{2,1,0:T(1,128)S(1)}, bf16[3,64,1024]{2,1,0:T(8,128)(2,1)S(1)}, f32[3,64,1024]{2,1,0:T(8,128)}) custom-call(bf16[9,1024,64]{2,1,0:T(8,128)(2,1)} %get-tuple-element.154.q_ref.k_ref.v_ref, bf16[9,1024,64]{2,1,0:T(8,128)(2,1)} %get-tuple-element.154.q_ref.k_ref.v_ref, ...), custom_call_target="tpu_custom_call" | custom-call | flops 3221225472 | bytes 8000000 | tf_op jit(solution)/shard_map/pallas_call | solution.py:586
  65.5 4.0 %shard_map.316 = (bf16[768,768]{1,0:T(8,128)(2,1)S(1)}, f32[8,768]{1,0:T(8,128)S(1)}, bf16[9,1024,64]{2,1,0:T(8,128)(2,1)}) custom-call(s32[2]{0:T(128)S(1)} %pad_add_fusion.x_ref, bf16[1024,768]{1,0:T(8,128)(2,1)} %get-tuple-element.158.refs_0_, bf16[4,104,768]{2,1,0:T(8,128)(2,1)S(1)} %collective-permute-done.7.refs_1_, bf16[4,48,768]{2,1,0:T(8,128)(2,1)S(1)} %copy-done.3, ...), custom_call_target="tpu_custom_call" | custom-call | flops 905969664 | bytes 8000000 | tf_op jit(solution)/shard_map/pallas_call | solution.py:568
  69.5 8.1 %shard_map.317 = (bf16[3,1024,1024]{2,1,0:T(8,128)(2,1)}, f32[3,1,1024]{2,1,0:T(1,128)S(1)}, bf16[3,64,1024]{2,1,0:T(8,128)(2,1)S(1)}, f32[3,64,1024]{2,1,0:T(8,128)}) custom-call(bf16[9,1024,64]{2,1,0:T(8,128)(2,1)} %get-tuple-element.161.q_ref.k_ref.v_ref, bf16[9,1024,64]{2,1,0:T(8,128)(2,1)} %get-tuple-element.161.q_ref.k_ref.v_ref, ...), custom_call_target="tpu_custom_call" | custom-call | flops 3221225472 | bytes 8000000 | tf_op jit(solution)/shard_map/pallas_call | solution.py:586
  77.6 4.0 %collective-permute-done.10.w_ox = bf16[4,192,768]{2,1,0:T(8,128)(2,1)S(1)} collective-permute-done((bf16[4,192,768]{2,1,0:T(8,128)(2,1)}, bf16[4,192,768]{2,1,0:T(8,128)(2,1)S(1)}, u32[]{:S(2)}, u32[]{:S(2)}) %collective-permute-start.10) | collective-permute-done | bytes 1179680 | tf_op jit(solution)/shard_map/ppermute | solution.py:425
  81.6 1.2 collective-permute-done.11.w_yo
  82.8 2.0 shard_map.318.a0_ref
  84.9 1.6 collective-permute-start.13
  87.1 1.1 collective-permute-done.12.a1_ref
  88.2 12.4 %shard_map.319 = (f32[1024,768]{1,0:T(8,128)S(1)}, bf16[1024,768]{1,0:T(8,128)(2,1)S(1)}, f32[1024,768]{1,0:T(8,128)S(1)}, f32[1024,768]{1,0:T(8,128)S(1)}, f32[...) custom-call(s32[2]{0:T(128)S(1)} %pad_add_fusion.x_ref, ...), custom_call_target="tpu_custom_call" | custom-call | flops 7247757312 | bytes 16000000 | tf_op jit(solution)/shard_map/pallas_call | solution.py:644
  100.7 1.3 collective-permute-done.14.d_yx
  102.6 10.2 %shard_map.320 = (bf16[512,768]{1,0:T(8,128)(2,1)S(1)}, bf16[512,768]{1,0:T(8,128)(2,1)S(1)}, bf16[1024,768]{1,0:T(8,128)(2,1)S(1)}, f32[1,768]{1,0:T(1,128)S(1)...) custom-call(s32[2]{0:T(128)S(1)} %pad_add_fusion.x_ref, ...), custom_call_target="tpu_custom_call" | custom-call | flops 7247757312 | bytes 16000000 | tf_op jit(solution)/shard_map/pallas_call | solution.py:662
  112.8 3.9 %collective-permute-done.16 = bf16[4,96,768]{2,1,0:T(8,128)(2,1)S(1)} collective-permute-done((bf16[4,96,768]{2,1,0:T(8,128)(2,1)S(1)}, bf16[4,96,768]{2,1,0:T(8,128)(2,1)S(1)}, u32[]{:S(2)}, u32[]{:S(2)}) %collective-permute-start.16) | collective-permute-done | bytes 589856 | tf_op jit(solution)/shard_map/ppermute | solution.py:425
  118.6 2.5 %collective-permute-done.15.f1_ref = bf16[512,768]{1,0:T(8,128)(2,1)S(1)} collective-permute-done((bf16[512,768]{1,0:T(8,128)(2,1)S(1)}, bf16[512,768]{1,0:T(8,128)(2,1)S(1)}, u32[]{:S(2)}, u32[]{:S(2)}) %collective-permute-start.15) | collective-permute-done | bytes 786464 | tf_op jit(solution)/shard_map/ppermute | solution.py:429
  121.2 1.4 shard_map.321
  122.6 7.7 %shard_map.322 = (f32[1024,768]{1,0:T(8,128)}, bf16[192,1024]{1,0:T(8,128)(2,1)S(1)}, bf16[192,1024]{1,0:T(8,128)(2,1)S(1)}, bf16[768,192]{1,0:T(8,128)(2,1)}, b...) custom-call(f32[1024,768]{1,0:T(8,128)S(1)} %get-tuple-element.169.mid_ref, ...), custom_call_target="tpu_custom_call" | custom-call | flops 1207959552 | bytes 16000000 | tf_op jit(solution)/shard_map/pallas_call | solution.py:683
  130.3 2.1 collective-permute-done.18
  132.8 1.0 collective-permute-start.20
  134.0 1.6 collective-permute-start.21
  135.5 8.7 %shard_map.323 = (bf16[3,1024,64]{2,1,0:T(8,128)(2,1)S(1)}, bf16[3,1024,64]{2,1,0:T(8,128)(2,1)S(1)}, bf16[3,1024,64]{2,1,0:T(8,128)(2,1)S(1)}) custom-call(bf16[9,1024,64]{2,1,0:T(8,128)(2,1)} %get-tuple-element.161.q_ref.k_ref.v_ref, bf16[9,1024,64]{2,1,0:T(8,128)(2,1)} %get-tuple-element.161.q_ref.k_ref.v_ref, ...), custom_call_target="tpu_custom_call" | custom-call | flops 8053063680 | bytes 9000000 | tf_op jit(solution)/shard_map/pallas_call | solution.py:603
  144.3 6.1 %shard_map.324 = (bf16[4,96,768]{2,1,0:T(8,128)(2,1)}, bf16[4,96,768]{2,1,0:T(8,128)(2,1)}, f32[1024,768]{1,0:T(8,128)}, f32[1,576]{1,0:T(1,128)S(1)}) custom-call(s32[2]{0:T(128)S(1)} %pad_add_fusion.x_ref, bf16[3,1024,64]{2,1,0:T(8,128)(2,1)S(1)} %get-tuple-element.195.q_ref, bf16[3,1024,64]{2,1,0:T(8,128)(2,1)S(1)} %get-tuple-element.196.k_ref, ...), custom_call_target="tpu_custom_call" | custom-call | flops 1811939328 | bytes 10000000 | tf_op jit(solution)/shard_map/pallas_call | solution.py:709
  150.3 1.2 collective-permute-start.22
  152.2 9.2 %shard_map.325 = (bf16[3,1024,64]{2,1,0:T(8,128)(2,1)}, bf16[3,1024,64]{2,1,0:T(8,128)(2,1)}, bf16[3,1024,64]{2,1,0:T(8,128)(2,1)}) custom-call(bf16[9,1024,64]{2,1,0:T(8,128)(2,1)} %get-tuple-element.154.q_ref.k_ref.v_ref, bf16[9,1024,64]{2,1,0:T(8,128)(2,1)} %get-tuple-element.154.q_ref.k_ref.v_ref, ...), custom_call_target="tpu_custom_call" | custom-call | flops 8053063680 | bytes 9000000 | tf_op jit(solution)/shard_map/pallas_call | solution.py:603
  161.4 2.5 %collective-permute-done.22 = bf16[4,96,768]{2,1,0:T(8,128)(2,1)S(1)} collective-permute-done((bf16[4,96,768]{2,1,0:T(8,128)(2,1)S(1)}, bf16[4,96,768]{2,1,0:T(8,128)(2,1)S(1)}, u32[]{:S(2)}, u32[]{:S(2)}) %collective-permute-start.22) | collective-permute-done | bytes 589856 | tf_op jit(solution)/shard_map/ppermute | solution.py:421
  163.9 1.0 collective-permute-done.23
  164.9 0.9 collective-permute-start.24
  166.0 1.1 pad_maximum_fusion
  167.1 4.6 %all-to-all-start.1 = ((bf16[4,192,768]{2,1,0:T(8,128)(2,1)}), bf16[4,192,768]{2,1,0:T(8,128)(2,1)}, u32[]{:S(2)}, u32[]{:S(2)}) async-start(bf16[4,192,768]{2,1,0:T(8,128)(2,1)} %pad_maximum_fusion), calls=%async_computation.1 | async-start | bytes 2359296 | tf_op jit(solution)/shard_map/all_to_all | solution.py:438
  171.8 6.5 %shard_map.326 = (bf16[4,96,768]{2,1,0:T(8,128)(2,1)}, bf16[4,96,768]{2,1,0:T(8,128)(2,1)}, bf16[1024,768]{1,0:T(8,128)(2,1)S(1)}, f32[1,576]{1,0:T(1,128)S(1)}) custom-call(s32[2]{0:T(128)S(1)} %pad_add_fusion.x_ref, bf16[3,1024,64]{2,1,0:T(8,128)(2,1)} %get-tuple-element.216.q_ref, bf16[3,1024,64]{2,1,0:T(8,128)(2,1)} %get-tuple-element.217.k_ref, ...), custom_call_target="tpu_custom_call" | custom-call | flops 1811939328 | bytes 10000000 | tf_op jit(solution)/shard_map/pallas_call | solution.py:709
  179.0 1.1 collective-permute-start.28
  180.2 1.6 collective-permute-done.25.g1_ref
  181.8 6.4 %shard_map.327 = (bf16[256,768]{1,0:T(8,128)(2,1)S(1)}, bf16[256,768]{1,0:T(8,128)(2,1)}, f32[2,4,8,96]{3,2,1,0:T(8,128)S(1)}, f32[2,4,16,96]{3,2,1,0:T(8,128)S(1)}, f32[8,768]{1,0:T(8,128)S(1)}) custom-call(s32[2]{0:T(128)S(1)} %pad_add_fusion.x_ref, bf16[512,768]{1,0:T(8,128)(2,1)} %copy-done.4, bf16[512,768]{1,0:T(8,128)(2,1)} %collective-permute-done.3.refs_1_.s1.c1, ...), custom_call_target="tpu_custom_call" | custom-call | tf_op jit(solution)/shard_map/pallas_call | solution.py:756
  188.2 1.1 collective-permute-start.26
  189.3 2.1 maximum_select_fusion
  191.4 2.9 %collective-permute-done.27 = bf16[4,96,768]{2,1,0:T(8,128)(2,1)} collective-permute-done((bf16[4,96,768]{2,1,0:T(8,128)(2,1)}, bf16[4,96,768]{2,1,0:T(8,128)(2,1)}, u32[]{:S(2)}, u32[]{:S(2)}) %collective-permute-start.27) | collective-permute-done | bytes 589856 | tf_op jit(solution)/shard_map/ppermute | solution.py:425
  194.3 1.0 collective-permute-done.28
  195.3 2.1 all-to-all-done.1
  197.4 1.0 collective-permute-start.29
  198.5 2.1 add_add_fusion
  200.7 3.6 %all-to-all-start.2 = ((bf16[4,96,768]{2,1,0:T(8,128)(2,1)}), bf16[4,96,768]{2,1,0:T(8,128)(2,1)S(1)}, u32[]{:S(2)}, u32[]{:S(2)}) async-start(bf16[4,96,768]{2,1,0:T(8,128)(2,1)} %add_add_fusion), calls=%async_computation.2 | async-start | bytes 1179648 | tf_op jit(solution)/shard_map/all_to_all | solution.py:438
  204.4 1.5 collective-permute-start.30
  205.9 1.5 convert_reduce_fusion
  208.8 2.1 collective-permute-start.31
  210.9 2.4 %collective-permute-start.32 = (f32[8,96]{1,0:T(8,128)S(1)}, f32[8,96]{1,0:T(8,128)S(1)}, u32[]{:S(2)}, u32[]{:S(2)}) collective-permute-start(f32[8,96]{1,0:T(8,128)S(1)} %get-tuple-element.269), channel_id=1, source_target_pairs={{0,16},{8,24},{16,0},{24,8},{1,17},{9,25},{17,1},{25,9},{2,18},{10... | collective-permute-start | bytes 9224 | tf_op jit(solution)/shard_map/ppermute | solution.py:786
  213.3 1.5 collective-permute-start.33
  214.7 1.0 maximum_select_fusion.1
  215.7 1.9 collective-permute-done.31.p1_ref
  217.7 2.2 collective-permute-done.32.p2_ref
  (79 shorter events, 11.4 us)
Async XLA Ops:
  0.7 47.9 %copy-start = (bf16[2,768]{1,0:T(2,128)(2,1)S(1)}, bf16[2,768]{1,0:T(2,128)(2,1)}, u32[]{:S(2)}) copy-start(bf16[2,768]{1,0:T(2,128)(2,1)} %param.19) | copy-start | bytes 9220
  0.7 10.5 %copy-start.5 = (bf16[2,256,768]{2,1,0:T(8,128)(2,1)S(1)}, bf16[2,256,768]{2,1,0:T(8,128)(2,1)}, u32[]{:S(2)}) copy-start(bf16[2,256,768]{2,1,0:T(8,128)(2,1)} %param.35) | copy-start | bytes 2359300
  3.0 10.3 %collective-permute-start.2 = (bf16[104,768]{1,0:T(8,128)(2,1)}, bf16[104,768]{1,0:T(8,128)(2,1)S(1)}, u32[]{:S(2)}, u32[]{:S(2)}) collective-permute-start(bf16[104,768]{1,0:T(8,128)(2,1)} %get-tuple-element.144), channel_id=1, source_target_pairs={{24,0},{0,8},{8,16},{16,24},{25,1},{1,9},{9,17},{17,25},{26,2},{2,... | collective-permute-start | bytes 479240 | tf_op jit(solution)/shard_map/ppermute | solution.py:433
  6.1 13.3 %collective-permute-start.1 = (bf16[104,768]{1,0:T(8,128)(2,1)}, bf16[104,768]{1,0:T(8,128)(2,1)S(1)}, u32[]{:S(2)}, u32[]{:S(2)}) collective-permute-start(bf16[104,768]{1,0:T(8,128)(2,1)} %get-tuple-element.144), channel_id=1, source_target_pairs={{16,0},{24,8},{0,16},{8,24},{17,1},{25,9},{1,17},{9,25},{18,2},{26... | collective-permute-start | bytes 479240 | tf_op jit(solution)/shard_map/ppermute | solution.py:433
  8.6 10.7 %collective-permute-start = (bf16[104,768]{1,0:T(8,128)(2,1)}, bf16[104,768]{1,0:T(8,128)(2,1)}, u32[]{:S(2)}, u32[]{:S(2)}) collective-permute-start(bf16[104,768]{1,0:T(8,128)(2,1)} %get-tuple-element.144), channel_id=1, source_target_pairs={{8,0},{16,8},{24,16},{0,24},{9,1},{17,9},{25,17},{1,25},{10,2},{18... | collective-permute-start | bytes 479240 | tf_op jit(solution)/shard_map/ppermute | solution.py:433
  11.3 8.1 %copy-start.10 = (bf16[104,768]{1,0:T(8,128)(2,1)S(1)}, bf16[104,768]{1,0:T(8,128)(2,1)}, u32[]{:S(2)}) copy-start(bf16[104,768]{1,0:T(8,128)(2,1)} %get-tuple-element.144) | copy-start | bytes 479236
  11.4 9.0 %copy-start.4 = (bf16[512,768]{1,0:T(8,128)(2,1)}, bf16[512,768]{1,0:T(8,128)(2,1)S(1)}, u32[]{:S(2)}) copy-start(bf16[512,768]{1,0:T(8,128)(2,1)S(1)} %get-tuple-element.265.refs_0_.s0.c0) | copy-start | bytes 2359300
  11.4 18.6 %collective-permute-start.3 = (bf16[512,768]{1,0:T(8,128)(2,1)S(1)}, bf16[512,768]{1,0:T(8,128)(2,1)}, u32[]{:S(2)}, u32[]{:S(2)}) collective-permute-start(bf16[512,768]{1,0:T(8,128)(2,1)S(1)} %get-tuple-element.264), channel_id=1, source_target_pairs={{0,2},{2,0},{1,3},{3,1},{4,6},{6,4},{5,7},{7,5},{8,10},{10,8},{9,1... | collective-permute-start | bytes 2359304 | tf_op jit(solution)/shard_map/ppermute | solution.py:421
  13.0 17.0 %collective-permute-start.4 = (bf16[512,768]{1,0:T(8,128)(2,1)S(1)}, bf16[512,768]{1,0:T(8,128)(2,1)}, u32[]{:S(2)}, u32[]{:S(2)}) collective-permute-start(bf16[512,768]{1,0:T(8,128)(2,1)S(1)} %get-tuple-element.265.refs_0_.s0.c0), channel_id=1, source_target_pairs={{0,1},{1,0},{2,3},{3,2},{4,5},{5,4},{6,7},{7,6},{8,9},{9,8},{10,11... | collective-permute-start | bytes 2359304 | tf_op jit(solution)/shard_map/ppermute | solution.py:429
  20.4 34.7 %all-to-all-start = ((bf16[4,192,768]{2,1,0:T(8,128)(2,1)}), bf16[4,192,768]{2,1,0:T(8,128)(2,1)}, u32[]{:S(2)}, u32[]{:S(2)}) async-start(bf16[4,192,768]{2,1,0:T(8,128)(2,1)} %get-tuple-element.153), calls=%async_computation | async-start | bytes 2359296 | tf_op jit(solution)/shard_map/all_to_all | solution.py:438
  30.0 14.4 %collective-permute-start.6 = (bf16[4,104,768]{2,1,0:T(8,128)(2,1)S(1)}, bf16[4,104,768]{2,1,0:T(8,128)(2,1)S(1)}, u32[]{:S(2)}, u32[]{:S(2)}) collective-permute-start(bf16[4,104,768]{2,1,0:T(8,128)(2,1)S(1)} %pad_maximum_fusion.1.refs_5_), channel_id=1, source_target_pairs={{0,4},{4,0},{1,5},{5,1},{2,6},{6,2},{3,7},{7,3},{8,12},{12,8},{9,1... | collective-permute-start | bytes 1916936 | tf_op jit(solution)/shard_map/ppermute | solution.py:425
  31.5 14.1 %collective-permute-start.7 = (bf16[4,104,768]{2,1,0:T(8,128)(2,1)S(1)}, bf16[4,104,768]{2,1,0:T(8,128)(2,1)S(1)}, u32[]{:S(2)}, u32[]{:S(2)}) collective-permute-start(bf16[4,104,768]{2,1,0:T(8,128)(2,1)S(1)} %pad_maximum_fusion.1.refs_5_), channel_id=1, source_target_pairs={{0,2},{2,0},{1,3},{3,1},{4,6},{6,4},{5,7},{7,5},{8,10},{10,8},{9,1... | collective-permute-start | bytes 1916936 | tf_op jit(solution)/shard_map/ppermute | solution.py:421
  33.0 15.5 %collective-permute-start.5 = (bf16[512,768]{1,0:T(8,128)(2,1)}, bf16[512,768]{1,0:T(8,128)(2,1)}, u32[]{:S(2)}, u32[]{:S(2)}) collective-permute-start(bf16[512,768]{1,0:T(8,128)(2,1)} %collective-permute-done.3.refs_1_.s1.c1), channel_id=1, source_target_pairs={{0,1},{1,0},{2,3},{3,2},{4,5},{5,4},{6,7},{7,6},{8,9},{9,8},{10,11... | collective-permute-start | bytes 2359304 | tf_op jit(solution)/shard_map/ppermute | solution.py:429
  46.3 8.7 %collective-permute-start.9 = (bf16[4,56,768]{2,1,0:T(8,128)(2,1)}, bf16[4,56,768]{2,1,0:T(8,128)(2,1)S(1)}, u32[]{:S(2)}, u32[]{:S(2)}) collective-permute-start(bf16[4,56,768]{2,1,0:T(8,128)(2,1)} %slice.34), channel_id=1, source_target_pairs={{0,4},{4,0},{1,5},{5,1},{2,6},{6,2},{3,7},{7,3},{8,12},{12,8},{9,1... | collective-permute-start | bytes 1032200 | tf_op jit(solution)/shard_map/ppermute | solution.py:425
  46.9 7.5 %collective-permute-start.8 = (bf16[4,48,768]{2,1,0:T(8,128)(2,1)S(1)}, bf16[4,48,768]{2,1,0:T(8,128)(2,1)S(1)}, u32[]{:S(2)}, u32[]{:S(2)}) collective-permute-start(bf16[4,48,768]{2,1,0:T(8,128)(2,1)S(1)} %slice.33), channel_id=1, source_target_pairs={{0,2},{2,0},{1,3},{3,1},{4,6},{6,4},{5,7},{7,5},{8,10},{10,8},{9,1... | collective-permute-start | bytes 884744 | tf_op jit(solution)/shard_map/ppermute | solution.py:421
  54.4 0.7 copy-start.2
  55.1 10.4 %copy-start.3 = (bf16[4,48,768]{2,1,0:T(8,128)(2,1)S(1)}, bf16[4,48,768]{2,1,0:T(8,128)(2,1)}, u32[]{:S(2)}) copy-start(bf16[4,48,768]{2,1,0:T(8,128)(2,1)} %copy-done.2) | copy-start | bytes 884740
  55.1 26.5 %collective-permute-start.10 = (bf16[4,192,768]{2,1,0:T(8,128)(2,1)}, bf16[4,192,768]{2,1,0:T(8,128)(2,1)S(1)}, u32[]{:S(2)}, u32[]{:S(2)}) collective-permute-start(bf16[4,192,768]{2,1,0:T(8,128)(2,1)} %all-to-all-done.w_oo), channel_id=1, source_target_pairs={{0,4},{4,0},{1,5},{5,1},{2,6},{6,2},{3,7},{7,3},{8,12},{12,8},{9,1... | collective-permute-start | bytes 3538952 | tf_op jit(solution)/shard_map/ppermute | solution.py:425
  56.6 26.2 %collective-permute-start.11 = (bf16[4,192,768]{2,1,0:T(8,128)(2,1)}, bf16[4,192,768]{2,1,0:T(8,128)(2,1)S(1)}, u32[]{:S(2)}, u32[]{:S(2)}) collective-permute-start(bf16[4,192,768]{2,1,0:T(8,128)(2,1)} %all-to-all-done.w_oo), channel_id=1, source_target_pairs={{0,2},{2,0},{1,3},{3,1},{4,6},{6,4},{5,7},{7,5},{8,10},{10,8},{9,1... | collective-permute-start | bytes 3538952 | tf_op jit(solution)/shard_map/ppermute | solution.py:421
  84.8 3.5 %collective-permute-start.12 = (bf16[1024,768]{1,0:T(8,128)(2,1)S(1)}, bf16[1024,768]{1,0:T(8,128)(2,1)S(1)}, u32[]{:S(2)}, u32[]{:S(2)}) collective-permute-start(bf16[1024,768]{1,0:T(8,128)(2,1)S(1)} %shard_map.318.a0_ref), channel_id=1, source_target_pairs={{0,1},{1,0},{2,3},{3,2},{4,5},{5,4},{6,7},{7,6},{8,9},{9,8},{10,11... | collective-permute-start | bytes 4718600 | tf_op jit(solution)/shard_map/ppermute | solution.py:429
  84.9 15.8 %collective-permute-start.13 = (bf16[4,96,768]{2,1,0:T(8,128)(2,1)S(1)}, bf16[4,96,768]{2,1,0:T(8,128)(2,1)S(1)}, u32[]{:S(2)}, u32[]{:S(2)}) collective-permute-start(bf16[4,96,768]{2,1,0:T(8,128)(2,1)S(1)} %slice.35), channel_id=1, source_target_pairs={{0,2},{2,0},{1,3},{3,1},{4,6},{6,4},{5,7},{7,5},{8,10},{10,8},{9,1... | collective-permute-start | bytes 1769480 | tf_op jit(solution)/shard_map/ppermute | solution.py:421
  86.5 15.5 %collective-permute-start.14 = (bf16[4,96,768]{2,1,0:T(8,128)(2,1)S(1)}, bf16[4,96,768]{2,1,0:T(8,128)(2,1)S(1)}, u32[]{:S(2)}, u32[]{:S(2)}) collective-permute-start(bf16[4,96,768]{2,1,0:T(8,128)(2,1)S(1)} %slice.36), channel_id=1, source_target_pairs={{0,4},{4,0},{1,5},{5,1},{2,6},{6,2},{3,7},{7,3},{8,12},{12,8},{9,1... | collective-permute-start | bytes 1769480 | tf_op jit(solution)/shard_map/ppermute | solution.py:425
  102.0 14.6 %collective-permute-start.16 = (bf16[4,96,768]{2,1,0:T(8,128)(2,1)S(1)}, bf16[4,96,768]{2,1,0:T(8,128)(2,1)S(1)}, u32[]{:S(2)}, u32[]{:S(2)}) collective-permute-start(bf16[4,96,768]{2,1,0:T(8,128)(2,1)S(1)} %get-tuple-element.185), channel_id=1, source_target_pairs={{0,4},{4,0},{1,5},{5,1},{2,6},{6,2},{3,7},{7,3},{8,12},{12,8},{9,1... | collective-permute-start | bytes 1769480 | tf_op jit(solution)/shard_map/ppermute | solution.py:425
  116.7 5.9 %collective-permute-start.17 = (bf16[1024,768]{1,0:T(8,128)(2,1)S(1)}, bf16[1024,768]{1,0:T(8,128)(2,1)S(1)}, u32[]{:S(2)}, u32[]{:S(2)}) collective-permute-start(bf16[1024,768]{1,0:T(8,128)(2,1)S(1)} %get-tuple-element.186.g0_ref), channel_id=1, source_target_pairs={{0,1},{1,0},{2,3},{3,2},{4,5},{5,4},{6,7},{7,6},{8,9},{9,8},{10,11... | collective-permute-start | bytes 4718600 | tf_op jit(solution)/shard_map/ppermute | solution.py:429
  116.7 4.5 %collective-permute-start.15 = (bf16[512,768]{1,0:T(8,128)(2,1)S(1)}, bf16[512,768]{1,0:T(8,128)(2,1)S(1)}, u32[]{:S(2)}, u32[]{:S(2)}) collective-permute-start(bf16[512,768]{1,0:T(8,128)(2,1)S(1)} %get-tuple-element.179), channel_id=1, source_target_pairs={{0,1},{1,0},{2,3},{3,2},{4,5},{5,4},{6,7},{7,6},{8,9},{9,8},{10,11... | collective-permute-start | bytes 2359304 | tf_op jit(solution)/shard_map/ppermute | solution.py:429
  117.2 15.2 %collective-permute-start.18 = (bf16[4,96,768]{2,1,0:T(8,128)(2,1)S(1)}, bf16[4,96,768]{2,1,0:T(8,128)(2,1)S(1)}, u32[]{:S(2)}, u32[]{:S(2)}) collective-permute-start(bf16[4,96,768]{2,1,0:T(8,128)(2,1)S(1)} %get-tuple-element.192), channel_id=1, source_target_pairs={{0,4},{4,0},{1,5},{5,1},{2,6},{6,2},{3,7},{7,3},{8,12},{12,8},{9,1... | collective-permute-start | bytes 1769480 | tf_op jit(solution)/shard_map/ppermute | solution.py:425
  117.7 15.0 %collective-permute-start.19 = (bf16[4,96,768]{2,1,0:T(8,128)(2,1)S(1)}, bf16[4,96,768]{2,1,0:T(8,128)(2,1)S(1)}, u32[]{:S(2)}, u32[]{:S(2)}) collective-permute-start(bf16[4,96,768]{2,1,0:T(8,128)(2,1)S(1)} %get-tuple-element.193), channel_id=1, source_target_pairs={{0,2},{2,0},{1,3},{3,1},{4,6},{6,4},{5,7},{7,5},{8,10},{10,8},{9,1... | collective-permute-start | bytes 1769480 | tf_op jit(solution)/shard_map/ppermute | solution.py:421
  132.8 17.5 %collective-permute-start.20 = (bf16[4,96,768]{2,1,0:T(8,128)(2,1)S(1)}, bf16[4,96,768]{2,1,0:T(8,128)(2,1)S(1)}, u32[]{:S(2)}, u32[]{:S(2)}) collective-permute-start(bf16[4,96,768]{2,1,0:T(8,128)(2,1)S(1)} %add.80), channel_id=1, source_target_pairs={{0,2},{2,0},{1,3},{3,1},{4,6},{6,4},{5,7},{7,5},{8,10},{10,8},{9,1... | collective-permute-start | bytes 1769480 | tf_op jit(solution)/shard_map/ppermute | solution.py:421
  134.0 16.4 %collective-permute-start.21 = (bf16[4,96,768]{2,1,0:T(8,128)(2,1)S(1)}, bf16[4,96,768]{2,1,0:T(8,128)(2,1)S(1)}, u32[]{:S(2)}, u32[]{:S(2)}) collective-permute-start(bf16[4,96,768]{2,1,0:T(8,128)(2,1)S(1)} %add.81), channel_id=1, source_target_pairs={{0,4},{4,0},{1,5},{5,1},{2,6},{6,2},{3,7},{7,3},{8,12},{12,8},{9,1... | collective-permute-start | bytes 1769480 | tf_op jit(solution)/shard_map/ppermute | solution.py:425
  150.3 13.6 %collective-permute-start.22 = (bf16[4,96,768]{2,1,0:T(8,128)(2,1)S(1)}, bf16[4,96,768]{2,1,0:T(8,128)(2,1)S(1)}, u32[]{:S(2)}, u32[]{:S(2)}) collective-permute-start(bf16[4,96,768]{2,1,0:T(8,128)(2,1)S(1)} %get-tuple-element.213), channel_id=1, source_target_pairs={{0,2},{2,0},{1,3},{3,1},{4,6},{6,4},{5,7},{7,5},{8,10},{10,8},{9,1... | collective-permute-start | bytes 1769480 | tf_op jit(solution)/shard_map/ppermute | solution.py:421
  151.5 13.4 %collective-permute-start.23 = (bf16[4,96,768]{2,1,0:T(8,128)(2,1)}, bf16[4,96,768]{2,1,0:T(8,128)(2,1)S(1)}, u32[]{:S(2)}, u32[]{:S(2)}) collective-permute-start(bf16[4,96,768]{2,1,0:T(8,128)(2,1)} %get-tuple-element.214), channel_id=1, source_target_pairs={{0,4},{4,0},{1,5},{5,1},{2,6},{6,2},{3,7},{7,3},{8,12},{12,8},{9,1... | collective-permute-start | bytes 1769480 | tf_op jit(solution)/shard_map/ppermute | solution.py:425
  164.9 1.0 copy-start.7
  164.9 13.3 %collective-permute-start.24 = (bf16[256,768]{1,0:T(8,128)(2,1)}, bf16[256,768]{1,0:T(8,128)(2,1)}, u32[]{:S(2)}, u32[]{:S(2)}) collective-permute-start(bf16[256,768]{1,0:T(8,128)(2,1)} %get-tuple-element.222), channel_id=1, source_target_pairs={{0,2},{2,0},{1,3},{3,1},{4,6},{6,4},{5,7},{7,5},{8,10},{10,8},{9,1... | collective-permute-start | bytes 1179656 | tf_op jit(solution)/shard_map/ppermute | solution.py:421
  167.1 30.3 %all-to-all-start.1 = ((bf16[4,192,768]{2,1,0:T(8,128)(2,1)}), bf16[4,192,768]{2,1,0:T(8,128)(2,1)}, u32[]{:S(2)}, u32[]{:S(2)}) async-start(bf16[4,192,768]{2,1,0:T(8,128)(2,1)} %pad_maximum_fusion), calls=%async_computation.1 | async-start | bytes 2359296 | tf_op jit(solution)/shard_map/all_to_all | solution.py:438
  171.7 7.2 %copy-start.6 = (bf16[4,96,768]{2,1,0:T(8,128)(2,1)S(1)}, bf16[4,96,768]{2,1,0:T(8,128)(2,1)}, u32[]{:S(2)}) copy-start(bf16[4,96,768]{2,1,0:T(8,128)(2,1)} %get-tuple-element.235) | copy-start | bytes 1769476
  171.8 7.2 %copy-start.8 = (bf16[4,96,768]{2,1,0:T(8,128)(2,1)S(1)}, bf16[4,96,768]{2,1,0:T(8,128)(2,1)}, u32[]{:S(2)}) copy-start(bf16[4,96,768]{2,1,0:T(8,128)(2,1)} %copy-done.7) | copy-start | bytes 1769476
  178.2 3.5 %collective-permute-start.25 = (bf16[1024,768]{1,0:T(8,128)(2,1)S(1)}, bf16[1024,768]{1,0:T(8,128)(2,1)}, u32[]{:S(2)}, u32[]{:S(2)}) collective-permute-start(bf16[1024,768]{1,0:T(8,128)(2,1)S(1)} %get-tuple-element.224.g0_ref), channel_id=1, source_target_pairs={{0,1},{1,0},{2,3},{3,2},{4,5},{5,4},{6,7},{7,6},{8,9},{9,8},{10,11... | collective-permute-start | bytes 4718600 | tf_op jit(solution)/shard_map/ppermute | solution.py:429
  178.2 16.1 %collective-permute-start.27 = (bf16[4,96,768]{2,1,0:T(8,128)(2,1)}, bf16[4,96,768]{2,1,0:T(8,128)(2,1)}, u32[]{:S(2)}, u32[]{:S(2)}) collective-permute-start(bf16[4,96,768]{2,1,0:T(8,128)(2,1)} %get-tuple-element.234), channel_id=1, source_target_pairs={{0,4},{4,0},{1,5},{5,1},{2,6},{6,2},{3,7},{7,3},{8,12},{12,8},{9,1... | collective-permute-start | bytes 1769480 | tf_op jit(solution)/shard_map/ppermute | solution.py:425
  179.0 16.3 %collective-permute-start.28 = (bf16[4,96,768]{2,1,0:T(8,128)(2,1)S(1)}, bf16[4,96,768]{2,1,0:T(8,128)(2,1)}, u32[]{:S(2)}, u32[]{:S(2)}) collective-permute-start(bf16[4,96,768]{2,1,0:T(8,128)(2,1)S(1)} %add.82), channel_id=1, source_target_pairs={{0,2},{2,0},{1,3},{3,1},{4,6},{6,4},{5,7},{7,5},{8,10},{10,8},{9,1... | collective-permute-start | bytes 1769480 | tf_op jit(solution)/shard_map/ppermute | solution.py:421
  188.2 10.4 %copy-start.9 = (bf16[4,96,768]{2,1,0:T(8,128)(2,1)S(1)}, bf16[4,96,768]{2,1,0:T(8,128)(2,1)}, u32[]{:S(2)}) copy-start(bf16[4,96,768]{2,1,0:T(8,128)(2,1)} %get-tuple-element.246) | copy-start | bytes 1769476
  188.2 9.2 %collective-permute-start.26 = (f32[2,4,16,96]{3,2,1,0:T(8,128)S(1)}, f32[2,4,16,96]{3,2,1,0:T(8,128)S(1)}, u32[]{:S(2)}, u32[]{:S(2)}) collective-permute-start(f32[2,4,16,96]{3,2,1,0:T(8,128)S(1)} %get-tuple-element.232), channel_id=1, source_target_pairs={{0,2},{2,0},{1,3},{3,1},{4,6},{6,4},{5,7},{7,5},{8,10},{10,8},{9,1... | collective-permute-start | bytes 147464 | tf_op jit(solution)/shard_map/ppermute | solution.py:421
  197.4 17.3 %collective-permute-start.29 = (bf16[256,768]{1,0:T(8,128)(2,1)}, bf16[256,768]{1,0:T(8,128)(2,1)S(1)}, u32[]{:S(2)}, u32[]{:S(2)}) collective-permute-start(bf16[256,768]{1,0:T(8,128)(2,1)} %get-tuple-element.243), channel_id=1, source_target_pairs={{0,2},{2,0},{1,3},{3,1},{4,6},{6,4},{5,7},{7,5},{8,10},{10,8},{9,1... | collective-permute-start | bytes 1179656 | tf_op jit(solution)/shard_map/ppermute | solution.py:421
  200.7 19.2 %all-to-all-start.2 = ((bf16[4,96,768]{2,1,0:T(8,128)(2,1)}), bf16[4,96,768]{2,1,0:T(8,128)(2,1)S(1)}, u32[]{:S(2)}, u32[]{:S(2)}) async-start(bf16[4,96,768]{2,1,0:T(8,128)(2,1)} %add_add_fusion), calls=%async_computation.2 | async-start | bytes 1179648 | tf_op jit(solution)/shard_map/all_to_all | solution.py:438
  204.4 4.4 %collective-permute-start.30 = (f32[4,8,96]{2,1,0:T(8,128)S(1)}, f32[4,8,96]{2,1,0:T(8,128)S(1)}, u32[]{:S(2)}, u32[]{:S(2)}) collective-permute-start(f32[4,8,96]{2,1,0:T(8,128)S(1)} %slice_bitcast_fusion.1), channel_id=1, source_target_pairs={{0,4},{4,0},{1,5},{5,1},{2,6},{6,2},{3,7},{7,3},{8,12},{12,8},{9,1... | collective-permute-start | bytes 36872 | tf_op jit(solution)/shard_map/ppermute | solution.py:425
  205.9 14.9 %copy-start.1 = (bf16[2,768]{1,0:T(2,128)(2,1)S(1)}, bf16[2,768]{1,0:T(2,128)(2,1)}, u32[]{:S(2)}) copy-start(bf16[2,768]{1,0:T(2,128)(2,1)} %param.19) | copy-start | bytes 9220
  208.8 8.8 %collective-permute-start.31 = (f32[8,96]{1,0:T(8,128)S(1)}, f32[8,96]{1,0:T(8,128)S(1)}, u32[]{:S(2)}, u32[]{:S(2)}) collective-permute-start(f32[8,96]{1,0:T(8,128)S(1)} %get-tuple-element.270), channel_id=1, source_target_pairs={{0,8},{8,16},{16,24},{24,0},{1,9},{9,17},{17,25},{25,1},{2,10},{10... | collective-permute-start | bytes 9224 | tf_op jit(solution)/shard_map/ppermute | solution.py:786
  210.9 9.0 %collective-permute-start.32 = (f32[8,96]{1,0:T(8,128)S(1)}, f32[8,96]{1,0:T(8,128)S(1)}, u32[]{:S(2)}, u32[]{:S(2)}) collective-permute-start(f32[8,96]{1,0:T(8,128)S(1)} %get-tuple-element.269), channel_id=1, source_target_pairs={{0,16},{8,24},{16,0},{24,8},{1,17},{9,25},{17,1},{25,9},{2,18},{10... | collective-permute-start | bytes 9224 | tf_op jit(solution)/shard_map/ppermute | solution.py:786
  213.3 6.6 %collective-permute-start.33 = (f32[8,96]{1,0:T(8,128)S(1)}, f32[8,96]{1,0:T(8,128)S(1)}, u32[]{:S(2)}, u32[]{:S(2)}) collective-permute-start(f32[8,96]{1,0:T(8,128)S(1)} %get-tuple-element.268), channel_id=1, source_target_pairs={{0,24},{8,0},{16,8},{24,16},{1,25},{9,1},{17,9},{25,17},{2,26},{10... | collective-permute-start | bytes 9224 | tf_op jit(solution)/shard_map/ppermute | solution.py:786

commit v7 on v6

--- a/solution.py
+++ b/solution.py
@@ -17,7 +17,7 @@
 KINDS = 8
 HINT = 1.0
 TILE_PROJECT = 512
-TILE_OUT = 256
+TILE_OUT = 512
 TILE_MLP = 512
 TILE_SECOND = 512
 TILE_BACK = 1024
@@ -113,10 +113,10 @@
 def project_body(x_ref, *refs, rows, first):
     refs = list(refs)
     if first:
-        *tokens, te_ref, own_ref, oth_ref, w_ref, vec_ref, qkv_ref, normed_ref, normed_t_ref, bias_ref = refs
+        *tokens, te_ref, own_ref, oth_ref, w_ref, vec_ref, qkv_ref, normed_ref, bias_ref = refs
         oth_refs = (oth_ref,)
     else:
-        source_ref, own_ref, *oth_refs, w_ref, vec_ref, qkv_ref, bias_ref = refs
+        source_ref, own_ref, *oth_refs, w_ref, vec_ref, qkv_ref, normed_t_ref, bias_ref = refs
 
     @pl.when(pl.program_id(0) == 0)
     def _():
@@ -144,9 +144,9 @@
         xhat, _ = normalize(pick(tokens).astype(F32) + te_ref[...].astype(F32))
         normed = (xhat * vec_ref[0:1, :] + vec_ref[1:2, :]).astype(BF)
         normed_ref[...] = normed
-        normed_t_ref[...] = normed.T
     else:
         normed = source_ref[...]
+        normed_t_ref[...] = normed.T
     made = dot(normed, w_ref[:, :640])[:, :576] + bias_ref[0:1, :]
     made = made.astype(BF)
     for j in range(9):
@@ -561,10 +561,9 @@
             (pltpu.HBM((9, seq, HD), BF), pl.BlockSpec((9, tile, HD), lambda i: (0, i, 0))),
         ]
         if first:
-            outs += [
-                (pltpu.HBM((seq, width), BF), by(tile)),
-                (pltpu.HBM((width, seq), BF), pl.BlockSpec((width, tile), lambda i: (0, i))),
-            ]
+            outs += [(pltpu.HBM((seq, width), BF), by(tile))]
+        else:
+            outs += [(pltpu.HBM((width, seq), BF), pl.BlockSpec((width, tile), lambda i: (0, i)))]
         return call(
             functools.partial(project_body, rows=rows, first=first),
             (seq // tile,),
@@ -609,18 +608,15 @@
             moved=9e6,
         )(*[far(qkv)] * 3, far(expon), inverse, far(mixed), grad_mixed)
 
-    w_o, vec, qkv_o, normed, normed_t = project(True, (*tokens, te), attn_oo, attn_ox)
+    w_o, vec, qkv_o, normed = project(True, (*tokens, te), attn_oo, attn_ox)
     qkv_o, attn_yx, mlp_oo = lax.optimization_barrier((qkv_o, attn_yx, mlp_oo))
     mlp_yo = to_y(mlp_oo)
     if fast:
         mlp_ox = to_x(mlp_oo)
     exp_o, inv_o, mixed_o, wide_o = attend(qkv_o)
     normed, exp_o = lax.optimization_barrier((normed, exp_o))
-    w_y, vec_y, qkv_y = project(False, (far(normed),), attn_yo, *attn_yx)
+    w_y, vec_y, qkv_y, normed_t = project(False, (far(normed),), attn_yo, *attn_yx)
     exp_y, inv_y, mixed_y, wide_y = attend(qkv_y)
-    mixed_y, mlp_ox, mlp_yo = lax.optimization_barrier((mixed_y, mlp_ox, mlp_yo))
-    h_yx = to_y(mlp_ox[:, :rows])
-    d_yx = to_x(mlp_yo[:, rows:]) if fast else to_y(mlp_ox[:, rows:])
 
     tile = TILE_OUT
     half_t = pl.BlockSpec((3 * HD, tile), lambda i: (0, i))
@@ -634,7 +630,10 @@
         flops=2 * seq * width * 384,
         moved=6e6,
     )(flat_o, flat_y, w_o, w_y)
+    attended, mlp_ox, mlp_yo = lax.optimization_barrier((attended, mlp_ox, mlp_yo))
     attended_mate = to_core(attended)
+    h_yx = to_y(mlp_ox[:, :rows])
+    d_yx = to_x(mlp_yo[:, rows:]) if fast else to_y(mlp_ox[:, rows:])
 
     tile = TILE_MLP
     part = (ZS, rows, hidden)

time: 222 us -> 219 us (0.986)
  transfers between devices with their start and end apart: 37 -> 37, of which waited for: 22 -> 22; matrix products, arithmetic and copies ran while one was open for 6% -> 6% of each run, Pallas kernels for 43% -> 44%
where the time goes in v7:
time: 219 us
  Pallas kernels  98.7 us (45%)
  waiting for transfers between devices  52.5 us (24%)
  starting transfers between devices  52.2 us (24%)
  other arithmetic  10.2 us (5%)
  local copies, waits for them, and re-layouts  3.93 us (2%)
    ppermute x10, waiting for transfers between devices, to_x(): return lax.ppermute(values, 'b', swap(2))  24.8 us
    pallas_call x2, Pallas kernels, attend_back(): call(attend_back_body, (3,), [q_spec, k_spec, v_spec, e_spec, inv_spec, t...  17.7 us
    pallas_call x2, Pallas kernels, attend(): call(attend_body, (3,), [q_spec, k_spec, v_spec], [(pltpu.HBM((3, seq, se...  16.1 us
    ppermute x12, starting transfers between devices, to_y(): return lax.ppermute(values, 'y', swap(2))  14.8 us
    all_to_all x3, starting transfers between devices, spread_z(): return lax.all_to_all(values, 'a', 0, 0, tiled=True)  14.5 us
    pallas_call x2, Pallas kernels, project_back(): call(functools.partial(project_back_body, rows=rows, more=more), (seq //...  12.5 us
    pallas_call x1, Pallas kernels, body(): call(functools.partial(mlp_first_body, rows=rows), (seq // tile,), [scala...  12.2 us
    pallas_call x1, Pallas kernels, body(): call(functools.partial(mlp_second_body, rows=rows), (seq // tile,), [scal...  10.2 us
  transfers between devices with their start and end apart: 37, of which 22 were waited for; matrix products, arithmetic and copies ran while one was open for 6% of the time, Pallas kernels for 44%

profile of v7, /device:TPU:0, one launch (start us, length us, event | category | flops | bytes accessed | tf_op | source)
XLA Modules:
  0.0 218.7 jit_solution(17538864639321075533)
XLA Ops:
  0.7 2.3 %shard_map.313 = (bf16[104,768]{1,0:T(8,128)(2,1)}, bf16[4,192,768]{2,1,0:T(8,128)(2,1)}) custom-call(bf16[96,192]{1,0:T(8,128)(2,1)} %q_ref.1, bf16[96,192]{1,0:T(8,128)(2,1)} %k_ref.1, bf16[96,192]{1,0:T(8,128)(2,1)} %v_ref.1, bf16[192,96]{1,0:T(8,128)(2,1)} %o_ref.1, bf16[96,768]{1,0:T(8,128)(2,1)} %h_ref.1, bf16[96,768]{1,0:T(8,128)(2,1)} %bitcast.68, ...), custom_call_target="tpu_custom_call" | custom-call | flops 1000000 | bytes 2000000 | tf_op jit(solution)/shard_map/pallas_call | solution.py:473
  3.0 3.0 %collective-permute-start.2 = (bf16[104,768]{1,0:T(8,128)(2,1)}, bf16[104,768]{1,0:T(8,128)(2,1)S(1)}, u32[]{:S(2)}, u32[]{:S(2)}) collective-permute-start(bf16[104,768]{1,0:T(8,128)(2,1)} %get-tuple-element.144), channel_id=1, source_target_pairs={{24,0},{0,8},{8,16},{16,24},{25,1},{1,9},{9,17},{17,25},{26,2},{2,... | collective-permute-start | bytes 479240 | tf_op jit(solution)/shard_map/ppermute | solution.py:433
  6.1 2.6 %collective-permute-start.1 = (bf16[104,768]{1,0:T(8,128)(2,1)}, bf16[104,768]{1,0:T(8,128)(2,1)S(1)}, u32[]{:S(2)}, u32[]{:S(2)}) collective-permute-start(bf16[104,768]{1,0:T(8,128)(2,1)} %get-tuple-element.144), channel_id=1, source_target_pairs={{16,0},{24,8},{0,16},{8,24},{17,1},{25,9},{1,17},{9,25},{18,2},{26... | collective-permute-start | bytes 479240 | tf_op jit(solution)/shard_map/ppermute | solution.py:433
  8.6 1.3 collective-permute-start
  10.0 1.2 constant_dynamic-update-slice_fusion.1
  11.4 1.6 collective-permute-start.3
  13.3 6.0 %collective-permute-done.1 = bf16[104,768]{1,0:T(8,128)(2,1)S(1)} collective-permute-done((bf16[104,768]{1,0:T(8,128)(2,1)}, bf16[104,768]{1,0:T(8,128)(2,1)S(1)}, u32[]{:S(2)}, u32[]{:S(2)}) %collective-permute-start.1) | collective-permute-done | bytes 159776 | tf_op jit(solution)/shard_map/ppermute | solution.py:433
  19.3 1.0 pad_maximum_fusion.1.refs_5_
  20.4 6.2 %all-to-all-start = ((bf16[4,192,768]{2,1,0:T(8,128)(2,1)}), bf16[4,192,768]{2,1,0:T(8,128)(2,1)}, u32[]{:S(2)}, u32[]{:S(2)}) async-start(bf16[4,192,768]{2,1,0:T(8,128)(2,1)} %get-tuple-element.153), calls=%async_computation | async-start | bytes 2359296 | tf_op jit(solution)/shard_map/all_to_all | solution.py:438
  26.6 3.4 %collective-permute-done.3.refs_1_.s1.c1 = bf16[512,768]{1,0:T(8,128)(2,1)} collective-permute-done((bf16[512,768]{1,0:T(8,128)(2,1)S(1)}, bf16[512,768]{1,0:T(8,128)(2,1)}, u32[]{:S(2)}, u32[]{:S(2)}) %collective-permute-start.3) | collective-permute-done | bytes 786464 | tf_op jit(solution)/shard_map/ppermute | solution.py:421
  30.0 1.5 collective-permute-start.6
  31.5 1.5 collective-permute-start.7
  33.0 11.3 %collective-permute-done.6.refs_6_ = bf16[4,104,768]{2,1,0:T(8,128)(2,1)S(1)} collective-permute-done((bf16[4,104,768]{2,1,0:T(8,128)(2,1)S(1)}, bf16[4,104,768]{2,1,0:T(8,128)(2,1)S(1)}, u32[]{:S(2)}, u32[]{:S(2)}) %collective-permute-start.6) | collective-permute-done | bytes 639008 | tf_op jit(solution)/shard_map/ppermute | solution.py:425
  44.4 1.2 collective-permute-done.7.refs_1_
  46.9 1.6 collective-permute-start.8
  48.6 5.4 %shard_map.314 = (bf16[768,768]{1,0:T(8,128)(2,1)S(1)}, f32[8,768]{1,0:T(8,128)S(1)}, bf16[9,1024,64]{2,1,0:T(8,128)(2,1)}, bf16[1024,768]{1,0:T(8,128)(2,1)}) custom-call(s32[2]{0:T(128)S(1)} %pad_add_fusion.x_ref, bf16[512,768]{1,0:T(8,128)(2,1)} %copy-done.4, bf16[512,768]{1,0:T(8,128)(2,1)} %collective-permute-done.3.refs_1_.s1.c1, ...), custom_call_target="tpu_custom_call" | custom-call | flops 905969664 | bytes 8000000 | tf_op jit(solution)/shard_map/pallas_call | solution.py:567
  54.7 1.6 collective-permute-start.10
  56.2 1.2 collective-permute-start.11
  57.5 8.0 %shard_map.315 = (bf16[3,1024,1024]{2,1,0:T(8,128)(2,1)}, f32[3,1,1024]{2,1,0:T(1,128)S(1)}, bf16[3,64,1024]{2,1,0:T(8,128)(2,1)S(1)}, f32[3,64,1024]{2,1,0:T(8,128)}) custom-call(bf16[9,1024,64]{2,1,0:T(8,128)(2,1)} %get-tuple-element.154.q_ref.k_ref.v_ref, bf16[9,1024,64]{2,1,0:T(8,128)(2,1)} %get-tuple-element.154.q_ref.k_ref.v_ref, ...), custom_call_target="tpu_custom_call" | custom-call | flops 3221225472 | bytes 8000000 | tf_op jit(solution)/shard_map/pallas_call | solution.py:585
  65.5 4.3 %shard_map.316 = (bf16[768,768]{1,0:T(8,128)(2,1)S(1)}, f32[8,768]{1,0:T(8,128)S(1)}, bf16[9,1024,64]{2,1,0:T(8,128)(2,1)}, bf16[768,1024]{1,0:T(8,128)(2,1)}) custom-call(s32[2]{0:T(128)S(1)} %pad_add_fusion.x_ref, bf16[1024,768]{1,0:T(8,128)(2,1)} %get-tuple-element.158.refs_0_, bf16[4,104,768]{2,1,0:T(8,128)(2,1)S(1)} %collective-permute-done.7.refs_1_, ...), custom_call_target="tpu_custom_call" | custom-call | flops 905969664 | bytes 8000000 | tf_op jit(solution)/shard_map/pallas_call | solution.py:567
  69.8 8.1 %shard_map.317 = (bf16[3,1024,1024]{2,1,0:T(8,128)(2,1)}, f32[3,1,1024]{2,1,0:T(1,128)S(1)}, bf16[3,64,1024]{2,1,0:T(8,128)(2,1)S(1)}, f32[3,64,1024]{2,1,0:T(8,128)}) custom-call(bf16[9,1024,64]{2,1,0:T(8,128)(2,1)} %get-tuple-element.161.q_ref.k_ref.v_ref, bf16[9,1024,64]{2,1,0:T(8,128)(2,1)} %get-tuple-element.161.q_ref.k_ref.v_ref, ...), custom_call_target="tpu_custom_call" | custom-call | flops 3221225472 | bytes 8000000 | tf_op jit(solution)/shard_map/pallas_call | solution.py:585
  77.9 1.5 shard_map.318.a0_ref
  79.4 2.2 collective-permute-done.10.w_ox
  81.6 1.2 collective-permute-done.11.w_yo
  82.9 1.6 collective-permute-start.13
  85.1 1.1 collective-permute-done.12.a1_ref
  86.2 12.2 %shard_map.319 = (f32[1024,768]{1,0:T(8,128)S(1)}, bf16[1024,768]{1,0:T(8,128)(2,1)S(1)}, f32[1024,768]{1,0:T(8,128)S(1)}, f32[1024,768]{1,0:T(8,128)S(1)}, f32[...) custom-call(s32[2]{0:T(128)S(1)} %pad_add_fusion.x_ref, ...), custom_call_target="tpu_custom_call" | custom-call | flops 7247757312 | bytes 16000000 | tf_op jit(solution)/shard_map/pallas_call | solution.py:643
  98.7 1.3 collective-permute-done.14.d_yx
  100.5 10.2 %shard_map.320 = (bf16[512,768]{1,0:T(8,128)(2,1)S(1)}, bf16[512,768]{1,0:T(8,128)(2,1)S(1)}, bf16[1024,768]{1,0:T(8,128)(2,1)S(1)}, f32[1,768]{1,0:T(1,128)S(1)...) custom-call(s32[2]{0:T(128)S(1)} %pad_add_fusion.x_ref, ...), custom_call_target="tpu_custom_call" | custom-call | flops 7247757312 | bytes 16000000 | tf_op jit(solution)/shard_map/pallas_call | solution.py:661
  110.8 3.9 %collective-permute-done.16 = bf16[4,96,768]{2,1,0:T(8,128)(2,1)S(1)} collective-permute-done((bf16[4,96,768]{2,1,0:T(8,128)(2,1)S(1)}, bf16[4,96,768]{2,1,0:T(8,128)(2,1)S(1)}, u32[]{:S(2)}, u32[]{:S(2)}) %collective-permute-start.16) | collective-permute-done | bytes 589856 | tf_op jit(solution)/shard_map/ppermute | solution.py:425
  116.4 2.7 %collective-permute-done.15.f1_ref = bf16[512,768]{1,0:T(8,128)(2,1)S(1)} collective-permute-done((bf16[512,768]{1,0:T(8,128)(2,1)S(1)}, bf16[512,768]{1,0:T(8,128)(2,1)S(1)}, u32[]{:S(2)}, u32[]{:S(2)}) %collective-permute-start.15) | collective-permute-done | bytes 786464 | tf_op jit(solution)/shard_map/ppermute | solution.py:429
  119.2 1.4 shard_map.321
  120.6 7.7 %shard_map.322 = (f32[1024,768]{1,0:T(8,128)}, bf16[192,1024]{1,0:T(8,128)(2,1)S(1)}, bf16[192,1024]{1,0:T(8,128)(2,1)S(1)}, bf16[768,192]{1,0:T(8,128)(2,1)}, b...) custom-call(f32[1024,768]{1,0:T(8,128)S(1)} %get-tuple-element.169.mid_ref, ...), custom_call_target="tpu_custom_call" | custom-call | flops 1207959552 | bytes 16000000 | tf_op jit(solution)/shard_map/pallas_call | solution.py:682
  128.3 2.1 collective-permute-done.18
  131.8 1.6 collective-permute-start.21
  133.3 8.5 %shard_map.323 = (bf16[3,1024,64]{2,1,0:T(8,128)(2,1)S(1)}, bf16[3,1024,64]{2,1,0:T(8,128)(2,1)S(1)}, bf16[3,1024,64]{2,1,0:T(8,128)(2,1)S(1)}) custom-call(bf16[9,1024,64]{2,1,0:T(8,128)(2,1)} %get-tuple-element.161.q_ref.k_ref.v_ref, bf16[9,1024,64]{2,1,0:T(8,128)(2,1)} %get-tuple-element.161.q_ref.k_ref.v_ref, ...), custom_call_target="tpu_custom_call" | custom-call | flops 8053063680 | bytes 9000000 | tf_op jit(solution)/shard_map/pallas_call | solution.py:602
  141.8 6.1 %shard_map.324 = (bf16[4,96,768]{2,1,0:T(8,128)(2,1)}, bf16[4,96,768]{2,1,0:T(8,128)(2,1)}, f32[1024,768]{1,0:T(8,128)}, f32[1,576]{1,0:T(1,128)S(1)}) custom-call(s32[2]{0:T(128)S(1)} %pad_add_fusion.x_ref, bf16[3,1024,64]{2,1,0:T(8,128)(2,1)S(1)} %get-tuple-element.195.q_ref, bf16[3,1024,64]{2,1,0:T(8,128)(2,1)S(1)} %get-tuple-element.196.k_ref, ...), custom_call_target="tpu_custom_call" | custom-call | flops 1811939328 | bytes 10000000 | tf_op jit(solution)/shard_map/pallas_call | solution.py:708
  147.9 1.3 collective-permute-start.22
  149.9 9.2 %shard_map.325 = (bf16[3,1024,64]{2,1,0:T(8,128)(2,1)}, bf16[3,1024,64]{2,1,0:T(8,128)(2,1)}, bf16[3,1024,64]{2,1,0:T(8,128)(2,1)}) custom-call(bf16[9,1024,64]{2,1,0:T(8,128)(2,1)} %get-tuple-element.154.q_ref.k_ref.v_ref, bf16[9,1024,64]{2,1,0:T(8,128)(2,1)} %get-tuple-element.154.q_ref.k_ref.v_ref, ...), custom_call_target="tpu_custom_call" | custom-call | flops 8053063680 | bytes 9000000 | tf_op jit(solution)/shard_map/pallas_call | solution.py:602
  159.2 2.3 %collective-permute-done.22 = bf16[4,96,768]{2,1,0:T(8,128)(2,1)S(1)} collective-permute-done((bf16[4,96,768]{2,1,0:T(8,128)(2,1)S(1)}, bf16[4,96,768]{2,1,0:T(8,128)(2,1)S(1)}, u32[]{:S(2)}, u32[]{:S(2)}) %collective-permute-start.22) | collective-permute-done | bytes 589856 | tf_op jit(solution)/shard_map/ppermute | solution.py:421
  161.5 1.2 collective-permute-done.23
  163.5 1.1 pad_maximum_fusion
  164.7 4.7 %all-to-all-start.1 = ((bf16[4,192,768]{2,1,0:T(8,128)(2,1)}), bf16[4,192,768]{2,1,0:T(8,128)(2,1)}, u32[]{:S(2)}, u32[]{:S(2)}) async-start(bf16[4,192,768]{2,1,0:T(8,128)(2,1)} %pad_maximum_fusion), calls=%async_computation.1 | async-start | bytes 2359296 | tf_op jit(solution)/shard_map/all_to_all | solution.py:438
  169.3 6.5 %shard_map.326 = (bf16[4,96,768]{2,1,0:T(8,128)(2,1)}, bf16[4,96,768]{2,1,0:T(8,128)(2,1)}, bf16[1024,768]{1,0:T(8,128)(2,1)S(1)}, f32[1,576]{1,0:T(1,128)S(1)}) custom-call(s32[2]{0:T(128)S(1)} %pad_add_fusion.x_ref, bf16[3,1024,64]{2,1,0:T(8,128)(2,1)} %get-tuple-element.216.q_ref, bf16[3,1024,64]{2,1,0:T(8,128)(2,1)} %get-tuple-element.217.k_ref, ...), custom_call_target="tpu_custom_call" | custom-call | flops 1811939328 | bytes 10000000 | tf_op jit(solution)/shard_map/pallas_call | solution.py:708
  176.6 1.3 collective-permute-start.28
  178.0 1.4 collective-permute-done.25.g1_ref
  179.3 6.4 %shard_map.327 = (bf16[256,768]{1,0:T(8,128)(2,1)S(1)}, bf16[256,768]{1,0:T(8,128)(2,1)}, f32[2,4,8,96]{3,2,1,0:T(8,128)S(1)}, f32[2,4,16,96]{3,2,1,0:T(8,128)S(1)}, f32[8,768]{1,0:T(8,128)S(1)}) custom-call(s32[2]{0:T(128)S(1)} %pad_add_fusion.x_ref, bf16[512,768]{1,0:T(8,128)(2,1)} %copy-done.4, bf16[512,768]{1,0:T(8,128)(2,1)} %collective-permute-done.3.refs_1_.s1.c1, ...), custom_call_target="tpu_custom_call" | custom-call | tf_op jit(solution)/shard_map/pallas_call | solution.py:755
  185.8 1.3 collective-permute-start.26
  187.0 2.1 maximum_select_fusion
  189.2 2.7 %collective-permute-done.27 = bf16[4,96,768]{2,1,0:T(8,128)(2,1)} collective-permute-done((bf16[4,96,768]{2,1,0:T(8,128)(2,1)}, bf16[4,96,768]{2,1,0:T(8,128)(2,1)}, u32[]{:S(2)}, u32[]{:S(2)}) %collective-permute-start.27) | collective-permute-done | bytes 589856 | tf_op jit(solution)/shard_map/ppermute | solution.py:425
  191.9 1.0 collective-permute-done.28
  192.9 2.3 %all-to-all-done.1 = bf16[4,192,768]{2,1,0:T(8,128)(2,1)} async-done(((bf16[4,192,768]{2,1,0:T(8,128)(2,1)}), bf16[4,192,768]{2,1,0:T(8,128)(2,1)}, u32[]{:S(2)}, u32[]{:S(2)}) %all-to-all-start.1) | async-done | bytes 1179680 | tf_op jit(solution)/shard_map/all_to_all | solution.py:438
  195.2 1.0 collective-permute-start.29
  196.3 2.1 add_add_fusion
  198.5 3.7 %all-to-all-start.2 = ((bf16[4,96,768]{2,1,0:T(8,128)(2,1)}), bf16[4,96,768]{2,1,0:T(8,128)(2,1)S(1)}, u32[]{:S(2)}, u32[]{:S(2)}) async-start(bf16[4,96,768]{2,1,0:T(8,128)(2,1)} %add_add_fusion), calls=%async_computation.2 | async-start | bytes 1179648 | tf_op jit(solution)/shard_map/all_to_all | solution.py:438
  202.1 1.5 collective-permute-start.30
  203.6 1.5 convert_reduce_fusion
  206.6 2.1 collective-permute-start.31
  208.7 2.4 %collective-permute-start.32 = (f32[8,96]{1,0:T(8,128)S(1)}, f32[8,96]{1,0:T(8,128)S(1)}, u32[]{:S(2)}, u32[]{:S(2)}) collective-permute-start(f32[8,96]{1,0:T(8,128)S(1)} %get-tuple-element.269), channel_id=1, source_target_pairs={{0,16},{8,24},{16,0},{24,8},{1,17},{9,25},{17,1},{25,9},{2,18},{10... | collective-permute-start | bytes 9224 | tf_op jit(solution)/shard_map/ppermute | solution.py:785
  211.0 1.5 collective-permute-start.33
  212.5 1.0 maximum_select_fusion.1
  213.5 1.9 collective-permute-done.31.p1_ref
  215.4 2.2 %collective-permute-done.32.p2_ref = f32[8,96]{1,0:T(8,128)S(1)} collective-permute-done((f32[8,96]{1,0:T(8,128)S(1)}, f32[8,96]{1,0:T(8,128)S(1)}, u32[]{:S(2)}, u32[]{:S(2)}) %collective-permute-start.32) | collective-permute-done | bytes 3104 | tf_op jit(solution)/shard_map/ppermute | solution.py:785
  217.6 0.9 shard_map.328
  (79 shorter events, 11.2 us)
Async XLA Ops:
  0.7 47.9 %copy-start = (bf16[2,768]{1,0:T(2,128)(2,1)S(1)}, bf16[2,768]{1,0:T(2,128)(2,1)}, u32[]{:S(2)}) copy-start(bf16[2,768]{1,0:T(2,128)(2,1)} %param.19) | copy-start | bytes 9220
  0.7 10.5 %copy-start.5 = (bf16[2,256,768]{2,1,0:T(8,128)(2,1)S(1)}, bf16[2,256,768]{2,1,0:T(8,128)(2,1)}, u32[]{:S(2)}) copy-start(bf16[2,256,768]{2,1,0:T(8,128)(2,1)} %param.35) | copy-start | bytes 2359300
  3.0 10.3 %collective-permute-start.2 = (bf16[104,768]{1,0:T(8,128)(2,1)}, bf16[104,768]{1,0:T(8,128)(2,1)S(1)}, u32[]{:S(2)}, u32[]{:S(2)}) collective-permute-start(bf16[104,768]{1,0:T(8,128)(2,1)} %get-tuple-element.144), channel_id=1, source_target_pairs={{24,0},{0,8},{8,16},{16,24},{25,1},{1,9},{9,17},{17,25},{26,2},{2,... | collective-permute-start | bytes 479240 | tf_op jit(solution)/shard_map/ppermute | solution.py:433
  6.1 13.3 %collective-permute-start.1 = (bf16[104,768]{1,0:T(8,128)(2,1)}, bf16[104,768]{1,0:T(8,128)(2,1)S(1)}, u32[]{:S(2)}, u32[]{:S(2)}) collective-permute-start(bf16[104,768]{1,0:T(8,128)(2,1)} %get-tuple-element.144), channel_id=1, source_target_pairs={{16,0},{24,8},{0,16},{8,24},{17,1},{25,9},{1,17},{9,25},{18,2},{26... | collective-permute-start | bytes 479240 | tf_op jit(solution)/shard_map/ppermute | solution.py:433
  8.6 10.7 %collective-permute-start = (bf16[104,768]{1,0:T(8,128)(2,1)}, bf16[104,768]{1,0:T(8,128)(2,1)}, u32[]{:S(2)}, u32[]{:S(2)}) collective-permute-start(bf16[104,768]{1,0:T(8,128)(2,1)} %get-tuple-element.144), channel_id=1, source_target_pairs={{8,0},{16,8},{24,16},{0,24},{9,1},{17,9},{25,17},{1,25},{10,2},{18... | collective-permute-start | bytes 479240 | tf_op jit(solution)/shard_map/ppermute | solution.py:433
  11.3 8.1 %copy-start.10 = (bf16[104,768]{1,0:T(8,128)(2,1)S(1)}, bf16[104,768]{1,0:T(8,128)(2,1)}, u32[]{:S(2)}) copy-start(bf16[104,768]{1,0:T(8,128)(2,1)} %get-tuple-element.144) | copy-start | bytes 479236
  11.4 9.0 %copy-start.4 = (bf16[512,768]{1,0:T(8,128)(2,1)}, bf16[512,768]{1,0:T(8,128)(2,1)S(1)}, u32[]{:S(2)}) copy-start(bf16[512,768]{1,0:T(8,128)(2,1)S(1)} %get-tuple-element.265.refs_0_.s0.c0) | copy-start | bytes 2359300
  11.4 18.6 %collective-permute-start.3 = (bf16[512,768]{1,0:T(8,128)(2,1)S(1)}, bf16[512,768]{1,0:T(8,128)(2,1)}, u32[]{:S(2)}, u32[]{:S(2)}) collective-permute-start(bf16[512,768]{1,0:T(8,128)(2,1)S(1)} %get-tuple-element.264), channel_id=1, source_target_pairs={{0,2},{2,0},{1,3},{3,1},{4,6},{6,4},{5,7},{7,5},{8,10},{10,8},{9,1... | collective-permute-start | bytes 2359304 | tf_op jit(solution)/shard_map/ppermute | solution.py:421
  13.0 17.0 %collective-permute-start.4 = (bf16[512,768]{1,0:T(8,128)(2,1)S(1)}, bf16[512,768]{1,0:T(8,128)(2,1)}, u32[]{:S(2)}, u32[]{:S(2)}) collective-permute-start(bf16[512,768]{1,0:T(8,128)(2,1)S(1)} %get-tuple-element.265.refs_0_.s0.c0), channel_id=1, source_target_pairs={{0,1},{1,0},{2,3},{3,2},{4,5},{5,4},{6,7},{7,6},{8,9},{9,8},{10,11... | collective-permute-start | bytes 2359304 | tf_op jit(solution)/shard_map/ppermute | solution.py:429
  20.4 34.3 %all-to-all-start = ((bf16[4,192,768]{2,1,0:T(8,128)(2,1)}), bf16[4,192,768]{2,1,0:T(8,128)(2,1)}, u32[]{:S(2)}, u32[]{:S(2)}) async-start(bf16[4,192,768]{2,1,0:T(8,128)(2,1)} %get-tuple-element.153), calls=%async_computation | async-start | bytes 2359296 | tf_op jit(solution)/shard_map/all_to_all | solution.py:438
  30.0 14.4 %collective-permute-start.6 = (bf16[4,104,768]{2,1,0:T(8,128)(2,1)S(1)}, bf16[4,104,768]{2,1,0:T(8,128)(2,1)S(1)}, u32[]{:S(2)}, u32[]{:S(2)}) collective-permute-start(bf16[4,104,768]{2,1,0:T(8,128)(2,1)S(1)} %pad_maximum_fusion.1.refs_5_), channel_id=1, source_target_pairs={{0,4},{4,0},{1,5},{5,1},{2,6},{6,2},{3,7},{7,3},{8,12},{12,8},{9,1... | collective-permute-start | bytes 1916936 | tf_op jit(solution)/shard_map/ppermute | solution.py:425
  31.5 14.1 %collective-permute-start.7 = (bf16[4,104,768]{2,1,0:T(8,128)(2,1)S(1)}, bf16[4,104,768]{2,1,0:T(8,128)(2,1)S(1)}, u32[]{:S(2)}, u32[]{:S(2)}) collective-permute-start(bf16[4,104,768]{2,1,0:T(8,128)(2,1)S(1)} %pad_maximum_fusion.1.refs_5_), channel_id=1, source_target_pairs={{0,2},{2,0},{1,3},{3,1},{4,6},{6,4},{5,7},{7,5},{8,10},{10,8},{9,1... | collective-permute-start | bytes 1916936 | tf_op jit(solution)/shard_map/ppermute | solution.py:421
  33.0 15.5 %collective-permute-start.5 = (bf16[512,768]{1,0:T(8,128)(2,1)}, bf16[512,768]{1,0:T(8,128)(2,1)}, u32[]{:S(2)}, u32[]{:S(2)}) collective-permute-start(bf16[512,768]{1,0:T(8,128)(2,1)} %collective-permute-done.3.refs_1_.s1.c1), channel_id=1, source_target_pairs={{0,1},{1,0},{2,3},{3,2},{4,5},{5,4},{6,7},{7,6},{8,9},{9,8},{10,11... | collective-permute-start | bytes 2359304 | tf_op jit(solution)/shard_map/ppermute | solution.py:429
  46.3 8.3 %collective-permute-start.9 = (bf16[4,56,768]{2,1,0:T(8,128)(2,1)}, bf16[4,56,768]{2,1,0:T(8,128)(2,1)S(1)}, u32[]{:S(2)}, u32[]{:S(2)}) collective-permute-start(bf16[4,56,768]{2,1,0:T(8,128)(2,1)} %slice.34), channel_id=1, source_target_pairs={{0,4},{4,0},{1,5},{5,1},{2,6},{6,2},{3,7},{7,3},{8,12},{12,8},{9,1... | collective-permute-start | bytes 1032200 | tf_op jit(solution)/shard_map/ppermute | solution.py:425
  46.9 7.1 %collective-permute-start.8 = (bf16[4,48,768]{2,1,0:T(8,128)(2,1)S(1)}, bf16[4,48,768]{2,1,0:T(8,128)(2,1)S(1)}, u32[]{:S(2)}, u32[]{:S(2)}) collective-permute-start(bf16[4,48,768]{2,1,0:T(8,128)(2,1)S(1)} %slice.33), channel_id=1, source_target_pairs={{0,2},{2,0},{1,3},{3,1},{4,6},{6,4},{5,7},{7,5},{8,10},{10,8},{9,1... | collective-permute-start | bytes 884744 | tf_op jit(solution)/shard_map/ppermute | solution.py:421
  54.0 0.7 copy-start.2
  54.7 10.8 %copy-start.3 = (bf16[4,48,768]{2,1,0:T(8,128)(2,1)S(1)}, bf16[4,48,768]{2,1,0:T(8,128)(2,1)}, u32[]{:S(2)}) copy-start(bf16[4,48,768]{2,1,0:T(8,128)(2,1)} %copy-done.2) | copy-start | bytes 884740
  54.7 26.9 %collective-permute-start.10 = (bf16[4,192,768]{2,1,0:T(8,128)(2,1)}, bf16[4,192,768]{2,1,0:T(8,128)(2,1)S(1)}, u32[]{:S(2)}, u32[]{:S(2)}) collective-permute-start(bf16[4,192,768]{2,1,0:T(8,128)(2,1)} %all-to-all-done.w_oo), channel_id=1, source_target_pairs={{0,4},{4,0},{1,5},{5,1},{2,6},{6,2},{3,7},{7,3},{8,12},{12,8},{9,1... | collective-permute-start | bytes 3538952 | tf_op jit(solution)/shard_map/ppermute | solution.py:425
  56.2 26.6 %collective-permute-start.11 = (bf16[4,192,768]{2,1,0:T(8,128)(2,1)}, bf16[4,192,768]{2,1,0:T(8,128)(2,1)S(1)}, u32[]{:S(2)}, u32[]{:S(2)}) collective-permute-start(bf16[4,192,768]{2,1,0:T(8,128)(2,1)} %all-to-all-done.w_oo), channel_id=1, source_target_pairs={{0,2},{2,0},{1,3},{3,1},{4,6},{6,4},{5,7},{7,5},{8,10},{10,8},{9,1... | collective-permute-start | bytes 3538952 | tf_op jit(solution)/shard_map/ppermute | solution.py:421
  82.8 3.4 %collective-permute-start.12 = (bf16[1024,768]{1,0:T(8,128)(2,1)S(1)}, bf16[1024,768]{1,0:T(8,128)(2,1)S(1)}, u32[]{:S(2)}, u32[]{:S(2)}) collective-permute-start(bf16[1024,768]{1,0:T(8,128)(2,1)S(1)} %shard_map.318.a0_ref), channel_id=1, source_target_pairs={{0,1},{1,0},{2,3},{3,2},{4,5},{5,4},{6,7},{7,6},{8,9},{9,8},{10,11... | collective-permute-start | bytes 4718600 | tf_op jit(solution)/shard_map/ppermute | solution.py:429
  82.9 15.8 %collective-permute-start.13 = (bf16[4,96,768]{2,1,0:T(8,128)(2,1)S(1)}, bf16[4,96,768]{2,1,0:T(8,128)(2,1)S(1)}, u32[]{:S(2)}, u32[]{:S(2)}) collective-permute-start(bf16[4,96,768]{2,1,0:T(8,128)(2,1)S(1)} %slice.35), channel_id=1, source_target_pairs={{0,2},{2,0},{1,3},{3,1},{4,6},{6,4},{5,7},{7,5},{8,10},{10,8},{9,1... | collective-permute-start | bytes 1769480 | tf_op jit(solution)/shard_map/ppermute | solution.py:421
  84.5 15.5 %collective-permute-start.14 = (bf16[4,96,768]{2,1,0:T(8,128)(2,1)S(1)}, bf16[4,96,768]{2,1,0:T(8,128)(2,1)S(1)}, u32[]{:S(2)}, u32[]{:S(2)}) collective-permute-start(bf16[4,96,768]{2,1,0:T(8,128)(2,1)S(1)} %slice.36), channel_id=1, source_target_pairs={{0,4},{4,0},{1,5},{5,1},{2,6},{6,2},{3,7},{7,3},{8,12},{12,8},{9,1... | collective-permute-start | bytes 1769480 | tf_op jit(solution)/shard_map/ppermute | solution.py:425
  100.0 14.6 %collective-permute-start.16 = (bf16[4,96,768]{2,1,0:T(8,128)(2,1)S(1)}, bf16[4,96,768]{2,1,0:T(8,128)(2,1)S(1)}, u32[]{:S(2)}, u32[]{:S(2)}) collective-permute-start(bf16[4,96,768]{2,1,0:T(8,128)(2,1)S(1)} %get-tuple-element.185), channel_id=1, source_target_pairs={{0,4},{4,0},{1,5},{5,1},{2,6},{6,2},{3,7},{7,3},{8,12},{12,8},{9,1... | collective-permute-start | bytes 1769480 | tf_op jit(solution)/shard_map/ppermute | solution.py:425
  114.6 5.9 %collective-permute-start.17 = (bf16[1024,768]{1,0:T(8,128)(2,1)S(1)}, bf16[1024,768]{1,0:T(8,128)(2,1)S(1)}, u32[]{:S(2)}, u32[]{:S(2)}) collective-permute-start(bf16[1024,768]{1,0:T(8,128)(2,1)S(1)} %get-tuple-element.186.g0_ref), channel_id=1, source_target_pairs={{0,1},{1,0},{2,3},{3,2},{4,5},{5,4},{6,7},{7,6},{8,9},{9,8},{10,11... | collective-permute-start | bytes 4718600 | tf_op jit(solution)/shard_map/ppermute | solution.py:429
  114.6 4.5 %collective-permute-start.15 = (bf16[512,768]{1,0:T(8,128)(2,1)S(1)}, bf16[512,768]{1,0:T(8,128)(2,1)S(1)}, u32[]{:S(2)}, u32[]{:S(2)}) collective-permute-start(bf16[512,768]{1,0:T(8,128)(2,1)S(1)} %get-tuple-element.179), channel_id=1, source_target_pairs={{0,1},{1,0},{2,3},{3,2},{4,5},{5,4},{6,7},{7,6},{8,9},{9,8},{10,11... | collective-permute-start | bytes 2359304 | tf_op jit(solution)/shard_map/ppermute | solution.py:429
  115.2 15.2 %collective-permute-start.18 = (bf16[4,96,768]{2,1,0:T(8,128)(2,1)S(1)}, bf16[4,96,768]{2,1,0:T(8,128)(2,1)S(1)}, u32[]{:S(2)}, u32[]{:S(2)}) collective-permute-start(bf16[4,96,768]{2,1,0:T(8,128)(2,1)S(1)} %get-tuple-element.192), channel_id=1, source_target_pairs={{0,4},{4,0},{1,5},{5,1},{2,6},{6,2},{3,7},{7,3},{8,12},{12,8},{9,1... | collective-permute-start | bytes 1769480 | tf_op jit(solution)/shard_map/ppermute | solution.py:425
  115.7 15.0 %collective-permute-start.19 = (bf16[4,96,768]{2,1,0:T(8,128)(2,1)S(1)}, bf16[4,96,768]{2,1,0:T(8,128)(2,1)S(1)}, u32[]{:S(2)}, u32[]{:S(2)}) collective-permute-start(bf16[4,96,768]{2,1,0:T(8,128)(2,1)S(1)} %get-tuple-element.193), channel_id=1, source_target_pairs={{0,2},{2,0},{1,3},{3,1},{4,6},{6,4},{5,7},{7,5},{8,10},{10,8},{9,1... | collective-permute-start | bytes 1769480 | tf_op jit(solution)/shard_map/ppermute | solution.py:421
  130.8 17.1 %collective-permute-start.20 = (bf16[4,96,768]{2,1,0:T(8,128)(2,1)S(1)}, bf16[4,96,768]{2,1,0:T(8,128)(2,1)S(1)}, u32[]{:S(2)}, u32[]{:S(2)}) collective-permute-start(bf16[4,96,768]{2,1,0:T(8,128)(2,1)S(1)} %add.80), channel_id=1, source_target_pairs={{0,2},{2,0},{1,3},{3,1},{4,6},{6,4},{5,7},{7,5},{8,10},{10,8},{9,1... | collective-permute-start | bytes 1769480 | tf_op jit(solution)/shard_map/ppermute | solution.py:421
  131.8 16.2 %collective-permute-start.21 = (bf16[4,96,768]{2,1,0:T(8,128)(2,1)S(1)}, bf16[4,96,768]{2,1,0:T(8,128)(2,1)S(1)}, u32[]{:S(2)}, u32[]{:S(2)}) collective-permute-start(bf16[4,96,768]{2,1,0:T(8,128)(2,1)S(1)} %add.81), channel_id=1, source_target_pairs={{0,4},{4,0},{1,5},{5,1},{2,6},{6,2},{3,7},{7,3},{8,12},{12,8},{9,1... | collective-permute-start | bytes 1769480 | tf_op jit(solution)/shard_map/ppermute | solution.py:425
  147.9 13.6 %collective-permute-start.22 = (bf16[4,96,768]{2,1,0:T(8,128)(2,1)S(1)}, bf16[4,96,768]{2,1,0:T(8,128)(2,1)S(1)}, u32[]{:S(2)}, u32[]{:S(2)}) collective-permute-start(bf16[4,96,768]{2,1,0:T(8,128)(2,1)S(1)} %get-tuple-element.213), channel_id=1, source_target_pairs={{0,2},{2,0},{1,3},{3,1},{4,6},{6,4},{5,7},{7,5},{8,10},{10,8},{9,1... | collective-permute-start | bytes 1769480 | tf_op jit(solution)/shard_map/ppermute | solution.py:421
  149.3 13.4 %collective-permute-start.23 = (bf16[4,96,768]{2,1,0:T(8,128)(2,1)}, bf16[4,96,768]{2,1,0:T(8,128)(2,1)S(1)}, u32[]{:S(2)}, u32[]{:S(2)}) collective-permute-start(bf16[4,96,768]{2,1,0:T(8,128)(2,1)} %get-tuple-element.214), channel_id=1, source_target_pairs={{0,4},{4,0},{1,5},{5,1},{2,6},{6,2},{3,7},{7,3},{8,12},{12,8},{9,1... | collective-permute-start | bytes 1769480 | tf_op jit(solution)/shard_map/ppermute | solution.py:425
  162.7 0.8 copy-start.7
  162.7 13.1 %collective-permute-start.24 = (bf16[256,768]{1,0:T(8,128)(2,1)}, bf16[256,768]{1,0:T(8,128)(2,1)}, u32[]{:S(2)}, u32[]{:S(2)}) collective-permute-start(bf16[256,768]{1,0:T(8,128)(2,1)} %get-tuple-element.222), channel_id=1, source_target_pairs={{0,2},{2,0},{1,3},{3,1},{4,6},{6,4},{5,7},{7,5},{8,10},{10,8},{9,1... | collective-permute-start | bytes 1179656 | tf_op jit(solution)/shard_map/ppermute | solution.py:421
  164.7 30.5 %all-to-all-start.1 = ((bf16[4,192,768]{2,1,0:T(8,128)(2,1)}), bf16[4,192,768]{2,1,0:T(8,128)(2,1)}, u32[]{:S(2)}, u32[]{:S(2)}) async-start(bf16[4,192,768]{2,1,0:T(8,128)(2,1)} %pad_maximum_fusion), calls=%async_computation.1 | async-start | bytes 2359296 | tf_op jit(solution)/shard_map/all_to_all | solution.py:438
  169.3 7.2 %copy-start.6 = (bf16[4,96,768]{2,1,0:T(8,128)(2,1)S(1)}, bf16[4,96,768]{2,1,0:T(8,128)(2,1)}, u32[]{:S(2)}) copy-start(bf16[4,96,768]{2,1,0:T(8,128)(2,1)} %get-tuple-element.235) | copy-start | bytes 1769476
  169.3 7.2 %copy-start.8 = (bf16[4,96,768]{2,1,0:T(8,128)(2,1)S(1)}, bf16[4,96,768]{2,1,0:T(8,128)(2,1)}, u32[]{:S(2)}) copy-start(bf16[4,96,768]{2,1,0:T(8,128)(2,1)} %copy-done.7) | copy-start | bytes 1769476
  175.8 3.5 %collective-permute-start.25 = (bf16[1024,768]{1,0:T(8,128)(2,1)S(1)}, bf16[1024,768]{1,0:T(8,128)(2,1)}, u32[]{:S(2)}, u32[]{:S(2)}) collective-permute-start(bf16[1024,768]{1,0:T(8,128)(2,1)S(1)} %get-tuple-element.224.g0_ref), channel_id=1, source_target_pairs={{0,1},{1,0},{2,3},{3,2},{4,5},{5,4},{6,7},{7,6},{8,9},{9,8},{10,11... | collective-permute-start | bytes 4718600 | tf_op jit(solution)/shard_map/ppermute | solution.py:429
  175.8 16.1 %collective-permute-start.27 = (bf16[4,96,768]{2,1,0:T(8,128)(2,1)}, bf16[4,96,768]{2,1,0:T(8,128)(2,1)}, u32[]{:S(2)}, u32[]{:S(2)}) collective-permute-start(bf16[4,96,768]{2,1,0:T(8,128)(2,1)} %get-tuple-element.234), channel_id=1, source_target_pairs={{0,4},{4,0},{1,5},{5,1},{2,6},{6,2},{3,7},{7,3},{8,12},{12,8},{9,1... | collective-permute-start | bytes 1769480 | tf_op jit(solution)/shard_map/ppermute | solution.py:425
  176.6 16.3 %collective-permute-start.28 = (bf16[4,96,768]{2,1,0:T(8,128)(2,1)S(1)}, bf16[4,96,768]{2,1,0:T(8,128)(2,1)}, u32[]{:S(2)}, u32[]{:S(2)}) collective-permute-start(bf16[4,96,768]{2,1,0:T(8,128)(2,1)S(1)} %add.82), channel_id=1, source_target_pairs={{0,2},{2,0},{1,3},{3,1},{4,6},{6,4},{5,7},{7,5},{8,10},{10,8},{9,1... | collective-permute-start | bytes 1769480 | tf_op jit(solution)/shard_map/ppermute | solution.py:421
  185.8 10.6 %copy-start.9 = (bf16[4,96,768]{2,1,0:T(8,128)(2,1)S(1)}, bf16[4,96,768]{2,1,0:T(8,128)(2,1)}, u32[]{:S(2)}) copy-start(bf16[4,96,768]{2,1,0:T(8,128)(2,1)} %get-tuple-element.246) | copy-start | bytes 1769476
  185.8 9.4 %collective-permute-start.26 = (f32[2,4,16,96]{3,2,1,0:T(8,128)S(1)}, f32[2,4,16,96]{3,2,1,0:T(8,128)S(1)}, u32[]{:S(2)}, u32[]{:S(2)}) collective-permute-start(f32[2,4,16,96]{3,2,1,0:T(8,128)S(1)} %get-tuple-element.232), channel_id=1, source_target_pairs={{0,2},{2,0},{1,3},{3,1},{4,6},{6,4},{5,7},{7,5},{8,10},{10,8},{9,1... | collective-permute-start | bytes 147464 | tf_op jit(solution)/shard_map/ppermute | solution.py:421
  195.2 17.3 %collective-permute-start.29 = (bf16[256,768]{1,0:T(8,128)(2,1)}, bf16[256,768]{1,0:T(8,128)(2,1)S(1)}, u32[]{:S(2)}, u32[]{:S(2)}) collective-permute-start(bf16[256,768]{1,0:T(8,128)(2,1)} %get-tuple-element.243), channel_id=1, source_target_pairs={{0,2},{2,0},{1,3},{3,1},{4,6},{6,4},{5,7},{7,5},{8,10},{10,8},{9,1... | collective-permute-start | bytes 1179656 | tf_op jit(solution)/shard_map/ppermute | solution.py:421
  198.5 19.2 %all-to-all-start.2 = ((bf16[4,96,768]{2,1,0:T(8,128)(2,1)}), bf16[4,96,768]{2,1,0:T(8,128)(2,1)S(1)}, u32[]{:S(2)}, u32[]{:S(2)}) async-start(bf16[4,96,768]{2,1,0:T(8,128)(2,1)} %add_add_fusion), calls=%async_computation.2 | async-start | bytes 1179648 | tf_op jit(solution)/shard_map/all_to_all | solution.py:438
  202.1 4.4 %collective-permute-start.30 = (f32[4,8,96]{2,1,0:T(8,128)S(1)}, f32[4,8,96]{2,1,0:T(8,128)S(1)}, u32[]{:S(2)}, u32[]{:S(2)}) collective-permute-start(f32[4,8,96]{2,1,0:T(8,128)S(1)} %slice_bitcast_fusion.1), channel_id=1, source_target_pairs={{0,4},{4,0},{1,5},{5,1},{2,6},{6,2},{3,7},{7,3},{8,12},{12,8},{9,1... | collective-permute-start | bytes 36872 | tf_op jit(solution)/shard_map/ppermute | solution.py:425
  203.6 14.9 %copy-start.1 = (bf16[2,768]{1,0:T(2,128)(2,1)S(1)}, bf16[2,768]{1,0:T(2,128)(2,1)}, u32[]{:S(2)}) copy-start(bf16[2,768]{1,0:T(2,128)(2,1)} %param.19) | copy-start | bytes 9220
  206.6 8.8 %collective-permute-start.31 = (f32[8,96]{1,0:T(8,128)S(1)}, f32[8,96]{1,0:T(8,128)S(1)}, u32[]{:S(2)}, u32[]{:S(2)}) collective-permute-start(f32[8,96]{1,0:T(8,128)S(1)} %get-tuple-element.270), channel_id=1, source_target_pairs={{0,8},{8,16},{16,24},{24,0},{1,9},{9,17},{17,25},{25,1},{2,10},{10... | collective-permute-start | bytes 9224 | tf_op jit(solution)/shard_map/ppermute | solution.py:785
  208.7 9.0 %collective-permute-start.32 = (f32[8,96]{1,0:T(8,128)S(1)}, f32[8,96]{1,0:T(8,128)S(1)}, u32[]{:S(2)}, u32[]{:S(2)}) collective-permute-start(f32[8,96]{1,0:T(8,128)S(1)} %get-tuple-element.269), channel_id=1, source_target_pairs={{0,16},{8,24},{16,0},{24,8},{1,17},{9,25},{17,1},{25,9},{2,18},{10... | collective-permute-start | bytes 9224 | tf_op jit(solution)/shard_map/ppermute | solution.py:785
  211.0 6.6 %collective-permute-start.33 = (f32[8,96]{1,0:T(8,128)S(1)}, f32[8,96]{1,0:T(8,128)S(1)}, u32[]{:S(2)}, u32[]{:S(2)}) collective-permute-start(f32[8,96]{1,0:T(8,128)S(1)} %get-tuple-element.268), channel_id=1, source_target_pairs={{0,24},{8,0},{16,8},{24,16},{1,25},{9,1},{17,9},{25,17},{2,26},{10... | collective-permute-start | bytes 9224 | tf_op jit(solution)/shard_map/ppermute | solution.py:785

commit v8 on v7

--- a/solution.py
+++ b/solution.py
@@ -15,7 +15,7 @@
 F32 = jnp.float32
 ZS, XS = 4, 2
 KINDS = 8
-HINT = 1.0
+HINT = 2.0
 TILE_PROJECT = 512
 TILE_OUT = 512
 TILE_MLP = 512

time: 219 us -> 218 us (level)
  transfers between devices with their start and end apart: 37 -> 37, of which waited for: 22 -> 21; matrix products, arithmetic and copies ran while one was open for 6% -> 6% of each run, Pallas kernels for 44% -> 44%
where the time goes in v8:
time: 218 us
  Pallas kernels  98.6 us (45%)
  waiting for transfers between devices  52.1 us (24%)
  starting transfers between devices  51.3 us (24%)
  other arithmetic  9.28 us (4%)
  local copies, waits for them, and re-layouts  5.28 us (2%)
    ppermute x10, waiting for transfers between devices, to_x(): return lax.ppermute(values, 'b', swap(2))  24.8 us
    pallas_call x2, Pallas kernels, attend_back(): call(attend_back_body, (3,), [q_spec, k_spec, v_spec, e_spec, inv_spec, t...  17.8 us
    pallas_call x2, Pallas kernels, attend(): call(attend_body, (3,), [q_spec, k_spec, v_spec], [(pltpu.HBM((3, seq, se...  16.1 us
    all_to_all x3, starting transfers between devices, spread_z(): return lax.all_to_all(values, 'a', 0, 0, tiled=True)  14.7 us
    ppermute x12, starting transfers between devices, to_y(): return lax.ppermute(values, 'y', swap(2))  13.2 us
    pallas_call x2, Pallas kernels, project_back(): call(functools.partial(project_back_body, rows=rows, more=more), (seq //...  12.5 us
    pallas_call x1, Pallas kernels, body(): call(functools.partial(mlp_first_body, rows=rows), (seq // tile,), [scala...  11.8 us
    ppermute x12, waiting for transfers between devices, to_y(): return lax.ppermute(values, 'y', swap(2))  11.3 us
  transfers between devices with their start and end apart: 37, of which 21 were waited for; matrix products, arithmetic and copies ran while one was open for 6% of the time, Pallas kernels for 44%

profile of v8, /device:TPU:0, one launch (start us, length us, event | category | flops | bytes accessed | tf_op | source)
XLA Modules:
  0.0 217.6 jit_solution(9116842609549102948)
XLA Ops:
  0.7 2.3 %shard_map.313 = (bf16[104,768]{1,0:T(8,128)(2,1)}, bf16[4,192,768]{2,1,0:T(8,128)(2,1)}) custom-call(bf16[96,192]{1,0:T(8,128)(2,1)} %q_ref.1, bf16[96,192]{1,0:T(8,128)(2,1)} %k_ref.1, bf16[96,192]{1,0:T(8,128)(2,1)} %v_ref.1, bf16[192,96]{1,0:T(8,128)(2,1)} %o_ref.1, bf16[96,768]{1,0:T(8,128)(2,1)} %h_ref.1, bf16[96,768]{1,0:T(8,128)(2,1)} %bitcast.69, ...), custom_call_target="tpu_custom_call" | custom-call | flops 2000000 | bytes 4000000 | tf_op jit(solution)/shard_map/pallas_call | solution.py:473
  3.0 3.0 %collective-permute-start.2 = (bf16[104,768]{1,0:T(8,128)(2,1)}, bf16[104,768]{1,0:T(8,128)(2,1)S(1)}, u32[]{:S(2)}, u32[]{:S(2)}) collective-permute-start(bf16[104,768]{1,0:T(8,128)(2,1)} %get-tuple-element.144), channel_id=1, source_target_pairs={{24,0},{0,8},{8,16},{16,24},{25,1},{1,9},{9,17},{17,25},{26,2},{2,... | collective-permute-start | bytes 479240 | tf_op jit(solution)/shard_map/ppermute | solution.py:433
  6.1 2.6 %collective-permute-start.1 = (bf16[104,768]{1,0:T(8,128)(2,1)}, bf16[104,768]{1,0:T(8,128)(2,1)S(1)}, u32[]{:S(2)}, u32[]{:S(2)}) collective-permute-start(bf16[104,768]{1,0:T(8,128)(2,1)} %get-tuple-element.144), channel_id=1, source_target_pairs={{16,0},{24,8},{0,16},{8,24},{17,1},{25,9},{1,17},{9,25},{18,2},{26... | collective-permute-start | bytes 479240 | tf_op jit(solution)/shard_map/ppermute | solution.py:433
  8.6 1.3 collective-permute-start
  10.0 1.2 constant_dynamic-update-slice_fusion.1
  11.3 1.0 dynamic-slice_bitcast_fusion
  12.3 1.5 collective-permute-start.3
  13.8 5.6 %collective-permute-done.1 = bf16[104,768]{1,0:T(8,128)(2,1)S(1)} collective-permute-done((bf16[104,768]{1,0:T(8,128)(2,1)}, bf16[104,768]{1,0:T(8,128)(2,1)S(1)}, u32[]{:S(2)}, u32[]{:S(2)}) %collective-permute-start.1) | collective-permute-done | bytes 159776 | tf_op jit(solution)/shard_map/ppermute | solution.py:433
  19.4 6.2 %all-to-all-start = ((bf16[4,192,768]{2,1,0:T(8,128)(2,1)}), bf16[4,192,768]{2,1,0:T(8,128)(2,1)S(1)}, u32[]{:S(2)}, u32[]{:S(2)}) async-start(bf16[4,192,768]{2,1,0:T(8,128)(2,1)} %get-tuple-element.153), calls=%async_computation | async-start | bytes 2359296 | tf_op jit(solution)/shard_map/all_to_all | solution.py:438
  25.7 5.3 %collective-permute-done.3.refs_1_.s1.c1 = bf16[512,768]{1,0:T(8,128)(2,1)} collective-permute-done((bf16[512,768]{1,0:T(8,128)(2,1)}, bf16[512,768]{1,0:T(8,128)(2,1)}, u32[]{:S(2)}, u32[]{:S(2)}) %collective-permute-start.3) | collective-permute-done | bytes 786464 | tf_op jit(solution)/shard_map/ppermute | solution.py:421
  31.0 1.5 collective-permute-start.6
  32.5 1.5 collective-permute-start.7
  34.0 11.4 %collective-permute-done.6.refs_6_ = bf16[4,104,768]{2,1,0:T(8,128)(2,1)} collective-permute-done((bf16[4,104,768]{2,1,0:T(8,128)(2,1)S(1)}, bf16[4,104,768]{2,1,0:T(8,128)(2,1)}, u32[]{:S(2)}, u32[]{:S(2)}) %collective-permute-start.6) | collective-permute-done | bytes 639008 | tf_op jit(solution)/shard_map/ppermute | solution.py:425
  45.5 1.1 collective-permute-done.7.refs_1_
  46.6 1.2 slice.33
  47.8 1.6 collective-permute-start.8
  50.1 5.6 %shard_map.314 = (bf16[768,768]{1,0:T(8,128)(2,1)S(1)}, f32[8,768]{1,0:T(8,128)S(1)}, bf16[9,1024,64]{2,1,0:T(8,128)(2,1)}, bf16[1024,768]{1,0:T(8,128)(2,1)}) custom-call(s32[2]{0:T(128)S(1)} %pad_add_fusion.x_ref, bf16[512,768]{1,0:T(8,128)(2,1)} %copy-done.6, bf16[512,768]{1,0:T(8,128)(2,1)} %collective-permute-done.3.refs_1_.s1.c1, ...), custom_call_target="tpu_custom_call" | custom-call | flops 1811939328 | bytes 16000000 | tf_op jit(solution)/shard_map/pallas_call | solution.py:567
  55.7 1.7 collective-permute-done.9.refs_3_
  58.6 8.0 %shard_map.315 = (bf16[3,1024,1024]{2,1,0:T(8,128)(2,1)}, f32[3,1,1024]{2,1,0:T(1,128)S(1)}, bf16[3,64,1024]{2,1,0:T(8,128)(2,1)S(1)}, f32[3,64,1024]{2,1,0:T(8,128)}) custom-call(bf16[9,1024,64]{2,1,0:T(8,128)(2,1)} %get-tuple-element.154.q_ref.k_ref.v_ref, bf16[9,1024,64]{2,1,0:T(8,128)(2,1)} %get-tuple-element.154.q_ref.k_ref.v_ref, ...), custom_call_target="tpu_custom_call" | custom-call | flops 6442450944 | bytes 16000000 | tf_op jit(solution)/shard_map/pallas_call | solution.py:585
  66.6 4.3 %shard_map.316 = (bf16[768,768]{1,0:T(8,128)(2,1)S(1)}, f32[8,768]{1,0:T(8,128)S(1)}, bf16[9,1024,64]{2,1,0:T(8,128)(2,1)}, bf16[768,1024]{1,0:T(8,128)(2,1)}) custom-call(s32[2]{0:T(128)S(1)} %pad_add_fusion.x_ref, bf16[1024,768]{1,0:T(8,128)(2,1)} %get-tuple-element.158.refs_0_, bf16[4,104,768]{2,1,0:T(8,128)(2,1)S(1)} %copy-done.3, ...), custom_call_target="tpu_custom_call" | custom-call | flops 1811939328 | bytes 16000000 | tf_op jit(solution)/shard_map/pallas_call | solution.py:567
  70.9 8.1 %shard_map.317 = (bf16[3,1024,1024]{2,1,0:T(8,128)(2,1)}, f32[3,1,1024]{2,1,0:T(1,128)S(1)}, bf16[3,64,1024]{2,1,0:T(8,128)(2,1)S(1)}, f32[3,64,1024]{2,1,0:T(8,128)}) custom-call(bf16[9,1024,64]{2,1,0:T(8,128)(2,1)} %get-tuple-element.161.q_ref.k_ref.v_ref, bf16[9,1024,64]{2,1,0:T(8,128)(2,1)} %get-tuple-element.161.q_ref.k_ref.v_ref, ...), custom_call_target="tpu_custom_call" | custom-call | flops 6442450944 | bytes 16000000 | tf_op jit(solution)/shard_map/pallas_call | solution.py:585
  79.0 1.5 shard_map.318.a0_ref
  80.5 1.4 collective-permute-done.10.w_ox
  82.0 1.2 collective-permute-start.13
  83.3 1.3 collective-permute-start.14
  85.4 11.8 %shard_map.319 = (f32[1024,768]{1,0:T(8,128)S(1)}, bf16[1024,768]{1,0:T(8,128)(2,1)S(1)}, f32[1024,768]{1,0:T(8,128)S(1)}, f32[1024,768]{1,0:T(8,128)S(1)}, f32[...) custom-call(s32[2]{0:T(128)S(1)} %pad_add_fusion.x_ref, ...), custom_call_target="tpu_custom_call" | custom-call | flops 14495514624 | bytes 32000000 | tf_op jit(solution)/shard_map/pallas_call | solution.py:643
  98.8 1.2 collective-permute-start.16
  100.0 10.2 %shard_map.320 = (bf16[512,768]{1,0:T(8,128)(2,1)S(1)}, bf16[512,768]{1,0:T(8,128)(2,1)S(1)}, bf16[1024,768]{1,0:T(8,128)(2,1)S(1)}, f32[1,768]{1,0:T(1,128)S(1)...) custom-call(s32[2]{0:T(128)S(1)} %pad_add_fusion.x_ref, ...), custom_call_target="tpu_custom_call" | custom-call | flops 14495514624 | bytes 32000000 | tf_op jit(solution)/shard_map/pallas_call | solution.py:661
  110.2 3.2 %collective-permute-done.16 = bf16[4,96,768]{2,1,0:T(8,128)(2,1)S(1)} collective-permute-done((bf16[4,96,768]{2,1,0:T(8,128)(2,1)S(1)}, bf16[4,96,768]{2,1,0:T(8,128)(2,1)S(1)}, u32[]{:S(2)}, u32[]{:S(2)}) %collective-permute-start.16) | collective-permute-done | bytes 589856 | tf_op jit(solution)/shard_map/ppermute | solution.py:425
  113.9 1.2 collective-permute-start.18
  115.8 2.2 %collective-permute-done.15.f1_ref = bf16[512,768]{1,0:T(8,128)(2,1)S(1)} collective-permute-done((bf16[512,768]{1,0:T(8,128)(2,1)S(1)}, bf16[512,768]{1,0:T(8,128)(2,1)S(1)}, u32[]{:S(2)}, u32[]{:S(2)}) %collective-permute-start.15) | collective-permute-done | bytes 786464 | tf_op jit(solution)/shard_map/ppermute | solution.py:429
  118.0 1.4 shard_map.321
  119.4 7.7 %shard_map.322 = (f32[1024,768]{1,0:T(8,128)}, bf16[192,1024]{1,0:T(8,128)(2,1)S(1)}, bf16[192,1024]{1,0:T(8,128)(2,1)S(1)}, bf16[768,192]{1,0:T(8,128)(2,1)}, b...) custom-call(f32[1024,768]{1,0:T(8,128)S(1)} %get-tuple-element.169.mid_ref, ...), custom_call_target="tpu_custom_call" | custom-call | flops 2415919104 | bytes 32000000 | tf_op jit(solution)/shard_map/pallas_call | solution.py:682
  127.1 2.1 collective-permute-done.18
  131.1 1.2 collective-permute-start.21
  132.2 8.5 %shard_map.323 = (bf16[3,1024,64]{2,1,0:T(8,128)(2,1)S(1)}, bf16[3,1024,64]{2,1,0:T(8,128)(2,1)S(1)}, bf16[3,1024,64]{2,1,0:T(8,128)(2,1)S(1)}) custom-call(bf16[9,1024,64]{2,1,0:T(8,128)(2,1)} %get-tuple-element.161.q_ref.k_ref.v_ref, bf16[9,1024,64]{2,1,0:T(8,128)(2,1)} %get-tuple-element.161.q_ref.k_ref.v_ref, ...), custom_call_target="tpu_custom_call" | custom-call | flops 16106127360 | bytes 18000000 | tf_op jit(solution)/shard_map/pallas_call | solution.py:602
  140.8 6.1 %shard_map.324 = (bf16[4,96,768]{2,1,0:T(8,128)(2,1)}, bf16[4,96,768]{2,1,0:T(8,128)(2,1)}, f32[1024,768]{1,0:T(8,128)}, f32[1,576]{1,0:T(1,128)S(1)}) custom-call(s32[2]{0:T(128)S(1)} %pad_add_fusion.x_ref, bf16[3,1024,64]{2,1,0:T(8,128)(2,1)S(1)} %get-tuple-element.195.q_ref, bf16[3,1024,64]{2,1,0:T(8,128)(2,1)S(1)} %get-tuple-element.196.k_ref, ...), custom_call_target="tpu_custom_call" | custom-call | flops 3623878656 | bytes 20000000 | tf_op jit(solution)/shard_map/pallas_call | solution.py:708
  146.8 1.2 collective-permute-start.22
  148.0 1.2 collective-permute-start.23
  149.2 9.2 %shard_map.325 = (bf16[3,1024,64]{2,1,0:T(8,128)(2,1)}, bf16[3,1024,64]{2,1,0:T(8,128)(2,1)}, bf16[3,1024,64]{2,1,0:T(8,128)(2,1)}) custom-call(bf16[9,1024,64]{2,1,0:T(8,128)(2,1)} %get-tuple-element.154.q_ref.k_ref.v_ref, bf16[9,1024,64]{2,1,0:T(8,128)(2,1)} %get-tuple-element.154.q_ref.k_ref.v_ref, ...), custom_call_target="tpu_custom_call" | custom-call | flops 16106127360 | bytes 18000000 | tf_op jit(solution)/shard_map/pallas_call | solution.py:602
  158.5 1.9 collective-permute-done.22
  160.4 1.0 collective-permute-done.23
  162.5 1.1 pad_maximum_fusion
  163.6 4.5 %all-to-all-start.1 = ((bf16[4,192,768]{2,1,0:T(8,128)(2,1)}), bf16[4,192,768]{2,1,0:T(8,128)(2,1)}, u32[]{:S(2)}, u32[]{:S(2)}) async-start(bf16[4,192,768]{2,1,0:T(8,128)(2,1)} %pad_maximum_fusion), calls=%async_computation.1 | async-start | bytes 2359296 | tf_op jit(solution)/shard_map/all_to_all | solution.py:438
  168.2 6.5 %shard_map.326 = (bf16[4,96,768]{2,1,0:T(8,128)(2,1)}, bf16[4,96,768]{2,1,0:T(8,128)(2,1)}, bf16[1024,768]{1,0:T(8,128)(2,1)S(1)}, f32[1,576]{1,0:T(1,128)S(1)}) custom-call(s32[2]{0:T(128)S(1)} %pad_add_fusion.x_ref, bf16[3,1024,64]{2,1,0:T(8,128)(2,1)} %get-tuple-element.216.q_ref, bf16[3,1024,64]{2,1,0:T(8,128)(2,1)} %get-tuple-element.217.k_ref, ...), custom_call_target="tpu_custom_call" | custom-call | flops 3623878656 | bytes 20000000 | tf_op jit(solution)/shard_map/pallas_call | solution.py:708
  174.7 1.0 collective-permute-start.27
  175.8 1.4 collective-permute-start.28
  177.2 1.0 collective-permute-done.25.g1_ref
  178.2 6.4 %shard_map.327 = (bf16[256,768]{1,0:T(8,128)(2,1)S(1)}, bf16[256,768]{1,0:T(8,128)(2,1)}, f32[2,4,8,96]{3,2,1,0:T(8,128)S(1)}, f32[2,4,16,96]{3,2,1,0:T(8,128)S(1)}, f32[8,768]{1,0:T(8,128)S(1)}) custom-call(s32[2]{0:T(128)S(1)} %pad_add_fusion.x_ref, bf16[512,768]{1,0:T(8,128)(2,1)} %copy-done.6, bf16[512,768]{1,0:T(8,128)(2,1)} %collective-permute-done.3.refs_1_.s1.c1, ...), custom_call_target="tpu_custom_call" | custom-call | tf_op jit(solution)/shard_map/pallas_call | solution.py:755
  184.6 1.1 collective-permute-start.26
  185.7 2.1 maximum_select_fusion
  187.9 2.9 %collective-permute-done.27 = bf16[4,96,768]{2,1,0:T(8,128)(2,1)} collective-permute-done((bf16[4,96,768]{2,1,0:T(8,128)(2,1)}, bf16[4,96,768]{2,1,0:T(8,128)(2,1)}, u32[]{:S(2)}, u32[]{:S(2)}) %collective-permute-start.27) | collective-permute-done | bytes 589856 | tf_op jit(solution)/shard_map/ppermute | solution.py:425
  190.7 1.4 collective-permute-done.28
  192.1 1.7 all-to-all-done.1
  193.8 1.0 collective-permute-start.29
  195.0 2.2 add_add_fusion
  197.1 3.9 %all-to-all-start.2 = ((bf16[4,96,768]{2,1,0:T(8,128)(2,1)}), bf16[4,96,768]{2,1,0:T(8,128)(2,1)S(1)}, u32[]{:S(2)}, u32[]{:S(2)}) async-start(bf16[4,96,768]{2,1,0:T(8,128)(2,1)} %add_add_fusion), calls=%async_computation.2 | async-start | bytes 1179648 | tf_op jit(solution)/shard_map/all_to_all | solution.py:438
  202.0 1.5 convert_reduce_fusion
  205.0 2.1 collective-permute-start.31
  207.0 2.4 %collective-permute-start.32 = (f32[8,96]{1,0:T(8,128)S(1)}, f32[8,96]{1,0:T(8,128)S(1)}, u32[]{:S(2)}, u32[]{:S(2)}) collective-permute-start(f32[8,96]{1,0:T(8,128)S(1)} %get-tuple-element.269), channel_id=1, source_target_pairs={{0,16},{8,24},{16,0},{24,8},{1,17},{9,25},{17,1},{25,9},{2,18},{10... | collective-permute-start | bytes 9224 | tf_op jit(solution)/shard_map/ppermute | solution.py:785
  209.4 1.5 collective-permute-start.33
  210.9 1.0 maximum_select_fusion.1
  211.9 2.5 %collective-permute-done.31.p1_ref = f32[8,96]{1,0:T(8,128)S(1)} collective-permute-done((f32[8,96]{1,0:T(8,128)S(1)}, f32[8,96]{1,0:T(8,128)S(1)}, u32[]{:S(2)}, u32[]{:S(2)}) %collective-permute-start.31) | collective-permute-done | bytes 3104 | tf_op jit(solution)/shard_map/ppermute | solution.py:785
  214.4 2.2 %collective-permute-done.32.p2_ref = f32[8,96]{1,0:T(8,128)S(1)} collective-permute-done((f32[8,96]{1,0:T(8,128)S(1)}, f32[8,96]{1,0:T(8,128)S(1)}, u32[]{:S(2)}, u32[]{:S(2)}) %collective-permute-start.32) | collective-permute-done | bytes 3104 | tf_op jit(solution)/shard_map/ppermute | solution.py:785
  (83 shorter events, 12.3 us)
Async XLA Ops:
  0.7 49.4 %copy-start = (bf16[2,768]{1,0:T(2,128)(2,1)S(1)}, bf16[2,768]{1,0:T(2,128)(2,1)}, u32[]{:S(2)}) copy-start(bf16[2,768]{1,0:T(2,128)(2,1)} %param.19) | copy-start | bytes 9220
  0.7 10.5 %copy-start.7 = (bf16[2,256,768]{2,1,0:T(8,128)(2,1)S(1)}, bf16[2,256,768]{2,1,0:T(8,128)(2,1)}, u32[]{:S(2)}) copy-start(bf16[2,256,768]{2,1,0:T(8,128)(2,1)} %param.35) | copy-start | bytes 2359300
  3.0 10.8 %collective-permute-start.2 = (bf16[104,768]{1,0:T(8,128)(2,1)}, bf16[104,768]{1,0:T(8,128)(2,1)S(1)}, u32[]{:S(2)}, u32[]{:S(2)}) collective-permute-start(bf16[104,768]{1,0:T(8,128)(2,1)} %get-tuple-element.144), channel_id=1, source_target_pairs={{24,0},{0,8},{8,16},{16,24},{25,1},{1,9},{9,17},{17,25},{26,2},{2,... | collective-permute-start | bytes 479240 | tf_op jit(solution)/shard_map/ppermute | solution.py:433
  6.1 13.3 %collective-permute-start.1 = (bf16[104,768]{1,0:T(8,128)(2,1)}, bf16[104,768]{1,0:T(8,128)(2,1)S(1)}, u32[]{:S(2)}, u32[]{:S(2)}) collective-permute-start(bf16[104,768]{1,0:T(8,128)(2,1)} %get-tuple-element.144), channel_id=1, source_target_pairs={{16,0},{24,8},{0,16},{8,24},{17,1},{25,9},{1,17},{9,25},{18,2},{26... | collective-permute-start | bytes 479240 | tf_op jit(solution)/shard_map/ppermute | solution.py:433
  8.6 10.7 %collective-permute-start = (bf16[104,768]{1,0:T(8,128)(2,1)}, bf16[104,768]{1,0:T(8,128)(2,1)S(1)}, u32[]{:S(2)}, u32[]{:S(2)}) collective-permute-start(bf16[104,768]{1,0:T(8,128)(2,1)} %get-tuple-element.144), channel_id=1, source_target_pairs={{8,0},{16,8},{24,16},{0,24},{9,1},{17,9},{25,17},{1,25},{10,2},{18... | collective-permute-start | bytes 479240 | tf_op jit(solution)/shard_map/ppermute | solution.py:433
  11.3 8.1 %copy-start.12 = (bf16[104,768]{1,0:T(8,128)(2,1)S(1)}, bf16[104,768]{1,0:T(8,128)(2,1)}, u32[]{:S(2)}) copy-start(bf16[104,768]{1,0:T(8,128)(2,1)} %get-tuple-element.144) | copy-start | bytes 479236
  12.3 7.2 %copy-start.6 = (bf16[512,768]{1,0:T(8,128)(2,1)}, bf16[512,768]{1,0:T(8,128)(2,1)S(1)}, u32[]{:S(2)}) copy-start(bf16[512,768]{1,0:T(8,128)(2,1)S(1)} %get-tuple-element.265.refs_0_.s0.c0) | copy-start | bytes 2359300
  12.3 18.8 %collective-permute-start.3 = (bf16[512,768]{1,0:T(8,128)(2,1)}, bf16[512,768]{1,0:T(8,128)(2,1)}, u32[]{:S(2)}, u32[]{:S(2)}) collective-permute-start(bf16[512,768]{1,0:T(8,128)(2,1)} %get-tuple-element.264), channel_id=1, source_target_pairs={{0,2},{2,0},{1,3},{3,1},{4,6},{6,4},{5,7},{7,5},{8,10},{10,8},{9,1... | collective-permute-start | bytes 2359304 | tf_op jit(solution)/shard_map/ppermute | solution.py:421
  13.8 17.2 %collective-permute-start.4 = (bf16[512,768]{1,0:T(8,128)(2,1)S(1)}, bf16[512,768]{1,0:T(8,128)(2,1)}, u32[]{:S(2)}, u32[]{:S(2)}) collective-permute-start(bf16[512,768]{1,0:T(8,128)(2,1)S(1)} %get-tuple-element.265.refs_0_.s0.c0), channel_id=1, source_target_pairs={{0,1},{1,0},{2,3},{3,2},{4,5},{5,4},{6,7},{7,6},{8,9},{9,8},{10,11... | collective-permute-start | bytes 2359304 | tf_op jit(solution)/shard_map/ppermute | solution.py:429
  19.4 38.7 %all-to-all-start = ((bf16[4,192,768]{2,1,0:T(8,128)(2,1)}), bf16[4,192,768]{2,1,0:T(8,128)(2,1)S(1)}, u32[]{:S(2)}, u32[]{:S(2)}) async-start(bf16[4,192,768]{2,1,0:T(8,128)(2,1)} %get-tuple-element.153), calls=%async_computation | async-start | bytes 2359296 | tf_op jit(solution)/shard_map/all_to_all | solution.py:438
  31.0 14.5 %collective-permute-start.6 = (bf16[4,104,768]{2,1,0:T(8,128)(2,1)S(1)}, bf16[4,104,768]{2,1,0:T(8,128)(2,1)}, u32[]{:S(2)}, u32[]{:S(2)}) collective-permute-start(bf16[4,104,768]{2,1,0:T(8,128)(2,1)S(1)} %pad_maximum_fusion.1.refs_5_), channel_id=1, source_target_pairs={{0,4},{4,0},{1,5},{5,1},{2,6},{6,2},{3,7},{7,3},{8,12},{12,8},{9,1... | collective-permute-start | bytes 1916936 | tf_op jit(solution)/shard_map/ppermute | solution.py:425
  32.5 14.1 %collective-permute-start.7 = (bf16[4,104,768]{2,1,0:T(8,128)(2,1)S(1)}, bf16[4,104,768]{2,1,0:T(8,128)(2,1)S(1)}, u32[]{:S(2)}, u32[]{:S(2)}) collective-permute-start(bf16[4,104,768]{2,1,0:T(8,128)(2,1)S(1)} %pad_maximum_fusion.1.refs_5_), channel_id=1, source_target_pairs={{0,2},{2,0},{1,3},{3,1},{4,6},{6,4},{5,7},{7,5},{8,10},{10,8},{9,1... | collective-permute-start | bytes 1916936 | tf_op jit(solution)/shard_map/ppermute | solution.py:421
  34.0 16.0 %collective-permute-start.5 = (bf16[512,768]{1,0:T(8,128)(2,1)}, bf16[512,768]{1,0:T(8,128)(2,1)}, u32[]{:S(2)}, u32[]{:S(2)}) collective-permute-start(bf16[512,768]{1,0:T(8,128)(2,1)} %collective-permute-done.3.refs_1_.s1.c1), channel_id=1, source_target_pairs={{0,1},{1,0},{2,3},{3,2},{4,5},{5,4},{6,7},{7,6},{8,9},{9,8},{10,11... | collective-permute-start | bytes 2359304 | tf_op jit(solution)/shard_map/ppermute | solution.py:429
  46.6 3.5 %copy-start.2 = (bf16[4,104,768]{2,1,0:T(8,128)(2,1)}, bf16[4,104,768]{2,1,0:T(8,128)(2,1)S(1)}, u32[]{:S(2)}) copy-start(bf16[4,104,768]{2,1,0:T(8,128)(2,1)S(1)} %collective-permute-done.7.refs_1_) | copy-start | bytes 1916932
  47.8 7.9 %collective-permute-start.8 = (bf16[4,48,768]{2,1,0:T(8,128)(2,1)S(1)}, bf16[4,48,768]{2,1,0:T(8,128)(2,1)S(1)}, u32[]{:S(2)}, u32[]{:S(2)}) collective-permute-start(bf16[4,48,768]{2,1,0:T(8,128)(2,1)S(1)} %slice.33), channel_id=1, source_target_pairs={{0,2},{2,0},{1,3},{3,1},{4,6},{6,4},{5,7},{7,5},{8,10},{10,8},{9,1... | collective-permute-start | bytes 884744 | tf_op jit(solution)/shard_map/ppermute | solution.py:421
  49.4 8.1 %collective-permute-start.9 = (bf16[4,56,768]{2,1,0:T(8,128)(2,1)S(1)}, bf16[4,56,768]{2,1,0:T(8,128)(2,1)S(1)}, u32[]{:S(2)}, u32[]{:S(2)}) collective-permute-start(bf16[4,56,768]{2,1,0:T(8,128)(2,1)S(1)} %slice.34), channel_id=1, source_target_pairs={{0,4},{4,0},{1,5},{5,1},{2,6},{6,2},{3,7},{7,3},{8,12},{12,8},{9,1... | collective-permute-start | bytes 1032200 | tf_op jit(solution)/shard_map/ppermute | solution.py:425
  57.4 0.8 copy-start.4
  58.2 8.4 %copy-start.3 = (bf16[4,104,768]{2,1,0:T(8,128)(2,1)S(1)}, bf16[4,104,768]{2,1,0:T(8,128)(2,1)}, u32[]{:S(2)}) copy-start(bf16[4,104,768]{2,1,0:T(8,128)(2,1)} %copy-done.2) | copy-start | bytes 1916932
  58.2 8.4 %copy-start.5 = (bf16[4,56,768]{2,1,0:T(8,128)(2,1)S(1)}, bf16[4,56,768]{2,1,0:T(8,128)(2,1)}, u32[]{:S(2)}) copy-start(bf16[4,56,768]{2,1,0:T(8,128)(2,1)} %copy-done.4) | copy-start | bytes 1032196
  58.2 23.8 %collective-permute-start.10 = (bf16[4,192,768]{2,1,0:T(8,128)(2,1)S(1)}, bf16[4,192,768]{2,1,0:T(8,128)(2,1)S(1)}, u32[]{:S(2)}, u32[]{:S(2)}) collective-permute-start(bf16[4,192,768]{2,1,0:T(8,128)(2,1)S(1)} %all-to-all-done.w_oo), channel_id=1, source_target_pairs={{0,4},{4,0},{1,5},{5,1},{2,6},{6,2},{3,7},{7,3},{8,12},{12,8},{9,1... | collective-permute-start | bytes 3538952 | tf_op jit(solution)/shard_map/ppermute | solution.py:425
  58.2 23.8 %collective-permute-start.11 = (bf16[4,192,768]{2,1,0:T(8,128)(2,1)S(1)}, bf16[4,192,768]{2,1,0:T(8,128)(2,1)S(1)}, u32[]{:S(2)}, u32[]{:S(2)}) collective-permute-start(bf16[4,192,768]{2,1,0:T(8,128)(2,1)S(1)} %all-to-all-done.w_oo), channel_id=1, source_target_pairs={{0,2},{2,0},{1,3},{3,1},{4,6},{6,4},{5,7},{7,5},{8,10},{10,8},{9,1... | collective-permute-start | bytes 3538952 | tf_op jit(solution)/shard_map/ppermute | solution.py:421
  82.0 3.4 %collective-permute-start.12 = (bf16[1024,768]{1,0:T(8,128)(2,1)S(1)}, bf16[1024,768]{1,0:T(8,128)(2,1)S(1)}, u32[]{:S(2)}, u32[]{:S(2)}) collective-permute-start(bf16[1024,768]{1,0:T(8,128)(2,1)S(1)} %shard_map.318.a0_ref), channel_id=1, source_target_pairs={{0,1},{1,0},{2,3},{3,2},{4,5},{5,4},{6,7},{7,6},{8,9},{9,8},{10,11... | collective-permute-start | bytes 4718600 | tf_op jit(solution)/shard_map/ppermute | solution.py:429
  82.0 15.8 %collective-permute-start.13 = (bf16[4,96,768]{2,1,0:T(8,128)(2,1)S(1)}, bf16[4,96,768]{2,1,0:T(8,128)(2,1)S(1)}, u32[]{:S(2)}, u32[]{:S(2)}) collective-permute-start(bf16[4,96,768]{2,1,0:T(8,128)(2,1)S(1)} %slice.35), channel_id=1, source_target_pairs={{0,2},{2,0},{1,3},{3,1},{4,6},{6,4},{5,7},{7,5},{8,10},{10,8},{9,1... | collective-permute-start | bytes 1769480 | tf_op jit(solution)/shard_map/ppermute | solution.py:421
  83.3 15.5 %collective-permute-start.14 = (bf16[4,96,768]{2,1,0:T(8,128)(2,1)S(1)}, bf16[4,96,768]{2,1,0:T(8,128)(2,1)S(1)}, u32[]{:S(2)}, u32[]{:S(2)}) collective-permute-start(bf16[4,96,768]{2,1,0:T(8,128)(2,1)S(1)} %slice.36), channel_id=1, source_target_pairs={{0,4},{4,0},{1,5},{5,1},{2,6},{6,2},{3,7},{7,3},{8,12},{12,8},{9,1... | collective-permute-start | bytes 1769480 | tf_op jit(solution)/shard_map/ppermute | solution.py:425
  98.8 14.6 %collective-permute-start.16 = (bf16[4,96,768]{2,1,0:T(8,128)(2,1)S(1)}, bf16[4,96,768]{2,1,0:T(8,128)(2,1)S(1)}, u32[]{:S(2)}, u32[]{:S(2)}) collective-permute-start(bf16[4,96,768]{2,1,0:T(8,128)(2,1)S(1)} %get-tuple-element.185), channel_id=1, source_target_pairs={{0,4},{4,0},{1,5},{5,1},{2,6},{6,2},{3,7},{7,3},{8,12},{12,8},{9,1... | collective-permute-start | bytes 1769480 | tf_op jit(solution)/shard_map/ppermute | solution.py:425
  113.4 5.9 %collective-permute-start.17 = (bf16[1024,768]{1,0:T(8,128)(2,1)S(1)}, bf16[1024,768]{1,0:T(8,128)(2,1)S(1)}, u32[]{:S(2)}, u32[]{:S(2)}) collective-permute-start(bf16[1024,768]{1,0:T(8,128)(2,1)S(1)} %get-tuple-element.186.g0_ref), channel_id=1, source_target_pairs={{0,1},{1,0},{2,3},{3,2},{4,5},{5,4},{6,7},{7,6},{8,9},{9,8},{10,11... | collective-permute-start | bytes 4718600 | tf_op jit(solution)/shard_map/ppermute | solution.py:429
  113.4 4.5 %collective-permute-start.15 = (bf16[512,768]{1,0:T(8,128)(2,1)S(1)}, bf16[512,768]{1,0:T(8,128)(2,1)S(1)}, u32[]{:S(2)}, u32[]{:S(2)}) collective-permute-start(bf16[512,768]{1,0:T(8,128)(2,1)S(1)} %get-tuple-element.179), channel_id=1, source_target_pairs={{0,1},{1,0},{2,3},{3,2},{4,5},{5,4},{6,7},{7,6},{8,9},{9,8},{10,11... | collective-permute-start | bytes 2359304 | tf_op jit(solution)/shard_map/ppermute | solution.py:429
  113.9 15.2 %collective-permute-start.18 = (bf16[4,96,768]{2,1,0:T(8,128)(2,1)S(1)}, bf16[4,96,768]{2,1,0:T(8,128)(2,1)S(1)}, u32[]{:S(2)}, u32[]{:S(2)}) collective-permute-start(bf16[4,96,768]{2,1,0:T(8,128)(2,1)S(1)} %get-tuple-element.192), channel_id=1, source_target_pairs={{0,4},{4,0},{1,5},{5,1},{2,6},{6,2},{3,7},{7,3},{8,12},{12,8},{9,1... | collective-permute-start | bytes 1769480 | tf_op jit(solution)/shard_map/ppermute | solution.py:425
  115.1 15.0 %collective-permute-start.19 = (bf16[4,96,768]{2,1,0:T(8,128)(2,1)S(1)}, bf16[4,96,768]{2,1,0:T(8,128)(2,1)S(1)}, u32[]{:S(2)}, u32[]{:S(2)}) collective-permute-start(bf16[4,96,768]{2,1,0:T(8,128)(2,1)S(1)} %get-tuple-element.193), channel_id=1, source_target_pairs={{0,2},{2,0},{1,3},{3,1},{4,6},{6,4},{5,7},{7,5},{8,10},{10,8},{9,1... | collective-permute-start | bytes 1769480 | tf_op jit(solution)/shard_map/ppermute | solution.py:421
  130.2 16.6 %collective-permute-start.20 = (bf16[4,96,768]{2,1,0:T(8,128)(2,1)S(1)}, bf16[4,96,768]{2,1,0:T(8,128)(2,1)S(1)}, u32[]{:S(2)}, u32[]{:S(2)}) collective-permute-start(bf16[4,96,768]{2,1,0:T(8,128)(2,1)S(1)} %add.80), channel_id=1, source_target_pairs={{0,2},{2,0},{1,3},{3,1},{4,6},{6,4},{5,7},{7,5},{8,10},{10,8},{9,1... | collective-permute-start | bytes 1769480 | tf_op jit(solution)/shard_map/ppermute | solution.py:421
  131.1 15.8 %collective-permute-start.21 = (bf16[4,96,768]{2,1,0:T(8,128)(2,1)S(1)}, bf16[4,96,768]{2,1,0:T(8,128)(2,1)S(1)}, u32[]{:S(2)}, u32[]{:S(2)}) collective-permute-start(bf16[4,96,768]{2,1,0:T(8,128)(2,1)S(1)} %add.81), channel_id=1, source_target_pairs={{0,4},{4,0},{1,5},{5,1},{2,6},{6,2},{3,7},{7,3},{8,12},{12,8},{9,1... | collective-permute-start | bytes 1769480 | tf_op jit(solution)/shard_map/ppermute | solution.py:425
  146.8 13.6 %collective-permute-start.22 = (bf16[4,96,768]{2,1,0:T(8,128)(2,1)S(1)}, bf16[4,96,768]{2,1,0:T(8,128)(2,1)S(1)}, u32[]{:S(2)}, u32[]{:S(2)}) collective-permute-start(bf16[4,96,768]{2,1,0:T(8,128)(2,1)S(1)} %get-tuple-element.213), channel_id=1, source_target_pairs={{0,2},{2,0},{1,3},{3,1},{4,6},{6,4},{5,7},{7,5},{8,10},{10,8},{9,1... | collective-permute-start | bytes 1769480 | tf_op jit(solution)/shard_map/ppermute | solution.py:421
  148.0 13.4 %collective-permute-start.23 = (bf16[4,96,768]{2,1,0:T(8,128)(2,1)}, bf16[4,96,768]{2,1,0:T(8,128)(2,1)S(1)}, u32[]{:S(2)}, u32[]{:S(2)}) collective-permute-start(bf16[4,96,768]{2,1,0:T(8,128)(2,1)} %get-tuple-element.214), channel_id=1, source_target_pairs={{0,4},{4,0},{1,5},{5,1},{2,6},{6,2},{3,7},{7,3},{8,12},{12,8},{9,1... | collective-permute-start | bytes 1769480 | tf_op jit(solution)/shard_map/ppermute | solution.py:425
  161.5 1.0 copy-start.9
  161.5 13.2 %collective-permute-start.24 = (bf16[256,768]{1,0:T(8,128)(2,1)}, bf16[256,768]{1,0:T(8,128)(2,1)}, u32[]{:S(2)}, u32[]{:S(2)}) collective-permute-start(bf16[256,768]{1,0:T(8,128)(2,1)} %get-tuple-element.222), channel_id=1, source_target_pairs={{0,2},{2,0},{1,3},{3,1},{4,6},{6,4},{5,7},{7,5},{8,10},{10,8},{9,1... | collective-permute-start | bytes 1179656 | tf_op jit(solution)/shard_map/ppermute | solution.py:421
  163.6 30.2 %all-to-all-start.1 = ((bf16[4,192,768]{2,1,0:T(8,128)(2,1)}), bf16[4,192,768]{2,1,0:T(8,128)(2,1)}, u32[]{:S(2)}, u32[]{:S(2)}) async-start(bf16[4,192,768]{2,1,0:T(8,128)(2,1)} %pad_maximum_fusion), calls=%async_computation.1 | async-start | bytes 2359296 | tf_op jit(solution)/shard_map/all_to_all | solution.py:438
  168.2 7.5 %copy-start.8 = (bf16[4,96,768]{2,1,0:T(8,128)(2,1)S(1)}, bf16[4,96,768]{2,1,0:T(8,128)(2,1)}, u32[]{:S(2)}) copy-start(bf16[4,96,768]{2,1,0:T(8,128)(2,1)} %get-tuple-element.235) | copy-start | bytes 1769476
  168.2 7.5 %copy-start.10 = (bf16[4,96,768]{2,1,0:T(8,128)(2,1)S(1)}, bf16[4,96,768]{2,1,0:T(8,128)(2,1)}, u32[]{:S(2)}) copy-start(bf16[4,96,768]{2,1,0:T(8,128)(2,1)} %copy-done.9) | copy-start | bytes 1769476
  174.7 3.5 %collective-permute-start.25 = (bf16[1024,768]{1,0:T(8,128)(2,1)S(1)}, bf16[1024,768]{1,0:T(8,128)(2,1)}, u32[]{:S(2)}, u32[]{:S(2)}) collective-permute-start(bf16[1024,768]{1,0:T(8,128)(2,1)S(1)} %get-tuple-element.224.g0_ref), channel_id=1, source_target_pairs={{0,1},{1,0},{2,3},{3,2},{4,5},{5,4},{6,7},{7,6},{8,9},{9,8},{10,11... | collective-permute-start | bytes 4718600 | tf_op jit(solution)/shard_map/ppermute | solution.py:429
  174.7 16.1 %collective-permute-start.27 = (bf16[4,96,768]{2,1,0:T(8,128)(2,1)}, bf16[4,96,768]{2,1,0:T(8,128)(2,1)}, u32[]{:S(2)}, u32[]{:S(2)}) collective-permute-start(bf16[4,96,768]{2,1,0:T(8,128)(2,1)} %get-tuple-element.234), channel_id=1, source_target_pairs={{0,4},{4,0},{1,5},{5,1},{2,6},{6,2},{3,7},{7,3},{8,12},{12,8},{9,1... | collective-permute-start | bytes 1769480 | tf_op jit(solution)/shard_map/ppermute | solution.py:425
  175.8 16.3 %collective-permute-start.28 = (bf16[4,96,768]{2,1,0:T(8,128)(2,1)S(1)}, bf16[4,96,768]{2,1,0:T(8,128)(2,1)}, u32[]{:S(2)}, u32[]{:S(2)}) collective-permute-start(bf16[4,96,768]{2,1,0:T(8,128)(2,1)S(1)} %add.82), channel_id=1, source_target_pairs={{0,2},{2,0},{1,3},{3,1},{4,6},{6,4},{5,7},{7,5},{8,10},{10,8},{9,1... | collective-permute-start | bytes 1769480 | tf_op jit(solution)/shard_map/ppermute | solution.py:421
  184.6 10.3 %copy-start.11 = (bf16[4,96,768]{2,1,0:T(8,128)(2,1)S(1)}, bf16[4,96,768]{2,1,0:T(8,128)(2,1)}, u32[]{:S(2)}) copy-start(bf16[4,96,768]{2,1,0:T(8,128)(2,1)} %get-tuple-element.246) | copy-start | bytes 1769476
  184.6 9.2 %collective-permute-start.26 = (f32[2,4,16,96]{3,2,1,0:T(8,128)S(1)}, f32[2,4,16,96]{3,2,1,0:T(8,128)S(1)}, u32[]{:S(2)}, u32[]{:S(2)}) collective-permute-start(f32[2,4,16,96]{3,2,1,0:T(8,128)S(1)} %get-tuple-element.232), channel_id=1, source_target_pairs={{0,2},{2,0},{1,3},{3,1},{4,6},{6,4},{5,7},{7,5},{8,10},{10,8},{9,1... | collective-permute-start | bytes 147464 | tf_op jit(solution)/shard_map/ppermute | solution.py:421
  193.8 17.1 %collective-permute-start.29 = (bf16[256,768]{1,0:T(8,128)(2,1)}, bf16[256,768]{1,0:T(8,128)(2,1)S(1)}, u32[]{:S(2)}, u32[]{:S(2)}) collective-permute-start(bf16[256,768]{1,0:T(8,128)(2,1)} %get-tuple-element.243), channel_id=1, source_target_pairs={{0,2},{2,0},{1,3},{3,1},{4,6},{6,4},{5,7},{7,5},{8,10},{10,8},{9,1... | collective-permute-start | bytes 1179656 | tf_op jit(solution)/shard_map/ppermute | solution.py:421
  197.1 19.5 %all-to-all-start.2 = ((bf16[4,96,768]{2,1,0:T(8,128)(2,1)}), bf16[4,96,768]{2,1,0:T(8,128)(2,1)S(1)}, u32[]{:S(2)}, u32[]{:S(2)}) async-start(bf16[4,96,768]{2,1,0:T(8,128)(2,1)} %add_add_fusion), calls=%async_computation.2 | async-start | bytes 1179648 | tf_op jit(solution)/shard_map/all_to_all | solution.py:438
  201.1 3.9 %collective-permute-start.30 = (f32[4,8,96]{2,1,0:T(8,128)S(1)}, f32[4,8,96]{2,1,0:T(8,128)S(1)}, u32[]{:S(2)}, u32[]{:S(2)}) collective-permute-start(f32[4,8,96]{2,1,0:T(8,128)S(1)} %slice_bitcast_fusion.1), channel_id=1, source_target_pairs={{0,4},{4,0},{1,5},{5,1},{2,6},{6,2},{3,7},{7,3},{8,12},{12,8},{9,1... | collective-permute-start | bytes 36872 | tf_op jit(solution)/shard_map/ppermute | solution.py:425
  202.0 15.4 %copy-start.1 = (bf16[2,768]{1,0:T(2,128)(2,1)S(1)}, bf16[2,768]{1,0:T(2,128)(2,1)}, u32[]{:S(2)}) copy-start(bf16[2,768]{1,0:T(2,128)(2,1)} %param.19) | copy-start | bytes 9220
  205.0 9.4 %collective-permute-start.31 = (f32[8,96]{1,0:T(8,128)S(1)}, f32[8,96]{1,0:T(8,128)S(1)}, u32[]{:S(2)}, u32[]{:S(2)}) collective-permute-start(f32[8,96]{1,0:T(8,128)S(1)} %get-tuple-element.270), channel_id=1, source_target_pairs={{0,8},{8,16},{16,24},{24,0},{1,9},{9,17},{17,25},{25,1},{2,10},{10... | collective-permute-start | bytes 9224 | tf_op jit(solution)/shard_map/ppermute | solution.py:785
  207.0 9.5 %collective-permute-start.32 = (f32[8,96]{1,0:T(8,128)S(1)}, f32[8,96]{1,0:T(8,128)S(1)}, u32[]{:S(2)}, u32[]{:S(2)}) collective-permute-start(f32[8,96]{1,0:T(8,128)S(1)} %get-tuple-element.269), channel_id=1, source_target_pairs={{0,16},{8,24},{16,0},{24,8},{1,17},{9,25},{17,1},{25,9},{2,18},{10... | collective-permute-start | bytes 9224 | tf_op jit(solution)/shard_map/ppermute | solution.py:785
  209.4 7.2 %collective-permute-start.33 = (f32[8,96]{1,0:T(8,128)S(1)}, f32[8,96]{1,0:T(8,128)S(1)}, u32[]{:S(2)}, u32[]{:S(2)}) collective-permute-start(f32[8,96]{1,0:T(8,128)S(1)} %get-tuple-element.268), channel_id=1, source_target_pairs={{0,24},{8,0},{16,8},{24,16},{1,25},{9,1},{17,9},{25,17},{2,26},{10... | collective-permute-start | bytes 9224 | tf_op jit(solution)/shard_map/ppermute | solution.py:785
